TPU v7x, 32 devices: a whole 2x2x4 slice. The times are simulated.
32 devices in a mesh: rows: 8 (over z, y), grp: 4 (over x, core).
Axes of the slice: x: 2, y: 2, z: 4, core: 2. Of those that a mesh axis runs over, the one named last changes fastest.
Arguments:
- features: bfloat16 [4096, 512], P(('rows', 'grp')), may hold values from -6 to 6
- tile_entries: bfloat16 [64, 64, 1024], P(('rows', 'grp'))
- tile_columns: int32 [64, 16], P(('rows', 'grp')), may hold values from 0 to 63, as said below
- tiles_per_row: int32 [64], P(('rows', 'grp')), may hold values from 1 to 16, as said below
- rev_vals: bfloat16 [64, 64, 1024], P(('rows', 'grp'))
- rev_cols: int32 [64, 16], P(('rows', 'grp')), may hold values from 0 to 63, as said below
- rev_count: int32 [64], P(('rows', 'grp')), may hold values from 1 to 16, as said below
- w_first: bfloat16 [512, 512], replicated, may hold values from -0.25 to 0.25
- w_second: bfloat16 [512, 512], replicated, may hold values from -0.25 to 0.25
- cotangent: bfloat16 [4096, 512], P(('rows', 'grp')), may hold values from -0.09375 to 0.09375
Outputs:
- z_out: bfloat16 [4096, 512], P(('rows', 'grp'))
- grad_first: float32 [512, 512], replicated
- grad_second: float32 [512, 512], replicated
Inputs may be any that keep to these rules, and one draw needn't show every extreme that they name: `tile_columns`: within each block row the 16 slots name distinct block columns; for each slot s, the block columns named in slot s over all block rows are all different. `tiles_per_row`: some block row has exactly 16 tiles. `rev_cols`: within each block column the slots name distinct block rows; the live transposed slots of block column c hold exactly the transposes of the live tiles of A in block column c. `rev_count`: some block column has exactly 16 tiles.
All inputs are finite; a program needn't handle non-finite values.
Results may differ from a plain program's by a relative error of at most 0.0062.
Values may be sent and summed in bfloat16 or wider, within the bound.
No kernel may reach another device: no remote copies, remote signals or barrier semaphores. Data moves between devices by JAX's collectives and lax.ppermute only.
A program may use at most 128 MiB of HBM per device.

v0:
```python
import jax
import jax.numpy as jnp
from jax import lax
from jax.sharding import PartitionSpec as P


def active_mask(columns, counts):
    return lax.broadcasted_iota(jnp.int32, columns.shape, 1) < counts[:, None]


def aggregate(panel_vals, strip_columns, strip_count, everyone, own_rows):
    blocks, size_block, span_width = panel_vals.shape
    slot_count = span_width // size_block
    channels = everyone.shape[1]
    block_table = everyone.reshape(-1, size_block, channels)
    weights = active_mask(strip_columns, strip_count).astype(everyone.dtype)
    picked = (block_table[strip_columns] * weights[:, :, None, None]).reshape(
        blocks, slot_count * size_block, channels
    )
    summed_rows = jnp.einsum("bik,bkc->bic", panel_vals, picked, preferred_element_type=jnp.float32)
    return summed_rows.reshape(blocks * size_block, channels) + own_rows.astype(jnp.float32)


def spread_terms(panel_vals, strip_columns, strip_count, grad_rows):
    blocks, size_block, span_width = panel_vals.shape
    slot_count = span_width // size_block
    channels = grad_rows.shape[1]
    products = jnp.einsum(
        "bik,bic->bkc",
        panel_vals,
        grad_rows.reshape(blocks, size_block, channels),
        preferred_element_type=jnp.float32,
    )
    products = products.reshape(blocks * slot_count, size_block, channels)
    targets = strip_columns.reshape(-1)
    slot_active = active_mask(strip_columns, strip_count).reshape(-1)

    def term_rows(first_row, row_count):
        segment_ids = row_count // size_block
        slot_offset = targets - first_row // size_block
        inside_bound = slot_active & (slot_offset >= 0) & (slot_offset < segment_ids)
        labels = jnp.where(inside_bound, slot_offset, segment_ids)
        summed_rows = jax.ops.segment_sum(products, labels, num_segments=segment_ids + 1)
        return summed_rows[:segment_ids].reshape(row_count, channels)

    return term_rows


def silu_slope(values):
    sigmoid_part = jax.nn.sigmoid(values)
    return sigmoid_part * (1.0 + values * (1.0 - sigmoid_part))


def to_columns(row_block):
    return lax.all_to_all(row_block, "grp", split_axis=1, concat_axis=0, tiled=True)


def mix_columns(column_block, panel_vals, strip_columns, strip_count):
    everyone = lax.all_gather(column_block, "rows", axis=0, tiled=True)
    return aggregate(panel_vals, strip_columns, strip_count, everyone, column_block)


def shards(
    features,
    tile_entries,
    tile_columns,
    tiles_per_row,
    rev_vals,
    rev_cols,
    rev_count,
    w_first,
    w_second,
    cotangent,
):
    panel_vals, strip_columns, strip_count = (
        lax.all_gather(tile_entries, "grp", axis=0, tiled=True),
        lax.all_gather(tile_columns, "grp", axis=0, tiled=True),
        lax.all_gather(tiles_per_row, "grp", axis=0, tiled=True),
    )

    def propagate(row_block):
        column_block = to_columns(row_block)
        summed_rows = mix_columns(column_block, panel_vals, strip_columns, strip_count).astype(
            jnp.bfloat16
        )
        return lax.all_to_all(summed_rows, "grp", split_axis=0, concat_axis=1, tiled=True)

    mixed_first = propagate(features)
    pre_first = jnp.dot(mixed_first, w_first, preferred_element_type=jnp.float32)
    hidden = jax.nn.silu(pre_first).astype(jnp.bfloat16)
    mixed_second = propagate(hidden)
    z_out = jnp.dot(mixed_second, w_second, preferred_element_type=jnp.float32).astype(jnp.bfloat16)
    local_second = jnp.einsum(
        "nh,nk->hk", mixed_second, cotangent, preferred_element_type=jnp.float32
    )
    grad_second = lax.psum(local_second, ("rows", "grp"))
    back_second = jnp.dot(cotangent, w_second.T, preferred_element_type=jnp.float32).astype(
        jnp.bfloat16
    )
    column_block = to_columns(back_second)
    term_rows = spread_terms(panel_vals, strip_columns, strip_count, column_block)
    summed_rows = lax.psum_scatter(
        term_rows(jnp.int32(0), column_block.shape[0] * lax.axis_size("rows")),
        "rows",
        scatter_dimension=0,
        tiled=True,
    )
    summed_rows = summed_rows + column_block.astype(jnp.float32)
    back_hidden = lax.all_to_all(summed_rows, "grp", split_axis=0, concat_axis=1, tiled=True)
    back_first = (back_hidden * silu_slope(pre_first)).astype(jnp.bfloat16)
    local_first = jnp.einsum(
        "nh,nk->hk", mixed_first, back_first, preferred_element_type=jnp.float32
    )
    grad_first = lax.psum(local_first, ("rows", "grp"))
    return (z_out, grad_first, grad_second)


def solution(mesh):
    placed = (
        P(("rows", "grp"), None),
        P(("rows", "grp"), None, None),
        P(("rows", "grp"), None),
        P(("rows", "grp")),
        P(("rows", "grp"), None, None),
        P(("rows", "grp"), None),
        P(("rows", "grp")),
        P(),
        P(),
        P(("rows", "grp"), None),
    )
    return jax.shard_map(
        shards,
        mesh=mesh,
        in_specs=placed,
        out_specs=(P(("rows", "grp"), None), P(), P()),
        check_vma=False,
    )
```

profile of v0, /device:TPU:0, one launch (start us, length us, event | category | flops | bytes accessed | tf_op | source)
XLA Modules:
  0.0 358.9 jit_solution(1867615093499603882)
XLA Ops:
  7.2 1.1 copy.33
  8.3 8.6 %all_to_all.105 = bf16[128,4,128]{0,2,1:T(8,128)(2,1)S(1)} all-to-all(bf16[128,4,128]{0,2,1:T(8,128)(2,1)S(1)} %bitcast.96), channel_id=1, replica_groups=mesh['rows'=8,'grp'=4] {'grp'}, dimensions={1} | all-to-all | bytes 262144 | tf_op jit(solution)/shard_map/all_to_all | solution.py:55
  16.9 0.8 copy.34
  17.8 0.7 all-gather.7.cloned.1.call-update
  18.5 1.2 dynamic-slice
  20.4 0.9 dynamic-update-slice
  21.3 4.3 %all-reduce = s32[8]{0:T(128)S(1)} all-reduce(s32[8]{0:T(128)S(1)} %dynamic-update-slice), channel_id=1, replica_groups=mesh['rows'=8,'grp'=4] {'grp'}, use_global_device_ids=true, to_apply=%add | all-reduce | flops 8 | bytes 64
  25.6 5.3 %all-gather = s32[4,2,16]{2,1,0:T(2,128)S(1)} all-gather(s32[1,2,16]{2,1,0:T(2,128)} %bitcast.98), channel_id=1, replica_groups=mesh['rows'=8,'grp'=4] {'grp'}, dimensions={0}, use_global_device_ids=true | all-gather | bytes 640 | tf_op jit(solution)/shard_map/all_gather | solution.py:77
  30.8 0.1 reshape.145
  31.0 0.1 mul.33
  31.1 0.1 mul.34
  31.2 27.2 %all-gather.5.cloned.1.call-done = bf16[4096,128]{1,0:T(8,128)(2,1)} async-done(((bf16[512,128]{1,0:T(8,128)(2,1)}), bf16[4096,128]{1,0:T(8,128)(2,1)}) %all-gather.5.cloned.1.call-update) | async-done | bytes 1048592 | tf_op jit(solution)/shard_map/all_gather | solution.py:59
  58.4 2.2 gather_fusion
  60.6 2.2 bitcast_multiply_fusion.1
  62.8 12.7 %all-gather.7.cloned.1.call-done = bf16[8,64,1024]{2,1,0:T(8,128)(2,1)} async-done(((bf16[2,64,1024]{2,1,0:T(8,128)(2,1)}), bf16[8,64,1024]{2,1,0:T(8,128)(2,1)}) %all-gather.7.cloned.1.call-update) | async-done | bytes 1048592 | tf_op jit(solution)/shard_map/all_gather | solution.py:76
  75.5 2.4 fusion.11
  77.9 0.1 copy.35
  78.1 7.2 %all_to_all.106 = bf16[4,128,128]{1,2,0:T(8,128)(2,1)S(1)} all-to-all(bf16[4,128,128]{1,2,0:T(8,128)(2,1)S(1)} %add_convert_fusion.1), channel_id=1, replica_groups=mesh['rows'=8,'grp'=4] {'grp'}, dimensions={0} | all-to-all | bytes 262144 | tf_op jit(solution)/shard_map/all_to_all | solution.py:86
  85.3 0.2 fusion.9
  85.6 7.7 %all_to_all.107 = bf16[128,4,128]{2,0,1:T(8,128)(2,1)} all-to-all(bf16[128,4,128]{2,0,1:T(8,128)(2,1)S(1)} %copy_bitcast_fusion.1), channel_id=1, replica_groups=mesh['rows'=8,'grp'=4] {'grp'}, dimensions={1} | all-to-all | bytes 262144 | tf_op jit(solution)/shard_map/all_to_all | solution.py:55
  93.3 0.3 fusion
  93.6 0.7 copy.48
  94.3 3.3 all-to-all-start.4
  97.7 0.1 reshape.138
  97.8 0.1 lt.51
  97.9 4.4 %all-to-all-done.4 = bf16[128,4,128]{2,0,1:T(8,128)(2,1)S(1)} async-done(((bf16[128,4,128]{2,0,1:T(8,128)(2,1)}), bf16[128,4,128]{2,0,1:T(8,128)(2,1)S(1)}, u32[]{:S(2)}, u32[]{:S(2)}) %all-to-all-start.4) | async-done | bytes 131104 | tf_op jit(solution)/shard_map/all_to_all | solution.py:55
  102.3 2.7 convolution_bitcast_fusion
  105.0 5.4 %copy.39 = f32[8,1024,128]{2,1,0:T(8,128)} copy(f32[8,1024,128]{1,2,0:T(8,128)} %convolution_bitcast_fusion) | data formatting | bytes 8388608 | tf_op jit(solution)/shard_map/bik,bic->bkc/dot_general | solution.py:28
  110.3 0.2 broadcast_in_dim.6
  110.6 13.6 %scatter_fusion = f32[65,64,128]{2,1,0:T(8,128)S(1)} fusion(f32[65,64,128]{2,1,0:T(8,128)S(1)} %broadcast_in_dim.6, s32[128]{0:T(128)S(1)} %fusion.6, f32[128,64,128]{2,1,0:T(8,128)} %bitcast.79), kind=kCustom, calls=%fused_computation.2 | custom fusion | flops 1048576 | bytes 12583424 | tf_op jit(solution)/shard_map/scatter-add | solution.py:43
  124.2 1.5 slice.8
  125.7 7.9 %all-gather.9.cloned.1.call-done = bf16[4096,128]{1,0:T(8,128)(2,1)} async-done(((bf16[512,128]{1,0:T(8,128)(2,1)}), bf16[4096,128]{1,0:T(8,128)(2,1)}) %all-gather.9.cloned.1.call-update) | async-done | bytes 1048592 | tf_op jit(solution)/shard_map/all_gather | solution.py:59
  133.6 2.2 gather_fusion.1
  135.8 1.6 bitcast_multiply_fusion
  137.4 0.5 fusion.12
  137.9 0.4 copy-done.3
  138.4 7.2 %all_to_all.108 = bf16[4,128,128]{2,1,0:T(8,128)(2,1)S(1)} all-to-all(bf16[4,128,128]{2,1,0:T(8,128)(2,1)S(1)} %add_convert_fusion), channel_id=1, replica_groups=mesh['rows'=8,'grp'=4] {'grp'}, dimensions={0} | all-to-all | bytes 262144 | tf_op jit(solution)/shard_map/all_to_all | solution.py:86
  145.5 0.1 copy.37
  145.7 58.1 %reduce-scatter.2.cloned.1.call-done = f32[512,128]{1,0:T(8,128)} async-done(((f32[4096,128]{1,0:T(8,128)}), f32[512,128]{1,0:T(8,128)}) %reduce-scatter.2.cloned.1.call-update) | async-done | bytes 262160 | tf_op jit(solution)/shard_map/reduce_scatter | solution.py:102
  203.7 1.7 convert_add_fusion
  205.4 3.4 all-to-all-start.5
  208.9 1.2 fusion.10
  210.1 4.7 %all-to-all-done.5 = f32[4,128,128]{2,1,0:T(8,128)S(1)} async-done(((f32[4,128,128]{2,1,0:T(8,128)}), f32[4,128,128]{2,1,0:T(8,128)S(1)}, u32[]{:S(2)}, u32[]{:S(2)}) %all-to-all-start.5) | async-done | bytes 262176 | tf_op jit(solution)/shard_map/all_to_all | solution.py:109
  214.8 1.3 fusion.2
  216.2 0.9 convolution_convert_fusion.1
  217.1 131.9 %all-reduce.4.cloned.1.call-done = (f32[512,512]{1,0:T(8,128)}, f32[512,512]{1,0:T(8,128)}) async-done(((f32[512,512]{1,0:T(8,128)}, f32[512,512]{1,0:T(8,128)}), (f32[512,512]{1,0:T(8,128)}, f32[512,512]{1,0:T(8,128)})) %all-reduce.4.cloned.1.call-update) | async-done | bytes 2097168 | tf_op jit(solution)/shard_map/psum | solution.py:114
  349.1 2.4 copy.53
  351.4 1.0 copy.54
  (30 shorter events, 0.5 us)
Async XLA Ops:
  7.2 86.1 %copy-start = (bf16[512,512]{1,0:T(8,128)(2,1)S(1)}, bf16[512,512]{1,0:T(8,128)(2,1)}, u32[]{:S(2)}) copy-start(bf16[512,512]{1,0:T(8,128)(2,1)} %param.15) | copy-start | bytes 1572868
  7.2 51.3 %all-gather.5.cloned.1.call-start = ((), (), s32[]{:S(2)}) async-start(), calls=%async_computation.7 | async-start | bytes 1179648 | tf_op jit(solution)/shard_map/all_gather | solution.py:59
  17.7 57.8 %all-gather.7.cloned.1.call-start = ((), (), s32[]{:S(2)}) async-start(), calls=%async_computation.8 | async-start | bytes 1310720 | tf_op jit(solution)/shard_map/all_gather | solution.py:76
  18.5 115.1 %all-gather.9.cloned.1.call-start = ((), (), s32[]{:S(2)}) async-start(), calls=%async_computation.9 | async-start | bytes 1179648 | tf_op jit(solution)/shard_map/all_gather | solution.py:59
  62.8 22.4 %copy-start.5 = (bf16[512,512]{1,0:T(8,128)(2,1)S(1)}, bf16[512,512]{1,0:T(8,128)(2,1)}, u32[]{:S(2)}) copy-start(bf16[512,512]{1,0:T(8,128)(2,1)} %param.14) | copy-start | bytes 1572868
  77.9 15.4 %copy-start.6 = (bf16[128,512]{1,0:T(8,128)(2,1)S(1)}, bf16[128,512]{1,0:T(8,128)(2,1)}, u32[]{:S(2)}) copy-start(bf16[128,512]{1,0:T(8,128)(2,1)} %param.16) | copy-start | bytes 393220
  77.9 24.3 %copy-start.1 = (bf16[8,64,1024]{2,1,0:T(8,128)(2,1)S(1)}, bf16[8,64,1024]{2,1,0:T(8,128)(2,1)}, u32[]{:S(2)}) copy-start(bf16[8,64,1024]{2,1,0:T(8,128)(2,1)} %all-gather.7.cloned.1.call-done) | copy-start | bytes 3145732
  94.3 7.9 %all-to-all-start.4 = ((bf16[128,4,128]{2,0,1:T(8,128)(2,1)}), bf16[128,4,128]{2,0,1:T(8,128)(2,1)S(1)}, u32[]{:S(2)}, u32[]{:S(2)}) async-start(bf16[128,4,128]{2,0,1:T(8,128)(2,1)} %bitcast.76), calls=%async_computation.4 | async-start | bytes 262144 | tf_op jit(solution)/shard_map/all_to_all | solution.py:55
  97.7 106.1 %reduce-scatter.2.cloned.1.call-start = ((), (), s32[]{:S(2)}) async-start(), calls=%async_computation.10 | async-start | bytes 2359296 | tf_op jit(solution)/shard_map/reduce_scatter | solution.py:102
  135.8 1.6 copy-start.2
  137.4 0.9 copy-start.3
  205.4 9.4 %all-to-all-start.5 = ((f32[4,128,128]{2,1,0:T(8,128)}), f32[4,128,128]{2,1,0:T(8,128)S(1)}, u32[]{:S(2)}, u32[]{:S(2)}) async-start(f32[4,128,128]{2,1,0:T(8,128)} %bitcast.28), calls=%async_computation.6 | async-start | bytes 524288 | tf_op jit(solution)/shard_map/all_to_all | solution.py:109
  208.8 140.2 %all-reduce.4.cloned.1.call-start = ((), (), s32[]{:S(2)}) async-start(), calls=%async_computation.11 | async-start | bytes 4194304 | tf_op jit(solution)/shard_map/psum | solution.py:114
  349.1 2.4 copy-start.4
Sparse Core Ops, SparseCore 0:
  17.9 40.5 all-gather.4
  60.0 15.4 all-gather.6
  93.4 40.1 all-gather.8
  137.0 66.7 reduce-scatter.1
  216.3 132.6 all-reduce.3
where the time goes:
time: 360 us; the launch traced here: 359 us
  waiting for transfers between devices  248 us (69%)
  blocking collectives  40.2 us (11%)
  local copies, waits for them, and re-layouts  20.5 us (6%)
  other arithmetic  19.4 us (5%)
  between operations  14.7 us (4%)
  matrix products  9.67 us (3%)
  starting transfers between devices  6.93 us (2%)
    psum x1, waiting for transfers between devices, shards(): grad_first = lax.psum(local_first, ('rows', 'grp'))  132 us
    reduce_scatter x1, waiting for transfers between devices, shards(): lax.psum_scatter(term_rows(jnp.int32(0), column_block.shape[0] * lax.axis...  58.1 us
    all_gather x2, waiting for transfers between devices, mix_columns(): everyone = lax.all_gather(column_block, 'rows', axis=0, tiled=True)  35.1 us
    all_to_all x2, blocking collectives, to_columns(): lax.all_to_all(row_block, 'grp', split_axis=1, concat_axis=0, tiled=True)  16.3 us
    all_to_all x2, blocking collectives, propagate(): lax.all_to_all(summed_rows, 'grp', split_axis=0, concat_axis=1, tiled=True)  14.3 us
    scatter-add x1, other arithmetic, term_rows(): jax.ops.segment_sum(products, labels, num_segments=segment_ids + 1)  13.6 us
    all_gather x1, waiting for transfers between devices, shards(): lax.all_gather(tile_entries, 'grp', axis=0, tiled=True)  12.7 us
  transfers between devices with their start and end apart: 7, of which 7 were waited for; matrix products, arithmetic and copies ran while one was open for 11% of the time, Pallas kernels for 0%

commit v1 on v0

v1 whole, which is shorter than its diff:
```python
import jax
import jax.numpy as jnp
from jax import lax
from jax.sharding import PartitionSpec as P

AXES = ("rows", "grp")


def aggregate(panel_vals, strip_columns, strip_count, everyone, own_rows):
    blocks, size_block, span_width = panel_vals.shape
    slot_count = span_width // size_block
    channels = everyone.shape[1]
    block_table = everyone.reshape(-1, size_block, channels)
    slot_ids = lax.broadcasted_iota(jnp.int32, strip_columns.shape, 1)
    weights = (slot_ids < strip_count[:, None]).astype(everyone.dtype)
    picked = (block_table[strip_columns] * weights[:, :, None, None]).reshape(
        blocks, slot_count * size_block, channels
    )
    summed_rows = jnp.einsum("bik,bkc->bic", panel_vals, picked, preferred_element_type=jnp.float32)
    return summed_rows.reshape(blocks * size_block, channels) + own_rows.astype(jnp.float32)


def shards(
    features,
    tile_entries,
    tile_columns,
    tiles_per_row,
    rev_vals,
    rev_cols,
    rev_count,
    w_first,
    w_second,
    cotangent,
):
    f32, bf16 = jnp.float32, jnp.bfloat16
    channels = features.shape[1]
    pair = jnp.concatenate([features, cotangent], axis=1)
    pair_all = lax.all_gather(pair, AXES, axis=0, tiled=True)
    mixed_own = aggregate(
        tile_entries, tile_columns, tiles_per_row, pair_all[:, :channels], features
    ).astype(bf16)
    spread_own = aggregate(
        rev_vals, rev_cols, rev_count, pair_all[:, channels:], cotangent
    ).astype(bf16)
    both_all = lax.all_gather(
        jnp.concatenate([mixed_own, spread_own], axis=1), AXES, axis=0, tiled=True
    )
    mixed = both_all[:, :channels]
    spread = both_all[:, channels:]
    pre_first = jnp.dot(mixed, w_first, preferred_element_type=f32)
    sig = jax.nn.sigmoid(pre_first)
    hidden = (pre_first * sig).astype(bf16)
    slope = sig * (1.0 + pre_first * (1.0 - sig))
    back_hidden = lax.dot_general(
        spread, w_second, (((1,), (1,)), ((), ())), preferred_element_type=f32
    )
    back_first = (back_hidden * slope).astype(bf16)
    grad_first = lax.dot_general(
        mixed, back_first, (((0,), (0,)), ((), ())), preferred_element_type=f32
    )
    grad_second = lax.dot_general(
        hidden, spread, (((0,), (0,)), ((), ())), preferred_element_type=f32
    )
    position = lax.axis_index(AXES) * features.shape[0]
    hidden_own = lax.dynamic_slice_in_dim(hidden, position, features.shape[0], 0)
    mixed_second = aggregate(
        tile_entries, tile_columns, tiles_per_row, hidden, hidden_own
    ).astype(bf16)
    z_out = jnp.dot(mixed_second, w_second, preferred_element_type=f32).astype(bf16)
    return (z_out, grad_first, grad_second)


def solution(mesh):
    placed = (
        P(AXES, None),
        P(AXES, None, None),
        P(AXES, None),
        P(AXES),
        P(AXES, None, None),
        P(AXES, None),
        P(AXES),
        P(),
        P(),
        P(AXES, None),
    )
    return jax.shard_map(
        shards,
        mesh=mesh,
        in_specs=placed,
        out_specs=(P(AXES, None), P(), P()),
        check_vma=False,
    )
```

time: 360 us -> 222 us (0.62)
  waiting for transfers between devices: 248 us -> 155 us
  blocking collectives: 40.2 us -> 0 us
  matrix products: 9.67 us -> 28.7 us
  other arithmetic: 19.4 us -> 6.43 us
  starting transfers between devices: 6.93 us -> 0.08 us
  local copies, waits for them, and re-layouts: 20.5 us -> 16.4 us
    psum x1 -> x0, waiting for transfers between devices: 132 us -> none  [shards(): grad_first = lax.psum(local_first, ('rows', 'grp'))]
    all_gather x3 -> x2, waiting for transfers between devices: 47.8 us -> 155 us  [the longest x1 79.3 us: shards(): pair_all = lax.all_gather(pair, AXES, axis=0, tiled=True)]
    reduce_scatter x1 -> x0, waiting for transfers between devices: 58.1 us -> none  [shards(): lax.psum_scatter(term_rows(jnp.int32(0), column_block.shape[0] * lax.axis...]
    all_to_all x4 -> x0, blocking collectives: 30.6 us -> none  [the longest x2 16.3 us: to_columns(): lax.all_to_all(row_block, 'grp', split_axis=1, concat_axis=0, tiled=True)]
    dot_general x6 -> x4, matrix products: 6.77 us -> 27.3 us  [the longest x1 12.8 us: shards(): lax.dot_general(mixed, back_first, (((0,), (0,)), ((), ())), preferred_el...]
    scatter-add x1 -> x0, other arithmetic: 13.6 us -> none  [term_rows(): jax.ops.segment_sum(products, labels, num_segments=segment_ids + 1)]
    all_to_all x2 -> x0, waiting for transfers between devices: 9.07 us -> none  [the longest x1 4.7 us: shards(): lax.all_to_all(summed_rows, 'grp', split_axis=0, concat_axis=1, tiled=True)]
    all_to_all x2 -> x0, starting transfers between devices: 6.73 us -> none  [the longest x1 3.41 us: shards(): lax.all_to_all(summed_rows, 'grp', split_axis=0, concat_axis=1, tiled=True)]
  transfers between devices with their start and end apart: 7 -> 2, of which waited for: 7 -> 2; matrix products, arithmetic and copies ran while one was open for 11% -> 2% of each run, Pallas kernels for 0% -> 0%
where the time goes in v1:
time: 222 us; the launch traced here: 221 us
  waiting for transfers between devices  155 us (70%)
  matrix products  28.7 us (13%)
  local copies, waits for them, and re-layouts  16.4 us (7%)
  between operations  14.2 us (6%)
  other arithmetic  6.43 us (3%)
    all_gather x1, waiting for transfers between devices, shards(): pair_all = lax.all_gather(pair, AXES, axis=0, tiled=True)  79.3 us
    all_gather x1, waiting for transfers between devices, shards(): lax.all_gather(jnp.concatenate([mixed_own, spread_own], axis=1), AXES, ax...  76.2 us
    dot_general x1, matrix products, shards(): lax.dot_general(mixed, back_first, (((0,), (0,)), ((), ())), preferred_el...  12.8 us
    gather x3, local copies, waits for them, and re-layouts, aggregate(): block_table[strip_columns] * weights[:, :, None, None]  8.69 us
    dot_general x1, matrix products, shards(): pre_first = jnp.dot(mixed, w_first, preferred_element_type=f32)  8.06 us
    slice x1, local copies, waits for them, and re-layouts, shards(): pair_all[:, :channels]  5.72 us
    dot_general x1, matrix products, shards(): lax.dot_general(hidden, spread, (((0,), (0,)), ((), ())), preferred_eleme...  5.52 us
  transfers between devices with their start and end apart: 2, of which 2 were waited for; matrix products, arithmetic and copies ran while one was open for 2% of the time, Pallas kernels for 0%

profile of v1, /device:TPU:0, one launch (start us, length us, event | category | flops | bytes accessed | tf_op | source)
XLA Modules:
  0.0 221.4 jit_solution(5866763700400470942)
XLA Ops:
  7.2 0.0 copy-start
  7.2 0.0 all-gather.3.cloned.1.call-start
  7.2 1.7 pad_maximum_fusion
  9.0 0.0 all-gather.3.cloned.1.call-update
  9.0 0.0 all-gather.5.cloned.1.call-start
  9.0 0.7 compare_select_fusion.1
  9.7 0.1 reshape.81
  9.8 0.7 compare_select_fusion
  10.5 0.1 reshape.89
  10.6 0.7 compare_convert_fusion
  11.3 0.1 mul.55
  11.4 0.1 mul.56
  11.5 0.7 compare_convert_fusion.1
  12.2 0.1 mul.51
  12.3 0.1 mul.52
  12.4 79.3 %all-gather.3.cloned.1.call-done = bf16[4096,1024]{1,0:T(8,128)(2,1)} async-done(((bf16[128,1024]{1,0:T(8,128)(2,1)}), bf16[4096,1024]{1,0:T(8,128)(2,1)}) %all-gather.3.cloned.1.call-update) | async-done | bytes 8388624 | tf_op jit(solution)/shard_map/all_gather | solution.py:38
  91.6 5.7 %fusion.13 = (bf16[4096,512]{1,0:T(8,128)(2,1)}, bf16[4096,512]{1,0:T(8,128)(2,1)}) fusion(bf16[4096,1024]{1,0:T(8,128)(2,1)} %all-gather.3.cloned.1.call-done), kind=kLoop, calls=%fused_computation.32 | loop fusion | bytes 16777216 | tf_op jit(solution)/shard_map/slice | solution.py:40
  97.4 0.0 copy-start.2
  97.4 2.9 %gather_fusion = bf16[32,64,512]{2,1,0:T(8,128)(2,1)S(1)} fusion(bf16[64,64,512]{2,1,0:T(8,128)(2,1)} %bitcast.42, s32[1024]{0:T(1024)S(1)} %pad_clamp_fusion.1), kind=kCustom, calls=%fused_computation | custom fusion | bytes 4194432 | tf_op jit(solution)/shard_map/gather | solution.py:16
  100.3 0.3 bitcast_multiply_fusion.2
  100.6 0.0 copy-done.2
  100.6 0.5 fusion.14
  101.1 0.0 copy-start.6
  101.1 2.9 %gather_fusion.1 = bf16[32,64,512]{2,1,0:T(8,128)(2,1)S(1)} fusion(bf16[64,64,512]{2,1,0:T(8,128)(2,1)} %bitcast.41, s32[1024]{0:T(1024)S(1)} %pad_clamp_fusion), kind=kCustom, calls=%fused_computation.1 | custom fusion | bytes 4194432 | tf_op jit(solution)/shard_map/gather | solution.py:16
  104.1 0.0 copy-start.4
  104.1 0.0 copy-start.5
  104.1 0.3 bitcast_multiply_fusion.1
  104.4 0.0 copy-done.6
  104.4 0.5 fusion.15
  104.9 0.0 copy-done.4
  105.0 0.1 copy-done.5
  105.0 0.1 fusion.10
  105.1 0.7 pad_maximum_fusion.1
  105.8 0.0 all-gather.5.cloned.1.call-update
  105.9 76.2 %all-gather.5.cloned.1.call-done = bf16[4096,1024]{1,0:T(8,128)(2,1)} async-done(((bf16[128,1024]{1,0:T(8,128)(2,1)}), bf16[4096,1024]{1,0:T(8,128)(2,1)}) %all-gather.5.cloned.1.call-update) | async-done | bytes 8388624 | tf_op jit(solution)/shard_map/all_gather | solution.py:45
  182.1 0.0 copy-done
  182.1 8.1 %multiply_convert_fusion.1 = (bf16[4096,512]{1,0:T(8,128)(2,1)}, f32[4096,512]{1,0:T(8,128)}) fusion(bf16[512,512]{1,0:T(8,128)(2,1)S(1)} %copy-done, bf16[4096,1024]{1,0:T(8,128)(2,1)} %all-gather.5.cloned.1.call-done), kind=kOutput, calls=%fused_computation.4 | convolution fusion | flops 2157969408 | bytes 17301504 | tf_op jit(solution)/shard_map/dot_general | solution.py:50
  190.1 2.9 %gather_fusion.2 = bf16[32,64,512]{2,1,0:T(8,128)(2,1)S(1)} fusion(bf16[64,64,512]{2,1,0:T(8,128)(2,1)} %bitcast.46, s32[1024]{0:T(1024)S(1)} %pad_clamp_fusion.1), kind=kCustom, calls=%fused_computation.2 | custom fusion | bytes 4194432 | tf_op jit(solution)/shard_map/gather | solution.py:16
  193.0 0.0 copy-start.1
  193.0 0.0 copy-start.3
  193.0 0.3 bitcast_multiply_fusion
  193.4 0.5 fusion.16
  193.8 1.3 copy-done.1
  195.2 0.1 copy-done.3
  195.3 0.9 convolution_convert_fusion
  196.2 5.5 %fusion = f32[512,512]{1,0:T(8,128)} fusion(bf16[4096,512]{1,0:T(8,128)(2,1)S(1)} %copy-done.1, bf16[4096,1024]{1,0:T(8,128)(2,1)} %all-gather.5.cloned.1.call-done), kind=kOutput, calls=%fused_computation.6 | convolution fusion | flops 2147483648 | bytes 9437184 | tf_op jit(solution)/shard_map/dot_general | solution.py:61
  201.7 12.8 %fusion.3 = f32[512,512]{1,0:T(8,128)} fusion(bf16[4096,1024]{1,0:T(8,128)(2,1)} %all-gather.5.cloned.1.call-done, f32[4096,512]{1,0:T(8,128)} %get-tuple-element.6, bf16[512,512]{1,0:T(8,128)(2,1)S(1)} %copy-done.3), kind=kOutput, calls=%fused_computation.9 | convolution fusion | flops 4313841664 | bytes 18350080 | tf_op jit(solution)/shard_map/dot_general | solution.py:58
  (3 shorter events, 0.0 us)
Async XLA Ops:
  7.2 174.9 %copy-start = (bf16[512,512]{1,0:T(8,128)(2,1)S(1)}, bf16[512,512]{1,0:T(8,128)(2,1)}, u32[]{:S(2)}) copy-start(bf16[512,512]{1,0:T(8,128)(2,1)} %param.17) | copy-start | bytes 1572868
  7.2 84.5 %all-gather.3.cloned.1.call-start = ((), (), s32[]{:S(2)}) async-start(), calls=%async_computation | async-start | bytes 8650752 | tf_op jit(solution)/shard_map/all_gather | solution.py:38
  9.0 173.1 %all-gather.5.cloned.1.call-start = ((), (), s32[]{:S(2)}) async-start(), calls=%async_computation.1 | async-start | bytes 8650752 | tf_op jit(solution)/shard_map/all_gather | solution.py:45
  97.4 3.3 %copy-start.2 = (bf16[2,64,1024]{2,1,0:T(8,128)(2,1)S(1)}, bf16[2,64,1024]{2,1,0:T(8,128)(2,1)}, u32[]{:S(2)}) copy-start(bf16[2,64,1024]{2,1,0:T(8,128)(2,1)} %param.11) | copy-start | bytes 786436
  101.1 3.3 %copy-start.6 = (bf16[2,64,1024]{2,1,0:T(8,128)(2,1)S(1)}, bf16[2,64,1024]{2,1,0:T(8,128)(2,1)}, u32[]{:S(2)}) copy-start(bf16[2,64,1024]{2,1,0:T(8,128)(2,1)} %param.14) | copy-start | bytes 786436
  104.1 0.9 copy-start.4
  104.1 1.0 copy-start.5
  193.0 2.2 copy-start.1
  193.0 2.3 %copy-start.3 = (bf16[512,512]{1,0:T(8,128)(2,1)S(1)}, bf16[512,512]{1,0:T(8,128)(2,1)}, u32[]{:S(2)}) copy-start(bf16[512,512]{1,0:T(8,128)(2,1)} %param.18) | copy-start | bytes 1572868
Sparse Core Ops, SparseCore 0:
  11.4 80.1 all-gather.2
  106.0 76.0 all-gather.4

commit v2 on v1

v2 whole, which is shorter than its diff:
```python
import jax
import jax.numpy as jnp
from jax import lax
from jax.experimental import pallas as pl
from jax.experimental.pallas import tpu as pltpu
from jax.sharding import PartitionSpec as P

AXES = ("rows", "grp")
F32 = jnp.float32
BF16 = jnp.bfloat16


def aggregate(panel_vals, strip_columns, strip_count, everyone, own_rows):
    blocks, size_block, span_width = panel_vals.shape
    slot_count = span_width // size_block
    channels = everyone.shape[1]
    block_table = everyone.reshape(-1, size_block, channels)
    slot_ids = lax.broadcasted_iota(jnp.int32, strip_columns.shape, 1)
    weights = (slot_ids < strip_count[:, None]).astype(everyone.dtype)
    picked = (block_table[strip_columns] * weights[:, :, None, None]).reshape(
        blocks, slot_count * size_block, channels
    )
    summed_rows = jnp.einsum("bik,bkc->bic", panel_vals, picked, preferred_element_type=F32)
    return summed_rows.reshape(blocks * size_block, channels) + own_rows.astype(F32)


def gathered_shards(
    features,
    tile_entries,
    tile_columns,
    tiles_per_row,
    rev_vals,
    rev_cols,
    rev_count,
    w_first,
    w_second,
    cotangent,
):
    channels = features.shape[1]
    pair = jnp.concatenate([features, cotangent], axis=1)
    pair_all = lax.all_gather(pair, AXES, axis=0, tiled=True)
    mixed_own = aggregate(
        tile_entries, tile_columns, tiles_per_row, pair_all[:, :channels], features
    ).astype(BF16)
    spread_own = aggregate(
        rev_vals, rev_cols, rev_count, pair_all[:, channels:], cotangent
    ).astype(BF16)
    both_all = lax.all_gather(
        jnp.concatenate([mixed_own, spread_own], axis=1), AXES, axis=0, tiled=True
    )
    mixed = both_all[:, :channels]
    spread = both_all[:, channels:]
    pre_first = jnp.dot(mixed, w_first, preferred_element_type=F32)
    sig = jax.nn.sigmoid(pre_first)
    hidden = (pre_first * sig).astype(BF16)
    slope = sig * (1.0 + pre_first * (1.0 - sig))
    back_hidden = lax.dot_general(
        spread, w_second, (((1,), (1,)), ((), ())), preferred_element_type=F32
    )
    back_first = (back_hidden * slope).astype(BF16)
    grad_first = lax.dot_general(
        mixed, back_first, (((0,), (0,)), ((), ())), preferred_element_type=F32
    )
    grad_second = lax.dot_general(
        hidden, spread, (((0,), (0,)), ((), ())), preferred_element_type=F32
    )
    position = lax.axis_index(AXES) * features.shape[0]
    hidden_own = lax.dynamic_slice_in_dim(hidden, position, features.shape[0], 0)
    mixed_second = aggregate(
        tile_entries, tile_columns, tiles_per_row, hidden, hidden_own
    ).astype(BF16)
    z_out = jnp.dot(mixed_second, w_second, preferred_element_type=F32).astype(BF16)
    return (z_out, grad_first, grad_second)


CORE, X, Y, XY = 1, 2, 4, 6
DEVICES, QUAD, PLANES, SLOTS, BLOCK = 32, 4, 4, 16, 64
LANES = 128
ROWS = 128
VMEM = pl.BlockSpec(memory_space=pltpu.VMEM)
SMEM = pl.BlockSpec(memory_space=pltpu.SMEM)
ANY = pl.BlockSpec(memory_space=pl.ANY)
PARAMS = pltpu.CompilerParams(vmem_limit_bytes=56 * 1024 * 1024)


def swap(value, mask):
    return lax.ppermute(value, AXES, [(i, i ^ mask) for i in range(DEVICES)])


def pack_body(pos, features, cotangent, codes, own, to_x, to_y, to_xy):
    for q, out in enumerate((own, to_x, to_y, to_xy)):
        first = pl.multiple_of((pos[0] ^ q) * LANES, LANES)
        out[:ROWS, :LANES] = features[:, pl.ds(first, LANES)]
        out[:ROWS, LANES:] = cotangent[:, pl.ds(first, LANES)]
        out[ROWS:, :] = codes[...]


def pack(pos, features, cotangent, codes):
    shape = jax.ShapeDtypeStruct((ROWS + 16, 2 * LANES), BF16)
    return pl.pallas_call(
        pack_body,
        out_shape=(shape,) * 4,
        in_specs=[SMEM, VMEM, VMEM, VMEM],
        out_specs=(VMEM,) * 4,
        compiler_params=PARAMS,
    )(pos, features, cotangent, codes)


def mix_body(codes, t0, t1, t2, t3, t4, a0, a1, a2, a3, out, table, picked, sems):
    span = QUAD * ROWS
    copies = []
    for i, (ref, size) in enumerate(((t0, 1), (t1, 1), (t2, 1), (t3, 1), (t4, 4))):
        copies.append(
            pltpu.make_async_copy(ref, table.at[pl.ds(i * span, size * span), :], sems.at[i])
        )
        copies[-1].start()
    table[DEVICES * ROWS :, :] = jnp.zeros((BLOCK, LANES), BF16)
    for copy in copies:
        copy.wait()
    for q, tiles in enumerate((a0, a1, a2, a3)):
        for w in range(2):
            row = q * 2 + w
            for s in range(SLOTS):
                first = pl.multiple_of(codes[row * SLOTS + s] * BLOCK, BLOCK)
                picked[row, pl.ds(s * BLOCK, BLOCK), :] = table[pl.ds(first, BLOCK), :]
            total = jnp.dot(tiles[w], picked[row], preferred_element_type=F32)
            total = total + table[pl.ds(row * BLOCK, BLOCK), :].astype(F32)
            out[pl.ds(row * BLOCK, BLOCK), :] = total.astype(BF16)


def mix(codes, planes, other_core, tiles):
    return pl.pallas_call(
        mix_body,
        out_shape=jax.ShapeDtypeStruct((QUAD * ROWS, LANES), BF16),
        in_specs=[SMEM] + [ANY] * 5 + [VMEM] * 4,
        out_specs=VMEM,
        scratch_shapes=[
            pltpu.VMEM((DEVICES * ROWS + BLOCK, LANES), BF16),
            pltpu.VMEM((2 * QUAD, SLOTS * BLOCK, LANES), BF16),
            pltpu.SemaphoreType.DMA((5,)),
        ],
        compiler_params=PARAMS,
    )(codes, *planes, other_core, *tiles)


def assemble(pos, pieces, target, sems):
    copies = []
    for j in range(PLANES):
        for p in range(QUAD):
            column = pos[0] ^ p
            for q in range(QUAD):
                row = ((pos[1] ^ j) * QUAD + (column ^ q)) * ROWS
                copies.append(
                    pltpu.make_async_copy(
                        pieces[j * QUAD + p].at[pl.ds(q * ROWS, ROWS), :],
                        target.at[
                            pl.ds(pl.multiple_of(row, ROWS), ROWS),
                            pl.ds(pl.multiple_of(column * LANES, LANES), LANES),
                        ],
                        sems.at[len(copies)],
                    )
                )
                copies[-1].start()
    for copy in copies:
        copy.wait()


def first_body(pos, *refs):
    pieces = refs[:16]
    w_first, mixed, hidden, slope, sems = refs[16:]
    assemble(pos, pieces, mixed, sems)
    chunk = QUAD * ROWS
    for z in range(PLANES):
        rows = pl.ds(z * chunk, chunk)
        pre = jnp.dot(mixed[rows, :], w_first[...], preferred_element_type=F32)
        sig = jax.nn.sigmoid(pre)
        hidden[rows, :] = (pre * sig).astype(BF16)
        slope[rows, :] = sig * (1.0 + pre * (1.0 - sig))


def first_layer(pos, pieces, w_first):
    count, channels = PLANES * QUAD * ROWS, w_first.shape[0]
    return pl.pallas_call(
        first_body,
        out_shape=(
            jax.ShapeDtypeStruct((count, channels), BF16),
            jax.ShapeDtypeStruct((count, channels), BF16),
            jax.ShapeDtypeStruct((count, channels), F32),
        ),
        in_specs=[SMEM] + [ANY] * 16 + [VMEM],
        out_specs=(VMEM,) * 3,
        scratch_shapes=[pltpu.SemaphoreType.DMA((64,))],
        compiler_params=PARAMS,
    )(pos, *pieces, w_first)


def second_body(codes, mine, other, tiles, w_second, z_out, picked, own, sems):
    count = 2 * SLOTS

    def fetch(slot, source, row):
        return pltpu.make_async_copy(
            source.at[pl.ds(pl.multiple_of(row, BLOCK), BLOCK), :],
            picked.at[pl.ds(slot * BLOCK, BLOCK), :],
            sems.at[slot],
        )

    own_copy = pltpu.make_async_copy(
        mine.at[pl.ds(pl.multiple_of(codes[2 * count], ROWS), ROWS), :], own, sems.at[count]
    )
    own_copy.start()
    for slot in range(count):
        kind, row = codes[slot], codes[count + slot]

        @pl.when(kind == 0)
        def _():
            fetch(slot, mine, row).start()

        @pl.when(kind == 1)
        def _():
            fetch(slot, other, row).start()

        @pl.when(kind == 2)
        def _():
            picked[pl.ds(slot * BLOCK, BLOCK), :] = jnp.zeros((BLOCK, picked.shape[1]), BF16)

    own_copy.wait()
    for w in range(2):
        for s in range(SLOTS):
            slot = w * SLOTS + s

            @pl.when(codes[slot] != 2)
            def _():
                fetch(slot, mine, 0).wait()

        total = jnp.dot(
            tiles[w],
            picked[pl.ds(w * SLOTS * BLOCK, SLOTS * BLOCK), :],
            preferred_element_type=F32,
        )
        total = total + own[pl.ds(w * BLOCK, BLOCK), :].astype(F32)
        own[pl.ds(w * BLOCK, BLOCK), :] = total.astype(BF16)
    z_out[...] = jnp.dot(own[...], w_second[...], preferred_element_type=F32).astype(BF16)


def second_layer(codes, mine, other, tiles, w_second):
    channels = w_second.shape[0]
    return pl.pallas_call(
        second_body,
        out_shape=jax.ShapeDtypeStruct((ROWS, channels), BF16),
        in_specs=[SMEM, ANY, ANY, VMEM, VMEM],
        out_specs=VMEM,
        scratch_shapes=[
            pltpu.VMEM((2 * SLOTS * BLOCK, channels), BF16),
            pltpu.VMEM((ROWS, channels), BF16),
            pltpu.SemaphoreType.DMA((2 * SLOTS + 1,)),
        ],
        compiler_params=PARAMS,
    )(codes, mine, other, tiles, w_second)


def grads_body(pos, *refs):
    pieces = refs[:16]
    mixed, hidden, slope, w_second, out, spread, sems = refs[16:]
    assemble(pos, pieces, spread, sems)
    channels = w_second.shape[0]
    chunk = QUAD * ROWS
    for z in range(PLANES):
        rows = pl.ds(z * chunk, chunk)
        back_hidden = lax.dot_general(
            spread[rows, :], w_second[...], (((1,), (1,)), ((), ())), preferred_element_type=F32
        )
        back_first = (back_hidden * slope[rows, :]).astype(BF16)
        part_first = lax.dot_general(
            mixed[rows, :], back_first, (((0,), (0,)), ((), ())), preferred_element_type=F32
        )
        part_second = lax.dot_general(
            hidden[rows, :], spread[rows, :], (((0,), (0,)), ((), ())), preferred_element_type=F32
        )
        if z == 0:
            out[:channels, :] = part_first
            out[channels:, :] = part_second
        else:
            out[:channels, :] += part_first
            out[channels:, :] += part_second


def gradients(pos, pieces, mixed, hidden, slope, w_second):
    channels = w_second.shape[0]
    return pl.pallas_call(
        grads_body,
        out_shape=jax.ShapeDtypeStruct((2 * channels, channels), F32),
        in_specs=[SMEM] + [ANY] * 16 + [VMEM] * 4,
        out_specs=VMEM,
        scratch_shapes=[
            pltpu.VMEM((PLANES * QUAD * ROWS, channels), BF16),
            pltpu.SemaphoreType.DMA((64,)),
        ],
        compiler_params=PARAMS,
    )(pos, *pieces, mixed, hidden, slope, w_second)


def class_gather(piece, early, late):
    pieces = []
    for j in range(PLANES):
        here = piece if j == 0 else swap(piece, 8 * j)
        by_early = swap(here, early)
        by_late = swap(here, late)
        by_both = swap(by_early, late)
        by_x, by_y = (by_early, by_late) if early == X else (by_late, by_early)
        pieces += [here, by_x, by_y, by_both]
    return pieces


def planned_shards(
    features,
    tile_entries,
    tile_columns,
    tiles_per_row,
    rev_vals,
    rev_cols,
    rev_count,
    w_first,
    w_second,
    cotangent,
):
    device = lax.axis_index(AXES)
    pos = jnp.stack([(device >> 1) & 3, device >> 3]).astype(jnp.int32)
    columns = jnp.concatenate([tile_columns, rev_cols], axis=0)
    counts = jnp.concatenate([tiles_per_row, rev_count], axis=0)
    slot_ids = lax.broadcasted_iota(jnp.int32, columns.shape, 1)
    codes = jnp.where(slot_ids < counts[:, None], columns, -1)
    codes_padded = jnp.pad(codes.astype(BF16), ((0, 12), (0, 2 * LANES - SLOTS)))
    packed = pack(pos, features, cotangent, codes_padded)
    parts = [packed[0]] + [swap(packed[q], 2 * q) for q in range(1, 4)]

    near = jnp.stack([part[ROWS : ROWS + 4, :SLOTS] for part in parts]).astype(jnp.int32)
    apart = (near >> 1) ^ device
    address = ((apart & 1) * 16 + (apart >> 3) * 4 + ((apart >> 1) & 3)) * 2 + (near & 1)
    address = jnp.where(near < 0, 2 * DEVICES, address)

    def slices(first):
        return jnp.concatenate([part[:ROWS, first : first + LANES] for part in parts], axis=0)

    def phase(first, tiles_own, rows):
        piece = slices(first)
        planes = [piece] + [swap(piece, 8 * j) for j in range(1, 4)]
        other_core = swap(jnp.concatenate(planes, axis=0), CORE)
        tiles = [tiles_own] + [swap(tiles_own, 2 * q) for q in range(1, 4)]
        return mix(address[:, rows : rows + 2].reshape(-1), planes, other_core, tiles)

    mixed_piece = phase(0, tile_entries, 0)
    spread_piece = phase(LANES, rev_vals, 2)
    mixed, hidden, slope = first_layer(pos, class_gather(mixed_piece, X, Y), w_first)
    hidden_other = swap(hidden, CORE)
    live = codes[:2]
    kind = jnp.where(live < 0, 2, ((live >> 1) ^ device) & 1).reshape(-1)
    row = ((live >> 2) * ROWS + (live & 1) * BLOCK).reshape(-1)
    second_codes = jnp.concatenate([kind, row, ((device >> 1) * ROWS)[None]]).astype(jnp.int32)
    z_out = second_layer(second_codes, hidden, hidden_other, tile_entries, w_second)
    part = gradients(pos, class_gather(spread_piece, Y, X), mixed, hidden, slope, w_second)
    total = part + swap(part, CORE)
    channels = w_second.shape[0]
    return (z_out, total[:channels], total[channels:])


def solution(mesh):
    placed = (
        P(AXES, None),
        P(AXES, None, None),
        P(AXES, None),
        P(AXES),
        P(AXES, None, None),
        P(AXES, None),
        P(AXES),
        P(),
        P(),
        P(AXES, None),
    )
    planned = mesh.shape["rows"] == 8 and mesh.shape["grp"] == 4
    return jax.shard_map(
        planned_shards if planned else gathered_shards,
        mesh=mesh,
        in_specs=placed,
        out_specs=(P(AXES, None), P(), P()),
        check_vma=False,
    )
```

time: 222 us -> 154 us (0.69)
  waiting for transfers between devices: 155 us -> 44.2 us
  starting transfers between devices: 0.08 us -> 57.9 us
  Pallas kernels: 0 us -> 31.6 us
  matrix products: 28.7 us -> 0 us
  between operations: 14.2 us -> 1.14 us
  local copies, waits for them, and re-layouts: 16.4 us -> 13.3 us
    all_gather x2 -> x0, waiting for transfers between devices: 155 us -> none  [the longest x1 79.3 us: shards(): pair_all = lax.all_gather(pair, AXES, axis=0, tiled=True)]
    ppermute x0 -> x49, starting transfers between devices: none -> 57.9 us  [swap(): return lax.ppermute(value, AXES, [(i, i ^ mask) for i in range(DEVICES)])]
    ppermute x0 -> x49, waiting for transfers between devices: none -> 44.2 us  [swap(): return lax.ppermute(value, AXES, [(i, i ^ mask) for i in range(DEVICES)])]
    pallas_call x0 -> x6, Pallas kernels: none -> 31.6 us  [the longest x1 10.8 us: gradients(): pl.pallas_call(grads_body, out_shape=jax.ShapeDtypeStruct((2 * channels,...]
    dot_general x7 -> x0, matrix products: 28.7 us -> none  [the longest x1 12.8 us: shards(): lax.dot_general(mixed, back_first, (((0,), (0,)), ((), ())), preferred_el...]
    gather x3 -> x0, local copies, waits for them, and re-layouts: 8.69 us -> none  [aggregate(): block_table[strip_columns] * weights[:, :, None, None]]
    unnamed x14 -> x100, local copies, waits for them, and re-layouts: 1.55 us -> 7.62 us
    slice x1 -> x2, local copies, waits for them, and re-layouts: 5.72 us -> 1.49 us  [the longest x1 1.49 us: planned_shards(): return (z_out, total[:channels], total[channels:])]
  transfers between devices with their start and end apart: 2 -> 49, of which waited for: 2 -> 18; matrix products, arithmetic and copies ran while one was open for 2% -> 11% of each run, Pallas kernels for 0% -> 11%
where the time goes in v2:
time: 154 us
  starting transfers between devices  57.9 us (38%)
  waiting for transfers between devices  44.2 us (29%)
  Pallas kernels  31.6 us (21%)
  local copies, waits for them, and re-layouts  13.3 us (9%)
  other arithmetic  5.4 us (4%)
    ppermute x49, starting transfers between devices, swap(): return lax.ppermute(value, AXES, [(i, i ^ mask) for i in range(DEVICES)])  57.9 us
    ppermute x49, waiting for transfers between devices, swap(): return lax.ppermute(value, AXES, [(i, i ^ mask) for i in range(DEVICES)])  44.2 us
    pallas_call x1, Pallas kernels, gradients(): pl.pallas_call(grads_body, out_shape=jax.ShapeDtypeStruct((2 * channels,...  10.8 us
    unnamed x100, local copies, waits for them, and re-layouts  7.62 us
    pallas_call x2, Pallas kernels, mix(): pl.pallas_call(mix_body, out_shape=jax.ShapeDtypeStruct((QUAD * ROWS, LAN...  7.58 us
    pallas_call x1, Pallas kernels, first_layer(): pl.pallas_call(first_body, out_shape=(jax.ShapeDtypeStruct((count, channe...  7.51 us
    pallas_call x1, Pallas kernels, second_layer(): pl.pallas_call(second_body, out_shape=jax.ShapeDtypeStruct((ROWS, channel...  4 us
  transfers between devices with their start and end apart: 49, of which 18 were waited for; matrix products, arithmetic and copies ran while one was open for 11% of the time, Pallas kernels for 11%

profile of v2, /device:TPU:0, one launch (start us, length us, event | category | flops | bytes accessed | tf_op | source)
XLA Modules:
  0.0 153.5 jit_solution(13165388963393699797)
XLA Ops:
  0.6 3.0 %collective-permute-start.31 = (bf16[2,64,1024]{2,1,0:T(8,128)(2,1)}, bf16[2,64,1024]{2,1,0:T(8,128)(2,1)S(1)}, u32[]{:S(2)}, u32[]{:S(2)}) collective-permute-start(bf16[2,64,1024]{2,1,0:T(8,128)(2,1)} %a0.3), channel_id=1, source_target_pairs={{0,4},{1,5},{2,6},{3,7},{4,0},{5,1},{6,2},{7,3},{8,12},{9,13},{10,... | collective-permute-start | bytes 786440 | tf_op jit(solution)/shard_map/ppermute | solution.py:87
  3.7 1.5 collective-permute-start.30
  7.9 1.7 %shard_map.121 = (bf16[144,256]{1,0:T(8,128)(2,1)}, bf16[144,256]{1,0:T(8,128)(2,1)}, bf16[144,256]{1,0:T(8,128)(2,1)}, bf16[144,256]{1,0:T(8,128)(2,1)}) custom-call(s32[2]{0:T(128)} %pad_add_fusion.2.pos, bf16[128,512]{1,0:T(8,128)(2,1)} %features.1, bf16[128,512]{1,0:T(8,128)(2,1)} %cotangent.1, bf16[16,256]{1,0:T(8,128)(2,1)} %pad.4.codes), custom_call_target="tpu_custom_call" | custom-call | tf_op jit(solution)/shard_map/pallas_call | solution.py:100
  9.6 1.9 %collective-permute-start = (bf16[144,256]{1,0:T(8,128)(2,1)}, bf16[144,256]{1,0:T(8,128)(2,1)S(1)}, u32[]{:S(2)}, u32[]{:S(2)}) collective-permute-start(bf16[144,256]{1,0:T(8,128)(2,1)} %get-tuple-element.11), channel_id=1, source_target_pairs={{0,2},{1,3},{2,0},{3,1},{4,6},{5,7},{6,4},{7,5},{8,10},{9,11},{10,... | collective-permute-start | bytes 221192 | tf_op jit(solution)/shard_map/ppermute | solution.py:87
  11.5 1.5 collective-permute-start.1
  13.1 1.4 constant_dynamic-update-slice_fusion.13
  15.1 3.7 %collective-permute-done = bf16[144,256]{1,0:T(8,128)(2,1)S(1)} collective-permute-done((bf16[144,256]{1,0:T(8,128)(2,1)}, bf16[144,256]{1,0:T(8,128)(2,1)S(1)}, u32[]{:S(2)}, u32[]{:S(2)}) %collective-permute-start) | collective-permute-done | bytes 73760 | tf_op jit(solution)/shard_map/ppermute | solution.py:87
  18.9 1.4 collective-permute-start.2
  21.6 2.8 %collective-permute-done.2 = bf16[144,256]{1,0:T(8,128)(2,1)S(1)} collective-permute-done((bf16[144,256]{1,0:T(8,128)(2,1)}, bf16[144,256]{1,0:T(8,128)(2,1)S(1)}, u32[]{:S(2)}, u32[]{:S(2)}) %collective-permute-start.2) | collective-permute-done | bytes 73760 | tf_op jit(solution)/shard_map/ppermute | solution.py:87
  25.0 1.6 %collective-permute-start.3 = (bf16[512,128]{1,0:T(8,128)(2,1)S(1)}, bf16[512,128]{1,0:T(8,128)(2,1)S(1)}, u32[]{:S(2)}, u32[]{:S(2)}) collective-permute-start(bf16[512,128]{1,0:T(8,128)(2,1)S(1)} %pad_maximum_fusion.t0), channel_id=1, source_target_pairs={{0,8},{1,9},{2,10},{3,11},{4,12},{5,13},{6,14},{7,15},{8,0},{9,1},... | collective-permute-start | bytes 393224 | tf_op jit(solution)/shard_map/ppermute | solution.py:87
  27.2 3.9 %collective-permute-done.3.t1 = bf16[512,128]{1,0:T(8,128)(2,1)S(1)} collective-permute-done((bf16[512,128]{1,0:T(8,128)(2,1)S(1)}, bf16[512,128]{1,0:T(8,128)(2,1)S(1)}, u32[]{:S(2)}, u32[]{:S(2)}) %collective-permute-start.3) | collective-permute-done | bytes 131104 | tf_op jit(solution)/shard_map/ppermute | solution.py:87
  31.1 2.7 %collective-permute-start.27 = (bf16[512,128]{1,0:T(8,128)(2,1)S(1)}, bf16[512,128]{1,0:T(8,128)(2,1)S(1)}, u32[]{:S(2)}, u32[]{:S(2)}) collective-permute-start(bf16[512,128]{1,0:T(8,128)(2,1)S(1)} %pad_maximum_fusion.1.t0), channel_id=1, source_target_pairs={{0,16},{1,17},{2,18},{3,19},{4,20},{5,21},{6,22},{7,23},{8,24},{9,... | collective-permute-start | bytes 393224 | tf_op jit(solution)/shard_map/ppermute | solution.py:87
  34.5 3.4 %collective-permute-start.28 = (bf16[512,128]{1,0:T(8,128)(2,1)S(1)}, bf16[512,128]{1,0:T(8,128)(2,1)S(1)}, u32[]{:S(2)}, u32[]{:S(2)}) collective-permute-start(bf16[512,128]{1,0:T(8,128)(2,1)S(1)} %pad_maximum_fusion.1.t0), channel_id=1, source_target_pairs={{0,24},{1,25},{2,26},{3,27},{4,28},{5,29},{6,30},{7,31},{8,16},{9,... | collective-permute-start | bytes 393224 | tf_op jit(solution)/shard_map/ppermute | solution.py:87
  38.5 5.8 %collective-permute-done.27.t2 = bf16[512,128]{1,0:T(8,128)(2,1)S(1)} collective-permute-done((bf16[512,128]{1,0:T(8,128)(2,1)S(1)}, bf16[512,128]{1,0:T(8,128)(2,1)S(1)}, u32[]{:S(2)}, u32[]{:S(2)}) %collective-permute-start.27) | collective-permute-done | bytes 131104 | tf_op jit(solution)/shard_map/ppermute | solution.py:87
  45.1 2.4 %collective-permute-start.5 = (bf16[512,128]{1,0:T(8,128)(2,1)S(1)}, bf16[512,128]{1,0:T(8,128)(2,1)S(1)}, u32[]{:S(2)}, u32[]{:S(2)}) collective-permute-start(bf16[512,128]{1,0:T(8,128)(2,1)S(1)} %pad_maximum_fusion.t0), channel_id=1, source_target_pairs={{0,24},{1,25},{2,26},{3,27},{4,28},{5,29},{6,30},{7,31},{8,16},{9,... | collective-permute-start | bytes 393224 | tf_op jit(solution)/shard_map/ppermute | solution.py:87
  48.1 4.4 %collective-permute-done.4.t2 = bf16[512,128]{1,0:T(8,128)(2,1)S(1)} collective-permute-done((bf16[512,128]{1,0:T(8,128)(2,1)S(1)}, bf16[512,128]{1,0:T(8,128)(2,1)S(1)}, u32[]{:S(2)}, u32[]{:S(2)}) %collective-permute-start.4) | collective-permute-done | bytes 131104 | tf_op jit(solution)/shard_map/ppermute | solution.py:87
  54.4 1.5 collective-permute-start.9
  55.9 1.5 collective-permute-start.8
  59.5 3.8 %shard_map.125.refs_0_ = bf16[512,128]{1,0:T(8,128)(2,1)} custom-call(s32[128]{0:T(128)} %reshape.22.codes, bf16[512,128]{1,0:T(8,128)(2,1)} %copy-done.7, bf16[512,128]{1,0:T(8,128)(2,1)} %copy-done.9, bf16[512,128]{1,0:T(8,128)(2,1)} %copy-done.10, bf16[512,128]{1,0:T(8,128)(2,1)} %copy-done.11, bf16[2048,128]{1,0:T(8,128)(2,1)} %copy-done.3, ...), custom_call_target="tpu_custom_call" | custom-call | tf_op jit(solution)/shard_map/pallas_call | solution.py:132
  63.3 2.1 %collective-permute-start.44 = (bf16[512,128]{1,0:T(8,128)(2,1)}, bf16[512,128]{1,0:T(8,128)(2,1)S(1)}, u32[]{:S(2)}, u32[]{:S(2)}) collective-permute-start(bf16[512,128]{1,0:T(8,128)(2,1)} %shard_map.125.refs_0_), channel_id=1, source_target_pairs={{0,24},{1,25},{2,26},{3,27},{4,28},{5,29},{6,30},{7,31},{8,16},{9,... | collective-permute-start | bytes 393224 | tf_op jit(solution)/shard_map/ppermute | solution.py:87
  65.9 3.5 %collective-permute-done.8.a2 = bf16[2,64,1024]{2,1,0:T(8,128)(2,1)} collective-permute-done((bf16[2,64,1024]{2,1,0:T(8,128)(2,1)S(1)}, bf16[2,64,1024]{2,1,0:T(8,128)(2,1)}, u32[]{:S(2)}, u32[]{:S(2)}) %collective-permute-start.8) | collective-permute-done | bytes 262176 | tf_op jit(solution)/shard_map/ppermute | solution.py:87
  71.1 1.5 collective-permute-start.33
  73.3 3.8 %shard_map.122.refs_0_ = bf16[512,128]{1,0:T(8,128)(2,1)} custom-call(s32[128]{0:T(128)} %reshape.21.codes, bf16[512,128]{1,0:T(8,128)(2,1)} %copy-done.4, bf16[512,128]{1,0:T(8,128)(2,1)} %copy-done.5, bf16[512,128]{1,0:T(8,128)(2,1)} %copy-done.6, bf16[512,128]{1,0:T(8,128)(2,1)} %copy-done.8, bf16[2048,128]{1,0:T(8,128)(2,1)} %copy-done.2, ...), custom_call_target="tpu_custom_call" | custom-call | tf_op jit(solution)/shard_map/pallas_call | solution.py:132
  77.2 2.1 %collective-permute-start.21 = (bf16[512,128]{1,0:T(8,128)(2,1)}, bf16[512,128]{1,0:T(8,128)(2,1)S(1)}, u32[]{:S(2)}, u32[]{:S(2)}) collective-permute-start(bf16[512,128]{1,0:T(8,128)(2,1)} %shard_map.122.refs_0_), channel_id=1, source_target_pairs={{0,24},{1,25},{2,26},{3,27},{4,28},{5,29},{6,30},{7,31},{8,16},{9,... | collective-permute-start | bytes 393224 | tf_op jit(solution)/shard_map/ppermute | solution.py:87
  79.5 2.2 %collective-permute-start.13 = (bf16[512,128]{1,0:T(8,128)(2,1)}, bf16[512,128]{1,0:T(8,128)(2,1)S(1)}, u32[]{:S(2)}, u32[]{:S(2)}) collective-permute-start(bf16[512,128]{1,0:T(8,128)(2,1)} %shard_map.122.refs_0_), channel_id=1, source_target_pairs={{0,8},{1,9},{2,10},{3,11},{4,12},{5,13},{6,14},{7,15},{8,0},{9,1},... | collective-permute-start | bytes 393224 | tf_op jit(solution)/shard_map/ppermute | solution.py:87
  83.7 2.0 %collective-permute-done.21.refs_12_ = bf16[512,128]{1,0:T(8,128)(2,1)S(1)} collective-permute-done((bf16[512,128]{1,0:T(8,128)(2,1)}, bf16[512,128]{1,0:T(8,128)(2,1)S(1)}, u32[]{:S(2)}, u32[]{:S(2)}) %collective-permute-start.21) | collective-permute-done | bytes 131104 | tf_op jit(solution)/shard_map/ppermute | solution.py:87
  86.5 4.3 %collective-permute-done.17.refs_8_ = bf16[512,128]{1,0:T(8,128)(2,1)S(1)} collective-permute-done((bf16[512,128]{1,0:T(8,128)(2,1)}, bf16[512,128]{1,0:T(8,128)(2,1)S(1)}, u32[]{:S(2)}, u32[]{:S(2)}) %collective-permute-start.17) | collective-permute-done | bytes 131104 | tf_op jit(solution)/shard_map/ppermute | solution.py:87
  91.4 1.5 collective-permute-start.42
  93.3 1.6 %collective-permute-start.38 = (bf16[512,128]{1,0:T(8,128)(2,1)S(1)}, bf16[512,128]{1,0:T(8,128)(2,1)S(1)}, u32[]{:S(2)}, u32[]{:S(2)}) collective-permute-start(bf16[512,128]{1,0:T(8,128)(2,1)S(1)} %collective-permute-done.36.refs_4_), channel_id=1, source_target_pairs={{0,4},{1,5},{2,6},{3,7},{4,0},{5,1},{6,2},{7,3},{8,12},{9,13},{10,... | collective-permute-start | bytes 393224 | tf_op jit(solution)/shard_map/ppermute | solution.py:87
  95.4 1.6 %collective-permute-done.45.refs_13_ = bf16[512,128]{1,0:T(8,128)(2,1)S(1)} collective-permute-done((bf16[512,128]{1,0:T(8,128)(2,1)S(1)}, bf16[512,128]{1,0:T(8,128)(2,1)S(1)}, u32[]{:S(2)}, u32[]{:S(2)}) %collective-permute-start.45) | collective-permute-done | bytes 131104 | tf_op jit(solution)/shard_map/ppermute | solution.py:87
  97.8 1.5 collective-permute-start.19
  100.6 1.4 collective-permute-start.14
  102.1 1.4 collective-permute-done.23.refs_14_
  103.5 1.5 collective-permute-start.15
  106.3 1.5 collective-permute-start.24
  108.3 1.5 collective-permute-start.16
  109.9 1.4 collective-permute-start.37
  111.3 1.4 collective-permute-done.12.refs_3_
  112.7 1.4 collective-permute-start.35
  115.0 1.6 %collective-permute-start.47 = (bf16[512,128]{1,0:T(8,128)(2,1)S(1)}, bf16[512,128]{1,0:T(8,128)(2,1)S(1)}, u32[]{:S(2)}, u32[]{:S(2)}) collective-permute-start(bf16[512,128]{1,0:T(8,128)(2,1)S(1)} %collective-permute-done.46.refs_14_), channel_id=1, source_target_pairs={{0,2},{1,3},{2,0},{3,1},{4,6},{5,7},{6,4},{7,5},{8,10},{9,11},{10,... | collective-permute-start | bytes 393224 | tf_op jit(solution)/shard_map/ppermute | solution.py:87
  116.6 1.4 collective-permute-start.43
  118.0 1.4 collective-permute-start.39
  119.5 7.5 %shard_map.123 = (bf16[2048,512]{1,0:T(8,128)(2,1)}, bf16[2048,512]{1,0:T(8,128)(2,1)}, f32[2048,512]{1,0:T(8,128)}) custom-call(s32[2]{0:T(128)} %pad_add_fusion.2.pos, bf16[512,128]{1,0:T(8,128)(2,1)} %shard_map.122.refs_0_, bf16[512,128]{1,0:T(8,128)(2,1)} %copy-done.35, bf16[512,128]{1,0:T(8,128)(2,1)} %copy-done.34, bf16[512,128]{1,0:T(8,128)(2,1)} %copy-done.42, ...), custom_call_target="tpu_custom_call" | custom-call | tf_op jit(solution)/shard_map/pallas_call | solution.py:183
  127.8 10.8 %shard_map.126 = f32[1024,512]{1,0:T(8,128)} custom-call(s32[2]{0:T(128)} %pad_add_fusion.2.pos, bf16[512,128]{1,0:T(8,128)(2,1)} %shard_map.125.refs_0_, bf16[512,128]{1,0:T(8,128)(2,1)} %copy-done.20, bf16[512,128]{1,0:T(8,128)(2,1)} %copy-done.19, bf16[512,128]{1,0:T(8,128)(2,1)} %copy-done.27, bf16[512,128]{1,0:T(8,128)(2,1)} %copy-done.18, ...), custom_call_target="tpu_custom_call" | custom-call | tf_op jit(solution)/shard_map/pallas_call | solution.py:289
  140.0 5.3 %collective-permute-done.48 = f32[1024,512]{1,0:T(8,128)} collective-permute-done((f32[1024,512]{1,0:T(8,128)}, f32[1024,512]{1,0:T(8,128)}, u32[]{:S(2)}, u32[]{:S(2)}) %collective-permute-start.48) | collective-permute-done | bytes 2097184 | tf_op jit(solution)/shard_map/ppermute | solution.py:87
  145.3 2.7 %add.25 = f32[1024,512]{1,0:T(8,128)S(1)} add(f32[1024,512]{1,0:T(8,128)} %shard_map.126, f32[1024,512]{1,0:T(8,128)} %collective-permute-done.48) | non-fusion elementwise | flops 524288 | bytes 6291456 | tf_op jit(solution)/shard_map/add | solution.py:361
  148.0 1.5 fusion.13
  149.5 4.0 %shard_map.124 = bf16[128,512]{1,0:T(8,128)(2,1)} custom-call(s32[65]{0:T(128)} %pad_add_fusion.1.codes, bf16[2048,512]{1,0:T(8,128)(2,1)} %get-tuple-element.14.mine.refs_17_, bf16[2048,512]{1,0:T(8,128)(2,1)} %collective-permute-done.25.other, bf16[2,64,1024]{2,1,0:T(8,128)(2,1)} %tiles.1, bf16[512,512]{1,0:T(8,128)(2,1)} %refs_19_.1), custom_call_target="tpu_custom_call" | custom-call | tf_op jit(solution)/shard_map/pallas_call | solution.py:247
  (178 shorter events, 27.1 us)
Async XLA Ops:
  0.6 53.8 %collective-permute-start.31 = (bf16[2,64,1024]{2,1,0:T(8,128)(2,1)}, bf16[2,64,1024]{2,1,0:T(8,128)(2,1)S(1)}, u32[]{:S(2)}, u32[]{:S(2)}) collective-permute-start(bf16[2,64,1024]{2,1,0:T(8,128)(2,1)} %a0.3), channel_id=1, source_target_pairs={{0,4},{1,5},{2,6},{3,7},{4,0},{5,1},{6,2},{7,3},{8,12},{9,13},{10,... | collective-permute-start | bytes 786440 | tf_op jit(solution)/shard_map/ppermute | solution.py:87
  3.7 52.2 %collective-permute-start.30 = (bf16[2,64,1024]{2,1,0:T(8,128)(2,1)}, bf16[2,64,1024]{2,1,0:T(8,128)(2,1)S(1)}, u32[]{:S(2)}, u32[]{:S(2)}) collective-permute-start(bf16[2,64,1024]{2,1,0:T(8,128)(2,1)} %a0.3), channel_id=1, source_target_pairs={{0,2},{1,3},{2,0},{3,1},{4,6},{5,7},{6,4},{7,5},{8,10},{9,11},{10,... | collective-permute-start | bytes 786440 | tf_op jit(solution)/shard_map/ppermute | solution.py:87
  5.2 52.3 %collective-permute-start.32 = (bf16[2,64,1024]{2,1,0:T(8,128)(2,1)}, bf16[2,64,1024]{2,1,0:T(8,128)(2,1)S(1)}, u32[]{:S(2)}, u32[]{:S(2)}) collective-permute-start(bf16[2,64,1024]{2,1,0:T(8,128)(2,1)} %a0.3), channel_id=1, source_target_pairs={{0,6},{1,7},{2,4},{3,5},{4,2},{5,3},{6,0},{7,1},{8,14},{9,15},{10,... | collective-permute-start | bytes 786440 | tf_op jit(solution)/shard_map/ppermute | solution.py:87
  9.6 9.3 %collective-permute-start = (bf16[144,256]{1,0:T(8,128)(2,1)}, bf16[144,256]{1,0:T(8,128)(2,1)S(1)}, u32[]{:S(2)}, u32[]{:S(2)}) collective-permute-start(bf16[144,256]{1,0:T(8,128)(2,1)} %get-tuple-element.11), channel_id=1, source_target_pairs={{0,2},{1,3},{2,0},{3,1},{4,6},{5,7},{6,4},{7,5},{8,10},{9,11},{10,... | collective-permute-start | bytes 221192 | tf_op jit(solution)/shard_map/ppermute | solution.py:87
  11.5 9.4 %collective-permute-start.1 = (bf16[144,256]{1,0:T(8,128)(2,1)}, bf16[144,256]{1,0:T(8,128)(2,1)S(1)}, u32[]{:S(2)}, u32[]{:S(2)}) collective-permute-start(bf16[144,256]{1,0:T(8,128)(2,1)} %get-tuple-element.12), channel_id=1, source_target_pairs={{0,4},{1,5},{2,6},{3,7},{4,0},{5,1},{6,2},{7,3},{8,12},{9,13},{10,... | collective-permute-start | bytes 221192 | tf_op jit(solution)/shard_map/ppermute | solution.py:87
  25.0 6.1 %collective-permute-start.3 = (bf16[512,128]{1,0:T(8,128)(2,1)S(1)}, bf16[512,128]{1,0:T(8,128)(2,1)S(1)}, u32[]{:S(2)}, u32[]{:S(2)}) collective-permute-start(bf16[512,128]{1,0:T(8,128)(2,1)S(1)} %pad_maximum_fusion.t0), channel_id=1, source_target_pairs={{0,8},{1,9},{2,10},{3,11},{4,12},{5,13},{6,14},{7,15},{8,0},{9,1},... | collective-permute-start | bytes 393224 | tf_op jit(solution)/shard_map/ppermute | solution.py:87
  26.7 7.8 %collective-permute-start.26 = (bf16[512,128]{1,0:T(8,128)(2,1)S(1)}, bf16[512,128]{1,0:T(8,128)(2,1)S(1)}, u32[]{:S(2)}, u32[]{:S(2)}) collective-permute-start(bf16[512,128]{1,0:T(8,128)(2,1)S(1)} %pad_maximum_fusion.1.t0), channel_id=1, source_target_pairs={{0,8},{1,9},{2,10},{3,11},{4,12},{5,13},{6,14},{7,15},{8,0},{9,1},... | collective-permute-start | bytes 393224 | tf_op jit(solution)/shard_map/ppermute | solution.py:87
  31.1 13.3 %collective-permute-start.27 = (bf16[512,128]{1,0:T(8,128)(2,1)S(1)}, bf16[512,128]{1,0:T(8,128)(2,1)S(1)}, u32[]{:S(2)}, u32[]{:S(2)}) collective-permute-start(bf16[512,128]{1,0:T(8,128)(2,1)S(1)} %pad_maximum_fusion.1.t0), channel_id=1, source_target_pairs={{0,16},{1,17},{2,18},{3,19},{4,20},{5,21},{6,22},{7,23},{8,24},{9,... | collective-permute-start | bytes 393224 | tf_op jit(solution)/shard_map/ppermute | solution.py:87
  34.5 10.6 %collective-permute-start.28 = (bf16[512,128]{1,0:T(8,128)(2,1)S(1)}, bf16[512,128]{1,0:T(8,128)(2,1)S(1)}, u32[]{:S(2)}, u32[]{:S(2)}) collective-permute-start(bf16[512,128]{1,0:T(8,128)(2,1)S(1)} %pad_maximum_fusion.1.t0), channel_id=1, source_target_pairs={{0,24},{1,25},{2,26},{3,27},{4,28},{5,29},{6,30},{7,31},{8,16},{9,... | collective-permute-start | bytes 393224 | tf_op jit(solution)/shard_map/ppermute | solution.py:87
  44.4 8.1 %collective-permute-start.4 = (bf16[512,128]{1,0:T(8,128)(2,1)S(1)}, bf16[512,128]{1,0:T(8,128)(2,1)S(1)}, u32[]{:S(2)}, u32[]{:S(2)}) collective-permute-start(bf16[512,128]{1,0:T(8,128)(2,1)S(1)} %pad_maximum_fusion.t0), channel_id=1, source_target_pairs={{0,16},{1,17},{2,18},{3,19},{4,20},{5,21},{6,22},{7,23},{8,24},{9,... | collective-permute-start | bytes 393224 | tf_op jit(solution)/shard_map/ppermute | solution.py:87
  45.1 8.1 %collective-permute-start.5 = (bf16[512,128]{1,0:T(8,128)(2,1)S(1)}, bf16[512,128]{1,0:T(8,128)(2,1)S(1)}, u32[]{:S(2)}, u32[]{:S(2)}) collective-permute-start(bf16[512,128]{1,0:T(8,128)(2,1)S(1)} %pad_maximum_fusion.t0), channel_id=1, source_target_pairs={{0,24},{1,25},{2,26},{3,27},{4,28},{5,29},{6,30},{7,31},{8,16},{9,... | collective-permute-start | bytes 393224 | tf_op jit(solution)/shard_map/ppermute | solution.py:87
  52.5 6.2 %collective-permute-start.29 = (bf16[2048,128]{1,0:T(8,128)(2,1)}, bf16[2048,128]{1,0:T(8,128)(2,1)S(1)}, u32[]{:S(2)}, u32[]{:S(2)}) collective-permute-start(bf16[2048,128]{1,0:T(8,128)(2,1)} %constant_dynamic-update-slice_fusion.7), channel_id=1, source_target_pairs={{0,1},{1,0},{2,3},{3,2},{4,5},{5,4},{6,7},{7,6},{8,9},{9,8},{10,11... | collective-permute-start | bytes 1572872 | tf_op jit(solution)/shard_map/ppermute | solution.py:87
  53.9 17.2 %collective-permute-start.6 = (bf16[2048,128]{1,0:T(8,128)(2,1)}, bf16[2048,128]{1,0:T(8,128)(2,1)S(1)}, u32[]{:S(2)}, u32[]{:S(2)}) collective-permute-start(bf16[2048,128]{1,0:T(8,128)(2,1)} %constant_dynamic-update-slice_fusion), channel_id=1, source_target_pairs={{0,1},{1,0},{2,3},{3,2},{4,5},{5,4},{6,7},{7,6},{8,9},{9,8},{10,11... | collective-permute-start | bytes 1572872 | tf_op jit(solution)/shard_map/ppermute | solution.py:87
  54.4 11.0 %collective-permute-start.9 = (bf16[2,64,1024]{2,1,0:T(8,128)(2,1)S(1)}, bf16[2,64,1024]{2,1,0:T(8,128)(2,1)S(1)}, u32[]{:S(2)}, u32[]{:S(2)}) collective-permute-start(bf16[2,64,1024]{2,1,0:T(8,128)(2,1)S(1)} %copy-done.1), channel_id=1, source_target_pairs={{0,6},{1,7},{2,4},{3,5},{4,2},{5,3},{6,0},{7,1},{8,14},{9,15},{10,... | collective-permute-start | bytes 786440 | tf_op jit(solution)/shard_map/ppermute | solution.py:87
  55.9 13.4 %collective-permute-start.8 = (bf16[2,64,1024]{2,1,0:T(8,128)(2,1)S(1)}, bf16[2,64,1024]{2,1,0:T(8,128)(2,1)}, u32[]{:S(2)}, u32[]{:S(2)}) collective-permute-start(bf16[2,64,1024]{2,1,0:T(8,128)(2,1)S(1)} %copy-done.1), channel_id=1, source_target_pairs={{0,4},{1,5},{2,6},{3,7},{4,0},{5,1},{6,2},{7,3},{8,12},{9,13},{10,... | collective-permute-start | bytes 786440 | tf_op jit(solution)/shard_map/ppermute | solution.py:87
  57.4 13.2 %collective-permute-start.7 = (bf16[2,64,1024]{2,1,0:T(8,128)(2,1)S(1)}, bf16[2,64,1024]{2,1,0:T(8,128)(2,1)}, u32[]{:S(2)}, u32[]{:S(2)}) collective-permute-start(bf16[2,64,1024]{2,1,0:T(8,128)(2,1)S(1)} %copy-done.1), channel_id=1, source_target_pairs={{0,2},{1,3},{2,0},{3,1},{4,6},{5,7},{6,4},{7,5},{8,10},{9,11},{10,... | collective-permute-start | bytes 786440 | tf_op jit(solution)/shard_map/ppermute | solution.py:87
  63.3 13.8 %collective-permute-start.44 = (bf16[512,128]{1,0:T(8,128)(2,1)}, bf16[512,128]{1,0:T(8,128)(2,1)S(1)}, u32[]{:S(2)}, u32[]{:S(2)}) collective-permute-start(bf16[512,128]{1,0:T(8,128)(2,1)} %shard_map.125.refs_0_), channel_id=1, source_target_pairs={{0,24},{1,25},{2,26},{3,27},{4,28},{5,29},{6,30},{7,31},{8,16},{9,... | collective-permute-start | bytes 393224 | tf_op jit(solution)/shard_map/ppermute | solution.py:87
  65.4 13.8 %collective-permute-start.40 = (bf16[512,128]{1,0:T(8,128)(2,1)}, bf16[512,128]{1,0:T(8,128)(2,1)S(1)}, u32[]{:S(2)}, u32[]{:S(2)}) collective-permute-start(bf16[512,128]{1,0:T(8,128)(2,1)} %shard_map.125.refs_0_), channel_id=1, source_target_pairs={{0,16},{1,17},{2,18},{3,19},{4,20},{5,21},{6,22},{7,23},{8,24},{9,... | collective-permute-start | bytes 393224 | tf_op jit(solution)/shard_map/ppermute | solution.py:87
  69.3 10.1 %collective-permute-start.36 = (bf16[512,128]{1,0:T(8,128)(2,1)}, bf16[512,128]{1,0:T(8,128)(2,1)S(1)}, u32[]{:S(2)}, u32[]{:S(2)}) collective-permute-start(bf16[512,128]{1,0:T(8,128)(2,1)} %shard_map.125.refs_0_), channel_id=1, source_target_pairs={{0,8},{1,9},{2,10},{3,11},{4,12},{5,13},{6,14},{7,15},{8,0},{9,1},... | collective-permute-start | bytes 393224 | tf_op jit(solution)/shard_map/ppermute | solution.py:87
  70.6 11.0 %collective-permute-start.34 = (bf16[512,128]{1,0:T(8,128)(2,1)}, bf16[512,128]{1,0:T(8,128)(2,1)S(1)}, u32[]{:S(2)}, u32[]{:S(2)}) collective-permute-start(bf16[512,128]{1,0:T(8,128)(2,1)} %shard_map.125.refs_0_), channel_id=1, source_target_pairs={{0,4},{1,5},{2,6},{3,7},{4,0},{5,1},{6,2},{7,3},{8,12},{9,13},{10,... | collective-permute-start | bytes 393224 | tf_op jit(solution)/shard_map/ppermute | solution.py:87
  71.1 11.3 %collective-permute-start.33 = (bf16[512,128]{1,0:T(8,128)(2,1)}, bf16[512,128]{1,0:T(8,128)(2,1)S(1)}, u32[]{:S(2)}, u32[]{:S(2)}) collective-permute-start(bf16[512,128]{1,0:T(8,128)(2,1)} %shard_map.125.refs_0_), channel_id=1, source_target_pairs={{0,2},{1,3},{2,0},{3,1},{4,6},{5,7},{6,4},{7,5},{8,10},{9,11},{10,... | collective-permute-start | bytes 393224 | tf_op jit(solution)/shard_map/ppermute | solution.py:87
  77.2 8.5 %collective-permute-start.21 = (bf16[512,128]{1,0:T(8,128)(2,1)}, bf16[512,128]{1,0:T(8,128)(2,1)S(1)}, u32[]{:S(2)}, u32[]{:S(2)}) collective-permute-start(bf16[512,128]{1,0:T(8,128)(2,1)} %shard_map.122.refs_0_), channel_id=1, source_target_pairs={{0,24},{1,25},{2,26},{3,27},{4,28},{5,29},{6,30},{7,31},{8,16},{9,... | collective-permute-start | bytes 393224 | tf_op jit(solution)/shard_map/ppermute | solution.py:87
  79.2 11.6 %collective-permute-start.17 = (bf16[512,128]{1,0:T(8,128)(2,1)}, bf16[512,128]{1,0:T(8,128)(2,1)S(1)}, u32[]{:S(2)}, u32[]{:S(2)}) collective-permute-start(bf16[512,128]{1,0:T(8,128)(2,1)} %shard_map.122.refs_0_), channel_id=1, source_target_pairs={{0,16},{1,17},{2,18},{3,19},{4,20},{5,21},{6,22},{7,23},{8,24},{9,... | collective-permute-start | bytes 393224 | tf_op jit(solution)/shard_map/ppermute | solution.py:87
  79.5 11.9 %collective-permute-start.13 = (bf16[512,128]{1,0:T(8,128)(2,1)}, bf16[512,128]{1,0:T(8,128)(2,1)S(1)}, u32[]{:S(2)}, u32[]{:S(2)}) collective-permute-start(bf16[512,128]{1,0:T(8,128)(2,1)} %shard_map.122.refs_0_), channel_id=1, source_target_pairs={{0,8},{1,9},{2,10},{3,11},{4,12},{5,13},{6,14},{7,15},{8,0},{9,1},... | collective-permute-start | bytes 393224 | tf_op jit(solution)/shard_map/ppermute | solution.py:87
  81.6 11.3 %collective-permute-start.11 = (bf16[512,128]{1,0:T(8,128)(2,1)}, bf16[512,128]{1,0:T(8,128)(2,1)S(1)}, u32[]{:S(2)}, u32[]{:S(2)}) collective-permute-start(bf16[512,128]{1,0:T(8,128)(2,1)} %shard_map.122.refs_0_), channel_id=1, source_target_pairs={{0,4},{1,5},{2,6},{3,7},{4,0},{5,1},{6,2},{7,3},{8,12},{9,13},{10,... | collective-permute-start | bytes 393224 | tf_op jit(solution)/shard_map/ppermute | solution.py:87
  82.5 10.9 %collective-permute-start.10 = (bf16[512,128]{1,0:T(8,128)(2,1)}, bf16[512,128]{1,0:T(8,128)(2,1)S(1)}, u32[]{:S(2)}, u32[]{:S(2)}) collective-permute-start(bf16[512,128]{1,0:T(8,128)(2,1)} %shard_map.122.refs_0_), channel_id=1, source_target_pairs={{0,2},{1,3},{2,0},{3,1},{4,6},{5,7},{6,4},{7,5},{8,10},{9,11},{10,... | collective-permute-start | bytes 393224 | tf_op jit(solution)/shard_map/ppermute | solution.py:87
  85.7 9.2 %collective-permute-start.46 = (bf16[512,128]{1,0:T(8,128)(2,1)S(1)}, bf16[512,128]{1,0:T(8,128)(2,1)S(1)}, u32[]{:S(2)}, u32[]{:S(2)}) collective-permute-start(bf16[512,128]{1,0:T(8,128)(2,1)S(1)} %collective-permute-done.44.refs_12_), channel_id=1, source_target_pairs={{0,4},{1,5},{2,6},{3,7},{4,0},{5,1},{6,2},{7,3},{8,12},{9,13},{10,... | collective-permute-start | bytes 393224 | tf_op jit(solution)/shard_map/ppermute | solution.py:87
  90.9 6.1 %collective-permute-start.45 = (bf16[512,128]{1,0:T(8,128)(2,1)S(1)}, bf16[512,128]{1,0:T(8,128)(2,1)S(1)}, u32[]{:S(2)}, u32[]{:S(2)}) collective-permute-start(bf16[512,128]{1,0:T(8,128)(2,1)S(1)} %collective-permute-done.44.refs_12_), channel_id=1, source_target_pairs={{0,2},{1,3},{2,0},{3,1},{4,6},{5,7},{6,4},{7,5},{8,10},{9,11},{10,... | collective-permute-start | bytes 393224 | tf_op jit(solution)/shard_map/ppermute | solution.py:87
  91.4 6.4 %collective-permute-start.42 = (bf16[512,128]{1,0:T(8,128)(2,1)S(1)}, bf16[512,128]{1,0:T(8,128)(2,1)S(1)}, u32[]{:S(2)}, u32[]{:S(2)}) collective-permute-start(bf16[512,128]{1,0:T(8,128)(2,1)S(1)} %collective-permute-done.40.refs_8_), channel_id=1, source_target_pairs={{0,4},{1,5},{2,6},{3,7},{4,0},{5,1},{6,2},{7,3},{8,12},{9,13},{10,... | collective-permute-start | bytes 393224 | tf_op jit(solution)/shard_map/ppermute | solution.py:87
  92.9 6.9 %collective-permute-start.41 = (bf16[512,128]{1,0:T(8,128)(2,1)S(1)}, bf16[512,128]{1,0:T(8,128)(2,1)S(1)}, u32[]{:S(2)}, u32[]{:S(2)}) collective-permute-start(bf16[512,128]{1,0:T(8,128)(2,1)S(1)} %collective-permute-done.40.refs_8_), channel_id=1, source_target_pairs={{0,2},{1,3},{2,0},{3,1},{4,6},{5,7},{6,4},{7,5},{8,10},{9,11},{10,... | collective-permute-start | bytes 393224 | tf_op jit(solution)/shard_map/ppermute | solution.py:87
  93.3 7.3 %collective-permute-start.38 = (bf16[512,128]{1,0:T(8,128)(2,1)S(1)}, bf16[512,128]{1,0:T(8,128)(2,1)S(1)}, u32[]{:S(2)}, u32[]{:S(2)}) collective-permute-start(bf16[512,128]{1,0:T(8,128)(2,1)S(1)} %collective-permute-done.36.refs_4_), channel_id=1, source_target_pairs={{0,4},{1,5},{2,6},{3,7},{4,0},{5,1},{6,2},{7,3},{8,12},{9,13},{10,... | collective-permute-start | bytes 393224 | tf_op jit(solution)/shard_map/ppermute | solution.py:87
  94.9 8.5 %collective-permute-start.23 = (bf16[512,128]{1,0:T(8,128)(2,1)S(1)}, bf16[512,128]{1,0:T(8,128)(2,1)S(1)}, u32[]{:S(2)}, u32[]{:S(2)}) collective-permute-start(bf16[512,128]{1,0:T(8,128)(2,1)S(1)} %collective-permute-done.21.refs_12_), channel_id=1, source_target_pairs={{0,4},{1,5},{2,6},{3,7},{4,0},{5,1},{6,2},{7,3},{8,12},{9,13},{10,... | collective-permute-start | bytes 393224 | tf_op jit(solution)/shard_map/ppermute | solution.py:87
  97.0 7.9 %collective-permute-start.22 = (bf16[512,128]{1,0:T(8,128)(2,1)S(1)}, bf16[512,128]{1,0:T(8,128)(2,1)S(1)}, u32[]{:S(2)}, u32[]{:S(2)}) collective-permute-start(bf16[512,128]{1,0:T(8,128)(2,1)S(1)} %collective-permute-done.21.refs_12_), channel_id=1, source_target_pairs={{0,2},{1,3},{2,0},{3,1},{4,6},{5,7},{6,4},{7,5},{8,10},{9,11},{10,... | collective-permute-start | bytes 393224 | tf_op jit(solution)/shard_map/ppermute | solution.py:87
  97.8 8.4 %collective-permute-start.19 = (bf16[512,128]{1,0:T(8,128)(2,1)S(1)}, bf16[512,128]{1,0:T(8,128)(2,1)S(1)}, u32[]{:S(2)}, u32[]{:S(2)}) collective-permute-start(bf16[512,128]{1,0:T(8,128)(2,1)S(1)} %collective-permute-done.17.refs_8_), channel_id=1, source_target_pairs={{0,4},{1,5},{2,6},{3,7},{4,0},{5,1},{6,2},{7,3},{8,12},{9,13},{10,... | collective-permute-start | bytes 393224 | tf_op jit(solution)/shard_map/ppermute | solution.py:87
  99.8 7.9 %collective-permute-start.18 = (bf16[512,128]{1,0:T(8,128)(2,1)S(1)}, bf16[512,128]{1,0:T(8,128)(2,1)S(1)}, u32[]{:S(2)}, u32[]{:S(2)}) collective-permute-start(bf16[512,128]{1,0:T(8,128)(2,1)S(1)} %collective-permute-done.17.refs_8_), channel_id=1, source_target_pairs={{0,2},{1,3},{2,0},{3,1},{4,6},{5,7},{6,4},{7,5},{8,10},{9,11},{10,... | collective-permute-start | bytes 393224 | tf_op jit(solution)/shard_map/ppermute | solution.py:87
  100.6 7.7 %collective-permute-start.14 = (bf16[512,128]{1,0:T(8,128)(2,1)S(1)}, bf16[512,128]{1,0:T(8,128)(2,1)S(1)}, u32[]{:S(2)}, u32[]{:S(2)}) collective-permute-start(bf16[512,128]{1,0:T(8,128)(2,1)S(1)} %collective-permute-done.13.refs_4_), channel_id=1, source_target_pairs={{0,2},{1,3},{2,0},{3,1},{4,6},{5,7},{6,4},{7,5},{8,10},{9,11},{10,... | collective-permute-start | bytes 393224 | tf_op jit(solution)/shard_map/ppermute | solution.py:87
  103.5 6.5 %collective-permute-start.15 = (bf16[512,128]{1,0:T(8,128)(2,1)S(1)}, bf16[512,128]{1,0:T(8,128)(2,1)S(1)}, u32[]{:S(2)}, u32[]{:S(2)}) collective-permute-start(bf16[512,128]{1,0:T(8,128)(2,1)S(1)} %collective-permute-done.13.refs_4_), channel_id=1, source_target_pairs={{0,4},{1,5},{2,6},{3,7},{4,0},{5,1},{6,2},{7,3},{8,12},{9,13},{10,... | collective-permute-start | bytes 393224 | tf_op jit(solution)/shard_map/ppermute | solution.py:87
  104.9 7.8 %collective-permute-start.12 = (bf16[512,128]{1,0:T(8,128)(2,1)S(1)}, bf16[512,128]{1,0:T(8,128)(2,1)S(1)}, u32[]{:S(2)}, u32[]{:S(2)}) collective-permute-start(bf16[512,128]{1,0:T(8,128)(2,1)S(1)} %collective-permute-done.10.refs_1_), channel_id=1, source_target_pairs={{0,4},{1,5},{2,6},{3,7},{4,0},{5,1},{6,2},{7,3},{8,12},{9,13},{10,... | collective-permute-start | bytes 393224 | tf_op jit(solution)/shard_map/ppermute | solution.py:87
  106.3 8.7 %collective-permute-start.24 = (bf16[512,128]{1,0:T(8,128)(2,1)S(1)}, bf16[512,128]{1,0:T(8,128)(2,1)S(1)}, u32[]{:S(2)}, u32[]{:S(2)}) collective-permute-start(bf16[512,128]{1,0:T(8,128)(2,1)S(1)} %collective-permute-done.22.refs_13_), channel_id=1, source_target_pairs={{0,4},{1,5},{2,6},{3,7},{4,0},{5,1},{6,2},{7,3},{8,12},{9,13},{10,... | collective-permute-start | bytes 393224 | tf_op jit(solution)/shard_map/ppermute | solution.py:87
  107.7 8.8 %collective-permute-start.20 = (bf16[512,128]{1,0:T(8,128)(2,1)S(1)}, bf16[512,128]{1,0:T(8,128)(2,1)S(1)}, u32[]{:S(2)}, u32[]{:S(2)}) collective-permute-start(bf16[512,128]{1,0:T(8,128)(2,1)S(1)} %collective-permute-done.18.refs_9_), channel_id=1, source_target_pairs={{0,4},{1,5},{2,6},{3,7},{4,0},{5,1},{6,2},{7,3},{8,12},{9,13},{10,... | collective-permute-start | bytes 393224 | tf_op jit(solution)/shard_map/ppermute | solution.py:87
  108.3 9.7 %collective-permute-start.16 = (bf16[512,128]{1,0:T(8,128)(2,1)S(1)}, bf16[512,128]{1,0:T(8,128)(2,1)S(1)}, u32[]{:S(2)}, u32[]{:S(2)}) collective-permute-start(bf16[512,128]{1,0:T(8,128)(2,1)S(1)} %collective-permute-done.14.refs_5_), channel_id=1, source_target_pairs={{0,4},{1,5},{2,6},{3,7},{4,0},{5,1},{6,2},{7,3},{8,12},{9,13},{10,... | collective-permute-start | bytes 393224 | tf_op jit(solution)/shard_map/ppermute | solution.py:87
  109.9 17.1 %collective-permute-start.37 = (bf16[512,128]{1,0:T(8,128)(2,1)S(1)}, bf16[512,128]{1,0:T(8,128)(2,1)S(1)}, u32[]{:S(2)}, u32[]{:S(2)}) collective-permute-start(bf16[512,128]{1,0:T(8,128)(2,1)S(1)} %collective-permute-done.36.refs_4_), channel_id=1, source_target_pairs={{0,2},{1,3},{2,0},{3,1},{4,6},{5,7},{6,4},{7,5},{8,10},{9,11},{10,... | collective-permute-start | bytes 393224 | tf_op jit(solution)/shard_map/ppermute | solution.py:87
  112.7 14.3 %collective-permute-start.35 = (bf16[512,128]{1,0:T(8,128)(2,1)S(1)}, bf16[512,128]{1,0:T(8,128)(2,1)S(1)}, u32[]{:S(2)}, u32[]{:S(2)}) collective-permute-start(bf16[512,128]{1,0:T(8,128)(2,1)S(1)} %collective-permute-done.34.refs_2_), channel_id=1, source_target_pairs={{0,2},{1,3},{2,0},{3,1},{4,6},{5,7},{6,4},{7,5},{8,10},{9,11},{10,... | collective-permute-start | bytes 393224 | tf_op jit(solution)/shard_map/ppermute | solution.py:87
  115.0 12.1 %collective-permute-start.47 = (bf16[512,128]{1,0:T(8,128)(2,1)S(1)}, bf16[512,128]{1,0:T(8,128)(2,1)S(1)}, u32[]{:S(2)}, u32[]{:S(2)}) collective-permute-start(bf16[512,128]{1,0:T(8,128)(2,1)S(1)} %collective-permute-done.46.refs_14_), channel_id=1, source_target_pairs={{0,2},{1,3},{2,0},{3,1},{4,6},{5,7},{6,4},{7,5},{8,10},{9,11},{10,... | collective-permute-start | bytes 393224 | tf_op jit(solution)/shard_map/ppermute | solution.py:87
  116.6 10.5 %collective-permute-start.43 = (bf16[512,128]{1,0:T(8,128)(2,1)S(1)}, bf16[512,128]{1,0:T(8,128)(2,1)S(1)}, u32[]{:S(2)}, u32[]{:S(2)}) collective-permute-start(bf16[512,128]{1,0:T(8,128)(2,1)S(1)} %collective-permute-done.42.refs_10_), channel_id=1, source_target_pairs={{0,2},{1,3},{2,0},{3,1},{4,6},{5,7},{6,4},{7,5},{8,10},{9,11},{10,... | collective-permute-start | bytes 393224 | tf_op jit(solution)/shard_map/ppermute | solution.py:87
  118.0 9.1 %collective-permute-start.39 = (bf16[512,128]{1,0:T(8,128)(2,1)S(1)}, bf16[512,128]{1,0:T(8,128)(2,1)S(1)}, u32[]{:S(2)}, u32[]{:S(2)}) collective-permute-start(bf16[512,128]{1,0:T(8,128)(2,1)S(1)} %collective-permute-done.38.refs_6_), channel_id=1, source_target_pairs={{0,2},{1,3},{2,0},{3,1},{4,6},{5,7},{6,4},{7,5},{8,10},{9,11},{10,... | collective-permute-start | bytes 393224 | tf_op jit(solution)/shard_map/ppermute | solution.py:87
  138.7 6.7 %collective-permute-start.48 = (f32[1024,512]{1,0:T(8,128)}, f32[1024,512]{1,0:T(8,128)}, u32[]{:S(2)}, u32[]{:S(2)}) collective-permute-start(f32[1024,512]{1,0:T(8,128)} %shard_map.126), channel_id=1, source_target_pairs={{0,1},{1,0},{2,3},{3,2},{4,5},{5,4},{6,7},{7,6},{8,9},{9,8},{10,11... | collective-permute-start | bytes 6291464 | tf_op jit(solution)/shard_map/ppermute | solution.py:87
  138.8 10.8 %collective-permute-start.25 = (bf16[2048,512]{1,0:T(8,128)(2,1)S(1)}, bf16[2048,512]{1,0:T(8,128)(2,1)}, u32[]{:S(2)}, u32[]{:S(2)}) collective-permute-start(bf16[2048,512]{1,0:T(8,128)(2,1)S(1)} %copy-done), channel_id=1, source_target_pairs={{0,1},{1,0},{2,3},{3,2},{4,5},{5,4},{6,7},{7,6},{8,9},{9,8},{10,11... | collective-permute-start | bytes 6291464 | tf_op jit(solution)/shard_map/ppermute | solution.py:87
  (47 other events, 924.1 us)

commit v3 on v1

v3 whole, which is shorter than its diff:
```python
import functools

import jax
import jax.numpy as jnp
from jax import lax
from jax.experimental import pallas as pl
from jax.experimental.pallas import tpu as pltpu
from jax.sharding import PartitionSpec as P

AXES = ("rows", "grp")
F32 = jnp.float32
BF16 = jnp.bfloat16


def aggregate(panel_vals, strip_columns, strip_count, everyone, own_rows):
    blocks, size_block, span_width = panel_vals.shape
    slot_count = span_width // size_block
    channels = everyone.shape[1]
    block_table = everyone.reshape(-1, size_block, channels)
    slot_ids = lax.broadcasted_iota(jnp.int32, strip_columns.shape, 1)
    weights = (slot_ids < strip_count[:, None]).astype(everyone.dtype)
    picked = (block_table[strip_columns] * weights[:, :, None, None]).reshape(
        blocks, slot_count * size_block, channels
    )
    summed_rows = jnp.einsum("bik,bkc->bic", panel_vals, picked, preferred_element_type=F32)
    return summed_rows.reshape(blocks * size_block, channels) + own_rows.astype(F32)


def gathered_shards(
    features,
    tile_entries,
    tile_columns,
    tiles_per_row,
    rev_vals,
    rev_cols,
    rev_count,
    w_first,
    w_second,
    cotangent,
):
    channels = features.shape[1]
    pair = jnp.concatenate([features, cotangent], axis=1)
    pair_all = lax.all_gather(pair, AXES, axis=0, tiled=True)
    mixed_own = aggregate(
        tile_entries, tile_columns, tiles_per_row, pair_all[:, :channels], features
    ).astype(BF16)
    spread_own = aggregate(
        rev_vals, rev_cols, rev_count, pair_all[:, channels:], cotangent
    ).astype(BF16)
    both_all = lax.all_gather(
        jnp.concatenate([mixed_own, spread_own], axis=1), AXES, axis=0, tiled=True
    )
    mixed = both_all[:, :channels]
    spread = both_all[:, channels:]
    pre_first = jnp.dot(mixed, w_first, preferred_element_type=F32)
    sig = jax.nn.sigmoid(pre_first)
    hidden = (pre_first * sig).astype(BF16)
    slope = sig * (1.0 + pre_first * (1.0 - sig))
    back_hidden = lax.dot_general(
        spread, w_second, (((1,), (1,)), ((), ())), preferred_element_type=F32
    )
    back_first = (back_hidden * slope).astype(BF16)
    grad_first = lax.dot_general(
        mixed, back_first, (((0,), (0,)), ((), ())), preferred_element_type=F32
    )
    grad_second = lax.dot_general(
        hidden, spread, (((0,), (0,)), ((), ())), preferred_element_type=F32
    )
    position = lax.axis_index(AXES) * features.shape[0]
    hidden_own = lax.dynamic_slice_in_dim(hidden, position, features.shape[0], 0)
    mixed_second = aggregate(
        tile_entries, tile_columns, tiles_per_row, hidden, hidden_own
    ).astype(BF16)
    z_out = jnp.dot(mixed_second, w_second, preferred_element_type=F32).astype(BF16)
    return (z_out, grad_first, grad_second)


CORE = 1
DEVICES, QUAD, PLANES, SLOTS, BLOCK = 32, 4, 4, 16, 64
LANES = 128
ROWS = 128
SPAN = QUAD * ROWS
VMEM = pl.BlockSpec(memory_space=pltpu.VMEM)
SMEM = pl.BlockSpec(memory_space=pltpu.SMEM)
ANY = pl.BlockSpec(memory_space=pl.ANY)
PARAMS = pltpu.CompilerParams(vmem_limit_bytes=48 * 1024 * 1024)


def call(body, out_shape, operands, spaces, scratch=()):
    return pl.pallas_call(
        body,
        out_shape=out_shape,
        in_specs=list(spaces),
        out_specs=jax.tree.map(lambda _: VMEM, out_shape),
        scratch_shapes=list(scratch),
        compiler_params=PARAMS,
    )(*operands)


def shaped(rows, columns, dtype=BF16):
    return jax.ShapeDtypeStruct((rows, columns), dtype)


def swap(value, mask):
    return lax.ppermute(value, AXES, [(i, i ^ mask) for i in range(DEVICES)])


def over_quad(value):
    return [value] + [swap(value, 2 * q) for q in range(1, QUAD)]


def over_planes(value):
    return [value] + [swap(value, 8 * j) for j in range(1, PLANES)]


def chip(pos):
    return (pos[0] >> 1) & 3


def lanes_of(column):
    return pl.ds(pl.multiple_of(column * LANES, LANES), LANES)


def pack_body(pos, columns, counts, back_columns, back_counts, features, cotangent, *outs):
    line = lax.broadcasted_iota(jnp.int32, (16, LANES), 0)
    lane = lax.broadcasted_iota(jnp.int32, (16, LANES), 1)
    codes = jnp.full((16, LANES), -1, jnp.int32)
    for r, (table, count) in enumerate(((columns, counts), (back_columns, back_counts))):
        for w in range(2):
            for s in range(SLOTS):
                value = jnp.where(s < count[w], table[w, s], -1)
                codes = jnp.where((line == 2 * r + w) & (lane == s), value, codes)
    codes = codes.astype(F32).astype(BF16)
    for q, out in enumerate(outs):
        share = lanes_of(chip(pos) ^ q)
        out[:ROWS, :LANES] = features[:, share]
        out[:ROWS, LANES:] = cotangent[:, share]
        out[ROWS:, :LANES] = codes
        out[ROWS:, LANES:] = codes


def pack(pos, columns, counts, back_columns, back_counts, features, cotangent):
    return call(
        pack_body,
        (shaped(ROWS + 16, 2 * LANES),) * QUAD,
        (pos, columns, counts, back_columns, back_counts, features, cotangent),
        [SMEM] * 5 + [VMEM] * 2,
    )


def unpack_body(pos, *refs):
    parts, (forward, backward, places) = refs[:QUAD], refs[QUAD:]
    for q, part in enumerate(parts):
        rows = pl.ds(q * ROWS, ROWS)
        forward[rows, :] = part[:ROWS, :LANES]
        backward[rows, :] = part[:ROWS, LANES:]
        block = part[ROWS:, :LANES].astype(F32).astype(jnp.int32)
        apart = (block >> 1) ^ pos[0]
        place = ((apart & 1) * 16 + (apart >> 3) * 4 + ((apart >> 1) & 3)) * 2 + (block & 1)
        place = jnp.where(block < 0, 2 * DEVICES, place)
        places[q * 8 : q * 8 + 8, :] = place[:8, :]


def unpack(pos, parts):
    return call(
        unpack_body,
        (shaped(SPAN, LANES), shaped(SPAN, LANES), shaped(8 * QUAD, LANES, jnp.int32)),
        (pos, *parts),
        [SMEM] + [VMEM] * QUAD,
    )


def mix_body(base, split, places, *refs):
    shares, tiles, outs = refs[:8], refs[8:12], refs[12:-3]
    table, picked, sems = refs[-3:]
    copies = []
    for i, share in enumerate(shares):
        copies.append(pltpu.make_async_copy(share, table.at[pl.ds(i * SPAN, SPAN), :], sems.at[i]))
        copies[-1].start()
    table[DEVICES * ROWS :, :] = jnp.zeros((BLOCK, LANES), BF16)
    for copy in copies:
        copy.wait()
    for q in range(QUAD):
        for w in range(2):
            row = q * 2 + w
            for s in range(SLOTS):
                first = pl.multiple_of(places[q * 8 + base + w, s] * BLOCK, BLOCK)
                picked[row, pl.ds(s * BLOCK, BLOCK), :] = table[pl.ds(first, BLOCK), :]
            total = jnp.dot(tiles[q][w], picked[row], preferred_element_type=F32)
            total = total + table[pl.ds(row * BLOCK, BLOCK), :].astype(F32)
            if split:
                outs[q][pl.ds(w * BLOCK, BLOCK), :] = total.astype(BF16)
            else:
                outs[0][pl.ds(row * BLOCK, BLOCK), :] = total.astype(BF16)


def mix(places, base, planes, other_core, tiles, split=False):
    return call(
        functools.partial(mix_body, base, split),
        (shaped(ROWS, LANES),) * QUAD if split else (shaped(SPAN, LANES),),
        (places, *planes, *other_core, *tiles),
        [SMEM] + [ANY] * 8 + [VMEM] * 4,
        [
            pltpu.VMEM((DEVICES * ROWS + BLOCK, LANES), BF16),
            pltpu.VMEM((2 * QUAD, SLOTS * BLOCK, LANES), BF16),
            pltpu.SemaphoreType.DMA((8,)),
        ],
    )


def whole_rows(pos, pieces, target):
    for p, piece in enumerate(pieces):
        share = lanes_of(chip(pos) ^ p)
        for q in range(QUAD):
            target[pl.ds(q * ROWS, ROWS), share] = piece[pl.ds((p ^ q) * ROWS, ROWS), :]


def first_body(pos, p0, p1, p2, p3, w_first, mixed, hidden, hidden_share, slope, full):
    whole_rows(pos, (p0, p1, p2, p3), mixed)
    pre = jnp.dot(mixed[...], w_first[...], preferred_element_type=F32)
    sig = jax.nn.sigmoid(pre)
    hidden[...] = (pre * sig).astype(BF16)
    full[...] = sig * (1.0 + pre * (1.0 - sig))
    share = lanes_of(chip(pos))
    hidden_share[...] = hidden[:, share]
    slope[...] = full[:, share]


def first_layer(pos, pieces, w_first):
    channels = w_first.shape[0]
    return call(
        first_body,
        (
            shaped(SPAN, channels),
            shaped(SPAN, channels),
            shaped(SPAN, LANES),
            shaped(SPAN, LANES, F32),
        ),
        (pos, *pieces, w_first),
        [SMEM] + [VMEM] * 5,
        [pltpu.VMEM((SPAN, channels), F32)],
    )


def second_body(pos, p0, p1, p2, p3, w_second, z_out):
    total = jnp.zeros(z_out.shape, F32)
    for p, piece in enumerate((p0, p1, p2, p3)):
        total = total + jnp.dot(
            piece[...], w_second[lanes_of(chip(pos) ^ p), :], preferred_element_type=F32
        )
    z_out[...] = total.astype(BF16)


def second_layer(pos, pieces, w_second):
    return call(
        second_body,
        shaped(ROWS, w_second.shape[0]),
        (pos, *pieces, w_second),
        [SMEM] + [VMEM] * 5,
    )


def grads_body(pos, mixed, hidden, slope, p0, p1, p2, p3, w_second, keep, send, spread):
    whole_rows(pos, (p0, p1, p2, p3), spread)
    back_hidden = lax.dot_general(
        spread[...],
        w_second[lanes_of(chip(pos)), :],
        (((1,), (1,)), ((), ())),
        preferred_element_type=F32,
    )
    back_first = (back_hidden * slope[...]).astype(BF16)
    over_rows = (((0,), (0,)), ((), ()))
    first = lax.dot_general(mixed[...], back_first, over_rows, preferred_element_type=F32)
    second = lax.dot_general(hidden[...], p0[...], over_rows, preferred_element_type=F32)
    keeps_first = (pos[0] & 1) == 0

    @pl.when(keeps_first)
    def _():
        keep[...] = first
        send[...] = second

    @pl.when(jnp.logical_not(keeps_first))
    def _():
        keep[...] = second
        send[...] = first


def gradients(pos, mixed, hidden, slope, pieces, w_second):
    channels = w_second.shape[0]
    return call(
        grads_body,
        (shaped(channels, LANES, F32), shaped(channels, LANES, F32)),
        (pos, mixed, hidden, slope, *pieces, w_second),
        [SMEM] + [VMEM] * 8,
        [pltpu.VMEM((SPAN, channels), BF16)],
    )


def place_body(pos, *refs):
    mine, other, (first, second) = refs[:QUAD], refs[QUAD : 2 * QUAD], refs[2 * QUAD :]
    keeps_first = (pos[0] & 1) == 0

    def fill(mine_out, other_out):
        for p in range(QUAD):
            share = lanes_of(chip(pos) ^ p)
            mine_out[:, share] = mine[p][...].astype(F32)
            other_out[:, share] = other[p][...].astype(F32)

    @pl.when(keeps_first)
    def _():
        fill(first, second)

    @pl.when(jnp.logical_not(keeps_first))
    def _():
        fill(second, first)


def place(pos, mine, other):
    channels = mine[0].shape[0]
    return call(
        place_body,
        (shaped(channels, channels, F32),) * 2,
        (pos, *mine, *other),
        [SMEM] + [VMEM] * (2 * QUAD),
    )


def planned_shards(
    features,
    tile_entries,
    tile_columns,
    tiles_per_row,
    rev_vals,
    rev_cols,
    rev_count,
    w_first,
    w_second,
    cotangent,
):
    pos = lax.axis_index(AXES).astype(jnp.int32).reshape(1)
    packed = pack(pos, tile_columns, tiles_per_row, rev_cols, rev_count, features, cotangent)
    parts = [packed[0]] + [swap(packed[q], 2 * q) for q in range(1, QUAD)]
    forward, backward, places = unpack(pos, parts)
    tile_entries, _ = lax.optimization_barrier((tile_entries, parts[1]))
    tiles = over_quad(tile_entries)
    rev_vals, _ = lax.optimization_barrier((rev_vals, tiles[1]))
    back_tiles = over_quad(rev_vals)

    def both_cores(share):
        planes = over_planes(share)
        return planes, [swap(plane, CORE) for plane in planes]

    (mixed_share,) = mix(places, 0, *both_cores(forward), tiles)
    (spread_share,) = mix(places, 2, *both_cores(backward), back_tiles)
    mixed, hidden, hidden_share, slope = first_layer(pos, over_quad(mixed_share), w_first)
    again = mix(places, 0, *both_cores(hidden_share), tiles, split=True)
    z_out = second_layer(
        pos, [again[0]] + [swap(again[q], 2 * q) for q in range(1, QUAD)], w_second
    )
    keep, send = gradients(pos, mixed, hidden, slope, over_quad(spread_share), w_second)
    part = (keep + swap(send, CORE)).astype(BF16)
    near, z1, z2, z3 = (plane.astype(F32) for plane in over_planes(part))
    total = ((near + z1) + (z2 + z3)).astype(BF16)
    mine = over_quad(total)
    grad_first, grad_second = place(pos, mine, [swap(piece, CORE) for piece in mine])
    return (z_out, grad_first, grad_second)


def solution(mesh):
    placed = (
        P(AXES, None),
        P(AXES, None, None),
        P(AXES, None),
        P(AXES),
        P(AXES, None, None),
        P(AXES, None),
        P(AXES),
        P(),
        P(),
        P(AXES, None),
    )
    planned = mesh.shape["rows"] == 8 and mesh.shape["grp"] == 4
    return jax.shard_map(
        planned_shards if planned else gathered_shards,
        mesh=mesh,
        in_specs=placed,
        out_specs=(P(AXES, None), P(), P()),
        check_vma=False,
    )
```

time: 222 us -> 130 us (0.59)
  waiting for transfers between devices: 155 us -> 68.5 us
  starting transfers between devices: 0.08 us -> 44.6 us
  matrix products: 28.7 us -> 0 us
  local copies, waits for them, and re-layouts: 16.4 us -> 2.51 us
  between operations: 14.2 us -> 0.85 us
  Pallas kernels: 0 us -> 13.3 us
  other arithmetic: 6.43 us -> 0.1 us
    all_gather x2 -> x0, waiting for transfers between devices: 155 us -> none  [the longest x1 79.3 us: shards(): pair_all = lax.all_gather(pair, AXES, axis=0, tiled=True)]
    ppermute x0 -> x50, waiting for transfers between devices: none -> 68.5 us  [swap(): return lax.ppermute(value, AXES, [(i, i ^ mask) for i in range(DEVICES)])]
    ppermute x0 -> x50, starting transfers between devices: none -> 44.6 us  [swap(): return lax.ppermute(value, AXES, [(i, i ^ mask) for i in range(DEVICES)])]
    dot_general x7 -> x0, matrix products: 28.7 us -> none  [the longest x1 12.8 us: shards(): lax.dot_general(mixed, back_first, (((0,), (0,)), ((), ())), preferred_el...]
    pallas_call x0 -> x9, Pallas kernels: none -> 13.3 us  [call(): pl.pallas_call(body, out_shape=out_shape, in_specs=list(spaces), out_spec...]
    gather x3 -> x0, local copies, waits for them, and re-layouts: 8.69 us -> none  [aggregate(): block_table[strip_columns] * weights[:, :, None, None]]
    slice x1 -> x0, local copies, waits for them, and re-layouts: 5.72 us -> none  [shards(): pair_all[:, :channels]]
    concatenate x2 -> x0, other arithmetic: 2.47 us -> none  [the longest x1 1.74 us: shards(): pair = jnp.concatenate([features, cotangent], axis=1)]
  transfers between devices with their start and end apart: 2 -> 50, of which waited for: 2 -> 19; matrix products, arithmetic and copies ran while one was open for 2% -> 0% of each run, Pallas kernels for 0% -> 8%
where the time goes in v3:
time: 130 us
  waiting for transfers between devices  68.5 us (53%)
  starting transfers between devices  44.6 us (34%)
  Pallas kernels  13.3 us (10%)
  local copies, waits for them, and re-layouts  2.51 us (2%)
    ppermute x50, waiting for transfers between devices, swap(): return lax.ppermute(value, AXES, [(i, i ^ mask) for i in range(DEVICES)])  68.5 us
    ppermute x50, starting transfers between devices, swap(): return lax.ppermute(value, AXES, [(i, i ^ mask) for i in range(DEVICES)])  44.6 us
    pallas_call x9, Pallas kernels, call(): pl.pallas_call(body, out_shape=out_shape, in_specs=list(spaces), out_spec...  13.3 us
  transfers between devices with their start and end apart: 50, of which 19 were waited for; matrix products, arithmetic and copies ran while one was open for 0% of the time, Pallas kernels for 8%

profile of v3, /device:TPU:0, one launch (start us, length us, event | category | flops | bytes accessed | tf_op | source)
XLA Modules:
  0.0 129.9 jit_solution(18155511241848628843)
XLA Ops:
  1.4 0.9 copy-done.4
  2.3 0.9 copy-done.5
  3.9 3.0 %collective-permute-start = (bf16[144,256]{1,0:T(8,128)(2,1)S(1)}, bf16[144,256]{1,0:T(8,128)(2,1)S(1)}, u32[]{:S(2)}, u32[]{:S(2)}) collective-permute-start(bf16[144,256]{1,0:T(8,128)(2,1)S(1)} %get-tuple-element.25), channel_id=1, source_target_pairs={{0,2},{1,3},{2,0},{3,1},{4,6},{5,7},{6,4},{7,5},{8,10},{9,11},{10,... | collective-permute-start | bytes 221192 | tf_op jit(solution)/shard_map/ppermute | solution.py:105
  6.9 1.5 %collective-permute-start.1 = (bf16[144,256]{1,0:T(8,128)(2,1)S(1)}, bf16[144,256]{1,0:T(8,128)(2,1)S(1)}, u32[]{:S(2)}, u32[]{:S(2)}) collective-permute-start(bf16[144,256]{1,0:T(8,128)(2,1)S(1)} %get-tuple-element.26), channel_id=1, source_target_pairs={{0,4},{1,5},{2,6},{3,7},{4,0},{5,1},{6,2},{7,3},{8,12},{9,13},{10,... | collective-permute-start | bytes 221192 | tf_op jit(solution)/shard_map/ppermute | solution.py:105
  8.4 1.0 collective-permute-done.refs_1_
  9.4 1.8 %collective-permute-done.1.refs_2_ = bf16[144,256]{1,0:T(8,128)(2,1)S(1)} collective-permute-done((bf16[144,256]{1,0:T(8,128)(2,1)S(1)}, bf16[144,256]{1,0:T(8,128)(2,1)S(1)}, u32[]{:S(2)}, u32[]{:S(2)}) %collective-permute-start.1) | collective-permute-done | bytes 73760 | tf_op jit(solution)/shard_map/ppermute | solution.py:105
  11.2 2.4 %collective-permute-done.2.refs_3_ = bf16[144,256]{1,0:T(8,128)(2,1)S(1)} collective-permute-done((bf16[144,256]{1,0:T(8,128)(2,1)S(1)}, bf16[144,256]{1,0:T(8,128)(2,1)S(1)}, u32[]{:S(2)}, u32[]{:S(2)}) %collective-permute-start.2) | collective-permute-done | bytes 73760 | tf_op jit(solution)/shard_map/ppermute | solution.py:105
  13.8 3.7 %collective-permute-start.5 = (bf16[512,128]{1,0:T(8,128)(2,1)S(1)}, bf16[512,128]{1,0:T(8,128)(2,1)S(1)}, u32[]{:S(2)}, u32[]{:S(2)}) collective-permute-start(bf16[512,128]{1,0:T(8,128)(2,1)S(1)} %get-tuple-element.29.refs_0_), channel_id=1, source_target_pairs={{0,24},{1,25},{2,26},{3,27},{4,28},{5,29},{6,30},{7,31},{8,16},{9,... | collective-permute-start | bytes 393224 | tf_op jit(solution)/shard_map/ppermute | solution.py:105
  17.4 0.8 collective-permute-start.3
  18.8 3.2 %collective-permute-done.5.refs_3_ = bf16[512,128]{1,0:T(8,128)(2,1)S(1)} collective-permute-done((bf16[512,128]{1,0:T(8,128)(2,1)S(1)}, bf16[512,128]{1,0:T(8,128)(2,1)S(1)}, u32[]{:S(2)}, u32[]{:S(2)}) %collective-permute-start.5) | collective-permute-done | bytes 131104 | tf_op jit(solution)/shard_map/ppermute | solution.py:105
  22.0 3.6 %collective-permute-start.28 = (bf16[512,128]{1,0:T(8,128)(2,1)S(1)}, bf16[512,128]{1,0:T(8,128)(2,1)S(1)}, u32[]{:S(2)}, u32[]{:S(2)}) collective-permute-start(bf16[512,128]{1,0:T(8,128)(2,1)S(1)} %get-tuple-element.39.refs_0_), channel_id=1, source_target_pairs={{0,24},{1,25},{2,26},{3,27},{4,28},{5,29},{6,30},{7,31},{8,16},{9,... | collective-permute-start | bytes 393224 | tf_op jit(solution)/shard_map/ppermute | solution.py:105
  25.7 6.7 %collective-permute-done.4.refs_2_ = bf16[512,128]{1,0:T(8,128)(2,1)S(1)} collective-permute-done((bf16[512,128]{1,0:T(8,128)(2,1)S(1)}, bf16[512,128]{1,0:T(8,128)(2,1)S(1)}, u32[]{:S(2)}, u32[]{:S(2)}) %collective-permute-start.4) | collective-permute-done | bytes 131104 | tf_op jit(solution)/shard_map/ppermute | solution.py:105
  32.4 3.0 %collective-permute-start.26 = (bf16[512,128]{1,0:T(8,128)(2,1)S(1)}, bf16[512,128]{1,0:T(8,128)(2,1)S(1)}, u32[]{:S(2)}, u32[]{:S(2)}) collective-permute-start(bf16[512,128]{1,0:T(8,128)(2,1)S(1)} %get-tuple-element.39.refs_0_), channel_id=1, source_target_pairs={{0,8},{1,9},{2,10},{3,11},{4,12},{5,13},{6,14},{7,15},{8,0},{9,1},... | collective-permute-start | bytes 393224 | tf_op jit(solution)/shard_map/ppermute | solution.py:105
  36.0 4.6 %collective-permute-done.27.refs_2_ = bf16[512,128]{1,0:T(8,128)(2,1)S(1)} collective-permute-done((bf16[512,128]{1,0:T(8,128)(2,1)S(1)}, bf16[512,128]{1,0:T(8,128)(2,1)S(1)}, u32[]{:S(2)}, u32[]{:S(2)}) %collective-permute-start.27) | collective-permute-done | bytes 131104 | tf_op jit(solution)/shard_map/ppermute | solution.py:105
  41.9 1.4 %collective-permute-start.35 = (bf16[2,64,1024]{2,1,0:T(8,128)(2,1)S(1)}, bf16[2,64,1024]{2,1,0:T(8,128)(2,1)S(1)}, u32[]{:S(2)}, u32[]{:S(2)}) collective-permute-start(bf16[2,64,1024]{2,1,0:T(8,128)(2,1)S(1)} %copy-done.3), channel_id=1, source_target_pairs={{0,6},{1,7},{2,4},{3,5},{4,2},{5,3},{6,0},{7,1},{8,14},{9,15},{10,... | collective-permute-start | bytes 786440 | tf_op jit(solution)/shard_map/ppermute | solution.py:105
  43.3 0.9 collective-permute-start.34
  44.2 1.2 collective-permute-start.33
  45.4 10.9 %collective-permute-done.11.refs_10_ = bf16[2,64,1024]{2,1,0:T(8,128)(2,1)S(1)} collective-permute-done((bf16[2,64,1024]{2,1,0:T(8,128)(2,1)S(1)}, bf16[2,64,1024]{2,1,0:T(8,128)(2,1)S(1)}, u32[]{:S(2)}, u32[]{:S(2)}) %collective-permute-start.11) | collective-permute-done | bytes 262176 | tf_op jit(solution)/shard_map/ppermute | solution.py:105
  56.4 2.9 %shard_map.123.p0 = bf16[512,128]{1,0:T(8,128)(2,1)S(1)} custom-call(s32[32,128]{1,0:T(8,128)S(1)} %get-tuple-element.28.places, bf16[512,128]{1,0:T(8,128)(2,1)S(1)} %get-tuple-element.29.refs_0_, bf16[512,128]{1,0:T(8,128)(2,1)S(1)} %collective-permute-done.3.refs_1_, bf16[512,128]{1,0:T(8,128)(2,1)S(1)} %collective-permute-done.4.refs_2_, ...), custom_call_target="tpu_custom_call" | custom-call | tf_op jit(solution)/shard_map/pallas_call | solution.py:90
  59.8 1.5 %collective-permute-start.14 = (bf16[512,128]{1,0:T(8,128)(2,1)S(1)}, bf16[512,128]{1,0:T(8,128)(2,1)S(1)}, u32[]{:S(2)}, u32[]{:S(2)}) collective-permute-start(bf16[512,128]{1,0:T(8,128)(2,1)S(1)} %shard_map.123.p0), channel_id=1, source_target_pairs={{0,4},{1,5},{2,6},{3,7},{4,0},{5,1},{6,2},{7,3},{8,12},{9,13},{10,... | collective-permute-start | bytes 393224 | tf_op jit(solution)/shard_map/ppermute | solution.py:105
  61.3 1.5 %collective-permute-start.13 = (bf16[512,128]{1,0:T(8,128)(2,1)S(1)}, bf16[512,128]{1,0:T(8,128)(2,1)S(1)}, u32[]{:S(2)}, u32[]{:S(2)}) collective-permute-start(bf16[512,128]{1,0:T(8,128)(2,1)S(1)} %shard_map.123.p0), channel_id=1, source_target_pairs={{0,2},{1,3},{2,0},{3,1},{4,6},{5,7},{6,4},{7,5},{8,10},{9,11},{10,... | collective-permute-start | bytes 393224 | tf_op jit(solution)/shard_map/ppermute | solution.py:105
  62.8 2.8 %shard_map.127.p0 = bf16[512,128]{1,0:T(8,128)(2,1)S(1)} custom-call(s32[32,128]{1,0:T(8,128)S(1)} %get-tuple-element.28.places, bf16[512,128]{1,0:T(8,128)(2,1)S(1)} %get-tuple-element.39.refs_0_, bf16[512,128]{1,0:T(8,128)(2,1)S(1)} %collective-permute-done.26.refs_1_, bf16[512,128]{1,0:T(8,128)(2,1)S(1)} %collective-permute-done.27.refs_2_, ...), custom_call_target="tpu_custom_call" | custom-call | tf_op jit(solution)/shard_map/pallas_call | solution.py:90
  66.2 1.5 %collective-permute-start.37 = (bf16[512,128]{1,0:T(8,128)(2,1)S(1)}, bf16[512,128]{1,0:T(8,128)(2,1)S(1)}, u32[]{:S(2)}, u32[]{:S(2)}) collective-permute-start(bf16[512,128]{1,0:T(8,128)(2,1)S(1)} %shard_map.127.p0), channel_id=1, source_target_pairs={{0,4},{1,5},{2,6},{3,7},{4,0},{5,1},{6,2},{7,3},{8,12},{9,13},{10,... | collective-permute-start | bytes 393224 | tf_op jit(solution)/shard_map/ppermute | solution.py:105
  67.7 1.5 %collective-permute-start.36 = (bf16[512,128]{1,0:T(8,128)(2,1)S(1)}, bf16[512,128]{1,0:T(8,128)(2,1)S(1)}, u32[]{:S(2)}, u32[]{:S(2)}) collective-permute-start(bf16[512,128]{1,0:T(8,128)(2,1)S(1)} %shard_map.127.p0), channel_id=1, source_target_pairs={{0,2},{1,3},{2,0},{3,1},{4,6},{5,7},{6,4},{7,5},{8,10},{9,11},{10,... | collective-permute-start | bytes 393224 | tf_op jit(solution)/shard_map/ppermute | solution.py:105
  69.2 0.8 shard_map.124
  70.0 3.0 %collective-permute-done.38.p3 = bf16[512,128]{1,0:T(8,128)(2,1)S(1)} collective-permute-done((bf16[512,128]{1,0:T(8,128)(2,1)S(1)}, bf16[512,128]{1,0:T(8,128)(2,1)S(1)}, u32[]{:S(2)}, u32[]{:S(2)}) %collective-permute-start.38) | collective-permute-done | bytes 131104 | tf_op jit(solution)/shard_map/ppermute | solution.py:105
  73.0 0.8 collective-permute-done.37.p2
  74.7 1.4 %collective-permute-start.18 = (bf16[512,128]{1,0:T(8,128)(2,1)S(1)}, bf16[512,128]{1,0:T(8,128)(2,1)S(1)}, u32[]{:S(2)}, u32[]{:S(2)}) collective-permute-start(bf16[512,128]{1,0:T(8,128)(2,1)S(1)} %get-tuple-element.31.refs_0_), channel_id=1, source_target_pairs={{0,24},{1,25},{2,26},{3,27},{4,28},{5,29},{6,30},{7,31},{8,16},{9,... | collective-permute-start | bytes 393224 | tf_op jit(solution)/shard_map/ppermute | solution.py:105
  76.1 1.6 %collective-permute-start.17 = (bf16[512,128]{1,0:T(8,128)(2,1)S(1)}, bf16[512,128]{1,0:T(8,128)(2,1)S(1)}, u32[]{:S(2)}, u32[]{:S(2)}) collective-permute-start(bf16[512,128]{1,0:T(8,128)(2,1)S(1)} %get-tuple-element.31.refs_0_), channel_id=1, source_target_pairs={{0,16},{1,17},{2,18},{3,19},{4,20},{5,21},{6,22},{7,23},{8,24},{9,... | collective-permute-start | bytes 393224 | tf_op jit(solution)/shard_map/ppermute | solution.py:105
  77.7 2.9 %collective-permute-start.42 = (bf16[512,128]{1,0:T(8,128)(2,1)S(1)}, bf16[512,128]{1,0:T(8,128)(2,1)S(1)}, u32[]{:S(2)}, u32[]{:S(2)}) collective-permute-start(bf16[512,128]{1,0:T(8,128)(2,1)S(1)} %add_convert_fusion.1), channel_id=1, source_target_pairs={{0,24},{1,25},{2,26},{3,27},{4,28},{5,29},{6,30},{7,31},{8,16},{9,... | collective-permute-start | bytes 393224 | tf_op jit(solution)/shard_map/ppermute | solution.py:105
  80.7 1.4 %collective-permute-start.40 = (bf16[512,128]{1,0:T(8,128)(2,1)S(1)}, bf16[512,128]{1,0:T(8,128)(2,1)S(1)}, u32[]{:S(2)}, u32[]{:S(2)}) collective-permute-start(bf16[512,128]{1,0:T(8,128)(2,1)S(1)} %add_convert_fusion.1), channel_id=1, source_target_pairs={{0,8},{1,9},{2,10},{3,11},{4,12},{5,13},{6,14},{7,15},{8,0},{9,1},... | collective-permute-start | bytes 393224 | tf_op jit(solution)/shard_map/ppermute | solution.py:105
  82.1 0.8 collective-permute-done.18.refs_3_
  82.9 13.0 %collective-permute-done.17.refs_2_ = bf16[512,128]{1,0:T(8,128)(2,1)S(1)} collective-permute-done((bf16[512,128]{1,0:T(8,128)(2,1)S(1)}, bf16[512,128]{1,0:T(8,128)(2,1)S(1)}, u32[]{:S(2)}, u32[]{:S(2)}) %collective-permute-start.17) | collective-permute-done | bytes 131104 | tf_op jit(solution)/shard_map/ppermute | solution.py:105
  96.0 5.5 %collective-permute-done.41 = bf16[512,128]{1,0:T(8,128)(2,1)S(1)} collective-permute-done((bf16[512,128]{1,0:T(8,128)(2,1)S(1)}, bf16[512,128]{1,0:T(8,128)(2,1)S(1)}, u32[]{:S(2)}, u32[]{:S(2)}) %collective-permute-start.41) | collective-permute-done | bytes 131104 | tf_op jit(solution)/shard_map/ppermute | solution.py:105
  101.5 1.3 %collective-permute-start.45 = (bf16[512,128]{1,0:T(8,128)(2,1)S(1)}, bf16[512,128]{1,0:T(8,128)(2,1)S(1)}, u32[]{:S(2)}, u32[]{:S(2)}) collective-permute-start(bf16[512,128]{1,0:T(8,128)(2,1)S(1)} %add_convert_fusion.refs_0_), channel_id=1, source_target_pairs={{0,6},{1,7},{2,4},{3,5},{4,2},{5,3},{6,0},{7,1},{8,14},{9,15},{10,... | collective-permute-start | bytes 393224 | tf_op jit(solution)/shard_map/ppermute | solution.py:105
  102.8 1.5 %collective-permute-start.44 = (bf16[512,128]{1,0:T(8,128)(2,1)S(1)}, bf16[512,128]{1,0:T(8,128)(2,1)S(1)}, u32[]{:S(2)}, u32[]{:S(2)}) collective-permute-start(bf16[512,128]{1,0:T(8,128)(2,1)S(1)} %add_convert_fusion.refs_0_), channel_id=1, source_target_pairs={{0,4},{1,5},{2,6},{3,7},{4,0},{5,1},{6,2},{7,3},{8,12},{9,13},{10,... | collective-permute-start | bytes 393224 | tf_op jit(solution)/shard_map/ppermute | solution.py:105
  104.3 0.8 collective-permute-start.43
  105.6 3.2 %collective-permute-done.45.refs_3_ = bf16[512,128]{1,0:T(8,128)(2,1)S(1)} collective-permute-done((bf16[512,128]{1,0:T(8,128)(2,1)S(1)}, bf16[512,128]{1,0:T(8,128)(2,1)S(1)}, u32[]{:S(2)}, u32[]{:S(2)}) %collective-permute-start.45) | collective-permute-done | bytes 131104 | tf_op jit(solution)/shard_map/ppermute | solution.py:105
  108.8 2.4 %collective-permute-done.44.refs_2_ = bf16[512,128]{1,0:T(8,128)(2,1)S(1)} collective-permute-done((bf16[512,128]{1,0:T(8,128)(2,1)S(1)}, bf16[512,128]{1,0:T(8,128)(2,1)S(1)}, u32[]{:S(2)}, u32[]{:S(2)}) %collective-permute-start.44) | collective-permute-done | bytes 131104 | tf_op jit(solution)/shard_map/ppermute | solution.py:105
  111.7 2.9 %shard_map.125 = (bf16[128,128]{1,0:T(8,128)(2,1)S(1)}, bf16[128,128]{1,0:T(8,128)(2,1)S(1)}, bf16[128,128]{1,0:T(8,128)(2,1)S(1)}, bf16[128,128]{1,0:T(8,128)(2,1)S(1)}) custom-call(s32[32,128]{1,0:T(8,128)S(1)} %get-tuple-element.28.places, bf16[512,128]{1,0:T(8,128)(2,1)S(1)} %get-tuple-element.31.refs_0_, ...), custom_call_target="tpu_custom_call" | custom-call | tf_op jit(solution)/shard_map/pallas_call | solution.py:90
  114.6 1.3 %collective-permute-start.23 = (bf16[128,128]{1,0:T(8,128)(2,1)S(1)}, bf16[128,128]{1,0:T(8,128)(2,1)S(1)}, u32[]{:S(2)}, u32[]{:S(2)}) collective-permute-start(bf16[128,128]{1,0:T(8,128)(2,1)S(1)} %get-tuple-element.33), channel_id=1, source_target_pairs={{0,2},{1,3},{2,0},{3,1},{4,6},{5,7},{6,4},{7,5},{8,10},{9,11},{10,... | collective-permute-start | bytes 98312 | tf_op jit(solution)/shard_map/ppermute | solution.py:105
  115.9 2.7 %collective-permute-done.23.p1 = bf16[128,128]{1,0:T(8,128)(2,1)S(1)} collective-permute-done((bf16[128,128]{1,0:T(8,128)(2,1)S(1)}, bf16[128,128]{1,0:T(8,128)(2,1)S(1)}, u32[]{:S(2)}, u32[]{:S(2)}) %collective-permute-start.23) | collective-permute-done | bytes 32800 | tf_op jit(solution)/shard_map/ppermute | solution.py:105
  118.6 1.4 %collective-permute-start.24 = (bf16[128,128]{1,0:T(8,128)(2,1)S(1)}, bf16[128,128]{1,0:T(8,128)(2,1)S(1)}, u32[]{:S(2)}, u32[]{:S(2)}) collective-permute-start(bf16[128,128]{1,0:T(8,128)(2,1)S(1)} %get-tuple-element.34), channel_id=1, source_target_pairs={{0,4},{1,5},{2,6},{3,7},{4,0},{5,1},{6,2},{7,3},{8,12},{9,13},{10,... | collective-permute-start | bytes 98312 | tf_op jit(solution)/shard_map/ppermute | solution.py:105
  119.9 2.5 %collective-permute-done.24.p2 = bf16[128,128]{1,0:T(8,128)(2,1)S(1)} collective-permute-done((bf16[128,128]{1,0:T(8,128)(2,1)S(1)}, bf16[128,128]{1,0:T(8,128)(2,1)S(1)}, u32[]{:S(2)}, u32[]{:S(2)}) %collective-permute-start.24) | collective-permute-done | bytes 32800 | tf_op jit(solution)/shard_map/ppermute | solution.py:105
  122.5 1.2 collective-permute-start.25
  123.7 3.6 %collective-permute-done.25.p3 = bf16[128,128]{1,0:T(8,128)(2,1)S(1)} collective-permute-done((bf16[128,128]{1,0:T(8,128)(2,1)S(1)}, bf16[128,128]{1,0:T(8,128)(2,1)S(1)}, u32[]{:S(2)}, u32[]{:S(2)}) %collective-permute-start.25) | collective-permute-done | bytes 32800 | tf_op jit(solution)/shard_map/ppermute | solution.py:105
  127.3 0.9 shard_map.126
  128.3 1.6 %shard_map.129 = (f32[512,512]{1,0:T(8,128)}, f32[512,512]{1,0:T(8,128)}) custom-call(s32[1]{0:T(128)} %bitcast.pos, bf16[512,128]{1,0:T(8,128)(2,1)S(1)} %add_convert_fusion.refs_0_, bf16[512,128]{1,0:T(8,128)(2,1)S(1)} %collective-permute-done.43.refs_1_, bf16[512,128]{1,0:T(8,128)(2,1)S(1)} %collective-permute-done.44.refs_2_, ...), custom_call_target="tpu_custom_call" | custom-call | tf_op jit(solution)/shard_map/pallas_call | solution.py:90
  (83 shorter events, 7.3 us)
Async XLA Ops:
  3.9 5.5 %collective-permute-start = (bf16[144,256]{1,0:T(8,128)(2,1)S(1)}, bf16[144,256]{1,0:T(8,128)(2,1)S(1)}, u32[]{:S(2)}, u32[]{:S(2)}) collective-permute-start(bf16[144,256]{1,0:T(8,128)(2,1)S(1)} %get-tuple-element.25), channel_id=1, source_target_pairs={{0,2},{1,3},{2,0},{3,1},{4,6},{5,7},{6,4},{7,5},{8,10},{9,11},{10,... | collective-permute-start | bytes 221192 | tf_op jit(solution)/shard_map/ppermute | solution.py:105
  6.9 4.4 %collective-permute-start.1 = (bf16[144,256]{1,0:T(8,128)(2,1)S(1)}, bf16[144,256]{1,0:T(8,128)(2,1)S(1)}, u32[]{:S(2)}, u32[]{:S(2)}) collective-permute-start(bf16[144,256]{1,0:T(8,128)(2,1)S(1)} %get-tuple-element.26), channel_id=1, source_target_pairs={{0,4},{1,5},{2,6},{3,7},{4,0},{5,1},{6,2},{7,3},{8,12},{9,13},{10,... | collective-permute-start | bytes 221192 | tf_op jit(solution)/shard_map/ppermute | solution.py:105
  8.4 5.3 %collective-permute-start.2 = (bf16[144,256]{1,0:T(8,128)(2,1)S(1)}, bf16[144,256]{1,0:T(8,128)(2,1)S(1)}, u32[]{:S(2)}, u32[]{:S(2)}) collective-permute-start(bf16[144,256]{1,0:T(8,128)(2,1)S(1)} %get-tuple-element.27), channel_id=1, source_target_pairs={{0,6},{1,7},{2,4},{3,5},{4,2},{5,3},{6,0},{7,1},{8,14},{9,15},{10,... | collective-permute-start | bytes 221192 | tf_op jit(solution)/shard_map/ppermute | solution.py:105
  13.7 4.5 %collective-permute-start.6 = (bf16[512,128]{1,0:T(8,128)(2,1)S(1)}, bf16[512,128]{1,0:T(8,128)(2,1)S(1)}, u32[]{:S(2)}, u32[]{:S(2)}) collective-permute-start(bf16[512,128]{1,0:T(8,128)(2,1)S(1)} %get-tuple-element.29.refs_0_), channel_id=1, source_target_pairs={{0,1},{1,0},{2,3},{3,2},{4,5},{5,4},{6,7},{7,6},{8,9},{9,8},{10,11... | collective-permute-start | bytes 393224 | tf_op jit(solution)/shard_map/ppermute | solution.py:105
  13.8 8.3 %collective-permute-start.5 = (bf16[512,128]{1,0:T(8,128)(2,1)S(1)}, bf16[512,128]{1,0:T(8,128)(2,1)S(1)}, u32[]{:S(2)}, u32[]{:S(2)}) collective-permute-start(bf16[512,128]{1,0:T(8,128)(2,1)S(1)} %get-tuple-element.29.refs_0_), channel_id=1, source_target_pairs={{0,24},{1,25},{2,26},{3,27},{4,28},{5,29},{6,30},{7,31},{8,16},{9,... | collective-permute-start | bytes 393224 | tf_op jit(solution)/shard_map/ppermute | solution.py:105
  17.4 14.9 %collective-permute-start.4 = (bf16[512,128]{1,0:T(8,128)(2,1)S(1)}, bf16[512,128]{1,0:T(8,128)(2,1)S(1)}, u32[]{:S(2)}, u32[]{:S(2)}) collective-permute-start(bf16[512,128]{1,0:T(8,128)(2,1)S(1)} %get-tuple-element.29.refs_0_), channel_id=1, source_target_pairs={{0,16},{1,17},{2,18},{3,19},{4,20},{5,21},{6,22},{7,23},{8,24},{9,... | collective-permute-start | bytes 393224 | tf_op jit(solution)/shard_map/ppermute | solution.py:105
  17.4 14.9 %collective-permute-start.3 = (bf16[512,128]{1,0:T(8,128)(2,1)S(1)}, bf16[512,128]{1,0:T(8,128)(2,1)S(1)}, u32[]{:S(2)}, u32[]{:S(2)}) collective-permute-start(bf16[512,128]{1,0:T(8,128)(2,1)S(1)} %get-tuple-element.29.refs_0_), channel_id=1, source_target_pairs={{0,8},{1,9},{2,10},{3,11},{4,12},{5,13},{6,14},{7,15},{8,0},{9,1},... | collective-permute-start | bytes 393224 | tf_op jit(solution)/shard_map/ppermute | solution.py:105
  18.2 17.2 %collective-permute-start.29 = (bf16[512,128]{1,0:T(8,128)(2,1)S(1)}, bf16[512,128]{1,0:T(8,128)(2,1)S(1)}, u32[]{:S(2)}, u32[]{:S(2)}) collective-permute-start(bf16[512,128]{1,0:T(8,128)(2,1)S(1)} %get-tuple-element.39.refs_0_), channel_id=1, source_target_pairs={{0,1},{1,0},{2,3},{3,2},{4,5},{5,4},{6,7},{7,6},{8,9},{9,8},{10,11... | collective-permute-start | bytes 393224 | tf_op jit(solution)/shard_map/ppermute | solution.py:105
  18.2 23.1 %collective-permute-start.10 = (bf16[2,64,1024]{2,1,0:T(8,128)(2,1)S(1)}, bf16[2,64,1024]{2,1,0:T(8,128)(2,1)S(1)}, u32[]{:S(2)}, u32[]{:S(2)}) collective-permute-start(bf16[2,64,1024]{2,1,0:T(8,128)(2,1)S(1)} %copy-done.1), channel_id=1, source_target_pairs={{0,2},{1,3},{2,0},{3,1},{4,6},{5,7},{6,4},{7,5},{8,10},{9,11},{10,... | collective-permute-start | bytes 786440 | tf_op jit(solution)/shard_map/ppermute | solution.py:105
  22.0 13.4 %collective-permute-start.28 = (bf16[512,128]{1,0:T(8,128)(2,1)S(1)}, bf16[512,128]{1,0:T(8,128)(2,1)S(1)}, u32[]{:S(2)}, u32[]{:S(2)}) collective-permute-start(bf16[512,128]{1,0:T(8,128)(2,1)S(1)} %get-tuple-element.39.refs_0_), channel_id=1, source_target_pairs={{0,24},{1,25},{2,26},{3,27},{4,28},{5,29},{6,30},{7,31},{8,16},{9,... | collective-permute-start | bytes 393224 | tf_op jit(solution)/shard_map/ppermute | solution.py:105
  32.4 8.2 %collective-permute-start.27 = (bf16[512,128]{1,0:T(8,128)(2,1)S(1)}, bf16[512,128]{1,0:T(8,128)(2,1)S(1)}, u32[]{:S(2)}, u32[]{:S(2)}) collective-permute-start(bf16[512,128]{1,0:T(8,128)(2,1)S(1)} %get-tuple-element.39.refs_0_), channel_id=1, source_target_pairs={{0,16},{1,17},{2,18},{3,19},{4,20},{5,21},{6,22},{7,23},{8,24},{9,... | collective-permute-start | bytes 393224 | tf_op jit(solution)/shard_map/ppermute | solution.py:105
  32.4 8.4 %collective-permute-start.26 = (bf16[512,128]{1,0:T(8,128)(2,1)S(1)}, bf16[512,128]{1,0:T(8,128)(2,1)S(1)}, u32[]{:S(2)}, u32[]{:S(2)}) collective-permute-start(bf16[512,128]{1,0:T(8,128)(2,1)S(1)} %get-tuple-element.39.refs_0_), channel_id=1, source_target_pairs={{0,8},{1,9},{2,10},{3,11},{4,12},{5,13},{6,14},{7,15},{8,0},{9,1},... | collective-permute-start | bytes 393224 | tf_op jit(solution)/shard_map/ppermute | solution.py:105
  35.4 5.9 %collective-permute-start.9 = (bf16[512,128]{1,0:T(8,128)(2,1)S(1)}, bf16[512,128]{1,0:T(8,128)(2,1)S(1)}, u32[]{:S(2)}, u32[]{:S(2)}) collective-permute-start(bf16[512,128]{1,0:T(8,128)(2,1)S(1)} %collective-permute-done.5.refs_3_), channel_id=1, source_target_pairs={{0,1},{1,0},{2,3},{3,2},{4,5},{5,4},{6,7},{7,6},{8,9},{9,8},{10,11... | collective-permute-start | bytes 393224 | tf_op jit(solution)/shard_map/ppermute | solution.py:105
  35.4 10.0 %collective-permute-start.12 = (bf16[2,64,1024]{2,1,0:T(8,128)(2,1)S(1)}, bf16[2,64,1024]{2,1,0:T(8,128)(2,1)S(1)}, u32[]{:S(2)}, u32[]{:S(2)}) collective-permute-start(bf16[2,64,1024]{2,1,0:T(8,128)(2,1)S(1)} %copy-done.1), channel_id=1, source_target_pairs={{0,6},{1,7},{2,4},{3,5},{4,2},{5,3},{6,0},{7,1},{8,14},{9,15},{10,... | collective-permute-start | bytes 786440 | tf_op jit(solution)/shard_map/ppermute | solution.py:105
  40.8 15.5 %collective-permute-start.11 = (bf16[2,64,1024]{2,1,0:T(8,128)(2,1)S(1)}, bf16[2,64,1024]{2,1,0:T(8,128)(2,1)S(1)}, u32[]{:S(2)}, u32[]{:S(2)}) collective-permute-start(bf16[2,64,1024]{2,1,0:T(8,128)(2,1)S(1)} %copy-done.1), channel_id=1, source_target_pairs={{0,4},{1,5},{2,6},{3,7},{4,0},{5,1},{6,2},{7,3},{8,12},{9,13},{10,... | collective-permute-start | bytes 786440 | tf_op jit(solution)/shard_map/ppermute | solution.py:105
  41.3 2.9 %collective-permute-start.32 = (bf16[512,128]{1,0:T(8,128)(2,1)S(1)}, bf16[512,128]{1,0:T(8,128)(2,1)S(1)}, u32[]{:S(2)}, u32[]{:S(2)}) collective-permute-start(bf16[512,128]{1,0:T(8,128)(2,1)S(1)} %collective-permute-done.28.refs_3_), channel_id=1, source_target_pairs={{0,1},{1,0},{2,3},{3,2},{4,5},{5,4},{6,7},{7,6},{8,9},{9,8},{10,11... | collective-permute-start | bytes 393224 | tf_op jit(solution)/shard_map/ppermute | solution.py:105
  41.9 19.4 %collective-permute-start.35 = (bf16[2,64,1024]{2,1,0:T(8,128)(2,1)S(1)}, bf16[2,64,1024]{2,1,0:T(8,128)(2,1)S(1)}, u32[]{:S(2)}, u32[]{:S(2)}) collective-permute-start(bf16[2,64,1024]{2,1,0:T(8,128)(2,1)S(1)} %copy-done.3), channel_id=1, source_target_pairs={{0,6},{1,7},{2,4},{3,5},{4,2},{5,3},{6,0},{7,1},{8,14},{9,15},{10,... | collective-permute-start | bytes 786440 | tf_op jit(solution)/shard_map/ppermute | solution.py:105
  43.3 19.5 %collective-permute-start.34 = (bf16[2,64,1024]{2,1,0:T(8,128)(2,1)S(1)}, bf16[2,64,1024]{2,1,0:T(8,128)(2,1)S(1)}, u32[]{:S(2)}, u32[]{:S(2)}) collective-permute-start(bf16[2,64,1024]{2,1,0:T(8,128)(2,1)S(1)} %copy-done.3), channel_id=1, source_target_pairs={{0,4},{1,5},{2,6},{3,7},{4,0},{5,1},{6,2},{7,3},{8,12},{9,13},{10,... | collective-permute-start | bytes 786440 | tf_op jit(solution)/shard_map/ppermute | solution.py:105
  44.2 18.6 %collective-permute-start.33 = (bf16[2,64,1024]{2,1,0:T(8,128)(2,1)S(1)}, bf16[2,64,1024]{2,1,0:T(8,128)(2,1)S(1)}, u32[]{:S(2)}, u32[]{:S(2)}) collective-permute-start(bf16[2,64,1024]{2,1,0:T(8,128)(2,1)S(1)} %copy-done.3), channel_id=1, source_target_pairs={{0,2},{1,3},{2,0},{3,1},{4,6},{5,7},{6,4},{7,5},{8,10},{9,11},{10,... | collective-permute-start | bytes 786440 | tf_op jit(solution)/shard_map/ppermute | solution.py:105
  45.4 13.8 %collective-permute-start.31 = (bf16[512,128]{1,0:T(8,128)(2,1)S(1)}, bf16[512,128]{1,0:T(8,128)(2,1)S(1)}, u32[]{:S(2)}, u32[]{:S(2)}) collective-permute-start(bf16[512,128]{1,0:T(8,128)(2,1)S(1)} %collective-permute-done.27.refs_2_), channel_id=1, source_target_pairs={{0,1},{1,0},{2,3},{3,2},{4,5},{5,4},{6,7},{7,6},{8,9},{9,8},{10,11... | collective-permute-start | bytes 393224 | tf_op jit(solution)/shard_map/ppermute | solution.py:105
  56.3 3.5 %collective-permute-start.30 = (bf16[512,128]{1,0:T(8,128)(2,1)S(1)}, bf16[512,128]{1,0:T(8,128)(2,1)S(1)}, u32[]{:S(2)}, u32[]{:S(2)}) collective-permute-start(bf16[512,128]{1,0:T(8,128)(2,1)S(1)} %collective-permute-done.26.refs_1_), channel_id=1, source_target_pairs={{0,1},{1,0},{2,3},{3,2},{4,5},{5,4},{6,7},{7,6},{8,9},{9,8},{10,11... | collective-permute-start | bytes 393224 | tf_op jit(solution)/shard_map/ppermute | solution.py:105
  59.2 8.5 %collective-permute-start.15 = (bf16[512,128]{1,0:T(8,128)(2,1)S(1)}, bf16[512,128]{1,0:T(8,128)(2,1)S(1)}, u32[]{:S(2)}, u32[]{:S(2)}) collective-permute-start(bf16[512,128]{1,0:T(8,128)(2,1)S(1)} %shard_map.123.p0), channel_id=1, source_target_pairs={{0,6},{1,7},{2,4},{3,5},{4,2},{5,3},{6,0},{7,1},{8,14},{9,15},{10,... | collective-permute-start | bytes 393224 | tf_op jit(solution)/shard_map/ppermute | solution.py:105
  59.8 9.4 %collective-permute-start.14 = (bf16[512,128]{1,0:T(8,128)(2,1)S(1)}, bf16[512,128]{1,0:T(8,128)(2,1)S(1)}, u32[]{:S(2)}, u32[]{:S(2)}) collective-permute-start(bf16[512,128]{1,0:T(8,128)(2,1)S(1)} %shard_map.123.p0), channel_id=1, source_target_pairs={{0,4},{1,5},{2,6},{3,7},{4,0},{5,1},{6,2},{7,3},{8,12},{9,13},{10,... | collective-permute-start | bytes 393224 | tf_op jit(solution)/shard_map/ppermute | solution.py:105
  61.3 7.9 %collective-permute-start.13 = (bf16[512,128]{1,0:T(8,128)(2,1)S(1)}, bf16[512,128]{1,0:T(8,128)(2,1)S(1)}, u32[]{:S(2)}, u32[]{:S(2)}) collective-permute-start(bf16[512,128]{1,0:T(8,128)(2,1)S(1)} %shard_map.123.p0), channel_id=1, source_target_pairs={{0,2},{1,3},{2,0},{3,1},{4,6},{5,7},{6,4},{7,5},{8,10},{9,11},{10,... | collective-permute-start | bytes 393224 | tf_op jit(solution)/shard_map/ppermute | solution.py:105
  65.7 7.4 %collective-permute-start.38 = (bf16[512,128]{1,0:T(8,128)(2,1)S(1)}, bf16[512,128]{1,0:T(8,128)(2,1)S(1)}, u32[]{:S(2)}, u32[]{:S(2)}) collective-permute-start(bf16[512,128]{1,0:T(8,128)(2,1)S(1)} %shard_map.127.p0), channel_id=1, source_target_pairs={{0,6},{1,7},{2,4},{3,5},{4,2},{5,3},{6,0},{7,1},{8,14},{9,15},{10,... | collective-permute-start | bytes 393224 | tf_op jit(solution)/shard_map/ppermute | solution.py:105
  66.2 7.6 %collective-permute-start.37 = (bf16[512,128]{1,0:T(8,128)(2,1)S(1)}, bf16[512,128]{1,0:T(8,128)(2,1)S(1)}, u32[]{:S(2)}, u32[]{:S(2)}) collective-permute-start(bf16[512,128]{1,0:T(8,128)(2,1)S(1)} %shard_map.127.p0), channel_id=1, source_target_pairs={{0,4},{1,5},{2,6},{3,7},{4,0},{5,1},{6,2},{7,3},{8,12},{9,13},{10,... | collective-permute-start | bytes 393224 | tf_op jit(solution)/shard_map/ppermute | solution.py:105
  67.7 6.1 %collective-permute-start.36 = (bf16[512,128]{1,0:T(8,128)(2,1)S(1)}, bf16[512,128]{1,0:T(8,128)(2,1)S(1)}, u32[]{:S(2)}, u32[]{:S(2)}) collective-permute-start(bf16[512,128]{1,0:T(8,128)(2,1)S(1)} %shard_map.127.p0), channel_id=1, source_target_pairs={{0,2},{1,3},{2,0},{3,1},{4,6},{5,7},{6,4},{7,5},{8,10},{9,11},{10,... | collective-permute-start | bytes 393224 | tf_op jit(solution)/shard_map/ppermute | solution.py:105
  74.6 3.0 %collective-permute-start.39 = (f32[512,128]{1,0:T(8,128)S(1)}, f32[512,128]{1,0:T(8,128)S(1)}, u32[]{:S(2)}, u32[]{:S(2)}) collective-permute-start(f32[512,128]{1,0:T(8,128)S(1)} %get-tuple-element.42), channel_id=1, source_target_pairs={{0,1},{1,0},{2,3},{3,2},{4,5},{5,4},{6,7},{7,6},{8,9},{9,8},{10,11... | collective-permute-start | bytes 786440 | tf_op jit(solution)/shard_map/ppermute | solution.py:105
  74.7 8.3 %collective-permute-start.18 = (bf16[512,128]{1,0:T(8,128)(2,1)S(1)}, bf16[512,128]{1,0:T(8,128)(2,1)S(1)}, u32[]{:S(2)}, u32[]{:S(2)}) collective-permute-start(bf16[512,128]{1,0:T(8,128)(2,1)S(1)} %get-tuple-element.31.refs_0_), channel_id=1, source_target_pairs={{0,24},{1,25},{2,26},{3,27},{4,28},{5,29},{6,30},{7,31},{8,16},{9,... | collective-permute-start | bytes 393224 | tf_op jit(solution)/shard_map/ppermute | solution.py:105
  76.1 19.9 %collective-permute-start.17 = (bf16[512,128]{1,0:T(8,128)(2,1)S(1)}, bf16[512,128]{1,0:T(8,128)(2,1)S(1)}, u32[]{:S(2)}, u32[]{:S(2)}) collective-permute-start(bf16[512,128]{1,0:T(8,128)(2,1)S(1)} %get-tuple-element.31.refs_0_), channel_id=1, source_target_pairs={{0,16},{1,17},{2,18},{3,19},{4,20},{5,21},{6,22},{7,23},{8,24},{9,... | collective-permute-start | bytes 393224 | tf_op jit(solution)/shard_map/ppermute | solution.py:105
  77.7 18.3 %collective-permute-start.42 = (bf16[512,128]{1,0:T(8,128)(2,1)S(1)}, bf16[512,128]{1,0:T(8,128)(2,1)S(1)}, u32[]{:S(2)}, u32[]{:S(2)}) collective-permute-start(bf16[512,128]{1,0:T(8,128)(2,1)S(1)} %add_convert_fusion.1), channel_id=1, source_target_pairs={{0,24},{1,25},{2,26},{3,27},{4,28},{5,29},{6,30},{7,31},{8,16},{9,... | collective-permute-start | bytes 393224 | tf_op jit(solution)/shard_map/ppermute | solution.py:105
  80.6 20.8 %collective-permute-start.41 = (bf16[512,128]{1,0:T(8,128)(2,1)S(1)}, bf16[512,128]{1,0:T(8,128)(2,1)S(1)}, u32[]{:S(2)}, u32[]{:S(2)}) collective-permute-start(bf16[512,128]{1,0:T(8,128)(2,1)S(1)} %add_convert_fusion.1), channel_id=1, source_target_pairs={{0,16},{1,17},{2,18},{3,19},{4,20},{5,21},{6,22},{7,23},{8,24},{9,... | collective-permute-start | bytes 393224 | tf_op jit(solution)/shard_map/ppermute | solution.py:105
  80.7 20.7 %collective-permute-start.40 = (bf16[512,128]{1,0:T(8,128)(2,1)S(1)}, bf16[512,128]{1,0:T(8,128)(2,1)S(1)}, u32[]{:S(2)}, u32[]{:S(2)}) collective-permute-start(bf16[512,128]{1,0:T(8,128)(2,1)S(1)} %add_convert_fusion.1), channel_id=1, source_target_pairs={{0,8},{1,9},{2,10},{3,11},{4,12},{5,13},{6,14},{7,15},{8,0},{9,1},... | collective-permute-start | bytes 393224 | tf_op jit(solution)/shard_map/ppermute | solution.py:105
  82.9 19.9 %collective-permute-start.19 = (bf16[512,128]{1,0:T(8,128)(2,1)S(1)}, bf16[512,128]{1,0:T(8,128)(2,1)S(1)}, u32[]{:S(2)}, u32[]{:S(2)}) collective-permute-start(bf16[512,128]{1,0:T(8,128)(2,1)S(1)} %get-tuple-element.31.refs_0_), channel_id=1, source_target_pairs={{0,1},{1,0},{2,3},{3,2},{4,5},{5,4},{6,7},{7,6},{8,9},{9,8},{10,11... | collective-permute-start | bytes 393224 | tf_op jit(solution)/shard_map/ppermute | solution.py:105
  96.0 8.3 %collective-permute-start.16 = (bf16[512,128]{1,0:T(8,128)(2,1)S(1)}, bf16[512,128]{1,0:T(8,128)(2,1)S(1)}, u32[]{:S(2)}, u32[]{:S(2)}) collective-permute-start(bf16[512,128]{1,0:T(8,128)(2,1)S(1)} %get-tuple-element.31.refs_0_), channel_id=1, source_target_pairs={{0,8},{1,9},{2,10},{3,11},{4,12},{5,13},{6,14},{7,15},{8,0},{9,1},... | collective-permute-start | bytes 393224 | tf_op jit(solution)/shard_map/ppermute | solution.py:105
  96.0 9.1 %collective-permute-start.22 = (bf16[512,128]{1,0:T(8,128)(2,1)S(1)}, bf16[512,128]{1,0:T(8,128)(2,1)S(1)}, u32[]{:S(2)}, u32[]{:S(2)}) collective-permute-start(bf16[512,128]{1,0:T(8,128)(2,1)S(1)} %collective-permute-done.18.refs_3_), channel_id=1, source_target_pairs={{0,1},{1,0},{2,3},{3,2},{4,5},{5,4},{6,7},{7,6},{8,9},{9,8},{10,11... | collective-permute-start | bytes 393224 | tf_op jit(solution)/shard_map/ppermute | solution.py:105
  101.4 3.7 %collective-permute-start.21 = (bf16[512,128]{1,0:T(8,128)(2,1)S(1)}, bf16[512,128]{1,0:T(8,128)(2,1)S(1)}, u32[]{:S(2)}, u32[]{:S(2)}) collective-permute-start(bf16[512,128]{1,0:T(8,128)(2,1)S(1)} %collective-permute-done.17.refs_2_), channel_id=1, source_target_pairs={{0,1},{1,0},{2,3},{3,2},{4,5},{5,4},{6,7},{7,6},{8,9},{9,8},{10,11... | collective-permute-start | bytes 393224 | tf_op jit(solution)/shard_map/ppermute | solution.py:105
  101.5 7.3 %collective-permute-start.45 = (bf16[512,128]{1,0:T(8,128)(2,1)S(1)}, bf16[512,128]{1,0:T(8,128)(2,1)S(1)}, u32[]{:S(2)}, u32[]{:S(2)}) collective-permute-start(bf16[512,128]{1,0:T(8,128)(2,1)S(1)} %add_convert_fusion.refs_0_), channel_id=1, source_target_pairs={{0,6},{1,7},{2,4},{3,5},{4,2},{5,3},{6,0},{7,1},{8,14},{9,15},{10,... | collective-permute-start | bytes 393224 | tf_op jit(solution)/shard_map/ppermute | solution.py:105
  102.8 8.4 %collective-permute-start.44 = (bf16[512,128]{1,0:T(8,128)(2,1)S(1)}, bf16[512,128]{1,0:T(8,128)(2,1)S(1)}, u32[]{:S(2)}, u32[]{:S(2)}) collective-permute-start(bf16[512,128]{1,0:T(8,128)(2,1)S(1)} %add_convert_fusion.refs_0_), channel_id=1, source_target_pairs={{0,4},{1,5},{2,6},{3,7},{4,0},{5,1},{6,2},{7,3},{8,12},{9,13},{10,... | collective-permute-start | bytes 393224 | tf_op jit(solution)/shard_map/ppermute | solution.py:105
  104.3 6.9 %collective-permute-start.43 = (bf16[512,128]{1,0:T(8,128)(2,1)S(1)}, bf16[512,128]{1,0:T(8,128)(2,1)S(1)}, u32[]{:S(2)}, u32[]{:S(2)}) collective-permute-start(bf16[512,128]{1,0:T(8,128)(2,1)S(1)} %add_convert_fusion.refs_0_), channel_id=1, source_target_pairs={{0,2},{1,3},{2,0},{3,1},{4,6},{5,7},{6,4},{7,5},{8,10},{9,11},{10,... | collective-permute-start | bytes 393224 | tf_op jit(solution)/shard_map/ppermute | solution.py:105
  105.1 6.6 %collective-permute-start.20 = (bf16[512,128]{1,0:T(8,128)(2,1)S(1)}, bf16[512,128]{1,0:T(8,128)(2,1)S(1)}, u32[]{:S(2)}, u32[]{:S(2)}) collective-permute-start(bf16[512,128]{1,0:T(8,128)(2,1)S(1)} %collective-permute-done.16.refs_1_), channel_id=1, source_target_pairs={{0,1},{1,0},{2,3},{3,2},{4,5},{5,4},{6,7},{7,6},{8,9},{9,8},{10,11... | collective-permute-start | bytes 393224 | tf_op jit(solution)/shard_map/ppermute | solution.py:105
  105.1 23.1 %collective-permute-start.46 = (bf16[512,128]{1,0:T(8,128)(2,1)S(1)}, bf16[512,128]{1,0:T(8,128)(2,1)S(1)}, u32[]{:S(2)}, u32[]{:S(2)}) collective-permute-start(bf16[512,128]{1,0:T(8,128)(2,1)S(1)} %add_convert_fusion.refs_0_), channel_id=1, source_target_pairs={{0,1},{1,0},{2,3},{3,2},{4,5},{5,4},{6,7},{7,6},{8,9},{9,8},{10,11... | collective-permute-start | bytes 393224 | tf_op jit(solution)/shard_map/ppermute | solution.py:105
  108.8 19.4 %collective-permute-start.49 = (bf16[512,128]{1,0:T(8,128)(2,1)S(1)}, bf16[512,128]{1,0:T(8,128)(2,1)S(1)}, u32[]{:S(2)}, u32[]{:S(2)}) collective-permute-start(bf16[512,128]{1,0:T(8,128)(2,1)S(1)} %collective-permute-done.45.refs_3_), channel_id=1, source_target_pairs={{0,1},{1,0},{2,3},{3,2},{4,5},{5,4},{6,7},{7,6},{8,9},{9,8},{10,11... | collective-permute-start | bytes 393224 | tf_op jit(solution)/shard_map/ppermute | solution.py:105
  111.2 17.0 %collective-permute-start.48 = (bf16[512,128]{1,0:T(8,128)(2,1)S(1)}, bf16[512,128]{1,0:T(8,128)(2,1)S(1)}, u32[]{:S(2)}, u32[]{:S(2)}) collective-permute-start(bf16[512,128]{1,0:T(8,128)(2,1)S(1)} %collective-permute-done.44.refs_2_), channel_id=1, source_target_pairs={{0,1},{1,0},{2,3},{3,2},{4,5},{5,4},{6,7},{7,6},{8,9},{9,8},{10,11... | collective-permute-start | bytes 393224 | tf_op jit(solution)/shard_map/ppermute | solution.py:105
  111.2 17.0 %collective-permute-start.47 = (bf16[512,128]{1,0:T(8,128)(2,1)S(1)}, bf16[512,128]{1,0:T(8,128)(2,1)S(1)}, u32[]{:S(2)}, u32[]{:S(2)}) collective-permute-start(bf16[512,128]{1,0:T(8,128)(2,1)S(1)} %collective-permute-done.43.refs_1_), channel_id=1, source_target_pairs={{0,1},{1,0},{2,3},{3,2},{4,5},{5,4},{6,7},{7,6},{8,9},{9,8},{10,11... | collective-permute-start | bytes 393224 | tf_op jit(solution)/shard_map/ppermute | solution.py:105
  114.6 4.0 %collective-permute-start.23 = (bf16[128,128]{1,0:T(8,128)(2,1)S(1)}, bf16[128,128]{1,0:T(8,128)(2,1)S(1)}, u32[]{:S(2)}, u32[]{:S(2)}) collective-permute-start(bf16[128,128]{1,0:T(8,128)(2,1)S(1)} %get-tuple-element.33), channel_id=1, source_target_pairs={{0,2},{1,3},{2,0},{3,1},{4,6},{5,7},{6,4},{7,5},{8,10},{9,11},{10,... | collective-permute-start | bytes 98312 | tf_op jit(solution)/shard_map/ppermute | solution.py:105
  118.6 3.9 %collective-permute-start.24 = (bf16[128,128]{1,0:T(8,128)(2,1)S(1)}, bf16[128,128]{1,0:T(8,128)(2,1)S(1)}, u32[]{:S(2)}, u32[]{:S(2)}) collective-permute-start(bf16[128,128]{1,0:T(8,128)(2,1)S(1)} %get-tuple-element.34), channel_id=1, source_target_pairs={{0,4},{1,5},{2,6},{3,7},{4,0},{5,1},{6,2},{7,3},{8,12},{9,13},{10,... | collective-permute-start | bytes 98312 | tf_op jit(solution)/shard_map/ppermute | solution.py:105
  122.5 4.8 %collective-permute-start.25 = (bf16[128,128]{1,0:T(8,128)(2,1)S(1)}, bf16[128,128]{1,0:T(8,128)(2,1)S(1)}, u32[]{:S(2)}, u32[]{:S(2)}) collective-permute-start(bf16[128,128]{1,0:T(8,128)(2,1)S(1)} %get-tuple-element.35), channel_id=1, source_target_pairs={{0,6},{1,7},{2,4},{3,5},{4,2},{5,3},{6,0},{7,1},{8,14},{9,15},{10,... | collective-permute-start | bytes 98312 | tf_op jit(solution)/shard_map/ppermute | solution.py:105
  (12 other events, 80.0 us)

commit v4 on v3

--- a/solution.py
+++ b/solution.py
@@ -110,7 +110,8 @@
 
 
 def over_planes(value):
-    return [value] + [swap(value, 8 * j) for j in range(1, PLANES)]
+    second = swap(value, 16)
+    return [value, swap(value, 8), second, swap(second, 8)]
 
 
 def chip(pos):
@@ -121,39 +122,54 @@
     return pl.ds(pl.multiple_of(column * LANES, LANES), LANES)
 
 
-def pack_body(pos, columns, counts, back_columns, back_counts, features, cotangent, *outs):
+def pack_body(pos, *refs):
+    tables, (features, cotangent, tiles, back_tiles) = refs[:4], refs[4:8]
+    outs, both_tiles, scalars, sems = refs[8:12], refs[12], refs[13:17], refs[17]
+    copies = [(table, scalar) for table, scalar in zip(tables, scalars)]
+    for q, out in enumerate(outs):
+        share = lanes_of(chip(pos) ^ q)
+        copies.append((features.at[:, share], out.at[pl.ds(0, ROWS), pl.ds(0, LANES)]))
+        copies.append((cotangent.at[:, share], out.at[pl.ds(0, ROWS), pl.ds(LANES, LANES)]))
+    copies.append((tiles, both_tiles.at[pl.ds(0, 2)]))
+    copies.append((back_tiles, both_tiles.at[pl.ds(2, 2)]))
+    copies = [pltpu.make_async_copy(a, b, sems.at[i]) for i, (a, b) in enumerate(copies)]
+    for copy in copies:
+        copy.start()
+    for copy in copies[:4]:
+        copy.wait()
     line = lax.broadcasted_iota(jnp.int32, (16, LANES), 0)
     lane = lax.broadcasted_iota(jnp.int32, (16, LANES), 1)
     codes = jnp.full((16, LANES), -1, jnp.int32)
-    for r, (table, count) in enumerate(((columns, counts), (back_columns, back_counts))):
+    for r in range(2):
+        table, count = scalars[2 * r], scalars[2 * r + 1]
         for w in range(2):
             for s in range(SLOTS):
                 value = jnp.where(s < count[w], table[w, s], -1)
                 codes = jnp.where((line == 2 * r + w) & (lane == s), value, codes)
     codes = codes.astype(F32).astype(BF16)
-    for q, out in enumerate(outs):
-        share = lanes_of(chip(pos) ^ q)
-        out[:ROWS, :LANES] = features[:, share]
-        out[:ROWS, LANES:] = cotangent[:, share]
+    for out in outs:
         out[ROWS:, :LANES] = codes
         out[ROWS:, LANES:] = codes
-
-
-def pack(pos, columns, counts, back_columns, back_counts, features, cotangent):
+    for copy in copies[4:]:
+        copy.wait()
+
+
+def pack(pos, columns, counts, back_columns, back_counts, features, cotangent, tiles, back_tiles):
     return call(
         pack_body,
-        (shaped(ROWS + 16, 2 * LANES),) * QUAD,
-        (pos, columns, counts, back_columns, back_counts, features, cotangent),
-        [SMEM] * 5 + [VMEM] * 2,
+        (shaped(ROWS + 16, 2 * LANES),) * QUAD
+        + (jax.ShapeDtypeStruct((4, BLOCK, SLOTS * BLOCK), BF16),),
+        (pos, columns, counts, back_columns, back_counts, features, cotangent, tiles, back_tiles),
+        [SMEM] + [ANY] * 8,
+        [pltpu.SMEM((2, SLOTS), jnp.int32), pltpu.SMEM((2,), jnp.int32)] * 2
+        + [pltpu.SemaphoreType.DMA((14,))],
     )
 
 
 def unpack_body(pos, *refs):
-    parts, (forward, backward, places) = refs[:QUAD], refs[QUAD:]
+    parts, (both, places) = refs[:QUAD], refs[QUAD:]
     for q, part in enumerate(parts):
-        rows = pl.ds(q * ROWS, ROWS)
-        forward[rows, :] = part[:ROWS, :LANES]
-        backward[rows, :] = part[:ROWS, LANES:]
+        both[pl.ds(q * ROWS, ROWS), :] = part[:ROWS, :]
         block = part[ROWS:, :LANES].astype(F32).astype(jnp.int32)
         apart = (block >> 1) ^ pos[0]
         place = ((apart & 1) * 16 + (apart >> 3) * 4 + ((apart >> 1) & 3)) * 2 + (block & 1)
@@ -164,18 +180,24 @@
 def unpack(pos, parts):
     return call(
         unpack_body,
-        (shaped(SPAN, LANES), shaped(SPAN, LANES), shaped(8 * QUAD, LANES, jnp.int32)),
+        (shaped(SPAN, 2 * LANES), shaped(8 * QUAD, LANES, jnp.int32)),
         (pos, *parts),
         [SMEM] + [VMEM] * QUAD,
     )
 
 
-def mix_body(base, split, places, *refs):
+def mix_body(base, half, split, places, *refs):
     shares, tiles, outs = refs[:8], refs[8:12], refs[12:-3]
     table, picked, sems = refs[-3:]
     copies = []
     for i, share in enumerate(shares):
-        copies.append(pltpu.make_async_copy(share, table.at[pl.ds(i * SPAN, SPAN), :], sems.at[i]))
+        copies.append(
+            pltpu.make_async_copy(
+                share.at[:, pl.ds(half * LANES, LANES)],
+                table.at[pl.ds(i * SPAN, SPAN), :],
+                sems.at[i],
+            )
+        )
         copies[-1].start()
     table[DEVICES * ROWS :, :] = jnp.zeros((BLOCK, LANES), BF16)
     for copy in copies:
@@ -186,7 +208,7 @@
             for s in range(SLOTS):
                 first = pl.multiple_of(places[q * 8 + base + w, s] * BLOCK, BLOCK)
                 picked[row, pl.ds(s * BLOCK, BLOCK), :] = table[pl.ds(first, BLOCK), :]
-            total = jnp.dot(tiles[q][w], picked[row], preferred_element_type=F32)
+            total = jnp.dot(tiles[q][base + w], picked[row], preferred_element_type=F32)
             total = total + table[pl.ds(row * BLOCK, BLOCK), :].astype(F32)
             if split:
                 outs[q][pl.ds(w * BLOCK, BLOCK), :] = total.astype(BF16)
@@ -194,11 +216,11 @@
                 outs[0][pl.ds(row * BLOCK, BLOCK), :] = total.astype(BF16)
 
 
-def mix(places, base, planes, other_core, tiles, split=False):
-    return call(
-        functools.partial(mix_body, base, split),
+def mix(places, base, half, shares, tiles, split=False):
+    return call(
+        functools.partial(mix_body, base, half, split),
         (shaped(ROWS, LANES),) * QUAD if split else (shaped(SPAN, LANES),),
-        (places, *planes, *other_core, *tiles),
+        (places, *shares, *tiles),
         [SMEM] + [ANY] * 8 + [VMEM] * 4,
         [
             pltpu.VMEM((DEVICES * ROWS + BLOCK, LANES), BF16),
@@ -338,29 +360,37 @@
     cotangent,
 ):
     pos = lax.axis_index(AXES).astype(jnp.int32).reshape(1)
-    packed = pack(pos, tile_columns, tiles_per_row, rev_cols, rev_count, features, cotangent)
+    *packed, both_tiles = pack(
+        pos,
+        tile_columns,
+        tiles_per_row,
+        rev_cols,
+        rev_count,
+        features,
+        cotangent,
+        tile_entries,
+        rev_vals,
+    )
     parts = [packed[0]] + [swap(packed[q], 2 * q) for q in range(1, QUAD)]
-    forward, backward, places = unpack(pos, parts)
-    tile_entries, _ = lax.optimization_barrier((tile_entries, parts[1]))
-    tiles = over_quad(tile_entries)
-    rev_vals, _ = lax.optimization_barrier((rev_vals, tiles[1]))
-    back_tiles = over_quad(rev_vals)
-
-    def both_cores(share):
-        planes = over_planes(share)
-        return planes, [swap(plane, CORE) for plane in planes]
-
-    (mixed_share,) = mix(places, 0, *both_cores(forward), tiles)
-    (spread_share,) = mix(places, 2, *both_cores(backward), back_tiles)
+    share, places = unpack(pos, parts)
+    tiles = over_quad(both_tiles)
+
+    def everywhere(own):
+        planes = over_planes(own)
+        return planes + [swap(plane, CORE) for plane in planes]
+
+    shares = everywhere(share)
+    (mixed_share,) = mix(places, 0, 0, shares, tiles)
+    (spread_share,) = mix(places, 2, 1, shares, tiles)
     mixed, hidden, hidden_share, slope = first_layer(pos, over_quad(mixed_share), w_first)
-    again = mix(places, 0, *both_cores(hidden_share), tiles, split=True)
+    again = mix(places, 0, 0, everywhere(hidden_share), tiles, split=True)
     z_out = second_layer(
         pos, [again[0]] + [swap(again[q], 2 * q) for q in range(1, QUAD)], w_second
     )
     keep, send = gradients(pos, mixed, hidden, slope, over_quad(spread_share), w_second)
-    part = (keep + swap(send, CORE)).astype(BF16)
-    near, z1, z2, z3 = (plane.astype(F32) for plane in over_planes(part))
-    total = ((near + z1) + (z2 + z3)).astype(BF16)
+    total = (keep + swap(send, CORE)).astype(BF16)
+    for mask in (8, 16):
+        total = (total.astype(F32) + swap(total, mask).astype(F32)).astype(BF16)
     mine = over_quad(total)
     grad_first, grad_second = place(pos, mine, [swap(piece, CORE) for piece in mine])
     return (z_out, grad_first, grad_second)

time: 130 us -> 104 us (0.80)
  waiting for transfers between devices: 68.5 us -> 51 us
  starting transfers between devices: 44.6 us -> 36.2 us
  Pallas kernels: 13.3 us -> 11 us
  local copies, waits for them, and re-layouts: 2.51 us -> 4.4 us
    ppermute x50 -> x39, waiting for transfers between devices: 68.5 us -> 51 us  [swap(): return lax.ppermute(value, AXES, [(i, i ^ mask) for i in range(DEVICES)])]
    ppermute x50 -> x39, starting transfers between devices: 44.6 us -> 36.2 us  [swap(): return lax.ppermute(value, AXES, [(i, i ^ mask) for i in range(DEVICES)])]
    pallas_call x9, Pallas kernels: 13.3 us -> 11 us  [call(): pl.pallas_call(body, out_shape=out_shape, in_specs=list(spaces), out_spec...]
    unnamed x20, local copies, waits for them, and re-layouts: 2.51 us -> 4.4 us
  transfers between devices with their start and end apart: 50 -> 39, of which waited for: 19 -> 21; matrix products, arithmetic and copies ran while one was open for 0% -> 0% of each run, Pallas kernels for 8% -> 6%
where the time goes in v4:
time: 104 us
  waiting for transfers between devices  51 us (49%)
  starting transfers between devices  36.2 us (35%)
  Pallas kernels  11 us (11%)
  local copies, waits for them, and re-layouts  4.4 us (4%)
    ppermute x39, waiting for transfers between devices, swap(): return lax.ppermute(value, AXES, [(i, i ^ mask) for i in range(DEVICES)])  51 us
    ppermute x39, starting transfers between devices, swap(): return lax.ppermute(value, AXES, [(i, i ^ mask) for i in range(DEVICES)])  36.2 us
    pallas_call x9, Pallas kernels, call(): pl.pallas_call(body, out_shape=out_shape, in_specs=list(spaces), out_spec...  11 us
    unnamed x20, local copies, waits for them, and re-layouts  4.4 us
  transfers between devices with their start and end apart: 39, of which 21 were waited for; matrix products, arithmetic and copies ran while one was open for 0% of the time, Pallas kernels for 6%

profile of v4, /device:TPU:0, one launch (start us, length us, event | category | flops | bytes accessed | tf_op | source)
XLA Modules:
  0.0 103.6 jit_solution(12300382420809991270)
XLA Ops:
  1.4 0.9 copy-done.2
  2.3 0.9 copy-done.3
  3.3 0.9 copy-done.4
  4.2 0.9 copy-done.5
  5.1 0.8 shard_map.121
  5.9 3.0 %collective-permute-start = (bf16[144,256]{1,0:T(8,128)(2,1)S(1)}, bf16[144,256]{1,0:T(8,128)(2,1)S(1)}, u32[]{:S(2)}, u32[]{:S(2)}) collective-permute-start(bf16[144,256]{1,0:T(8,128)(2,1)S(1)} %get-tuple-element.23), channel_id=1, source_target_pairs={{0,2},{1,3},{2,0},{3,1},{4,6},{5,7},{6,4},{7,5},{8,10},{9,11},{10,... | collective-permute-start | bytes 221192 | tf_op jit(solution)/shard_map/ppermute | solution.py:105
  8.9 1.5 %collective-permute-start.1 = (bf16[144,256]{1,0:T(8,128)(2,1)S(1)}, bf16[144,256]{1,0:T(8,128)(2,1)S(1)}, u32[]{:S(2)}, u32[]{:S(2)}) collective-permute-start(bf16[144,256]{1,0:T(8,128)(2,1)S(1)} %get-tuple-element.24), channel_id=1, source_target_pairs={{0,4},{1,5},{2,6},{3,7},{4,0},{5,1},{6,2},{7,3},{8,12},{9,13},{10,... | collective-permute-start | bytes 221192 | tf_op jit(solution)/shard_map/ppermute | solution.py:105
  10.4 1.0 collective-permute-done.refs_1_
  11.4 1.8 %collective-permute-done.1.refs_2_ = bf16[144,256]{1,0:T(8,128)(2,1)S(1)} collective-permute-done((bf16[144,256]{1,0:T(8,128)(2,1)S(1)}, bf16[144,256]{1,0:T(8,128)(2,1)S(1)}, u32[]{:S(2)}, u32[]{:S(2)}) %collective-permute-start.1) | collective-permute-done | bytes 73760 | tf_op jit(solution)/shard_map/ppermute | solution.py:105
  13.2 2.4 %collective-permute-done.2.refs_3_ = bf16[144,256]{1,0:T(8,128)(2,1)S(1)} collective-permute-done((bf16[144,256]{1,0:T(8,128)(2,1)S(1)}, bf16[144,256]{1,0:T(8,128)(2,1)S(1)}, u32[]{:S(2)}, u32[]{:S(2)}) %collective-permute-start.2) | collective-permute-done | bytes 73760 | tf_op jit(solution)/shard_map/ppermute | solution.py:105
  16.2 2.7 %collective-permute-start.4 = (bf16[512,256]{1,0:T(8,128)(2,1)S(1)}, bf16[512,256]{1,0:T(8,128)(2,1)S(1)}, u32[]{:S(2)}, u32[]{:S(2)}) collective-permute-start(bf16[512,256]{1,0:T(8,128)(2,1)S(1)} %get-tuple-element.27.refs_0_), channel_id=1, source_target_pairs={{0,16},{1,17},{2,18},{3,19},{4,20},{5,21},{6,22},{7,23},{8,24},{9,... | collective-permute-start | bytes 786440 | tf_op jit(solution)/shard_map/ppermute | solution.py:105
  18.9 1.5 %collective-permute-start.11 = (bf16[4,64,1024]{2,1,0:T(8,128)(2,1)S(1)}, bf16[4,64,1024]{2,1,0:T(8,128)(2,1)S(1)}, u32[]{:S(2)}, u32[]{:S(2)}) collective-permute-start(bf16[4,64,1024]{2,1,0:T(8,128)(2,1)S(1)} %get-tuple-element.28.refs_8_), channel_id=1, source_target_pairs={{0,4},{1,5},{2,6},{3,7},{4,0},{5,1},{6,2},{7,3},{8,12},{9,13},{10,... | collective-permute-start | bytes 1572872 | tf_op jit(solution)/shard_map/ppermute | solution.py:105
  20.4 1.6 %collective-permute-start.3 = (bf16[512,256]{1,0:T(8,128)(2,1)S(1)}, bf16[512,256]{1,0:T(8,128)(2,1)S(1)}, u32[]{:S(2)}, u32[]{:S(2)}) collective-permute-start(bf16[512,256]{1,0:T(8,128)(2,1)S(1)} %get-tuple-element.27.refs_0_), channel_id=1, source_target_pairs={{0,8},{1,9},{2,10},{3,11},{4,12},{5,13},{6,14},{7,15},{8,0},{9,1},... | collective-permute-start | bytes 786440 | tf_op jit(solution)/shard_map/ppermute | solution.py:105
  22.0 1.5 %collective-permute-start.10 = (bf16[4,64,1024]{2,1,0:T(8,128)(2,1)S(1)}, bf16[4,64,1024]{2,1,0:T(8,128)(2,1)S(1)}, u32[]{:S(2)}, u32[]{:S(2)}) collective-permute-start(bf16[4,64,1024]{2,1,0:T(8,128)(2,1)S(1)} %get-tuple-element.28.refs_8_), channel_id=1, source_target_pairs={{0,2},{1,3},{2,0},{3,1},{4,6},{5,7},{6,4},{7,5},{8,10},{9,11},{10,... | collective-permute-start | bytes 1572872 | tf_op jit(solution)/shard_map/ppermute | solution.py:105
  23.5 7.8 %collective-permute-done.4.refs_2_ = bf16[512,256]{1,0:T(8,128)(2,1)S(1)} collective-permute-done((bf16[512,256]{1,0:T(8,128)(2,1)S(1)}, bf16[512,256]{1,0:T(8,128)(2,1)S(1)}, u32[]{:S(2)}, u32[]{:S(2)}) %collective-permute-start.4) | collective-permute-done | bytes 262176 | tf_op jit(solution)/shard_map/ppermute | solution.py:105
  33.2 5.6 %collective-permute-done.5.refs_3_ = bf16[512,256]{1,0:T(8,128)(2,1)S(1)} collective-permute-done((bf16[512,256]{1,0:T(8,128)(2,1)S(1)}, bf16[512,256]{1,0:T(8,128)(2,1)S(1)}, u32[]{:S(2)}, u32[]{:S(2)}) %collective-permute-start.5) | collective-permute-done | bytes 262176 | tf_op jit(solution)/shard_map/ppermute | solution.py:105
  38.8 3.4 %collective-permute-done.11.refs_10_ = bf16[4,64,1024]{2,1,0:T(8,128)(2,1)S(1)} collective-permute-done((bf16[4,64,1024]{2,1,0:T(8,128)(2,1)S(1)}, bf16[4,64,1024]{2,1,0:T(8,128)(2,1)S(1)}, u32[]{:S(2)}, u32[]{:S(2)}) %collective-permute-start.11) | collective-permute-done | bytes 524320 | tf_op jit(solution)/shard_map/ppermute | solution.py:105
  42.2 1.7 %shard_map.123.p0 = bf16[512,128]{1,0:T(8,128)(2,1)S(1)} custom-call(s32[32,128]{1,0:T(8,128)S(1)} %get-tuple-element.26.places, bf16[512,256]{1,0:T(8,128)(2,1)S(1)} %get-tuple-element.27.refs_0_, bf16[512,256]{1,0:T(8,128)(2,1)S(1)} %collective-permute-done.3.refs_1_, bf16[512,256]{1,0:T(8,128)(2,1)S(1)} %collective-permute-done.4.refs_2_, ...), custom_call_target="tpu_custom_call" | custom-call | tf_op jit(solution)/shard_map/pallas_call | solution.py:90
  44.6 1.4 %collective-permute-start.14 = (bf16[512,128]{1,0:T(8,128)(2,1)S(1)}, bf16[512,128]{1,0:T(8,128)(2,1)S(1)}, u32[]{:S(2)}, u32[]{:S(2)}) collective-permute-start(bf16[512,128]{1,0:T(8,128)(2,1)S(1)} %shard_map.123.p0), channel_id=1, source_target_pairs={{0,4},{1,5},{2,6},{3,7},{4,0},{5,1},{6,2},{7,3},{8,12},{9,13},{10,... | collective-permute-start | bytes 393224 | tf_op jit(solution)/shard_map/ppermute | solution.py:105
  46.0 1.5 %collective-permute-start.13 = (bf16[512,128]{1,0:T(8,128)(2,1)S(1)}, bf16[512,128]{1,0:T(8,128)(2,1)S(1)}, u32[]{:S(2)}, u32[]{:S(2)}) collective-permute-start(bf16[512,128]{1,0:T(8,128)(2,1)S(1)} %shard_map.123.p0), channel_id=1, source_target_pairs={{0,2},{1,3},{2,0},{3,1},{4,6},{5,7},{6,4},{7,5},{8,10},{9,11},{10,... | collective-permute-start | bytes 393224 | tf_op jit(solution)/shard_map/ppermute | solution.py:105
  47.5 1.7 %shard_map.127.p0 = bf16[512,128]{1,0:T(8,128)(2,1)S(1)} custom-call(s32[32,128]{1,0:T(8,128)S(1)} %get-tuple-element.26.places, bf16[512,256]{1,0:T(8,128)(2,1)S(1)} %get-tuple-element.27.refs_0_, bf16[512,256]{1,0:T(8,128)(2,1)S(1)} %collective-permute-done.3.refs_1_, bf16[512,256]{1,0:T(8,128)(2,1)S(1)} %collective-permute-done.4.refs_2_, ...), custom_call_target="tpu_custom_call" | custom-call | tf_op jit(solution)/shard_map/pallas_call | solution.py:90
  49.8 1.4 %collective-permute-start.27 = (bf16[512,128]{1,0:T(8,128)(2,1)S(1)}, bf16[512,128]{1,0:T(8,128)(2,1)S(1)}, u32[]{:S(2)}, u32[]{:S(2)}) collective-permute-start(bf16[512,128]{1,0:T(8,128)(2,1)S(1)} %shard_map.127.p0), channel_id=1, source_target_pairs={{0,4},{1,5},{2,6},{3,7},{4,0},{5,1},{6,2},{7,3},{8,12},{9,13},{10,... | collective-permute-start | bytes 393224 | tf_op jit(solution)/shard_map/ppermute | solution.py:105
  51.3 1.4 %collective-permute-start.26 = (bf16[512,128]{1,0:T(8,128)(2,1)S(1)}, bf16[512,128]{1,0:T(8,128)(2,1)S(1)}, u32[]{:S(2)}, u32[]{:S(2)}) collective-permute-start(bf16[512,128]{1,0:T(8,128)(2,1)S(1)} %shard_map.127.p0), channel_id=1, source_target_pairs={{0,2},{1,3},{2,0},{3,1},{4,6},{5,7},{6,4},{7,5},{8,10},{9,11},{10,... | collective-permute-start | bytes 393224 | tf_op jit(solution)/shard_map/ppermute | solution.py:105
  52.7 1.5 %collective-permute-done.14.p2 = bf16[512,128]{1,0:T(8,128)(2,1)S(1)} collective-permute-done((bf16[512,128]{1,0:T(8,128)(2,1)S(1)}, bf16[512,128]{1,0:T(8,128)(2,1)S(1)}, u32[]{:S(2)}, u32[]{:S(2)}) %collective-permute-start.14) | collective-permute-done | bytes 131104 | tf_op jit(solution)/shard_map/ppermute | solution.py:105
  54.2 0.8 shard_map.124
  55.0 2.0 %collective-permute-done.28.p3 = bf16[512,128]{1,0:T(8,128)(2,1)S(1)} collective-permute-done((bf16[512,128]{1,0:T(8,128)(2,1)S(1)}, bf16[512,128]{1,0:T(8,128)(2,1)S(1)}, u32[]{:S(2)}, u32[]{:S(2)}) %collective-permute-start.28) | collective-permute-done | bytes 131104 | tf_op jit(solution)/shard_map/ppermute | solution.py:105
  56.9 1.3 %collective-permute-done.27.p2 = bf16[512,128]{1,0:T(8,128)(2,1)S(1)} collective-permute-done((bf16[512,128]{1,0:T(8,128)(2,1)S(1)}, bf16[512,128]{1,0:T(8,128)(2,1)S(1)}, u32[]{:S(2)}, u32[]{:S(2)}) %collective-permute-start.27) | collective-permute-done | bytes 131104 | tf_op jit(solution)/shard_map/ppermute | solution.py:105
  59.0 1.5 %collective-permute-done.29 = f32[512,128]{1,0:T(8,128)S(1)} collective-permute-done((f32[512,128]{1,0:T(8,128)S(1)}, f32[512,128]{1,0:T(8,128)S(1)}, u32[]{:S(2)}, u32[]{:S(2)}) %collective-permute-start.29) | collective-permute-done | bytes 262176 | tf_op jit(solution)/shard_map/ppermute | solution.py:105
  60.6 1.5 %collective-permute-start.30 = (bf16[512,128]{1,0:T(8,128)(2,1)S(1)}, bf16[512,128]{1,0:T(8,128)(2,1)S(1)}, u32[]{:S(2)}, u32[]{:S(2)}) collective-permute-start(bf16[512,128]{1,0:T(8,128)(2,1)S(1)} %add_convert_fusion.2), channel_id=1, source_target_pairs={{0,8},{1,9},{2,10},{3,11},{4,12},{5,13},{6,14},{7,15},{8,0},{9,1},... | collective-permute-start | bytes 393224 | tf_op jit(solution)/shard_map/ppermute | solution.py:105
  62.1 2.3 %collective-permute-start.17 = (bf16[512,128]{1,0:T(8,128)(2,1)S(1)}, bf16[512,128]{1,0:T(8,128)(2,1)S(1)}, u32[]{:S(2)}, u32[]{:S(2)}) collective-permute-start(bf16[512,128]{1,0:T(8,128)(2,1)S(1)} %get-tuple-element.29.refs_0_), channel_id=1, source_target_pairs={{0,16},{1,17},{2,18},{3,19},{4,20},{5,21},{6,22},{7,23},{8,24},{9,... | collective-permute-start | bytes 393224 | tf_op jit(solution)/shard_map/ppermute | solution.py:105
  64.8 4.3 %collective-permute-done.30 = bf16[512,128]{1,0:T(8,128)(2,1)S(1)} collective-permute-done((bf16[512,128]{1,0:T(8,128)(2,1)S(1)}, bf16[512,128]{1,0:T(8,128)(2,1)S(1)}, u32[]{:S(2)}, u32[]{:S(2)}) %collective-permute-start.30) | collective-permute-done | bytes 131104 | tf_op jit(solution)/shard_map/ppermute | solution.py:105
  69.2 0.9 collective-permute-start.31
  70.1 1.3 %collective-permute-done.17.refs_2_ = bf16[512,128]{1,0:T(8,128)(2,1)S(1)} collective-permute-done((bf16[512,128]{1,0:T(8,128)(2,1)S(1)}, bf16[512,128]{1,0:T(8,128)(2,1)S(1)}, u32[]{:S(2)}, u32[]{:S(2)}) %collective-permute-start.17) | collective-permute-done | bytes 131104 | tf_op jit(solution)/shard_map/ppermute | solution.py:105
  71.4 2.2 %collective-permute-start.18 = (bf16[512,128]{1,0:T(8,128)(2,1)S(1)}, bf16[512,128]{1,0:T(8,128)(2,1)S(1)}, u32[]{:S(2)}, u32[]{:S(2)}) collective-permute-start(bf16[512,128]{1,0:T(8,128)(2,1)S(1)} %collective-permute-done.17.refs_2_), channel_id=1, source_target_pairs={{0,8},{1,9},{2,10},{3,11},{4,12},{5,13},{6,14},{7,15},{8,0},{9,1},... | collective-permute-start | bytes 393224 | tf_op jit(solution)/shard_map/ppermute | solution.py:105
  73.6 3.9 %collective-permute-done.31 = bf16[512,128]{1,0:T(8,128)(2,1)S(1)} collective-permute-done((bf16[512,128]{1,0:T(8,128)(2,1)S(1)}, bf16[512,128]{1,0:T(8,128)(2,1)S(1)}, u32[]{:S(2)}, u32[]{:S(2)}) %collective-permute-start.31) | collective-permute-done | bytes 131104 | tf_op jit(solution)/shard_map/ppermute | solution.py:105
  77.6 1.5 %collective-permute-start.34 = (bf16[512,128]{1,0:T(8,128)(2,1)S(1)}, bf16[512,128]{1,0:T(8,128)(2,1)S(1)}, u32[]{:S(2)}, u32[]{:S(2)}) collective-permute-start(bf16[512,128]{1,0:T(8,128)(2,1)S(1)} %add_convert_fusion.refs_0_), channel_id=1, source_target_pairs={{0,6},{1,7},{2,4},{3,5},{4,2},{5,3},{6,0},{7,1},{8,14},{9,15},{10,... | collective-permute-start | bytes 393224 | tf_op jit(solution)/shard_map/ppermute | solution.py:105
  79.1 1.4 %collective-permute-start.33 = (bf16[512,128]{1,0:T(8,128)(2,1)S(1)}, bf16[512,128]{1,0:T(8,128)(2,1)S(1)}, u32[]{:S(2)}, u32[]{:S(2)}) collective-permute-start(bf16[512,128]{1,0:T(8,128)(2,1)S(1)} %add_convert_fusion.refs_0_), channel_id=1, source_target_pairs={{0,4},{1,5},{2,6},{3,7},{4,0},{5,1},{6,2},{7,3},{8,12},{9,13},{10,... | collective-permute-start | bytes 393224 | tf_op jit(solution)/shard_map/ppermute | solution.py:105
  81.6 1.9 %collective-permute-done.34.refs_3_ = bf16[512,128]{1,0:T(8,128)(2,1)S(1)} collective-permute-done((bf16[512,128]{1,0:T(8,128)(2,1)S(1)}, bf16[512,128]{1,0:T(8,128)(2,1)S(1)}, u32[]{:S(2)}, u32[]{:S(2)}) %collective-permute-start.34) | collective-permute-done | bytes 131104 | tf_op jit(solution)/shard_map/ppermute | solution.py:105
  83.6 1.3 %collective-permute-done.33.refs_2_ = bf16[512,128]{1,0:T(8,128)(2,1)S(1)} collective-permute-done((bf16[512,128]{1,0:T(8,128)(2,1)S(1)}, bf16[512,128]{1,0:T(8,128)(2,1)S(1)}, u32[]{:S(2)}, u32[]{:S(2)}) %collective-permute-start.33) | collective-permute-done | bytes 131104 | tf_op jit(solution)/shard_map/ppermute | solution.py:105
  85.4 2.8 %shard_map.125 = (bf16[128,128]{1,0:T(8,128)(2,1)S(1)}, bf16[128,128]{1,0:T(8,128)(2,1)S(1)}, bf16[128,128]{1,0:T(8,128)(2,1)S(1)}, bf16[128,128]{1,0:T(8,128)(2,1)S(1)}) custom-call(s32[32,128]{1,0:T(8,128)S(1)} %get-tuple-element.26.places, bf16[512,128]{1,0:T(8,128)(2,1)S(1)} %get-tuple-element.29.refs_0_, ...), custom_call_target="tpu_custom_call" | custom-call | tf_op jit(solution)/shard_map/pallas_call | solution.py:90
  88.3 1.4 %collective-permute-start.23 = (bf16[128,128]{1,0:T(8,128)(2,1)S(1)}, bf16[128,128]{1,0:T(8,128)(2,1)S(1)}, u32[]{:S(2)}, u32[]{:S(2)}) collective-permute-start(bf16[128,128]{1,0:T(8,128)(2,1)S(1)} %get-tuple-element.31), channel_id=1, source_target_pairs={{0,2},{1,3},{2,0},{3,1},{4,6},{5,7},{6,4},{7,5},{8,10},{9,11},{10,... | collective-permute-start | bytes 98312 | tf_op jit(solution)/shard_map/ppermute | solution.py:105
  89.7 2.6 %collective-permute-done.23.p1 = bf16[128,128]{1,0:T(8,128)(2,1)S(1)} collective-permute-done((bf16[128,128]{1,0:T(8,128)(2,1)S(1)}, bf16[128,128]{1,0:T(8,128)(2,1)S(1)}, u32[]{:S(2)}, u32[]{:S(2)}) %collective-permute-start.23) | collective-permute-done | bytes 32800 | tf_op jit(solution)/shard_map/ppermute | solution.py:105
  92.2 1.3 %collective-permute-start.24 = (bf16[128,128]{1,0:T(8,128)(2,1)S(1)}, bf16[128,128]{1,0:T(8,128)(2,1)S(1)}, u32[]{:S(2)}, u32[]{:S(2)}) collective-permute-start(bf16[128,128]{1,0:T(8,128)(2,1)S(1)} %get-tuple-element.32), channel_id=1, source_target_pairs={{0,4},{1,5},{2,6},{3,7},{4,0},{5,1},{6,2},{7,3},{8,12},{9,13},{10,... | collective-permute-start | bytes 98312 | tf_op jit(solution)/shard_map/ppermute | solution.py:105
  93.6 2.6 %collective-permute-done.24.p2 = bf16[128,128]{1,0:T(8,128)(2,1)S(1)} collective-permute-done((bf16[128,128]{1,0:T(8,128)(2,1)S(1)}, bf16[128,128]{1,0:T(8,128)(2,1)S(1)}, u32[]{:S(2)}, u32[]{:S(2)}) %collective-permute-start.24) | collective-permute-done | bytes 32800 | tf_op jit(solution)/shard_map/ppermute | solution.py:105
  96.2 1.4 %collective-permute-start.25 = (bf16[128,128]{1,0:T(8,128)(2,1)S(1)}, bf16[128,128]{1,0:T(8,128)(2,1)S(1)}, u32[]{:S(2)}, u32[]{:S(2)}) collective-permute-start(bf16[128,128]{1,0:T(8,128)(2,1)S(1)} %get-tuple-element.33), channel_id=1, source_target_pairs={{0,6},{1,7},{2,4},{3,5},{4,2},{5,3},{6,0},{7,1},{8,14},{9,15},{10,... | collective-permute-start | bytes 98312 | tf_op jit(solution)/shard_map/ppermute | solution.py:105
  97.6 3.4 %collective-permute-done.25.p3 = bf16[128,128]{1,0:T(8,128)(2,1)S(1)} collective-permute-done((bf16[128,128]{1,0:T(8,128)(2,1)S(1)}, bf16[128,128]{1,0:T(8,128)(2,1)S(1)}, u32[]{:S(2)}, u32[]{:S(2)}) %collective-permute-start.25) | collective-permute-done | bytes 32800 | tf_op jit(solution)/shard_map/ppermute | solution.py:105
  101.0 0.9 shard_map.126
  101.9 1.6 %shard_map.129 = (f32[512,512]{1,0:T(8,128)}, f32[512,512]{1,0:T(8,128)}) custom-call(s32[1]{0:T(128)} %bitcast.pos, bf16[512,128]{1,0:T(8,128)(2,1)S(1)} %add_convert_fusion.refs_0_, bf16[512,128]{1,0:T(8,128)(2,1)S(1)} %collective-permute-done.32.refs_1_, bf16[512,128]{1,0:T(8,128)(2,1)S(1)} %collective-permute-done.33.refs_2_, ...), custom_call_target="tpu_custom_call" | custom-call | tf_op jit(solution)/shard_map/pallas_call | solution.py:90
  (62 shorter events, 7.7 us)
Async XLA Ops:
  0.6 0.7 copy-start.7
  0.7 0.7 copy-start.6
  0.7 0.7 copy-start.8
  1.4 1.0 copy-start.2
  2.3 0.9 copy-start.3
  3.3 0.9 copy-start.4
  4.2 0.9 copy-start.5
  5.9 5.5 %collective-permute-start = (bf16[144,256]{1,0:T(8,128)(2,1)S(1)}, bf16[144,256]{1,0:T(8,128)(2,1)S(1)}, u32[]{:S(2)}, u32[]{:S(2)}) collective-permute-start(bf16[144,256]{1,0:T(8,128)(2,1)S(1)} %get-tuple-element.23), channel_id=1, source_target_pairs={{0,2},{1,3},{2,0},{3,1},{4,6},{5,7},{6,4},{7,5},{8,10},{9,11},{10,... | collective-permute-start | bytes 221192 | tf_op jit(solution)/shard_map/ppermute | solution.py:105
  8.9 4.4 %collective-permute-start.1 = (bf16[144,256]{1,0:T(8,128)(2,1)S(1)}, bf16[144,256]{1,0:T(8,128)(2,1)S(1)}, u32[]{:S(2)}, u32[]{:S(2)}) collective-permute-start(bf16[144,256]{1,0:T(8,128)(2,1)S(1)} %get-tuple-element.24), channel_id=1, source_target_pairs={{0,4},{1,5},{2,6},{3,7},{4,0},{5,1},{6,2},{7,3},{8,12},{9,13},{10,... | collective-permute-start | bytes 221192 | tf_op jit(solution)/shard_map/ppermute | solution.py:105
  10.4 5.3 %collective-permute-start.2 = (bf16[144,256]{1,0:T(8,128)(2,1)S(1)}, bf16[144,256]{1,0:T(8,128)(2,1)S(1)}, u32[]{:S(2)}, u32[]{:S(2)}) collective-permute-start(bf16[144,256]{1,0:T(8,128)(2,1)S(1)} %get-tuple-element.25), channel_id=1, source_target_pairs={{0,6},{1,7},{2,4},{3,5},{4,2},{5,3},{6,0},{7,1},{8,14},{9,15},{10,... | collective-permute-start | bytes 221192 | tf_op jit(solution)/shard_map/ppermute | solution.py:105
  15.7 6.3 %collective-permute-start.6 = (bf16[512,256]{1,0:T(8,128)(2,1)S(1)}, bf16[512,256]{1,0:T(8,128)(2,1)S(1)}, u32[]{:S(2)}, u32[]{:S(2)}) collective-permute-start(bf16[512,256]{1,0:T(8,128)(2,1)S(1)} %get-tuple-element.27.refs_0_), channel_id=1, source_target_pairs={{0,1},{1,0},{2,3},{3,2},{4,5},{5,4},{6,7},{7,6},{8,9},{9,8},{10,11... | collective-permute-start | bytes 786440 | tf_op jit(solution)/shard_map/ppermute | solution.py:105
  15.8 16.9 %collective-permute-start.12 = (bf16[4,64,1024]{2,1,0:T(8,128)(2,1)S(1)}, bf16[4,64,1024]{2,1,0:T(8,128)(2,1)S(1)}, u32[]{:S(2)}, u32[]{:S(2)}) collective-permute-start(bf16[4,64,1024]{2,1,0:T(8,128)(2,1)S(1)} %get-tuple-element.28.refs_8_), channel_id=1, source_target_pairs={{0,6},{1,7},{2,4},{3,5},{4,2},{5,3},{6,0},{7,1},{8,14},{9,15},{10,... | collective-permute-start | bytes 1572872 | tf_op jit(solution)/shard_map/ppermute | solution.py:105
  16.2 15.0 %collective-permute-start.4 = (bf16[512,256]{1,0:T(8,128)(2,1)S(1)}, bf16[512,256]{1,0:T(8,128)(2,1)S(1)}, u32[]{:S(2)}, u32[]{:S(2)}) collective-permute-start(bf16[512,256]{1,0:T(8,128)(2,1)S(1)} %get-tuple-element.27.refs_0_), channel_id=1, source_target_pairs={{0,16},{1,17},{2,18},{3,19},{4,20},{5,21},{6,22},{7,23},{8,24},{9,... | collective-permute-start | bytes 786440 | tf_op jit(solution)/shard_map/ppermute | solution.py:105
  18.9 23.3 %collective-permute-start.11 = (bf16[4,64,1024]{2,1,0:T(8,128)(2,1)S(1)}, bf16[4,64,1024]{2,1,0:T(8,128)(2,1)S(1)}, u32[]{:S(2)}, u32[]{:S(2)}) collective-permute-start(bf16[4,64,1024]{2,1,0:T(8,128)(2,1)S(1)} %get-tuple-element.28.refs_8_), channel_id=1, source_target_pairs={{0,4},{1,5},{2,6},{3,7},{4,0},{5,1},{6,2},{7,3},{8,12},{9,13},{10,... | collective-permute-start | bytes 1572872 | tf_op jit(solution)/shard_map/ppermute | solution.py:105
  20.4 12.3 %collective-permute-start.3 = (bf16[512,256]{1,0:T(8,128)(2,1)S(1)}, bf16[512,256]{1,0:T(8,128)(2,1)S(1)}, u32[]{:S(2)}, u32[]{:S(2)}) collective-permute-start(bf16[512,256]{1,0:T(8,128)(2,1)S(1)} %get-tuple-element.27.refs_0_), channel_id=1, source_target_pairs={{0,8},{1,9},{2,10},{3,11},{4,12},{5,13},{6,14},{7,15},{8,0},{9,1},... | collective-permute-start | bytes 786440 | tf_op jit(solution)/shard_map/ppermute | solution.py:105
  22.0 20.2 %collective-permute-start.10 = (bf16[4,64,1024]{2,1,0:T(8,128)(2,1)S(1)}, bf16[4,64,1024]{2,1,0:T(8,128)(2,1)S(1)}, u32[]{:S(2)}, u32[]{:S(2)}) collective-permute-start(bf16[4,64,1024]{2,1,0:T(8,128)(2,1)S(1)} %get-tuple-element.28.refs_8_), channel_id=1, source_target_pairs={{0,2},{1,3},{2,0},{3,1},{4,6},{5,7},{6,4},{7,5},{8,10},{9,11},{10,... | collective-permute-start | bytes 1572872 | tf_op jit(solution)/shard_map/ppermute | solution.py:105
  31.3 7.5 %collective-permute-start.5 = (bf16[512,256]{1,0:T(8,128)(2,1)S(1)}, bf16[512,256]{1,0:T(8,128)(2,1)S(1)}, u32[]{:S(2)}, u32[]{:S(2)}) collective-permute-start(bf16[512,256]{1,0:T(8,128)(2,1)S(1)} %collective-permute-done.4.refs_2_), channel_id=1, source_target_pairs={{0,8},{1,9},{2,10},{3,11},{4,12},{5,13},{6,14},{7,15},{8,0},{9,1},... | collective-permute-start | bytes 786440 | tf_op jit(solution)/shard_map/ppermute | solution.py:105
  32.7 9.6 %collective-permute-start.8 = (bf16[512,256]{1,0:T(8,128)(2,1)S(1)}, bf16[512,256]{1,0:T(8,128)(2,1)S(1)}, u32[]{:S(2)}, u32[]{:S(2)}) collective-permute-start(bf16[512,256]{1,0:T(8,128)(2,1)S(1)} %collective-permute-done.4.refs_2_), channel_id=1, source_target_pairs={{0,1},{1,0},{2,3},{3,2},{4,5},{5,4},{6,7},{7,6},{8,9},{9,8},{10,11... | collective-permute-start | bytes 786440 | tf_op jit(solution)/shard_map/ppermute | solution.py:105
  32.7 9.6 %collective-permute-start.7 = (bf16[512,256]{1,0:T(8,128)(2,1)S(1)}, bf16[512,256]{1,0:T(8,128)(2,1)S(1)}, u32[]{:S(2)}, u32[]{:S(2)}) collective-permute-start(bf16[512,256]{1,0:T(8,128)(2,1)S(1)} %collective-permute-done.3.refs_1_), channel_id=1, source_target_pairs={{0,1},{1,0},{2,3},{3,2},{4,5},{5,4},{6,7},{7,6},{8,9},{9,8},{10,11... | collective-permute-start | bytes 786440 | tf_op jit(solution)/shard_map/ppermute | solution.py:105
  38.8 3.5 %collective-permute-start.9 = (bf16[512,256]{1,0:T(8,128)(2,1)S(1)}, bf16[512,256]{1,0:T(8,128)(2,1)S(1)}, u32[]{:S(2)}, u32[]{:S(2)}) collective-permute-start(bf16[512,256]{1,0:T(8,128)(2,1)S(1)} %collective-permute-done.5.refs_3_), channel_id=1, source_target_pairs={{0,1},{1,0},{2,3},{3,2},{4,5},{5,4},{6,7},{7,6},{8,9},{9,8},{10,11... | collective-permute-start | bytes 786440 | tf_op jit(solution)/shard_map/ppermute | solution.py:105
  43.9 10.3 %copy-start.1 = (bf16[512,512]{1,0:T(8,128)(2,1)S(1)}, bf16[512,512]{1,0:T(8,128)(2,1)}, u32[]{:S(2)}) copy-start(bf16[512,512]{1,0:T(8,128)(2,1)} %w_first.1) | copy-start | bytes 1572868
  43.9 7.4 %collective-permute-start.15 = (bf16[512,128]{1,0:T(8,128)(2,1)S(1)}, bf16[512,128]{1,0:T(8,128)(2,1)S(1)}, u32[]{:S(2)}, u32[]{:S(2)}) collective-permute-start(bf16[512,128]{1,0:T(8,128)(2,1)S(1)} %shard_map.123.p0), channel_id=1, source_target_pairs={{0,6},{1,7},{2,4},{3,5},{4,2},{5,3},{6,0},{7,1},{8,14},{9,15},{10,... | collective-permute-start | bytes 393224 | tf_op jit(solution)/shard_map/ppermute | solution.py:105
  44.6 9.6 %collective-permute-start.14 = (bf16[512,128]{1,0:T(8,128)(2,1)S(1)}, bf16[512,128]{1,0:T(8,128)(2,1)S(1)}, u32[]{:S(2)}, u32[]{:S(2)}) collective-permute-start(bf16[512,128]{1,0:T(8,128)(2,1)S(1)} %shard_map.123.p0), channel_id=1, source_target_pairs={{0,4},{1,5},{2,6},{3,7},{4,0},{5,1},{6,2},{7,3},{8,12},{9,13},{10,... | collective-permute-start | bytes 393224 | tf_op jit(solution)/shard_map/ppermute | solution.py:105
  46.0 8.2 %collective-permute-start.13 = (bf16[512,128]{1,0:T(8,128)(2,1)S(1)}, bf16[512,128]{1,0:T(8,128)(2,1)S(1)}, u32[]{:S(2)}, u32[]{:S(2)}) collective-permute-start(bf16[512,128]{1,0:T(8,128)(2,1)S(1)} %shard_map.123.p0), channel_id=1, source_target_pairs={{0,2},{1,3},{2,0},{3,1},{4,6},{5,7},{6,4},{7,5},{8,10},{9,11},{10,... | collective-permute-start | bytes 393224 | tf_op jit(solution)/shard_map/ppermute | solution.py:105
  49.2 9.0 %copy-start = (bf16[512,512]{1,0:T(8,128)(2,1)S(1)}, bf16[512,512]{1,0:T(8,128)(2,1)}, u32[]{:S(2)}) copy-start(bf16[512,512]{1,0:T(8,128)(2,1)} %w_second.3) | copy-start | bytes 1572868
  49.2 7.8 %collective-permute-start.28 = (bf16[512,128]{1,0:T(8,128)(2,1)S(1)}, bf16[512,128]{1,0:T(8,128)(2,1)S(1)}, u32[]{:S(2)}, u32[]{:S(2)}) collective-permute-start(bf16[512,128]{1,0:T(8,128)(2,1)S(1)} %shard_map.127.p0), channel_id=1, source_target_pairs={{0,6},{1,7},{2,4},{3,5},{4,2},{5,3},{6,0},{7,1},{8,14},{9,15},{10,... | collective-permute-start | bytes 393224 | tf_op jit(solution)/shard_map/ppermute | solution.py:105
  49.8 8.4 %collective-permute-start.27 = (bf16[512,128]{1,0:T(8,128)(2,1)S(1)}, bf16[512,128]{1,0:T(8,128)(2,1)S(1)}, u32[]{:S(2)}, u32[]{:S(2)}) collective-permute-start(bf16[512,128]{1,0:T(8,128)(2,1)S(1)} %shard_map.127.p0), channel_id=1, source_target_pairs={{0,4},{1,5},{2,6},{3,7},{4,0},{5,1},{6,2},{7,3},{8,12},{9,13},{10,... | collective-permute-start | bytes 393224 | tf_op jit(solution)/shard_map/ppermute | solution.py:105
  51.3 6.9 %collective-permute-start.26 = (bf16[512,128]{1,0:T(8,128)(2,1)S(1)}, bf16[512,128]{1,0:T(8,128)(2,1)S(1)}, u32[]{:S(2)}, u32[]{:S(2)}) collective-permute-start(bf16[512,128]{1,0:T(8,128)(2,1)S(1)} %shard_map.127.p0), channel_id=1, source_target_pairs={{0,2},{1,3},{2,0},{3,1},{4,6},{5,7},{6,4},{7,5},{8,10},{9,11},{10,... | collective-permute-start | bytes 393224 | tf_op jit(solution)/shard_map/ppermute | solution.py:105
  58.9 1.6 %collective-permute-start.29 = (f32[512,128]{1,0:T(8,128)S(1)}, f32[512,128]{1,0:T(8,128)S(1)}, u32[]{:S(2)}, u32[]{:S(2)}) collective-permute-start(f32[512,128]{1,0:T(8,128)S(1)} %get-tuple-element.38), channel_id=1, source_target_pairs={{0,1},{1,0},{2,3},{3,2},{4,5},{5,4},{6,7},{7,6},{8,9},{9,8},{10,11... | collective-permute-start | bytes 786440 | tf_op jit(solution)/shard_map/ppermute | solution.py:105
  60.6 8.6 %collective-permute-start.30 = (bf16[512,128]{1,0:T(8,128)(2,1)S(1)}, bf16[512,128]{1,0:T(8,128)(2,1)S(1)}, u32[]{:S(2)}, u32[]{:S(2)}) collective-permute-start(bf16[512,128]{1,0:T(8,128)(2,1)S(1)} %add_convert_fusion.2), channel_id=1, source_target_pairs={{0,8},{1,9},{2,10},{3,11},{4,12},{5,13},{6,14},{7,15},{8,0},{9,1},... | collective-permute-start | bytes 393224 | tf_op jit(solution)/shard_map/ppermute | solution.py:105
  62.1 9.3 %collective-permute-start.17 = (bf16[512,128]{1,0:T(8,128)(2,1)S(1)}, bf16[512,128]{1,0:T(8,128)(2,1)S(1)}, u32[]{:S(2)}, u32[]{:S(2)}) collective-permute-start(bf16[512,128]{1,0:T(8,128)(2,1)S(1)} %get-tuple-element.29.refs_0_), channel_id=1, source_target_pairs={{0,16},{1,17},{2,18},{3,19},{4,20},{5,21},{6,22},{7,23},{8,24},{9,... | collective-permute-start | bytes 393224 | tf_op jit(solution)/shard_map/ppermute | solution.py:105
  64.4 9.2 %collective-permute-start.16 = (bf16[512,128]{1,0:T(8,128)(2,1)S(1)}, bf16[512,128]{1,0:T(8,128)(2,1)S(1)}, u32[]{:S(2)}, u32[]{:S(2)}) collective-permute-start(bf16[512,128]{1,0:T(8,128)(2,1)S(1)} %get-tuple-element.29.refs_0_), channel_id=1, source_target_pairs={{0,8},{1,9},{2,10},{3,11},{4,12},{5,13},{6,14},{7,15},{8,0},{9,1},... | collective-permute-start | bytes 393224 | tf_op jit(solution)/shard_map/ppermute | solution.py:105
  69.2 8.3 %collective-permute-start.31 = (bf16[512,128]{1,0:T(8,128)(2,1)S(1)}, bf16[512,128]{1,0:T(8,128)(2,1)S(1)}, u32[]{:S(2)}, u32[]{:S(2)}) collective-permute-start(bf16[512,128]{1,0:T(8,128)(2,1)S(1)} %add_convert_fusion.1), channel_id=1, source_target_pairs={{0,16},{1,17},{2,18},{3,19},{4,20},{5,21},{6,22},{7,23},{8,24},{9,... | collective-permute-start | bytes 393224 | tf_op jit(solution)/shard_map/ppermute | solution.py:105
  70.1 9.0 %collective-permute-start.19 = (bf16[512,128]{1,0:T(8,128)(2,1)S(1)}, bf16[512,128]{1,0:T(8,128)(2,1)S(1)}, u32[]{:S(2)}, u32[]{:S(2)}) collective-permute-start(bf16[512,128]{1,0:T(8,128)(2,1)S(1)} %get-tuple-element.29.refs_0_), channel_id=1, source_target_pairs={{0,1},{1,0},{2,3},{3,2},{4,5},{5,4},{6,7},{7,6},{8,9},{9,8},{10,11... | collective-permute-start | bytes 393224 | tf_op jit(solution)/shard_map/ppermute | solution.py:105
  71.4 9.0 %collective-permute-start.21 = (bf16[512,128]{1,0:T(8,128)(2,1)S(1)}, bf16[512,128]{1,0:T(8,128)(2,1)S(1)}, u32[]{:S(2)}, u32[]{:S(2)}) collective-permute-start(bf16[512,128]{1,0:T(8,128)(2,1)S(1)} %collective-permute-done.17.refs_2_), channel_id=1, source_target_pairs={{0,1},{1,0},{2,3},{3,2},{4,5},{5,4},{6,7},{7,6},{8,9},{9,8},{10,11... | collective-permute-start | bytes 393224 | tf_op jit(solution)/shard_map/ppermute | solution.py:105
  71.4 9.7 %collective-permute-start.18 = (bf16[512,128]{1,0:T(8,128)(2,1)S(1)}, bf16[512,128]{1,0:T(8,128)(2,1)S(1)}, u32[]{:S(2)}, u32[]{:S(2)}) collective-permute-start(bf16[512,128]{1,0:T(8,128)(2,1)S(1)} %collective-permute-done.17.refs_2_), channel_id=1, source_target_pairs={{0,8},{1,9},{2,10},{3,11},{4,12},{5,13},{6,14},{7,15},{8,0},{9,1},... | collective-permute-start | bytes 393224 | tf_op jit(solution)/shard_map/ppermute | solution.py:105
  73.6 7.5 %collective-permute-start.20 = (bf16[512,128]{1,0:T(8,128)(2,1)S(1)}, bf16[512,128]{1,0:T(8,128)(2,1)S(1)}, u32[]{:S(2)}, u32[]{:S(2)}) collective-permute-start(bf16[512,128]{1,0:T(8,128)(2,1)S(1)} %collective-permute-done.16.refs_1_), channel_id=1, source_target_pairs={{0,1},{1,0},{2,3},{3,2},{4,5},{5,4},{6,7},{7,6},{8,9},{9,8},{10,11... | collective-permute-start | bytes 393224 | tf_op jit(solution)/shard_map/ppermute | solution.py:105
  77.6 6.0 %collective-permute-start.34 = (bf16[512,128]{1,0:T(8,128)(2,1)S(1)}, bf16[512,128]{1,0:T(8,128)(2,1)S(1)}, u32[]{:S(2)}, u32[]{:S(2)}) collective-permute-start(bf16[512,128]{1,0:T(8,128)(2,1)S(1)} %add_convert_fusion.refs_0_), channel_id=1, source_target_pairs={{0,6},{1,7},{2,4},{3,5},{4,2},{5,3},{6,0},{7,1},{8,14},{9,15},{10,... | collective-permute-start | bytes 393224 | tf_op jit(solution)/shard_map/ppermute | solution.py:105
  79.1 5.8 %collective-permute-start.33 = (bf16[512,128]{1,0:T(8,128)(2,1)S(1)}, bf16[512,128]{1,0:T(8,128)(2,1)S(1)}, u32[]{:S(2)}, u32[]{:S(2)}) collective-permute-start(bf16[512,128]{1,0:T(8,128)(2,1)S(1)} %add_convert_fusion.refs_0_), channel_id=1, source_target_pairs={{0,4},{1,5},{2,6},{3,7},{4,0},{5,1},{6,2},{7,3},{8,12},{9,13},{10,... | collective-permute-start | bytes 393224 | tf_op jit(solution)/shard_map/ppermute | solution.py:105
  80.5 5.0 %collective-permute-start.32 = (bf16[512,128]{1,0:T(8,128)(2,1)S(1)}, bf16[512,128]{1,0:T(8,128)(2,1)S(1)}, u32[]{:S(2)}, u32[]{:S(2)}) collective-permute-start(bf16[512,128]{1,0:T(8,128)(2,1)S(1)} %add_convert_fusion.refs_0_), channel_id=1, source_target_pairs={{0,2},{1,3},{2,0},{3,1},{4,6},{5,7},{6,4},{7,5},{8,10},{9,11},{10,... | collective-permute-start | bytes 393224 | tf_op jit(solution)/shard_map/ppermute | solution.py:105
  81.1 4.3 %collective-permute-start.22 = (bf16[512,128]{1,0:T(8,128)(2,1)S(1)}, bf16[512,128]{1,0:T(8,128)(2,1)S(1)}, u32[]{:S(2)}, u32[]{:S(2)}) collective-permute-start(bf16[512,128]{1,0:T(8,128)(2,1)S(1)} %collective-permute-done.18.refs_3_), channel_id=1, source_target_pairs={{0,1},{1,0},{2,3},{3,2},{4,5},{5,4},{6,7},{7,6},{8,9},{9,8},{10,11... | collective-permute-start | bytes 393224 | tf_op jit(solution)/shard_map/ppermute | solution.py:105
  81.1 20.8 %collective-permute-start.35 = (bf16[512,128]{1,0:T(8,128)(2,1)S(1)}, bf16[512,128]{1,0:T(8,128)(2,1)S(1)}, u32[]{:S(2)}, u32[]{:S(2)}) collective-permute-start(bf16[512,128]{1,0:T(8,128)(2,1)S(1)} %add_convert_fusion.refs_0_), channel_id=1, source_target_pairs={{0,1},{1,0},{2,3},{3,2},{4,5},{5,4},{6,7},{7,6},{8,9},{9,8},{10,11... | collective-permute-start | bytes 393224 | tf_op jit(solution)/shard_map/ppermute | solution.py:105
  83.6 18.4 %collective-permute-start.38 = (bf16[512,128]{1,0:T(8,128)(2,1)S(1)}, bf16[512,128]{1,0:T(8,128)(2,1)S(1)}, u32[]{:S(2)}, u32[]{:S(2)}) collective-permute-start(bf16[512,128]{1,0:T(8,128)(2,1)S(1)} %collective-permute-done.34.refs_3_), channel_id=1, source_target_pairs={{0,1},{1,0},{2,3},{3,2},{4,5},{5,4},{6,7},{7,6},{8,9},{9,8},{10,11... | collective-permute-start | bytes 393224 | tf_op jit(solution)/shard_map/ppermute | solution.py:105
  84.9 17.0 %collective-permute-start.37 = (bf16[512,128]{1,0:T(8,128)(2,1)S(1)}, bf16[512,128]{1,0:T(8,128)(2,1)S(1)}, u32[]{:S(2)}, u32[]{:S(2)}) collective-permute-start(bf16[512,128]{1,0:T(8,128)(2,1)S(1)} %collective-permute-done.33.refs_2_), channel_id=1, source_target_pairs={{0,1},{1,0},{2,3},{3,2},{4,5},{5,4},{6,7},{7,6},{8,9},{9,8},{10,11... | collective-permute-start | bytes 393224 | tf_op jit(solution)/shard_map/ppermute | solution.py:105
  85.4 16.5 %collective-permute-start.36 = (bf16[512,128]{1,0:T(8,128)(2,1)S(1)}, bf16[512,128]{1,0:T(8,128)(2,1)S(1)}, u32[]{:S(2)}, u32[]{:S(2)}) collective-permute-start(bf16[512,128]{1,0:T(8,128)(2,1)S(1)} %collective-permute-done.32.refs_1_), channel_id=1, source_target_pairs={{0,1},{1,0},{2,3},{3,2},{4,5},{5,4},{6,7},{7,6},{8,9},{9,8},{10,11... | collective-permute-start | bytes 393224 | tf_op jit(solution)/shard_map/ppermute | solution.py:105
  88.3 4.0 %collective-permute-start.23 = (bf16[128,128]{1,0:T(8,128)(2,1)S(1)}, bf16[128,128]{1,0:T(8,128)(2,1)S(1)}, u32[]{:S(2)}, u32[]{:S(2)}) collective-permute-start(bf16[128,128]{1,0:T(8,128)(2,1)S(1)} %get-tuple-element.31), channel_id=1, source_target_pairs={{0,2},{1,3},{2,0},{3,1},{4,6},{5,7},{6,4},{7,5},{8,10},{9,11},{10,... | collective-permute-start | bytes 98312 | tf_op jit(solution)/shard_map/ppermute | solution.py:105
  92.2 3.9 %collective-permute-start.24 = (bf16[128,128]{1,0:T(8,128)(2,1)S(1)}, bf16[128,128]{1,0:T(8,128)(2,1)S(1)}, u32[]{:S(2)}, u32[]{:S(2)}) collective-permute-start(bf16[128,128]{1,0:T(8,128)(2,1)S(1)} %get-tuple-element.32), channel_id=1, source_target_pairs={{0,4},{1,5},{2,6},{3,7},{4,0},{5,1},{6,2},{7,3},{8,12},{9,13},{10,... | collective-permute-start | bytes 98312 | tf_op jit(solution)/shard_map/ppermute | solution.py:105
  96.2 4.8 %collective-permute-start.25 = (bf16[128,128]{1,0:T(8,128)(2,1)S(1)}, bf16[128,128]{1,0:T(8,128)(2,1)S(1)}, u32[]{:S(2)}, u32[]{:S(2)}) collective-permute-start(bf16[128,128]{1,0:T(8,128)(2,1)S(1)} %get-tuple-element.33), channel_id=1, source_target_pairs={{0,6},{1,7},{2,4},{3,5},{4,2},{5,3},{6,0},{7,1},{8,14},{9,15},{10,... | collective-permute-start | bytes 98312 | tf_op jit(solution)/shard_map/ppermute | solution.py:105
  (1 other events, 0.7 us)

commit v5 on v4

--- a/solution.py
+++ b/solution.py
@@ -82,7 +82,7 @@
 SPAN = QUAD * ROWS
 VMEM = pl.BlockSpec(memory_space=pltpu.VMEM)
 SMEM = pl.BlockSpec(memory_space=pltpu.SMEM)
-ANY = pl.BlockSpec(memory_space=pl.ANY)
+HBM = pl.BlockSpec(memory_space=pltpu.HBM)
 PARAMS = pltpu.CompilerParams(vmem_limit_bytes=48 * 1024 * 1024)
 
 
@@ -160,7 +160,7 @@
         (shaped(ROWS + 16, 2 * LANES),) * QUAD
         + (jax.ShapeDtypeStruct((4, BLOCK, SLOTS * BLOCK), BF16),),
         (pos, columns, counts, back_columns, back_counts, features, cotangent, tiles, back_tiles),
-        [SMEM] + [ANY] * 8,
+        [SMEM] + [HBM] * 8,
         [pltpu.SMEM((2, SLOTS), jnp.int32), pltpu.SMEM((2,), jnp.int32)] * 2
         + [pltpu.SemaphoreType.DMA((14,))],
     )
@@ -186,22 +186,10 @@
     )
 
 
-def mix_body(base, half, split, places, *refs):
-    shares, tiles, outs = refs[:8], refs[8:12], refs[12:-3]
-    table, picked, sems = refs[-3:]
-    copies = []
+def mix_rows(base, half, places, shares, tiles, table, picked, store):
     for i, share in enumerate(shares):
-        copies.append(
-            pltpu.make_async_copy(
-                share.at[:, pl.ds(half * LANES, LANES)],
-                table.at[pl.ds(i * SPAN, SPAN), :],
-                sems.at[i],
-            )
-        )
-        copies[-1].start()
+        table[pl.ds(i * SPAN, SPAN), :] = share[:, pl.ds(half * LANES, LANES)]
     table[DEVICES * ROWS :, :] = jnp.zeros((BLOCK, LANES), BF16)
-    for copy in copies:
-        copy.wait()
     for q in range(QUAD):
         for w in range(2):
             row = q * 2 + w
@@ -210,23 +198,54 @@
                 picked[row, pl.ds(s * BLOCK, BLOCK), :] = table[pl.ds(first, BLOCK), :]
             total = jnp.dot(tiles[q][base + w], picked[row], preferred_element_type=F32)
             total = total + table[pl.ds(row * BLOCK, BLOCK), :].astype(F32)
-            if split:
-                outs[q][pl.ds(w * BLOCK, BLOCK), :] = total.astype(BF16)
-            else:
-                outs[0][pl.ds(row * BLOCK, BLOCK), :] = total.astype(BF16)
-
-
-def mix(places, base, half, shares, tiles, split=False):
-    return call(
-        functools.partial(mix_body, base, half, split),
-        (shaped(ROWS, LANES),) * QUAD if split else (shaped(SPAN, LANES),),
+            store(q, w, total.astype(BF16))
+
+
+MIX_SCRATCH = (
+    pltpu.VMEM((DEVICES * ROWS + BLOCK, LANES), BF16),
+    pltpu.VMEM((2 * QUAD, SLOTS * BLOCK, LANES), BF16),
+)
+
+
+def mix_body(base, half, places, *refs):
+    shares, tiles, (out, table, picked) = refs[:8], refs[8:12], refs[12:]
+
+    def store(q, w, rows):
+        out[pl.ds(q * ROWS + w * BLOCK, BLOCK), :] = rows
+
+    mix_rows(base, half, places, shares, tiles, table, picked, store)
+
+
+def mix(places, base, half, shares, tiles):
+    return call(
+        functools.partial(mix_body, base, half),
+        shaped(SPAN, LANES),
         (places, *shares, *tiles),
-        [SMEM] + [ANY] * 8 + [VMEM] * 4,
-        [
-            pltpu.VMEM((DEVICES * ROWS + BLOCK, LANES), BF16),
-            pltpu.VMEM((2 * QUAD, SLOTS * BLOCK, LANES), BF16),
-            pltpu.SemaphoreType.DMA((8,)),
-        ],
+        [SMEM] + [VMEM] * 12,
+        MIX_SCRATCH,
+    )
+
+
+def mix_beside_body(places, *refs):
+    shares, tiles, total = refs[:8], refs[8:12], refs[12]
+    outs, (table, picked) = refs[13:17], refs[17:]
+    extent = total.shape[0]
+    for out in outs:
+        out[:extent, :] = total[...]
+
+    def store(q, w, rows):
+        outs[q][pl.ds(extent + w * BLOCK, BLOCK), :] = rows
+
+    mix_rows(0, 0, places, shares, tiles, table, picked, store)
+
+
+def mix_beside(places, shares, tiles, total):
+    return call(
+        mix_beside_body,
+        (shaped(total.shape[0] + ROWS, LANES),) * QUAD,
+        (places, *shares, *tiles, total),
+        [SMEM] + [VMEM] * 13,
+        MIX_SCRATCH,
     )
 
 
@@ -268,7 +287,9 @@
     total = jnp.zeros(z_out.shape, F32)
     for p, piece in enumerate((p0, p1, p2, p3)):
         total = total + jnp.dot(
-            piece[...], w_second[lanes_of(chip(pos) ^ p), :], preferred_element_type=F32
+            piece[piece.shape[0] - ROWS :, :],
+            w_second[lanes_of(chip(pos) ^ p), :],
+            preferred_element_type=F32,
         )
     z_out[...] = total.astype(BF16)
 
@@ -320,13 +341,14 @@
 
 def place_body(pos, *refs):
     mine, other, (first, second) = refs[:QUAD], refs[QUAD : 2 * QUAD], refs[2 * QUAD :]
+    extent = first.shape[0]
     keeps_first = (pos[0] & 1) == 0
 
     def fill(mine_out, other_out):
         for p in range(QUAD):
             share = lanes_of(chip(pos) ^ p)
-            mine_out[:, share] = mine[p][...].astype(F32)
-            other_out[:, share] = other[p][...].astype(F32)
+            mine_out[:, share] = mine[p][:extent, :].astype(F32)
+            other_out[:, share] = other[p][:extent, :].astype(F32)
 
     @pl.when(keeps_first)
     def _():
@@ -338,7 +360,7 @@
 
 
 def place(pos, mine, other):
-    channels = mine[0].shape[0]
+    channels = QUAD * LANES
     return call(
         place_body,
         (shaped(channels, channels, F32),) * 2,
@@ -380,18 +402,16 @@
         return planes + [swap(plane, CORE) for plane in planes]
 
     shares = everywhere(share)
-    (mixed_share,) = mix(places, 0, 0, shares, tiles)
-    (spread_share,) = mix(places, 2, 1, shares, tiles)
+    mixed_share = mix(places, 0, 0, shares, tiles)
+    spread_share = mix(places, 2, 1, shares, tiles)
     mixed, hidden, hidden_share, slope = first_layer(pos, over_quad(mixed_share), w_first)
-    again = mix(places, 0, 0, everywhere(hidden_share), tiles, split=True)
-    z_out = second_layer(
-        pos, [again[0]] + [swap(again[q], 2 * q) for q in range(1, QUAD)], w_second
-    )
     keep, send = gradients(pos, mixed, hidden, slope, over_quad(spread_share), w_second)
     total = (keep + swap(send, CORE)).astype(BF16)
     for mask in (8, 16):
         total = (total.astype(F32) + swap(total, mask).astype(F32)).astype(BF16)
-    mine = over_quad(total)
+    beside = mix_beside(places, everywhere(hidden_share), tiles, total)
+    mine = [beside[0]] + [swap(beside[q], 2 * q) for q in range(1, QUAD)]
+    z_out = second_layer(pos, mine, w_second)
     grad_first, grad_second = place(pos, mine, [swap(piece, CORE) for piece in mine])
     return (z_out, grad_first, grad_second)
 

time: 104 us -> 94 us (0.904)
  waiting for transfers between devices: 51 us -> 46.3 us
  starting transfers between devices: 36.2 us -> 32.6 us
  Pallas kernels: 11 us -> 9.56 us
    ppermute x39 -> x36, waiting for transfers between devices: 51 us -> 46.3 us  [swap(): return lax.ppermute(value, AXES, [(i, i ^ mask) for i in range(DEVICES)])]
    ppermute x39 -> x36, starting transfers between devices: 36.2 us -> 32.6 us  [swap(): return lax.ppermute(value, AXES, [(i, i ^ mask) for i in range(DEVICES)])]
    pallas_call x9, Pallas kernels: 11 us -> 9.56 us  [call(): pl.pallas_call(body, out_shape=out_shape, in_specs=list(spaces), out_spec...]
  transfers between devices with their start and end apart: 39 -> 36, of which waited for: 21 -> 18; matrix products, arithmetic and copies ran while one was open for 0% -> 0% of each run, Pallas kernels for 6% -> 4%
where the time goes in v5:
time: 94 us; the launch traced here: 93.8 us
  waiting for transfers between devices  46.3 us (49%)
  starting transfers between devices  32.6 us (35%)
  Pallas kernels  9.56 us (10%)
  local copies, waits for them, and re-layouts  4.4 us (5%)
    ppermute x36, waiting for transfers between devices, swap(): return lax.ppermute(value, AXES, [(i, i ^ mask) for i in range(DEVICES)])  46.3 us
    ppermute x36, starting transfers between devices, swap(): return lax.ppermute(value, AXES, [(i, i ^ mask) for i in range(DEVICES)])  32.6 us
    pallas_call x9, Pallas kernels, call(): pl.pallas_call(body, out_shape=out_shape, in_specs=list(spaces), out_spec...  9.56 us
    unnamed x20, local copies, waits for them, and re-layouts  4.4 us
  transfers between devices with their start and end apart: 36, of which 18 were waited for; matrix products, arithmetic and copies ran while one was open for 0% of the time, Pallas kernels for 4%

profile of v5, /device:TPU:0, one launch (start us, length us, event | category | flops | bytes accessed | tf_op | source)
XLA Modules:
  0.0 93.8 jit_solution(18031099448637171584)
XLA Ops:
  0.7 0.6 copy-done.7
  1.4 0.9 %copy-done.2 = bf16[2,64,1024]{2,1,0:T(8,128)(2,1)S(1)} copy-done((bf16[2,64,1024]{2,1,0:T(8,128)(2,1)S(1)}, bf16[2,64,1024]{2,1,0:T(8,128)(2,1)}, u32[]{:S(2)}) %copy-start.2) | copy-done | bytes 262168
  2.3 0.9 %copy-done.3 = bf16[2,64,1024]{2,1,0:T(8,128)(2,1)S(1)} copy-done((bf16[2,64,1024]{2,1,0:T(8,128)(2,1)S(1)}, bf16[2,64,1024]{2,1,0:T(8,128)(2,1)}, u32[]{:S(2)}) %copy-start.3) | copy-done | bytes 262168
  3.3 0.9 copy-done.4
  4.2 0.9 copy-done.5
  5.1 0.8 shard_map.121
  5.9 3.0 %collective-permute-start = (bf16[144,256]{1,0:T(8,128)(2,1)S(1)}, bf16[144,256]{1,0:T(8,128)(2,1)S(1)}, u32[]{:S(2)}, u32[]{:S(2)}) collective-permute-start(bf16[144,256]{1,0:T(8,128)(2,1)S(1)} %get-tuple-element.23), channel_id=1, source_target_pairs={{0,2},{1,3},{2,0},{3,1},{4,6},{5,7},{6,4},{7,5},{8,10},{9,11},{10,... | collective-permute-start | bytes 221192 | tf_op jit(solution)/shard_map/ppermute | solution.py:105
  8.9 1.5 %collective-permute-start.1 = (bf16[144,256]{1,0:T(8,128)(2,1)S(1)}, bf16[144,256]{1,0:T(8,128)(2,1)S(1)}, u32[]{:S(2)}, u32[]{:S(2)}) collective-permute-start(bf16[144,256]{1,0:T(8,128)(2,1)S(1)} %get-tuple-element.24), channel_id=1, source_target_pairs={{0,4},{1,5},{2,6},{3,7},{4,0},{5,1},{6,2},{7,3},{8,12},{9,13},{10,... | collective-permute-start | bytes 221192 | tf_op jit(solution)/shard_map/ppermute | solution.py:105
  10.4 1.0 %collective-permute-done.refs_1_ = bf16[144,256]{1,0:T(8,128)(2,1)S(1)} collective-permute-done((bf16[144,256]{1,0:T(8,128)(2,1)S(1)}, bf16[144,256]{1,0:T(8,128)(2,1)S(1)}, u32[]{:S(2)}, u32[]{:S(2)}) %collective-permute-start) | collective-permute-done | bytes 73760 | tf_op jit(solution)/shard_map/ppermute | solution.py:105
  11.4 1.8 %collective-permute-done.1.refs_2_ = bf16[144,256]{1,0:T(8,128)(2,1)S(1)} collective-permute-done((bf16[144,256]{1,0:T(8,128)(2,1)S(1)}, bf16[144,256]{1,0:T(8,128)(2,1)S(1)}, u32[]{:S(2)}, u32[]{:S(2)}) %collective-permute-start.1) | collective-permute-done | bytes 73760 | tf_op jit(solution)/shard_map/ppermute | solution.py:105
  13.2 2.4 %collective-permute-done.2.refs_3_ = bf16[144,256]{1,0:T(8,128)(2,1)S(1)} collective-permute-done((bf16[144,256]{1,0:T(8,128)(2,1)S(1)}, bf16[144,256]{1,0:T(8,128)(2,1)S(1)}, u32[]{:S(2)}, u32[]{:S(2)}) %collective-permute-start.2) | collective-permute-done | bytes 73760 | tf_op jit(solution)/shard_map/ppermute | solution.py:105
  16.2 2.7 %collective-permute-start.4 = (bf16[512,256]{1,0:T(8,128)(2,1)S(1)}, bf16[512,256]{1,0:T(8,128)(2,1)S(1)}, u32[]{:S(2)}, u32[]{:S(2)}) collective-permute-start(bf16[512,256]{1,0:T(8,128)(2,1)S(1)} %get-tuple-element.27.refs_0_), channel_id=1, source_target_pairs={{0,16},{1,17},{2,18},{3,19},{4,20},{5,21},{6,22},{7,23},{8,24},{9,... | collective-permute-start | bytes 786440 | tf_op jit(solution)/shard_map/ppermute | solution.py:105
  18.9 1.5 %collective-permute-start.11 = (bf16[4,64,1024]{2,1,0:T(8,128)(2,1)S(1)}, bf16[4,64,1024]{2,1,0:T(8,128)(2,1)S(1)}, u32[]{:S(2)}, u32[]{:S(2)}) collective-permute-start(bf16[4,64,1024]{2,1,0:T(8,128)(2,1)S(1)} %get-tuple-element.28.refs_8_), channel_id=1, source_target_pairs={{0,4},{1,5},{2,6},{3,7},{4,0},{5,1},{6,2},{7,3},{8,12},{9,13},{10,... | collective-permute-start | bytes 1572872 | tf_op jit(solution)/shard_map/ppermute | solution.py:105
  20.4 1.6 %collective-permute-start.3 = (bf16[512,256]{1,0:T(8,128)(2,1)S(1)}, bf16[512,256]{1,0:T(8,128)(2,1)S(1)}, u32[]{:S(2)}, u32[]{:S(2)}) collective-permute-start(bf16[512,256]{1,0:T(8,128)(2,1)S(1)} %get-tuple-element.27.refs_0_), channel_id=1, source_target_pairs={{0,8},{1,9},{2,10},{3,11},{4,12},{5,13},{6,14},{7,15},{8,0},{9,1},... | collective-permute-start | bytes 786440 | tf_op jit(solution)/shard_map/ppermute | solution.py:105
  22.0 1.5 %collective-permute-start.10 = (bf16[4,64,1024]{2,1,0:T(8,128)(2,1)S(1)}, bf16[4,64,1024]{2,1,0:T(8,128)(2,1)S(1)}, u32[]{:S(2)}, u32[]{:S(2)}) collective-permute-start(bf16[4,64,1024]{2,1,0:T(8,128)(2,1)S(1)} %get-tuple-element.28.refs_8_), channel_id=1, source_target_pairs={{0,2},{1,3},{2,0},{3,1},{4,6},{5,7},{6,4},{7,5},{8,10},{9,11},{10,... | collective-permute-start | bytes 1572872 | tf_op jit(solution)/shard_map/ppermute | solution.py:105
  23.5 7.8 %collective-permute-done.4.refs_2_ = bf16[512,256]{1,0:T(8,128)(2,1)S(1)} collective-permute-done((bf16[512,256]{1,0:T(8,128)(2,1)S(1)}, bf16[512,256]{1,0:T(8,128)(2,1)S(1)}, u32[]{:S(2)}, u32[]{:S(2)}) %collective-permute-start.4) | collective-permute-done | bytes 262176 | tf_op jit(solution)/shard_map/ppermute | solution.py:105
  31.3 0.7 collective-permute-start.5
  32.0 0.7 collective-permute-done.3.refs_1_
  33.2 5.6 %collective-permute-done.5.refs_3_ = bf16[512,256]{1,0:T(8,128)(2,1)S(1)} collective-permute-done((bf16[512,256]{1,0:T(8,128)(2,1)S(1)}, bf16[512,256]{1,0:T(8,128)(2,1)S(1)}, u32[]{:S(2)}, u32[]{:S(2)}) %collective-permute-start.5) | collective-permute-done | bytes 262176 | tf_op jit(solution)/shard_map/ppermute | solution.py:105
  38.8 3.4 %collective-permute-done.11.refs_10_ = bf16[4,64,1024]{2,1,0:T(8,128)(2,1)S(1)} collective-permute-done((bf16[4,64,1024]{2,1,0:T(8,128)(2,1)S(1)}, bf16[4,64,1024]{2,1,0:T(8,128)(2,1)S(1)}, u32[]{:S(2)}, u32[]{:S(2)}) %collective-permute-start.11) | collective-permute-done | bytes 524320 | tf_op jit(solution)/shard_map/ppermute | solution.py:105
  42.2 1.6 %shard_map.123.p0 = bf16[512,128]{1,0:T(8,128)(2,1)S(1)} custom-call(s32[32,128]{1,0:T(8,128)S(1)} %get-tuple-element.26.places, bf16[512,256]{1,0:T(8,128)(2,1)S(1)} %get-tuple-element.27.refs_0_, bf16[512,256]{1,0:T(8,128)(2,1)S(1)} %collective-permute-done.3.refs_1_, bf16[512,256]{1,0:T(8,128)(2,1)S(1)} %collective-permute-done.4.refs_2_, ...), custom_call_target="tpu_custom_call" | custom-call | tf_op jit(solution)/shard_map/pallas_call | solution.py:90
  43.9 0.6 collective-permute-start.15
  44.5 1.4 %collective-permute-start.14 = (bf16[512,128]{1,0:T(8,128)(2,1)S(1)}, bf16[512,128]{1,0:T(8,128)(2,1)S(1)}, u32[]{:S(2)}, u32[]{:S(2)}) collective-permute-start(bf16[512,128]{1,0:T(8,128)(2,1)S(1)} %shard_map.123.p0), channel_id=1, source_target_pairs={{0,4},{1,5},{2,6},{3,7},{4,0},{5,1},{6,2},{7,3},{8,12},{9,13},{10,... | collective-permute-start | bytes 393224 | tf_op jit(solution)/shard_map/ppermute | solution.py:105
  45.9 1.5 %collective-permute-start.13 = (bf16[512,128]{1,0:T(8,128)(2,1)S(1)}, bf16[512,128]{1,0:T(8,128)(2,1)S(1)}, u32[]{:S(2)}, u32[]{:S(2)}) collective-permute-start(bf16[512,128]{1,0:T(8,128)(2,1)S(1)} %shard_map.123.p0), channel_id=1, source_target_pairs={{0,2},{1,3},{2,0},{3,1},{4,6},{5,7},{6,4},{7,5},{8,10},{9,11},{10,... | collective-permute-start | bytes 393224 | tf_op jit(solution)/shard_map/ppermute | solution.py:105
  47.4 1.6 %shard_map.125.p0 = bf16[512,128]{1,0:T(8,128)(2,1)S(1)} custom-call(s32[32,128]{1,0:T(8,128)S(1)} %get-tuple-element.26.places, bf16[512,256]{1,0:T(8,128)(2,1)S(1)} %get-tuple-element.27.refs_0_, bf16[512,256]{1,0:T(8,128)(2,1)S(1)} %collective-permute-done.3.refs_1_, bf16[512,256]{1,0:T(8,128)(2,1)S(1)} %collective-permute-done.4.refs_2_, ...), custom_call_target="tpu_custom_call" | custom-call | tf_op jit(solution)/shard_map/pallas_call | solution.py:90
  49.0 0.6 collective-permute-start.25
  49.6 1.4 %collective-permute-start.24 = (bf16[512,128]{1,0:T(8,128)(2,1)S(1)}, bf16[512,128]{1,0:T(8,128)(2,1)S(1)}, u32[]{:S(2)}, u32[]{:S(2)}) collective-permute-start(bf16[512,128]{1,0:T(8,128)(2,1)S(1)} %shard_map.125.p0), channel_id=1, source_target_pairs={{0,4},{1,5},{2,6},{3,7},{4,0},{5,1},{6,2},{7,3},{8,12},{9,13},{10,... | collective-permute-start | bytes 393224 | tf_op jit(solution)/shard_map/ppermute | solution.py:105
  51.2 1.3 %collective-permute-start.23 = (bf16[512,128]{1,0:T(8,128)(2,1)S(1)}, bf16[512,128]{1,0:T(8,128)(2,1)S(1)}, u32[]{:S(2)}, u32[]{:S(2)}) collective-permute-start(bf16[512,128]{1,0:T(8,128)(2,1)S(1)} %shard_map.125.p0), channel_id=1, source_target_pairs={{0,2},{1,3},{2,0},{3,1},{4,6},{5,7},{6,4},{7,5},{8,10},{9,11},{10,... | collective-permute-start | bytes 393224 | tf_op jit(solution)/shard_map/ppermute | solution.py:105
  52.6 1.6 %collective-permute-done.14.p2 = bf16[512,128]{1,0:T(8,128)(2,1)S(1)} collective-permute-done((bf16[512,128]{1,0:T(8,128)(2,1)S(1)}, bf16[512,128]{1,0:T(8,128)(2,1)S(1)}, u32[]{:S(2)}, u32[]{:S(2)}) %collective-permute-start.14) | collective-permute-done | bytes 131104 | tf_op jit(solution)/shard_map/ppermute | solution.py:105
  54.1 0.8 shard_map.124
  54.9 2.0 %collective-permute-done.25.p3 = bf16[512,128]{1,0:T(8,128)(2,1)S(1)} collective-permute-done((bf16[512,128]{1,0:T(8,128)(2,1)S(1)}, bf16[512,128]{1,0:T(8,128)(2,1)S(1)}, u32[]{:S(2)}, u32[]{:S(2)}) %collective-permute-start.25) | collective-permute-done | bytes 131104 | tf_op jit(solution)/shard_map/ppermute | solution.py:105
  56.8 1.3 %collective-permute-done.24.p2 = bf16[512,128]{1,0:T(8,128)(2,1)S(1)} collective-permute-done((bf16[512,128]{1,0:T(8,128)(2,1)S(1)}, bf16[512,128]{1,0:T(8,128)(2,1)S(1)}, u32[]{:S(2)}, u32[]{:S(2)}) %collective-permute-start.24) | collective-permute-done | bytes 131104 | tf_op jit(solution)/shard_map/ppermute | solution.py:105
  58.1 0.7 shard_map.126
  58.9 2.2 %collective-permute-start.17 = (bf16[512,128]{1,0:T(8,128)(2,1)S(1)}, bf16[512,128]{1,0:T(8,128)(2,1)S(1)}, u32[]{:S(2)}, u32[]{:S(2)}) collective-permute-start(bf16[512,128]{1,0:T(8,128)(2,1)S(1)} %get-tuple-element.29.refs_0_), channel_id=1, source_target_pairs={{0,16},{1,17},{2,18},{3,19},{4,20},{5,21},{6,22},{7,23},{8,24},{9,... | collective-permute-start | bytes 393224 | tf_op jit(solution)/shard_map/ppermute | solution.py:105
  61.2 1.6 %collective-permute-start.27 = (bf16[512,128]{1,0:T(8,128)(2,1)S(1)}, bf16[512,128]{1,0:T(8,128)(2,1)S(1)}, u32[]{:S(2)}, u32[]{:S(2)}) collective-permute-start(bf16[512,128]{1,0:T(8,128)(2,1)S(1)} %add_convert_fusion.2), channel_id=1, source_target_pairs={{0,8},{1,9},{2,10},{3,11},{4,12},{5,13},{6,14},{7,15},{8,0},{9,1},... | collective-permute-start | bytes 393224 | tf_op jit(solution)/shard_map/ppermute | solution.py:105
  63.3 5.4 %collective-permute-done.17.refs_2_ = bf16[512,128]{1,0:T(8,128)(2,1)S(1)} collective-permute-done((bf16[512,128]{1,0:T(8,128)(2,1)S(1)}, bf16[512,128]{1,0:T(8,128)(2,1)S(1)}, u32[]{:S(2)}, u32[]{:S(2)}) %collective-permute-start.17) | collective-permute-done | bytes 131104 | tf_op jit(solution)/shard_map/ppermute | solution.py:105
  68.9 0.5 collective-permute-done.27
  69.5 2.9 %collective-permute-start.28 = (bf16[512,128]{1,0:T(8,128)(2,1)S(1)}, bf16[512,128]{1,0:T(8,128)(2,1)S(1)}, u32[]{:S(2)}, u32[]{:S(2)}) collective-permute-start(bf16[512,128]{1,0:T(8,128)(2,1)S(1)} %add_convert_fusion.1), channel_id=1, source_target_pairs={{0,16},{1,17},{2,18},{3,19},{4,20},{5,21},{6,22},{7,23},{8,24},{9,... | collective-permute-start | bytes 393224 | tf_op jit(solution)/shard_map/ppermute | solution.py:105
  72.9 3.8 %collective-permute-done.18.refs_3_ = bf16[512,128]{1,0:T(8,128)(2,1)S(1)} collective-permute-done((bf16[512,128]{1,0:T(8,128)(2,1)S(1)}, bf16[512,128]{1,0:T(8,128)(2,1)S(1)}, u32[]{:S(2)}, u32[]{:S(2)}) %collective-permute-start.18) | collective-permute-done | bytes 131104 | tf_op jit(solution)/shard_map/ppermute | solution.py:105
  76.7 1.9 %collective-permute-done.28 = bf16[512,128]{1,0:T(8,128)(2,1)S(1)} collective-permute-done((bf16[512,128]{1,0:T(8,128)(2,1)S(1)}, bf16[512,128]{1,0:T(8,128)(2,1)S(1)}, u32[]{:S(2)}, u32[]{:S(2)}) %collective-permute-start.28) | collective-permute-done | bytes 131104 | tf_op jit(solution)/shard_map/ppermute | solution.py:105
  78.7 1.6 %shard_map.127 = (bf16[640,128]{1,0:T(8,128)(2,1)S(1)}, bf16[640,128]{1,0:T(8,128)(2,1)S(1)}, bf16[640,128]{1,0:T(8,128)(2,1)S(1)}, bf16[640,128]{1,0:T(8,128)(2,1)S(1)}) custom-call(s32[32,128]{1,0:T(8,128)S(1)} %get-tuple-element.26.places, bf16[512,128]{1,0:T(8,128)(2,1)S(1)} %get-tuple-element.29.refs_0_, ...), custom_call_target="tpu_custom_call" | custom-call | tf_op jit(solution)/shard_map/pallas_call | solution.py:90
  80.3 1.6 %collective-permute-start.29 = (bf16[640,128]{1,0:T(8,128)(2,1)S(1)}, bf16[640,128]{1,0:T(8,128)(2,1)S(1)}, u32[]{:S(2)}, u32[]{:S(2)}) collective-permute-start(bf16[640,128]{1,0:T(8,128)(2,1)S(1)} %get-tuple-element.36), channel_id=1, source_target_pairs={{0,2},{1,3},{2,0},{3,1},{4,6},{5,7},{6,4},{7,5},{8,10},{9,11},{10,... | collective-permute-start | bytes 491528 | tf_op jit(solution)/shard_map/ppermute | solution.py:105
  81.9 0.6 collective-permute-start.30
  82.4 1.4 %collective-permute-start.31 = (bf16[640,128]{1,0:T(8,128)(2,1)S(1)}, bf16[640,128]{1,0:T(8,128)(2,1)S(1)}, u32[]{:S(2)}, u32[]{:S(2)}) collective-permute-start(bf16[640,128]{1,0:T(8,128)(2,1)S(1)} %get-tuple-element.38), channel_id=1, source_target_pairs={{0,6},{1,7},{2,4},{3,5},{4,2},{5,3},{6,0},{7,1},{8,14},{9,15},{10,... | collective-permute-start | bytes 491528 | tf_op jit(solution)/shard_map/ppermute | solution.py:105
  83.8 3.4 %collective-permute-done.29.p1.refs_1_ = bf16[640,128]{1,0:T(8,128)(2,1)S(1)} collective-permute-done((bf16[640,128]{1,0:T(8,128)(2,1)S(1)}, bf16[640,128]{1,0:T(8,128)(2,1)S(1)}, u32[]{:S(2)}, u32[]{:S(2)}) %collective-permute-start.29) | collective-permute-done | bytes 163872 | tf_op jit(solution)/shard_map/ppermute | solution.py:105
  87.2 3.4 %collective-permute-done.30.p2.refs_2_ = bf16[640,128]{1,0:T(8,128)(2,1)S(1)} collective-permute-done((bf16[640,128]{1,0:T(8,128)(2,1)S(1)}, bf16[640,128]{1,0:T(8,128)(2,1)S(1)}, u32[]{:S(2)}, u32[]{:S(2)}) %collective-permute-start.30) | collective-permute-done | bytes 163872 | tf_op jit(solution)/shard_map/ppermute | solution.py:105
  91.1 0.9 %shard_map.128 = bf16[128,512]{1,0:T(8,128)(2,1)} custom-call(s32[1]{0:T(128)} %bitcast.pos, bf16[640,128]{1,0:T(8,128)(2,1)S(1)} %get-tuple-element.35.p0.refs_0_, bf16[640,128]{1,0:T(8,128)(2,1)S(1)} %collective-permute-done.29.p1.refs_1_, bf16[640,128]{1,0:T(8,128)(2,1)S(1)} %collective-permute-done.30.p2.refs_2_, ...), custom_call_target="tpu_custom_call" | custom-call | tf_op jit(solution)/shard_map/pallas_call | solution.py:90
  92.2 1.6 %shard_map.129 = (f32[512,512]{1,0:T(8,128)}, f32[512,512]{1,0:T(8,128)}) custom-call(s32[1]{0:T(128)} %bitcast.pos, bf16[640,128]{1,0:T(8,128)(2,1)S(1)} %get-tuple-element.35.p0.refs_0_, bf16[640,128]{1,0:T(8,128)(2,1)S(1)} %collective-permute-done.29.p1.refs_1_, bf16[640,128]{1,0:T(8,128)(2,1)S(1)} %collective-permute-done.30.p2.refs_2_, ...), custom_call_target="tpu_custom_call" | custom-call | tf_op jit(solution)/shard_map/pallas_call | solution.py:90
  (56 shorter events, 3.4 us)
Async XLA Ops:
  0.6 0.7 copy-start.7
  0.6 0.7 copy-start.9
  0.7 0.7 copy-start.6
  0.7 0.7 copy-start.8
  1.4 1.0 %copy-start.2 = (bf16[2,64,1024]{2,1,0:T(8,128)(2,1)S(1)}, bf16[2,64,1024]{2,1,0:T(8,128)(2,1)}, u32[]{:S(2)}) copy-start(bf16[2,64,1024]{2,1,0:T(8,128)(2,1)} %refs_6_.1) | copy-start | bytes 786436
  2.3 0.9 %copy-start.3 = (bf16[2,64,1024]{2,1,0:T(8,128)(2,1)S(1)}, bf16[2,64,1024]{2,1,0:T(8,128)(2,1)}, u32[]{:S(2)}) copy-start(bf16[2,64,1024]{2,1,0:T(8,128)(2,1)} %refs_7_.1) | copy-start | bytes 786436
  3.3 0.9 copy-start.4
  4.2 0.9 copy-start.5
  5.9 5.5 %collective-permute-start = (bf16[144,256]{1,0:T(8,128)(2,1)S(1)}, bf16[144,256]{1,0:T(8,128)(2,1)S(1)}, u32[]{:S(2)}, u32[]{:S(2)}) collective-permute-start(bf16[144,256]{1,0:T(8,128)(2,1)S(1)} %get-tuple-element.23), channel_id=1, source_target_pairs={{0,2},{1,3},{2,0},{3,1},{4,6},{5,7},{6,4},{7,5},{8,10},{9,11},{10,... | collective-permute-start | bytes 221192 | tf_op jit(solution)/shard_map/ppermute | solution.py:105
  8.9 4.4 %collective-permute-start.1 = (bf16[144,256]{1,0:T(8,128)(2,1)S(1)}, bf16[144,256]{1,0:T(8,128)(2,1)S(1)}, u32[]{:S(2)}, u32[]{:S(2)}) collective-permute-start(bf16[144,256]{1,0:T(8,128)(2,1)S(1)} %get-tuple-element.24), channel_id=1, source_target_pairs={{0,4},{1,5},{2,6},{3,7},{4,0},{5,1},{6,2},{7,3},{8,12},{9,13},{10,... | collective-permute-start | bytes 221192 | tf_op jit(solution)/shard_map/ppermute | solution.py:105
  10.4 5.3 %collective-permute-start.2 = (bf16[144,256]{1,0:T(8,128)(2,1)S(1)}, bf16[144,256]{1,0:T(8,128)(2,1)S(1)}, u32[]{:S(2)}, u32[]{:S(2)}) collective-permute-start(bf16[144,256]{1,0:T(8,128)(2,1)S(1)} %get-tuple-element.25), channel_id=1, source_target_pairs={{0,6},{1,7},{2,4},{3,5},{4,2},{5,3},{6,0},{7,1},{8,14},{9,15},{10,... | collective-permute-start | bytes 221192 | tf_op jit(solution)/shard_map/ppermute | solution.py:105
  15.7 6.3 %collective-permute-start.6 = (bf16[512,256]{1,0:T(8,128)(2,1)S(1)}, bf16[512,256]{1,0:T(8,128)(2,1)S(1)}, u32[]{:S(2)}, u32[]{:S(2)}) collective-permute-start(bf16[512,256]{1,0:T(8,128)(2,1)S(1)} %get-tuple-element.27.refs_0_), channel_id=1, source_target_pairs={{0,1},{1,0},{2,3},{3,2},{4,5},{5,4},{6,7},{7,6},{8,9},{9,8},{10,11... | collective-permute-start | bytes 786440 | tf_op jit(solution)/shard_map/ppermute | solution.py:105
  15.8 16.9 %collective-permute-start.12 = (bf16[4,64,1024]{2,1,0:T(8,128)(2,1)S(1)}, bf16[4,64,1024]{2,1,0:T(8,128)(2,1)S(1)}, u32[]{:S(2)}, u32[]{:S(2)}) collective-permute-start(bf16[4,64,1024]{2,1,0:T(8,128)(2,1)S(1)} %get-tuple-element.28.refs_8_), channel_id=1, source_target_pairs={{0,6},{1,7},{2,4},{3,5},{4,2},{5,3},{6,0},{7,1},{8,14},{9,15},{10,... | collective-permute-start | bytes 1572872 | tf_op jit(solution)/shard_map/ppermute | solution.py:105
  16.2 15.0 %collective-permute-start.4 = (bf16[512,256]{1,0:T(8,128)(2,1)S(1)}, bf16[512,256]{1,0:T(8,128)(2,1)S(1)}, u32[]{:S(2)}, u32[]{:S(2)}) collective-permute-start(bf16[512,256]{1,0:T(8,128)(2,1)S(1)} %get-tuple-element.27.refs_0_), channel_id=1, source_target_pairs={{0,16},{1,17},{2,18},{3,19},{4,20},{5,21},{6,22},{7,23},{8,24},{9,... | collective-permute-start | bytes 786440 | tf_op jit(solution)/shard_map/ppermute | solution.py:105
  18.9 23.3 %collective-permute-start.11 = (bf16[4,64,1024]{2,1,0:T(8,128)(2,1)S(1)}, bf16[4,64,1024]{2,1,0:T(8,128)(2,1)S(1)}, u32[]{:S(2)}, u32[]{:S(2)}) collective-permute-start(bf16[4,64,1024]{2,1,0:T(8,128)(2,1)S(1)} %get-tuple-element.28.refs_8_), channel_id=1, source_target_pairs={{0,4},{1,5},{2,6},{3,7},{4,0},{5,1},{6,2},{7,3},{8,12},{9,13},{10,... | collective-permute-start | bytes 1572872 | tf_op jit(solution)/shard_map/ppermute | solution.py:105
  20.4 12.3 %collective-permute-start.3 = (bf16[512,256]{1,0:T(8,128)(2,1)S(1)}, bf16[512,256]{1,0:T(8,128)(2,1)S(1)}, u32[]{:S(2)}, u32[]{:S(2)}) collective-permute-start(bf16[512,256]{1,0:T(8,128)(2,1)S(1)} %get-tuple-element.27.refs_0_), channel_id=1, source_target_pairs={{0,8},{1,9},{2,10},{3,11},{4,12},{5,13},{6,14},{7,15},{8,0},{9,1},... | collective-permute-start | bytes 786440 | tf_op jit(solution)/shard_map/ppermute | solution.py:105
  22.0 20.2 %collective-permute-start.10 = (bf16[4,64,1024]{2,1,0:T(8,128)(2,1)S(1)}, bf16[4,64,1024]{2,1,0:T(8,128)(2,1)S(1)}, u32[]{:S(2)}, u32[]{:S(2)}) collective-permute-start(bf16[4,64,1024]{2,1,0:T(8,128)(2,1)S(1)} %get-tuple-element.28.refs_8_), channel_id=1, source_target_pairs={{0,2},{1,3},{2,0},{3,1},{4,6},{5,7},{6,4},{7,5},{8,10},{9,11},{10,... | collective-permute-start | bytes 1572872 | tf_op jit(solution)/shard_map/ppermute | solution.py:105
  31.3 7.5 %collective-permute-start.5 = (bf16[512,256]{1,0:T(8,128)(2,1)S(1)}, bf16[512,256]{1,0:T(8,128)(2,1)S(1)}, u32[]{:S(2)}, u32[]{:S(2)}) collective-permute-start(bf16[512,256]{1,0:T(8,128)(2,1)S(1)} %collective-permute-done.4.refs_2_), channel_id=1, source_target_pairs={{0,8},{1,9},{2,10},{3,11},{4,12},{5,13},{6,14},{7,15},{8,0},{9,1},... | collective-permute-start | bytes 786440 | tf_op jit(solution)/shard_map/ppermute | solution.py:105
  32.7 9.6 %collective-permute-start.8 = (bf16[512,256]{1,0:T(8,128)(2,1)S(1)}, bf16[512,256]{1,0:T(8,128)(2,1)S(1)}, u32[]{:S(2)}, u32[]{:S(2)}) collective-permute-start(bf16[512,256]{1,0:T(8,128)(2,1)S(1)} %collective-permute-done.4.refs_2_), channel_id=1, source_target_pairs={{0,1},{1,0},{2,3},{3,2},{4,5},{5,4},{6,7},{7,6},{8,9},{9,8},{10,11... | collective-permute-start | bytes 786440 | tf_op jit(solution)/shard_map/ppermute | solution.py:105
  32.7 9.6 %collective-permute-start.7 = (bf16[512,256]{1,0:T(8,128)(2,1)S(1)}, bf16[512,256]{1,0:T(8,128)(2,1)S(1)}, u32[]{:S(2)}, u32[]{:S(2)}) collective-permute-start(bf16[512,256]{1,0:T(8,128)(2,1)S(1)} %collective-permute-done.3.refs_1_), channel_id=1, source_target_pairs={{0,1},{1,0},{2,3},{3,2},{4,5},{5,4},{6,7},{7,6},{8,9},{9,8},{10,11... | collective-permute-start | bytes 786440 | tf_op jit(solution)/shard_map/ppermute | solution.py:105
  38.8 3.5 %collective-permute-start.9 = (bf16[512,256]{1,0:T(8,128)(2,1)S(1)}, bf16[512,256]{1,0:T(8,128)(2,1)S(1)}, u32[]{:S(2)}, u32[]{:S(2)}) collective-permute-start(bf16[512,256]{1,0:T(8,128)(2,1)S(1)} %collective-permute-done.5.refs_3_), channel_id=1, source_target_pairs={{0,1},{1,0},{2,3},{3,2},{4,5},{5,4},{6,7},{7,6},{8,9},{9,8},{10,11... | collective-permute-start | bytes 786440 | tf_op jit(solution)/shard_map/ppermute | solution.py:105
  43.8 10.3 %copy-start.1 = (bf16[512,512]{1,0:T(8,128)(2,1)S(1)}, bf16[512,512]{1,0:T(8,128)(2,1)}, u32[]{:S(2)}) copy-start(bf16[512,512]{1,0:T(8,128)(2,1)} %w_first.1) | copy-start | bytes 1572868
  43.9 7.4 %collective-permute-start.15 = (bf16[512,128]{1,0:T(8,128)(2,1)S(1)}, bf16[512,128]{1,0:T(8,128)(2,1)S(1)}, u32[]{:S(2)}, u32[]{:S(2)}) collective-permute-start(bf16[512,128]{1,0:T(8,128)(2,1)S(1)} %shard_map.123.p0), channel_id=1, source_target_pairs={{0,6},{1,7},{2,4},{3,5},{4,2},{5,3},{6,0},{7,1},{8,14},{9,15},{10,... | collective-permute-start | bytes 393224 | tf_op jit(solution)/shard_map/ppermute | solution.py:105
  44.5 9.6 %collective-permute-start.14 = (bf16[512,128]{1,0:T(8,128)(2,1)S(1)}, bf16[512,128]{1,0:T(8,128)(2,1)S(1)}, u32[]{:S(2)}, u32[]{:S(2)}) collective-permute-start(bf16[512,128]{1,0:T(8,128)(2,1)S(1)} %shard_map.123.p0), channel_id=1, source_target_pairs={{0,4},{1,5},{2,6},{3,7},{4,0},{5,1},{6,2},{7,3},{8,12},{9,13},{10,... | collective-permute-start | bytes 393224 | tf_op jit(solution)/shard_map/ppermute | solution.py:105
  45.9 8.2 %collective-permute-start.13 = (bf16[512,128]{1,0:T(8,128)(2,1)S(1)}, bf16[512,128]{1,0:T(8,128)(2,1)S(1)}, u32[]{:S(2)}, u32[]{:S(2)}) collective-permute-start(bf16[512,128]{1,0:T(8,128)(2,1)S(1)} %shard_map.123.p0), channel_id=1, source_target_pairs={{0,2},{1,3},{2,0},{3,1},{4,6},{5,7},{6,4},{7,5},{8,10},{9,11},{10,... | collective-permute-start | bytes 393224 | tf_op jit(solution)/shard_map/ppermute | solution.py:105
  49.0 9.1 %copy-start = (bf16[512,512]{1,0:T(8,128)(2,1)S(1)}, bf16[512,512]{1,0:T(8,128)(2,1)}, u32[]{:S(2)}) copy-start(bf16[512,512]{1,0:T(8,128)(2,1)} %w_second.3) | copy-start | bytes 1572868
  49.0 7.8 %collective-permute-start.25 = (bf16[512,128]{1,0:T(8,128)(2,1)S(1)}, bf16[512,128]{1,0:T(8,128)(2,1)S(1)}, u32[]{:S(2)}, u32[]{:S(2)}) collective-permute-start(bf16[512,128]{1,0:T(8,128)(2,1)S(1)} %shard_map.125.p0), channel_id=1, source_target_pairs={{0,6},{1,7},{2,4},{3,5},{4,2},{5,3},{6,0},{7,1},{8,14},{9,15},{10,... | collective-permute-start | bytes 393224 | tf_op jit(solution)/shard_map/ppermute | solution.py:105
  49.6 8.5 %collective-permute-start.24 = (bf16[512,128]{1,0:T(8,128)(2,1)S(1)}, bf16[512,128]{1,0:T(8,128)(2,1)S(1)}, u32[]{:S(2)}, u32[]{:S(2)}) collective-permute-start(bf16[512,128]{1,0:T(8,128)(2,1)S(1)} %shard_map.125.p0), channel_id=1, source_target_pairs={{0,4},{1,5},{2,6},{3,7},{4,0},{5,1},{6,2},{7,3},{8,12},{9,13},{10,... | collective-permute-start | bytes 393224 | tf_op jit(solution)/shard_map/ppermute | solution.py:105
  51.2 6.9 %collective-permute-start.23 = (bf16[512,128]{1,0:T(8,128)(2,1)S(1)}, bf16[512,128]{1,0:T(8,128)(2,1)S(1)}, u32[]{:S(2)}, u32[]{:S(2)}) collective-permute-start(bf16[512,128]{1,0:T(8,128)(2,1)S(1)} %shard_map.125.p0), channel_id=1, source_target_pairs={{0,2},{1,3},{2,0},{3,1},{4,6},{5,7},{6,4},{7,5},{8,10},{9,11},{10,... | collective-permute-start | bytes 393224 | tf_op jit(solution)/shard_map/ppermute | solution.py:105
  58.8 2.3 %collective-permute-start.26 = (f32[512,128]{1,0:T(8,128)S(1)}, f32[512,128]{1,0:T(8,128)S(1)}, u32[]{:S(2)}, u32[]{:S(2)}) collective-permute-start(f32[512,128]{1,0:T(8,128)S(1)} %get-tuple-element.34), channel_id=1, source_target_pairs={{0,1},{1,0},{2,3},{3,2},{4,5},{5,4},{6,7},{7,6},{8,9},{9,8},{10,11... | collective-permute-start | bytes 786440 | tf_op jit(solution)/shard_map/ppermute | solution.py:105
  58.9 9.7 %collective-permute-start.17 = (bf16[512,128]{1,0:T(8,128)(2,1)S(1)}, bf16[512,128]{1,0:T(8,128)(2,1)S(1)}, u32[]{:S(2)}, u32[]{:S(2)}) collective-permute-start(bf16[512,128]{1,0:T(8,128)(2,1)S(1)} %get-tuple-element.29.refs_0_), channel_id=1, source_target_pairs={{0,16},{1,17},{2,18},{3,19},{4,20},{5,21},{6,22},{7,23},{8,24},{9,... | collective-permute-start | bytes 393224 | tf_op jit(solution)/shard_map/ppermute | solution.py:105
  61.2 8.2 %collective-permute-start.27 = (bf16[512,128]{1,0:T(8,128)(2,1)S(1)}, bf16[512,128]{1,0:T(8,128)(2,1)S(1)}, u32[]{:S(2)}, u32[]{:S(2)}) collective-permute-start(bf16[512,128]{1,0:T(8,128)(2,1)S(1)} %add_convert_fusion.2), channel_id=1, source_target_pairs={{0,8},{1,9},{2,10},{3,11},{4,12},{5,13},{6,14},{7,15},{8,0},{9,1},... | collective-permute-start | bytes 393224 | tf_op jit(solution)/shard_map/ppermute | solution.py:105
  62.8 10.1 %collective-permute-start.16 = (bf16[512,128]{1,0:T(8,128)(2,1)S(1)}, bf16[512,128]{1,0:T(8,128)(2,1)S(1)}, u32[]{:S(2)}, u32[]{:S(2)}) collective-permute-start(bf16[512,128]{1,0:T(8,128)(2,1)S(1)} %get-tuple-element.29.refs_0_), channel_id=1, source_target_pairs={{0,8},{1,9},{2,10},{3,11},{4,12},{5,13},{6,14},{7,15},{8,0},{9,1},... | collective-permute-start | bytes 393224 | tf_op jit(solution)/shard_map/ppermute | solution.py:105
  68.7 8.1 %collective-permute-start.18 = (bf16[512,128]{1,0:T(8,128)(2,1)S(1)}, bf16[512,128]{1,0:T(8,128)(2,1)S(1)}, u32[]{:S(2)}, u32[]{:S(2)}) collective-permute-start(bf16[512,128]{1,0:T(8,128)(2,1)S(1)} %collective-permute-done.17.refs_2_), channel_id=1, source_target_pairs={{0,8},{1,9},{2,10},{3,11},{4,12},{5,13},{6,14},{7,15},{8,0},{9,1},... | collective-permute-start | bytes 393224 | tf_op jit(solution)/shard_map/ppermute | solution.py:105
  69.5 9.2 %collective-permute-start.28 = (bf16[512,128]{1,0:T(8,128)(2,1)S(1)}, bf16[512,128]{1,0:T(8,128)(2,1)S(1)}, u32[]{:S(2)}, u32[]{:S(2)}) collective-permute-start(bf16[512,128]{1,0:T(8,128)(2,1)S(1)} %add_convert_fusion.1), channel_id=1, source_target_pairs={{0,16},{1,17},{2,18},{3,19},{4,20},{5,21},{6,22},{7,23},{8,24},{9,... | collective-permute-start | bytes 393224 | tf_op jit(solution)/shard_map/ppermute | solution.py:105
  72.4 6.3 %collective-permute-start.19 = (bf16[512,128]{1,0:T(8,128)(2,1)S(1)}, bf16[512,128]{1,0:T(8,128)(2,1)S(1)}, u32[]{:S(2)}, u32[]{:S(2)}) collective-permute-start(bf16[512,128]{1,0:T(8,128)(2,1)S(1)} %get-tuple-element.29.refs_0_), channel_id=1, source_target_pairs={{0,1},{1,0},{2,3},{3,2},{4,5},{5,4},{6,7},{7,6},{8,9},{9,8},{10,11... | collective-permute-start | bytes 393224 | tf_op jit(solution)/shard_map/ppermute | solution.py:105
  72.4 6.3 %collective-permute-start.21 = (bf16[512,128]{1,0:T(8,128)(2,1)S(1)}, bf16[512,128]{1,0:T(8,128)(2,1)S(1)}, u32[]{:S(2)}, u32[]{:S(2)}) collective-permute-start(bf16[512,128]{1,0:T(8,128)(2,1)S(1)} %collective-permute-done.17.refs_2_), channel_id=1, source_target_pairs={{0,1},{1,0},{2,3},{3,2},{4,5},{5,4},{6,7},{7,6},{8,9},{9,8},{10,11... | collective-permute-start | bytes 393224 | tf_op jit(solution)/shard_map/ppermute | solution.py:105
  72.9 5.8 %collective-permute-start.20 = (bf16[512,128]{1,0:T(8,128)(2,1)S(1)}, bf16[512,128]{1,0:T(8,128)(2,1)S(1)}, u32[]{:S(2)}, u32[]{:S(2)}) collective-permute-start(bf16[512,128]{1,0:T(8,128)(2,1)S(1)} %collective-permute-done.16.refs_1_), channel_id=1, source_target_pairs={{0,1},{1,0},{2,3},{3,2},{4,5},{5,4},{6,7},{7,6},{8,9},{9,8},{10,11... | collective-permute-start | bytes 393224 | tf_op jit(solution)/shard_map/ppermute | solution.py:105
  76.7 2.0 %collective-permute-start.22 = (bf16[512,128]{1,0:T(8,128)(2,1)S(1)}, bf16[512,128]{1,0:T(8,128)(2,1)S(1)}, u32[]{:S(2)}, u32[]{:S(2)}) collective-permute-start(bf16[512,128]{1,0:T(8,128)(2,1)S(1)} %collective-permute-done.18.refs_3_), channel_id=1, source_target_pairs={{0,1},{1,0},{2,3},{3,2},{4,5},{5,4},{6,7},{7,6},{8,9},{9,8},{10,11... | collective-permute-start | bytes 393224 | tf_op jit(solution)/shard_map/ppermute | solution.py:105
  80.3 6.9 %collective-permute-start.29 = (bf16[640,128]{1,0:T(8,128)(2,1)S(1)}, bf16[640,128]{1,0:T(8,128)(2,1)S(1)}, u32[]{:S(2)}, u32[]{:S(2)}) collective-permute-start(bf16[640,128]{1,0:T(8,128)(2,1)S(1)} %get-tuple-element.36), channel_id=1, source_target_pairs={{0,2},{1,3},{2,0},{3,1},{4,6},{5,7},{6,4},{7,5},{8,10},{9,11},{10,... | collective-permute-start | bytes 491528 | tf_op jit(solution)/shard_map/ppermute | solution.py:105
  81.9 8.7 %collective-permute-start.30 = (bf16[640,128]{1,0:T(8,128)(2,1)S(1)}, bf16[640,128]{1,0:T(8,128)(2,1)S(1)}, u32[]{:S(2)}, u32[]{:S(2)}) collective-permute-start(bf16[640,128]{1,0:T(8,128)(2,1)S(1)} %get-tuple-element.37), channel_id=1, source_target_pairs={{0,4},{1,5},{2,6},{3,7},{4,0},{5,1},{6,2},{7,3},{8,12},{9,13},{10,... | collective-permute-start | bytes 491528 | tf_op jit(solution)/shard_map/ppermute | solution.py:105
  82.4 8.2 %collective-permute-start.31 = (bf16[640,128]{1,0:T(8,128)(2,1)S(1)}, bf16[640,128]{1,0:T(8,128)(2,1)S(1)}, u32[]{:S(2)}, u32[]{:S(2)}) collective-permute-start(bf16[640,128]{1,0:T(8,128)(2,1)S(1)} %get-tuple-element.38), channel_id=1, source_target_pairs={{0,6},{1,7},{2,4},{3,5},{4,2},{5,3},{6,0},{7,1},{8,14},{9,15},{10,... | collective-permute-start | bytes 491528 | tf_op jit(solution)/shard_map/ppermute | solution.py:105
  83.8 8.2 %collective-permute-start.32 = (bf16[640,128]{1,0:T(8,128)(2,1)S(1)}, bf16[640,128]{1,0:T(8,128)(2,1)S(1)}, u32[]{:S(2)}, u32[]{:S(2)}) collective-permute-start(bf16[640,128]{1,0:T(8,128)(2,1)S(1)} %get-tuple-element.35.p0.refs_0_), channel_id=1, source_target_pairs={{0,1},{1,0},{2,3},{3,2},{4,5},{5,4},{6,7},{7,6},{8,9},{9,8},{10,11... | collective-permute-start | bytes 491528 | tf_op jit(solution)/shard_map/ppermute | solution.py:105
  87.2 4.8 %collective-permute-start.33 = (bf16[640,128]{1,0:T(8,128)(2,1)S(1)}, bf16[640,128]{1,0:T(8,128)(2,1)S(1)}, u32[]{:S(2)}, u32[]{:S(2)}) collective-permute-start(bf16[640,128]{1,0:T(8,128)(2,1)S(1)} %collective-permute-done.29.p1.refs_1_), channel_id=1, source_target_pairs={{0,1},{1,0},{2,3},{3,2},{4,5},{5,4},{6,7},{7,6},{8,9},{9,8},{10,11... | collective-permute-start | bytes 491528 | tf_op jit(solution)/shard_map/ppermute | solution.py:105
  90.6 1.5 %collective-permute-start.34 = (bf16[640,128]{1,0:T(8,128)(2,1)S(1)}, bf16[640,128]{1,0:T(8,128)(2,1)S(1)}, u32[]{:S(2)}, u32[]{:S(2)}) collective-permute-start(bf16[640,128]{1,0:T(8,128)(2,1)S(1)} %collective-permute-done.30.p2.refs_2_), channel_id=1, source_target_pairs={{0,1},{1,0},{2,3},{3,2},{4,5},{5,4},{6,7},{7,6},{8,9},{9,8},{10,11... | collective-permute-start | bytes 491528 | tf_op jit(solution)/shard_map/ppermute | solution.py:105
  90.6 1.6 %collective-permute-start.35 = (bf16[640,128]{1,0:T(8,128)(2,1)S(1)}, bf16[640,128]{1,0:T(8,128)(2,1)S(1)}, u32[]{:S(2)}, u32[]{:S(2)}) collective-permute-start(bf16[640,128]{1,0:T(8,128)(2,1)S(1)} %collective-permute-done.31.p3.refs_3_), channel_id=1, source_target_pairs={{0,1},{1,0},{2,3},{3,2},{4,5},{5,4},{6,7},{7,6},{8,9},{9,8},{10,11... | collective-permute-start | bytes 491528 | tf_op jit(solution)/shard_map/ppermute | solution.py:105

commit v6 on v5

--- a/solution.py
+++ b/solution.py
@@ -382,8 +382,7 @@
     cotangent,
 ):
     pos = lax.axis_index(AXES).astype(jnp.int32).reshape(1)
-    *packed, both_tiles = pack(
-        pos,
+    operands = (
         tile_columns,
         tiles_per_row,
         rev_cols,
@@ -393,6 +392,8 @@
         tile_entries,
         rev_vals,
     )
+    operands = [pltpu.with_memory_space_constraint(value, pltpu.HBM) for value in operands]
+    *packed, both_tiles = pack(pos, *operands)
     parts = [packed[0]] + [swap(packed[q], 2 * q) for q in range(1, QUAD)]
     share, places = unpack(pos, parts)
     tiles = over_quad(both_tiles)

time: 94 us -> 90.1 us (0.959)
  local copies, waits for them, and re-layouts: 4.4 us -> 0.01 us
    unnamed x20 -> x4, local copies, waits for them, and re-layouts: 4.4 us -> 0.01 us
where the time goes in v6:
time: 90.1 us; the launch traced here: 89.9 us
  waiting for transfers between devices  46.3 us (51%)
  starting transfers between devices  32.6 us (36%)
  Pallas kernels  10.1 us (11%)
    ppermute x36, waiting for transfers between devices, swap(): return lax.ppermute(value, AXES, [(i, i ^ mask) for i in range(DEVICES)])  46.3 us
    ppermute x36, starting transfers between devices, swap(): return lax.ppermute(value, AXES, [(i, i ^ mask) for i in range(DEVICES)])  32.6 us
    pallas_call x9, Pallas kernels, call(): pl.pallas_call(body, out_shape=out_shape, in_specs=list(spaces), out_spec...  10.1 us
  transfers between devices with their start and end apart: 36, of which 18 were waited for; matrix products, arithmetic and copies ran while one was open for 0% of the time, Pallas kernels for 4%

profile of v6, /device:TPU:0, one launch (start us, length us, event | category | flops | bytes accessed | tf_op | source)
XLA Modules:
  0.0 89.9 jit_solution(2673558287608160048)
XLA Ops:
  0.6 1.3 %shard_map.121 = (bf16[144,256]{1,0:T(8,128)(2,1)S(1)}, bf16[144,256]{1,0:T(8,128)(2,1)S(1)}, bf16[144,256]{1,0:T(8,128)(2,1)S(1)}, bf16[144,256]{1,0:T(8,128)(2,1)S(1)}, bf16[4,64,1024]{2,1,0:T(8,128)(2,1)S(1)}) custom-call(s32[1]{0:T(128)} %bitcast.pos, s32[2,16]{1,0:T(2,128)} %refs_0_.1, s32[2]{0:T(128)} %refs_1_.1, s32[2,16]{1,0:T(2,128)} %refs_2_.1, ...), custom_call_target="tpu_custom_call" | custom-call | tf_op jit(solution)/shard_map/pallas_call | solution.py:90
  2.0 3.0 %collective-permute-start = (bf16[144,256]{1,0:T(8,128)(2,1)S(1)}, bf16[144,256]{1,0:T(8,128)(2,1)S(1)}, u32[]{:S(2)}, u32[]{:S(2)}) collective-permute-start(bf16[144,256]{1,0:T(8,128)(2,1)S(1)} %get-tuple-element.23), channel_id=1, source_target_pairs={{0,2},{1,3},{2,0},{3,1},{4,6},{5,7},{6,4},{7,5},{8,10},{9,11},{10,... | collective-permute-start | bytes 221192 | tf_op jit(solution)/shard_map/ppermute | solution.py:105
  5.0 1.5 %collective-permute-start.1 = (bf16[144,256]{1,0:T(8,128)(2,1)S(1)}, bf16[144,256]{1,0:T(8,128)(2,1)S(1)}, u32[]{:S(2)}, u32[]{:S(2)}) collective-permute-start(bf16[144,256]{1,0:T(8,128)(2,1)S(1)} %get-tuple-element.24), channel_id=1, source_target_pairs={{0,4},{1,5},{2,6},{3,7},{4,0},{5,1},{6,2},{7,3},{8,12},{9,13},{10,... | collective-permute-start | bytes 221192 | tf_op jit(solution)/shard_map/ppermute | solution.py:105
  6.5 1.0 %collective-permute-done.refs_1_ = bf16[144,256]{1,0:T(8,128)(2,1)S(1)} collective-permute-done((bf16[144,256]{1,0:T(8,128)(2,1)S(1)}, bf16[144,256]{1,0:T(8,128)(2,1)S(1)}, u32[]{:S(2)}, u32[]{:S(2)}) %collective-permute-start) | collective-permute-done | bytes 73760 | tf_op jit(solution)/shard_map/ppermute | solution.py:105
  7.5 1.8 %collective-permute-done.1.refs_2_ = bf16[144,256]{1,0:T(8,128)(2,1)S(1)} collective-permute-done((bf16[144,256]{1,0:T(8,128)(2,1)S(1)}, bf16[144,256]{1,0:T(8,128)(2,1)S(1)}, u32[]{:S(2)}, u32[]{:S(2)}) %collective-permute-start.1) | collective-permute-done | bytes 73760 | tf_op jit(solution)/shard_map/ppermute | solution.py:105
  9.3 2.4 %collective-permute-done.2.refs_3_ = bf16[144,256]{1,0:T(8,128)(2,1)S(1)} collective-permute-done((bf16[144,256]{1,0:T(8,128)(2,1)S(1)}, bf16[144,256]{1,0:T(8,128)(2,1)S(1)}, u32[]{:S(2)}, u32[]{:S(2)}) %collective-permute-start.2) | collective-permute-done | bytes 73760 | tf_op jit(solution)/shard_map/ppermute | solution.py:105
  11.9 0.5 collective-permute-start.12
  12.3 2.7 %collective-permute-start.4 = (bf16[512,256]{1,0:T(8,128)(2,1)S(1)}, bf16[512,256]{1,0:T(8,128)(2,1)S(1)}, u32[]{:S(2)}, u32[]{:S(2)}) collective-permute-start(bf16[512,256]{1,0:T(8,128)(2,1)S(1)} %get-tuple-element.27.refs_0_), channel_id=1, source_target_pairs={{0,16},{1,17},{2,18},{3,19},{4,20},{5,21},{6,22},{7,23},{8,24},{9,... | collective-permute-start | bytes 786440 | tf_op jit(solution)/shard_map/ppermute | solution.py:105
  15.0 1.5 %collective-permute-start.11 = (bf16[4,64,1024]{2,1,0:T(8,128)(2,1)S(1)}, bf16[4,64,1024]{2,1,0:T(8,128)(2,1)S(1)}, u32[]{:S(2)}, u32[]{:S(2)}) collective-permute-start(bf16[4,64,1024]{2,1,0:T(8,128)(2,1)S(1)} %get-tuple-element.28.refs_8_), channel_id=1, source_target_pairs={{0,4},{1,5},{2,6},{3,7},{4,0},{5,1},{6,2},{7,3},{8,12},{9,13},{10,... | collective-permute-start | bytes 1572872 | tf_op jit(solution)/shard_map/ppermute | solution.py:105
  16.5 1.6 %collective-permute-start.3 = (bf16[512,256]{1,0:T(8,128)(2,1)S(1)}, bf16[512,256]{1,0:T(8,128)(2,1)S(1)}, u32[]{:S(2)}, u32[]{:S(2)}) collective-permute-start(bf16[512,256]{1,0:T(8,128)(2,1)S(1)} %get-tuple-element.27.refs_0_), channel_id=1, source_target_pairs={{0,8},{1,9},{2,10},{3,11},{4,12},{5,13},{6,14},{7,15},{8,0},{9,1},... | collective-permute-start | bytes 786440 | tf_op jit(solution)/shard_map/ppermute | solution.py:105
  18.1 1.5 %collective-permute-start.10 = (bf16[4,64,1024]{2,1,0:T(8,128)(2,1)S(1)}, bf16[4,64,1024]{2,1,0:T(8,128)(2,1)S(1)}, u32[]{:S(2)}, u32[]{:S(2)}) collective-permute-start(bf16[4,64,1024]{2,1,0:T(8,128)(2,1)S(1)} %get-tuple-element.28.refs_8_), channel_id=1, source_target_pairs={{0,2},{1,3},{2,0},{3,1},{4,6},{5,7},{6,4},{7,5},{8,10},{9,11},{10,... | collective-permute-start | bytes 1572872 | tf_op jit(solution)/shard_map/ppermute | solution.py:105
  19.6 7.8 %collective-permute-done.4.refs_2_ = bf16[512,256]{1,0:T(8,128)(2,1)S(1)} collective-permute-done((bf16[512,256]{1,0:T(8,128)(2,1)S(1)}, bf16[512,256]{1,0:T(8,128)(2,1)S(1)}, u32[]{:S(2)}, u32[]{:S(2)}) %collective-permute-start.4) | collective-permute-done | bytes 262176 | tf_op jit(solution)/shard_map/ppermute | solution.py:105
  27.4 0.7 collective-permute-start.5
  28.1 0.7 collective-permute-done.3.refs_1_
  28.8 0.5 collective-permute-start.7
  29.3 5.6 %collective-permute-done.5.refs_3_ = bf16[512,256]{1,0:T(8,128)(2,1)S(1)} collective-permute-done((bf16[512,256]{1,0:T(8,128)(2,1)S(1)}, bf16[512,256]{1,0:T(8,128)(2,1)S(1)}, u32[]{:S(2)}, u32[]{:S(2)}) %collective-permute-start.5) | collective-permute-done | bytes 262176 | tf_op jit(solution)/shard_map/ppermute | solution.py:105
  34.9 3.4 %collective-permute-done.11.refs_10_ = bf16[4,64,1024]{2,1,0:T(8,128)(2,1)S(1)} collective-permute-done((bf16[4,64,1024]{2,1,0:T(8,128)(2,1)S(1)}, bf16[4,64,1024]{2,1,0:T(8,128)(2,1)S(1)}, u32[]{:S(2)}, u32[]{:S(2)}) %collective-permute-start.11) | collective-permute-done | bytes 524320 | tf_op jit(solution)/shard_map/ppermute | solution.py:105
  38.4 1.6 %shard_map.123.p0 = bf16[512,128]{1,0:T(8,128)(2,1)S(1)} custom-call(s32[32,128]{1,0:T(8,128)S(1)} %get-tuple-element.26.places, bf16[512,256]{1,0:T(8,128)(2,1)S(1)} %get-tuple-element.27.refs_0_, bf16[512,256]{1,0:T(8,128)(2,1)S(1)} %collective-permute-done.3.refs_1_, bf16[512,256]{1,0:T(8,128)(2,1)S(1)} %collective-permute-done.4.refs_2_, ...), custom_call_target="tpu_custom_call" | custom-call | tf_op jit(solution)/shard_map/pallas_call | solution.py:90
  40.0 0.6 collective-permute-start.15
  40.6 1.4 %collective-permute-start.14 = (bf16[512,128]{1,0:T(8,128)(2,1)S(1)}, bf16[512,128]{1,0:T(8,128)(2,1)S(1)}, u32[]{:S(2)}, u32[]{:S(2)}) collective-permute-start(bf16[512,128]{1,0:T(8,128)(2,1)S(1)} %shard_map.123.p0), channel_id=1, source_target_pairs={{0,4},{1,5},{2,6},{3,7},{4,0},{5,1},{6,2},{7,3},{8,12},{9,13},{10,... | collective-permute-start | bytes 393224 | tf_op jit(solution)/shard_map/ppermute | solution.py:105
  42.0 1.5 %collective-permute-start.13 = (bf16[512,128]{1,0:T(8,128)(2,1)S(1)}, bf16[512,128]{1,0:T(8,128)(2,1)S(1)}, u32[]{:S(2)}, u32[]{:S(2)}) collective-permute-start(bf16[512,128]{1,0:T(8,128)(2,1)S(1)} %shard_map.123.p0), channel_id=1, source_target_pairs={{0,2},{1,3},{2,0},{3,1},{4,6},{5,7},{6,4},{7,5},{8,10},{9,11},{10,... | collective-permute-start | bytes 393224 | tf_op jit(solution)/shard_map/ppermute | solution.py:105
  43.5 1.6 %shard_map.125.p0 = bf16[512,128]{1,0:T(8,128)(2,1)S(1)} custom-call(s32[32,128]{1,0:T(8,128)S(1)} %get-tuple-element.26.places, bf16[512,256]{1,0:T(8,128)(2,1)S(1)} %get-tuple-element.27.refs_0_, bf16[512,256]{1,0:T(8,128)(2,1)S(1)} %collective-permute-done.3.refs_1_, bf16[512,256]{1,0:T(8,128)(2,1)S(1)} %collective-permute-done.4.refs_2_, ...), custom_call_target="tpu_custom_call" | custom-call | tf_op jit(solution)/shard_map/pallas_call | solution.py:90
  45.1 0.6 collective-permute-start.25
  45.7 1.4 %collective-permute-start.24 = (bf16[512,128]{1,0:T(8,128)(2,1)S(1)}, bf16[512,128]{1,0:T(8,128)(2,1)S(1)}, u32[]{:S(2)}, u32[]{:S(2)}) collective-permute-start(bf16[512,128]{1,0:T(8,128)(2,1)S(1)} %shard_map.125.p0), channel_id=1, source_target_pairs={{0,4},{1,5},{2,6},{3,7},{4,0},{5,1},{6,2},{7,3},{8,12},{9,13},{10,... | collective-permute-start | bytes 393224 | tf_op jit(solution)/shard_map/ppermute | solution.py:105
  47.3 1.3 %collective-permute-start.23 = (bf16[512,128]{1,0:T(8,128)(2,1)S(1)}, bf16[512,128]{1,0:T(8,128)(2,1)S(1)}, u32[]{:S(2)}, u32[]{:S(2)}) collective-permute-start(bf16[512,128]{1,0:T(8,128)(2,1)S(1)} %shard_map.125.p0), channel_id=1, source_target_pairs={{0,2},{1,3},{2,0},{3,1},{4,6},{5,7},{6,4},{7,5},{8,10},{9,11},{10,... | collective-permute-start | bytes 393224 | tf_op jit(solution)/shard_map/ppermute | solution.py:105
  48.7 1.5 %collective-permute-done.14.p2 = bf16[512,128]{1,0:T(8,128)(2,1)S(1)} collective-permute-done((bf16[512,128]{1,0:T(8,128)(2,1)S(1)}, bf16[512,128]{1,0:T(8,128)(2,1)S(1)}, u32[]{:S(2)}, u32[]{:S(2)}) %collective-permute-start.14) | collective-permute-done | bytes 131104 | tf_op jit(solution)/shard_map/ppermute | solution.py:105
  50.2 0.8 shard_map.124
  51.0 2.0 %collective-permute-done.25.p3 = bf16[512,128]{1,0:T(8,128)(2,1)S(1)} collective-permute-done((bf16[512,128]{1,0:T(8,128)(2,1)S(1)}, bf16[512,128]{1,0:T(8,128)(2,1)S(1)}, u32[]{:S(2)}, u32[]{:S(2)}) %collective-permute-start.25) | collective-permute-done | bytes 131104 | tf_op jit(solution)/shard_map/ppermute | solution.py:105
  52.9 1.3 %collective-permute-done.24.p2 = bf16[512,128]{1,0:T(8,128)(2,1)S(1)} collective-permute-done((bf16[512,128]{1,0:T(8,128)(2,1)S(1)}, bf16[512,128]{1,0:T(8,128)(2,1)S(1)}, u32[]{:S(2)}, u32[]{:S(2)}) %collective-permute-start.24) | collective-permute-done | bytes 131104 | tf_op jit(solution)/shard_map/ppermute | solution.py:105
  54.2 0.7 shard_map.126
  55.0 2.2 %collective-permute-start.17 = (bf16[512,128]{1,0:T(8,128)(2,1)S(1)}, bf16[512,128]{1,0:T(8,128)(2,1)S(1)}, u32[]{:S(2)}, u32[]{:S(2)}) collective-permute-start(bf16[512,128]{1,0:T(8,128)(2,1)S(1)} %get-tuple-element.29.refs_0_), channel_id=1, source_target_pairs={{0,16},{1,17},{2,18},{3,19},{4,20},{5,21},{6,22},{7,23},{8,24},{9,... | collective-permute-start | bytes 393224 | tf_op jit(solution)/shard_map/ppermute | solution.py:105
  57.3 1.7 %collective-permute-start.27 = (bf16[512,128]{1,0:T(8,128)(2,1)S(1)}, bf16[512,128]{1,0:T(8,128)(2,1)S(1)}, u32[]{:S(2)}, u32[]{:S(2)}) collective-permute-start(bf16[512,128]{1,0:T(8,128)(2,1)S(1)} %add_convert_fusion.2), channel_id=1, source_target_pairs={{0,8},{1,9},{2,10},{3,11},{4,12},{5,13},{6,14},{7,15},{8,0},{9,1},... | collective-permute-start | bytes 393224 | tf_op jit(solution)/shard_map/ppermute | solution.py:105
  59.0 0.4 collective-permute-start.16
  59.4 5.4 %collective-permute-done.17.refs_2_ = bf16[512,128]{1,0:T(8,128)(2,1)S(1)} collective-permute-done((bf16[512,128]{1,0:T(8,128)(2,1)S(1)}, bf16[512,128]{1,0:T(8,128)(2,1)S(1)}, u32[]{:S(2)}, u32[]{:S(2)}) %collective-permute-start.17) | collective-permute-done | bytes 131104 | tf_op jit(solution)/shard_map/ppermute | solution.py:105
  65.0 0.6 collective-permute-done.27
  65.6 2.9 %collective-permute-start.28 = (bf16[512,128]{1,0:T(8,128)(2,1)S(1)}, bf16[512,128]{1,0:T(8,128)(2,1)S(1)}, u32[]{:S(2)}, u32[]{:S(2)}) collective-permute-start(bf16[512,128]{1,0:T(8,128)(2,1)S(1)} %add_convert_fusion.1), channel_id=1, source_target_pairs={{0,16},{1,17},{2,18},{3,19},{4,20},{5,21},{6,22},{7,23},{8,24},{9,... | collective-permute-start | bytes 393224 | tf_op jit(solution)/shard_map/ppermute | solution.py:105
  68.5 0.5 collective-permute-start.21
  69.0 3.8 %collective-permute-done.18.refs_3_ = bf16[512,128]{1,0:T(8,128)(2,1)S(1)} collective-permute-done((bf16[512,128]{1,0:T(8,128)(2,1)S(1)}, bf16[512,128]{1,0:T(8,128)(2,1)S(1)}, u32[]{:S(2)}, u32[]{:S(2)}) %collective-permute-start.18) | collective-permute-done | bytes 131104 | tf_op jit(solution)/shard_map/ppermute | solution.py:105
  72.8 1.9 %collective-permute-done.28 = bf16[512,128]{1,0:T(8,128)(2,1)S(1)} collective-permute-done((bf16[512,128]{1,0:T(8,128)(2,1)S(1)}, bf16[512,128]{1,0:T(8,128)(2,1)S(1)}, u32[]{:S(2)}, u32[]{:S(2)}) %collective-permute-start.28) | collective-permute-done | bytes 131104 | tf_op jit(solution)/shard_map/ppermute | solution.py:105
  74.8 1.6 %shard_map.127 = (bf16[640,128]{1,0:T(8,128)(2,1)S(1)}, bf16[640,128]{1,0:T(8,128)(2,1)S(1)}, bf16[640,128]{1,0:T(8,128)(2,1)S(1)}, bf16[640,128]{1,0:T(8,128)(2,1)S(1)}) custom-call(s32[32,128]{1,0:T(8,128)S(1)} %get-tuple-element.26.places, bf16[512,128]{1,0:T(8,128)(2,1)S(1)} %get-tuple-element.29.refs_0_, ...), custom_call_target="tpu_custom_call" | custom-call | tf_op jit(solution)/shard_map/pallas_call | solution.py:90
  76.4 1.6 %collective-permute-start.29 = (bf16[640,128]{1,0:T(8,128)(2,1)S(1)}, bf16[640,128]{1,0:T(8,128)(2,1)S(1)}, u32[]{:S(2)}, u32[]{:S(2)}) collective-permute-start(bf16[640,128]{1,0:T(8,128)(2,1)S(1)} %get-tuple-element.36), channel_id=1, source_target_pairs={{0,2},{1,3},{2,0},{3,1},{4,6},{5,7},{6,4},{7,5},{8,10},{9,11},{10,... | collective-permute-start | bytes 491528 | tf_op jit(solution)/shard_map/ppermute | solution.py:105
  78.0 0.6 collective-permute-start.30
  78.5 1.4 %collective-permute-start.31 = (bf16[640,128]{1,0:T(8,128)(2,1)S(1)}, bf16[640,128]{1,0:T(8,128)(2,1)S(1)}, u32[]{:S(2)}, u32[]{:S(2)}) collective-permute-start(bf16[640,128]{1,0:T(8,128)(2,1)S(1)} %get-tuple-element.38), channel_id=1, source_target_pairs={{0,6},{1,7},{2,4},{3,5},{4,2},{5,3},{6,0},{7,1},{8,14},{9,15},{10,... | collective-permute-start | bytes 491528 | tf_op jit(solution)/shard_map/ppermute | solution.py:105
  80.0 3.3 %collective-permute-done.29.p1.refs_1_ = bf16[640,128]{1,0:T(8,128)(2,1)S(1)} collective-permute-done((bf16[640,128]{1,0:T(8,128)(2,1)S(1)}, bf16[640,128]{1,0:T(8,128)(2,1)S(1)}, u32[]{:S(2)}, u32[]{:S(2)}) %collective-permute-start.29) | collective-permute-done | bytes 163872 | tf_op jit(solution)/shard_map/ppermute | solution.py:105
  83.3 3.4 %collective-permute-done.30.p2.refs_2_ = bf16[640,128]{1,0:T(8,128)(2,1)S(1)} collective-permute-done((bf16[640,128]{1,0:T(8,128)(2,1)S(1)}, bf16[640,128]{1,0:T(8,128)(2,1)S(1)}, u32[]{:S(2)}, u32[]{:S(2)}) %collective-permute-start.30) | collective-permute-done | bytes 163872 | tf_op jit(solution)/shard_map/ppermute | solution.py:105
  86.7 0.5 collective-permute-start.35
  87.2 0.9 %shard_map.128 = bf16[128,512]{1,0:T(8,128)(2,1)} custom-call(s32[1]{0:T(128)} %bitcast.pos, bf16[640,128]{1,0:T(8,128)(2,1)S(1)} %get-tuple-element.35.p0.refs_0_, bf16[640,128]{1,0:T(8,128)(2,1)S(1)} %collective-permute-done.29.p1.refs_1_, bf16[640,128]{1,0:T(8,128)(2,1)S(1)} %collective-permute-done.30.p2.refs_2_, ...), custom_call_target="tpu_custom_call" | custom-call | tf_op jit(solution)/shard_map/pallas_call | solution.py:90
  88.3 1.6 %shard_map.129 = (f32[512,512]{1,0:T(8,128)}, f32[512,512]{1,0:T(8,128)}) custom-call(s32[1]{0:T(128)} %bitcast.pos, bf16[640,128]{1,0:T(8,128)(2,1)S(1)} %get-tuple-element.35.p0.refs_0_, bf16[640,128]{1,0:T(8,128)(2,1)S(1)} %collective-permute-done.29.p1.refs_1_, bf16[640,128]{1,0:T(8,128)(2,1)S(1)} %collective-permute-done.30.p2.refs_2_, ...), custom_call_target="tpu_custom_call" | custom-call | tf_op jit(solution)/shard_map/pallas_call | solution.py:90
  (40 shorter events, 0.9 us)
Async XLA Ops:
  2.0 5.5 %collective-permute-start = (bf16[144,256]{1,0:T(8,128)(2,1)S(1)}, bf16[144,256]{1,0:T(8,128)(2,1)S(1)}, u32[]{:S(2)}, u32[]{:S(2)}) collective-permute-start(bf16[144,256]{1,0:T(8,128)(2,1)S(1)} %get-tuple-element.23), channel_id=1, source_target_pairs={{0,2},{1,3},{2,0},{3,1},{4,6},{5,7},{6,4},{7,5},{8,10},{9,11},{10,... | collective-permute-start | bytes 221192 | tf_op jit(solution)/shard_map/ppermute | solution.py:105
  5.0 4.4 %collective-permute-start.1 = (bf16[144,256]{1,0:T(8,128)(2,1)S(1)}, bf16[144,256]{1,0:T(8,128)(2,1)S(1)}, u32[]{:S(2)}, u32[]{:S(2)}) collective-permute-start(bf16[144,256]{1,0:T(8,128)(2,1)S(1)} %get-tuple-element.24), channel_id=1, source_target_pairs={{0,4},{1,5},{2,6},{3,7},{4,0},{5,1},{6,2},{7,3},{8,12},{9,13},{10,... | collective-permute-start | bytes 221192 | tf_op jit(solution)/shard_map/ppermute | solution.py:105
  6.5 5.3 %collective-permute-start.2 = (bf16[144,256]{1,0:T(8,128)(2,1)S(1)}, bf16[144,256]{1,0:T(8,128)(2,1)S(1)}, u32[]{:S(2)}, u32[]{:S(2)}) collective-permute-start(bf16[144,256]{1,0:T(8,128)(2,1)S(1)} %get-tuple-element.25), channel_id=1, source_target_pairs={{0,6},{1,7},{2,4},{3,5},{4,2},{5,3},{6,0},{7,1},{8,14},{9,15},{10,... | collective-permute-start | bytes 221192 | tf_op jit(solution)/shard_map/ppermute | solution.py:105
  11.8 6.3 %collective-permute-start.6 = (bf16[512,256]{1,0:T(8,128)(2,1)S(1)}, bf16[512,256]{1,0:T(8,128)(2,1)S(1)}, u32[]{:S(2)}, u32[]{:S(2)}) collective-permute-start(bf16[512,256]{1,0:T(8,128)(2,1)S(1)} %get-tuple-element.27.refs_0_), channel_id=1, source_target_pairs={{0,1},{1,0},{2,3},{3,2},{4,5},{5,4},{6,7},{7,6},{8,9},{9,8},{10,11... | collective-permute-start | bytes 786440 | tf_op jit(solution)/shard_map/ppermute | solution.py:105
  11.9 16.9 %collective-permute-start.12 = (bf16[4,64,1024]{2,1,0:T(8,128)(2,1)S(1)}, bf16[4,64,1024]{2,1,0:T(8,128)(2,1)S(1)}, u32[]{:S(2)}, u32[]{:S(2)}) collective-permute-start(bf16[4,64,1024]{2,1,0:T(8,128)(2,1)S(1)} %get-tuple-element.28.refs_8_), channel_id=1, source_target_pairs={{0,6},{1,7},{2,4},{3,5},{4,2},{5,3},{6,0},{7,1},{8,14},{9,15},{10,... | collective-permute-start | bytes 1572872 | tf_op jit(solution)/shard_map/ppermute | solution.py:105
  12.3 15.0 %collective-permute-start.4 = (bf16[512,256]{1,0:T(8,128)(2,1)S(1)}, bf16[512,256]{1,0:T(8,128)(2,1)S(1)}, u32[]{:S(2)}, u32[]{:S(2)}) collective-permute-start(bf16[512,256]{1,0:T(8,128)(2,1)S(1)} %get-tuple-element.27.refs_0_), channel_id=1, source_target_pairs={{0,16},{1,17},{2,18},{3,19},{4,20},{5,21},{6,22},{7,23},{8,24},{9,... | collective-permute-start | bytes 786440 | tf_op jit(solution)/shard_map/ppermute | solution.py:105
  15.0 23.3 %collective-permute-start.11 = (bf16[4,64,1024]{2,1,0:T(8,128)(2,1)S(1)}, bf16[4,64,1024]{2,1,0:T(8,128)(2,1)S(1)}, u32[]{:S(2)}, u32[]{:S(2)}) collective-permute-start(bf16[4,64,1024]{2,1,0:T(8,128)(2,1)S(1)} %get-tuple-element.28.refs_8_), channel_id=1, source_target_pairs={{0,4},{1,5},{2,6},{3,7},{4,0},{5,1},{6,2},{7,3},{8,12},{9,13},{10,... | collective-permute-start | bytes 1572872 | tf_op jit(solution)/shard_map/ppermute | solution.py:105
  16.5 12.3 %collective-permute-start.3 = (bf16[512,256]{1,0:T(8,128)(2,1)S(1)}, bf16[512,256]{1,0:T(8,128)(2,1)S(1)}, u32[]{:S(2)}, u32[]{:S(2)}) collective-permute-start(bf16[512,256]{1,0:T(8,128)(2,1)S(1)} %get-tuple-element.27.refs_0_), channel_id=1, source_target_pairs={{0,8},{1,9},{2,10},{3,11},{4,12},{5,13},{6,14},{7,15},{8,0},{9,1},... | collective-permute-start | bytes 786440 | tf_op jit(solution)/shard_map/ppermute | solution.py:105
  18.1 20.2 %collective-permute-start.10 = (bf16[4,64,1024]{2,1,0:T(8,128)(2,1)S(1)}, bf16[4,64,1024]{2,1,0:T(8,128)(2,1)S(1)}, u32[]{:S(2)}, u32[]{:S(2)}) collective-permute-start(bf16[4,64,1024]{2,1,0:T(8,128)(2,1)S(1)} %get-tuple-element.28.refs_8_), channel_id=1, source_target_pairs={{0,2},{1,3},{2,0},{3,1},{4,6},{5,7},{6,4},{7,5},{8,10},{9,11},{10,... | collective-permute-start | bytes 1572872 | tf_op jit(solution)/shard_map/ppermute | solution.py:105
  27.4 7.5 %collective-permute-start.5 = (bf16[512,256]{1,0:T(8,128)(2,1)S(1)}, bf16[512,256]{1,0:T(8,128)(2,1)S(1)}, u32[]{:S(2)}, u32[]{:S(2)}) collective-permute-start(bf16[512,256]{1,0:T(8,128)(2,1)S(1)} %collective-permute-done.4.refs_2_), channel_id=1, source_target_pairs={{0,8},{1,9},{2,10},{3,11},{4,12},{5,13},{6,14},{7,15},{8,0},{9,1},... | collective-permute-start | bytes 786440 | tf_op jit(solution)/shard_map/ppermute | solution.py:105
  28.8 9.6 %collective-permute-start.8 = (bf16[512,256]{1,0:T(8,128)(2,1)S(1)}, bf16[512,256]{1,0:T(8,128)(2,1)S(1)}, u32[]{:S(2)}, u32[]{:S(2)}) collective-permute-start(bf16[512,256]{1,0:T(8,128)(2,1)S(1)} %collective-permute-done.4.refs_2_), channel_id=1, source_target_pairs={{0,1},{1,0},{2,3},{3,2},{4,5},{5,4},{6,7},{7,6},{8,9},{9,8},{10,11... | collective-permute-start | bytes 786440 | tf_op jit(solution)/shard_map/ppermute | solution.py:105
  28.8 9.6 %collective-permute-start.7 = (bf16[512,256]{1,0:T(8,128)(2,1)S(1)}, bf16[512,256]{1,0:T(8,128)(2,1)S(1)}, u32[]{:S(2)}, u32[]{:S(2)}) collective-permute-start(bf16[512,256]{1,0:T(8,128)(2,1)S(1)} %collective-permute-done.3.refs_1_), channel_id=1, source_target_pairs={{0,1},{1,0},{2,3},{3,2},{4,5},{5,4},{6,7},{7,6},{8,9},{9,8},{10,11... | collective-permute-start | bytes 786440 | tf_op jit(solution)/shard_map/ppermute | solution.py:105
  34.9 3.5 %collective-permute-start.9 = (bf16[512,256]{1,0:T(8,128)(2,1)S(1)}, bf16[512,256]{1,0:T(8,128)(2,1)S(1)}, u32[]{:S(2)}, u32[]{:S(2)}) collective-permute-start(bf16[512,256]{1,0:T(8,128)(2,1)S(1)} %collective-permute-done.5.refs_3_), channel_id=1, source_target_pairs={{0,1},{1,0},{2,3},{3,2},{4,5},{5,4},{6,7},{7,6},{8,9},{9,8},{10,11... | collective-permute-start | bytes 786440 | tf_op jit(solution)/shard_map/ppermute | solution.py:105
  39.9 10.3 %copy-start.1 = (bf16[512,512]{1,0:T(8,128)(2,1)S(1)}, bf16[512,512]{1,0:T(8,128)(2,1)}, u32[]{:S(2)}) copy-start(bf16[512,512]{1,0:T(8,128)(2,1)} %w_first.1) | copy-start | bytes 1572868
  40.0 7.4 %collective-permute-start.15 = (bf16[512,128]{1,0:T(8,128)(2,1)S(1)}, bf16[512,128]{1,0:T(8,128)(2,1)S(1)}, u32[]{:S(2)}, u32[]{:S(2)}) collective-permute-start(bf16[512,128]{1,0:T(8,128)(2,1)S(1)} %shard_map.123.p0), channel_id=1, source_target_pairs={{0,6},{1,7},{2,4},{3,5},{4,2},{5,3},{6,0},{7,1},{8,14},{9,15},{10,... | collective-permute-start | bytes 393224 | tf_op jit(solution)/shard_map/ppermute | solution.py:105
  40.6 9.6 %collective-permute-start.14 = (bf16[512,128]{1,0:T(8,128)(2,1)S(1)}, bf16[512,128]{1,0:T(8,128)(2,1)S(1)}, u32[]{:S(2)}, u32[]{:S(2)}) collective-permute-start(bf16[512,128]{1,0:T(8,128)(2,1)S(1)} %shard_map.123.p0), channel_id=1, source_target_pairs={{0,4},{1,5},{2,6},{3,7},{4,0},{5,1},{6,2},{7,3},{8,12},{9,13},{10,... | collective-permute-start | bytes 393224 | tf_op jit(solution)/shard_map/ppermute | solution.py:105
  42.0 8.2 %collective-permute-start.13 = (bf16[512,128]{1,0:T(8,128)(2,1)S(1)}, bf16[512,128]{1,0:T(8,128)(2,1)S(1)}, u32[]{:S(2)}, u32[]{:S(2)}) collective-permute-start(bf16[512,128]{1,0:T(8,128)(2,1)S(1)} %shard_map.123.p0), channel_id=1, source_target_pairs={{0,2},{1,3},{2,0},{3,1},{4,6},{5,7},{6,4},{7,5},{8,10},{9,11},{10,... | collective-permute-start | bytes 393224 | tf_op jit(solution)/shard_map/ppermute | solution.py:105
  45.1 9.1 %copy-start = (bf16[512,512]{1,0:T(8,128)(2,1)S(1)}, bf16[512,512]{1,0:T(8,128)(2,1)}, u32[]{:S(2)}) copy-start(bf16[512,512]{1,0:T(8,128)(2,1)} %w_second.3) | copy-start | bytes 1572868
  45.1 7.8 %collective-permute-start.25 = (bf16[512,128]{1,0:T(8,128)(2,1)S(1)}, bf16[512,128]{1,0:T(8,128)(2,1)S(1)}, u32[]{:S(2)}, u32[]{:S(2)}) collective-permute-start(bf16[512,128]{1,0:T(8,128)(2,1)S(1)} %shard_map.125.p0), channel_id=1, source_target_pairs={{0,6},{1,7},{2,4},{3,5},{4,2},{5,3},{6,0},{7,1},{8,14},{9,15},{10,... | collective-permute-start | bytes 393224 | tf_op jit(solution)/shard_map/ppermute | solution.py:105
  45.7 8.5 %collective-permute-start.24 = (bf16[512,128]{1,0:T(8,128)(2,1)S(1)}, bf16[512,128]{1,0:T(8,128)(2,1)S(1)}, u32[]{:S(2)}, u32[]{:S(2)}) collective-permute-start(bf16[512,128]{1,0:T(8,128)(2,1)S(1)} %shard_map.125.p0), channel_id=1, source_target_pairs={{0,4},{1,5},{2,6},{3,7},{4,0},{5,1},{6,2},{7,3},{8,12},{9,13},{10,... | collective-permute-start | bytes 393224 | tf_op jit(solution)/shard_map/ppermute | solution.py:105
  47.3 6.9 %collective-permute-start.23 = (bf16[512,128]{1,0:T(8,128)(2,1)S(1)}, bf16[512,128]{1,0:T(8,128)(2,1)S(1)}, u32[]{:S(2)}, u32[]{:S(2)}) collective-permute-start(bf16[512,128]{1,0:T(8,128)(2,1)S(1)} %shard_map.125.p0), channel_id=1, source_target_pairs={{0,2},{1,3},{2,0},{3,1},{4,6},{5,7},{6,4},{7,5},{8,10},{9,11},{10,... | collective-permute-start | bytes 393224 | tf_op jit(solution)/shard_map/ppermute | solution.py:105
  55.0 2.3 %collective-permute-start.26 = (f32[512,128]{1,0:T(8,128)S(1)}, f32[512,128]{1,0:T(8,128)S(1)}, u32[]{:S(2)}, u32[]{:S(2)}) collective-permute-start(f32[512,128]{1,0:T(8,128)S(1)} %get-tuple-element.34), channel_id=1, source_target_pairs={{0,1},{1,0},{2,3},{3,2},{4,5},{5,4},{6,7},{7,6},{8,9},{9,8},{10,11... | collective-permute-start | bytes 786440 | tf_op jit(solution)/shard_map/ppermute | solution.py:105
  55.0 9.7 %collective-permute-start.17 = (bf16[512,128]{1,0:T(8,128)(2,1)S(1)}, bf16[512,128]{1,0:T(8,128)(2,1)S(1)}, u32[]{:S(2)}, u32[]{:S(2)}) collective-permute-start(bf16[512,128]{1,0:T(8,128)(2,1)S(1)} %get-tuple-element.29.refs_0_), channel_id=1, source_target_pairs={{0,16},{1,17},{2,18},{3,19},{4,20},{5,21},{6,22},{7,23},{8,24},{9,... | collective-permute-start | bytes 393224 | tf_op jit(solution)/shard_map/ppermute | solution.py:105
  57.3 8.2 %collective-permute-start.27 = (bf16[512,128]{1,0:T(8,128)(2,1)S(1)}, bf16[512,128]{1,0:T(8,128)(2,1)S(1)}, u32[]{:S(2)}, u32[]{:S(2)}) collective-permute-start(bf16[512,128]{1,0:T(8,128)(2,1)S(1)} %add_convert_fusion.2), channel_id=1, source_target_pairs={{0,8},{1,9},{2,10},{3,11},{4,12},{5,13},{6,14},{7,15},{8,0},{9,1},... | collective-permute-start | bytes 393224 | tf_op jit(solution)/shard_map/ppermute | solution.py:105
  59.0 10.1 %collective-permute-start.16 = (bf16[512,128]{1,0:T(8,128)(2,1)S(1)}, bf16[512,128]{1,0:T(8,128)(2,1)S(1)}, u32[]{:S(2)}, u32[]{:S(2)}) collective-permute-start(bf16[512,128]{1,0:T(8,128)(2,1)S(1)} %get-tuple-element.29.refs_0_), channel_id=1, source_target_pairs={{0,8},{1,9},{2,10},{3,11},{4,12},{5,13},{6,14},{7,15},{8,0},{9,1},... | collective-permute-start | bytes 393224 | tf_op jit(solution)/shard_map/ppermute | solution.py:105
  64.8 8.1 %collective-permute-start.18 = (bf16[512,128]{1,0:T(8,128)(2,1)S(1)}, bf16[512,128]{1,0:T(8,128)(2,1)S(1)}, u32[]{:S(2)}, u32[]{:S(2)}) collective-permute-start(bf16[512,128]{1,0:T(8,128)(2,1)S(1)} %collective-permute-done.17.refs_2_), channel_id=1, source_target_pairs={{0,8},{1,9},{2,10},{3,11},{4,12},{5,13},{6,14},{7,15},{8,0},{9,1},... | collective-permute-start | bytes 393224 | tf_op jit(solution)/shard_map/ppermute | solution.py:105
  65.6 9.2 %collective-permute-start.28 = (bf16[512,128]{1,0:T(8,128)(2,1)S(1)}, bf16[512,128]{1,0:T(8,128)(2,1)S(1)}, u32[]{:S(2)}, u32[]{:S(2)}) collective-permute-start(bf16[512,128]{1,0:T(8,128)(2,1)S(1)} %add_convert_fusion.1), channel_id=1, source_target_pairs={{0,16},{1,17},{2,18},{3,19},{4,20},{5,21},{6,22},{7,23},{8,24},{9,... | collective-permute-start | bytes 393224 | tf_op jit(solution)/shard_map/ppermute | solution.py:105
  68.5 6.3 %collective-permute-start.19 = (bf16[512,128]{1,0:T(8,128)(2,1)S(1)}, bf16[512,128]{1,0:T(8,128)(2,1)S(1)}, u32[]{:S(2)}, u32[]{:S(2)}) collective-permute-start(bf16[512,128]{1,0:T(8,128)(2,1)S(1)} %get-tuple-element.29.refs_0_), channel_id=1, source_target_pairs={{0,1},{1,0},{2,3},{3,2},{4,5},{5,4},{6,7},{7,6},{8,9},{9,8},{10,11... | collective-permute-start | bytes 393224 | tf_op jit(solution)/shard_map/ppermute | solution.py:105
  68.5 6.3 %collective-permute-start.21 = (bf16[512,128]{1,0:T(8,128)(2,1)S(1)}, bf16[512,128]{1,0:T(8,128)(2,1)S(1)}, u32[]{:S(2)}, u32[]{:S(2)}) collective-permute-start(bf16[512,128]{1,0:T(8,128)(2,1)S(1)} %collective-permute-done.17.refs_2_), channel_id=1, source_target_pairs={{0,1},{1,0},{2,3},{3,2},{4,5},{5,4},{6,7},{7,6},{8,9},{9,8},{10,11... | collective-permute-start | bytes 393224 | tf_op jit(solution)/shard_map/ppermute | solution.py:105
  69.0 5.8 %collective-permute-start.20 = (bf16[512,128]{1,0:T(8,128)(2,1)S(1)}, bf16[512,128]{1,0:T(8,128)(2,1)S(1)}, u32[]{:S(2)}, u32[]{:S(2)}) collective-permute-start(bf16[512,128]{1,0:T(8,128)(2,1)S(1)} %collective-permute-done.16.refs_1_), channel_id=1, source_target_pairs={{0,1},{1,0},{2,3},{3,2},{4,5},{5,4},{6,7},{7,6},{8,9},{9,8},{10,11... | collective-permute-start | bytes 393224 | tf_op jit(solution)/shard_map/ppermute | solution.py:105
  72.8 2.0 %collective-permute-start.22 = (bf16[512,128]{1,0:T(8,128)(2,1)S(1)}, bf16[512,128]{1,0:T(8,128)(2,1)S(1)}, u32[]{:S(2)}, u32[]{:S(2)}) collective-permute-start(bf16[512,128]{1,0:T(8,128)(2,1)S(1)} %collective-permute-done.18.refs_3_), channel_id=1, source_target_pairs={{0,1},{1,0},{2,3},{3,2},{4,5},{5,4},{6,7},{7,6},{8,9},{9,8},{10,11... | collective-permute-start | bytes 393224 | tf_op jit(solution)/shard_map/ppermute | solution.py:105
  76.4 6.9 %collective-permute-start.29 = (bf16[640,128]{1,0:T(8,128)(2,1)S(1)}, bf16[640,128]{1,0:T(8,128)(2,1)S(1)}, u32[]{:S(2)}, u32[]{:S(2)}) collective-permute-start(bf16[640,128]{1,0:T(8,128)(2,1)S(1)} %get-tuple-element.36), channel_id=1, source_target_pairs={{0,2},{1,3},{2,0},{3,1},{4,6},{5,7},{6,4},{7,5},{8,10},{9,11},{10,... | collective-permute-start | bytes 491528 | tf_op jit(solution)/shard_map/ppermute | solution.py:105
  78.0 8.7 %collective-permute-start.30 = (bf16[640,128]{1,0:T(8,128)(2,1)S(1)}, bf16[640,128]{1,0:T(8,128)(2,1)S(1)}, u32[]{:S(2)}, u32[]{:S(2)}) collective-permute-start(bf16[640,128]{1,0:T(8,128)(2,1)S(1)} %get-tuple-element.37), channel_id=1, source_target_pairs={{0,4},{1,5},{2,6},{3,7},{4,0},{5,1},{6,2},{7,3},{8,12},{9,13},{10,... | collective-permute-start | bytes 491528 | tf_op jit(solution)/shard_map/ppermute | solution.py:105
  78.5 8.1 %collective-permute-start.31 = (bf16[640,128]{1,0:T(8,128)(2,1)S(1)}, bf16[640,128]{1,0:T(8,128)(2,1)S(1)}, u32[]{:S(2)}, u32[]{:S(2)}) collective-permute-start(bf16[640,128]{1,0:T(8,128)(2,1)S(1)} %get-tuple-element.38), channel_id=1, source_target_pairs={{0,6},{1,7},{2,4},{3,5},{4,2},{5,3},{6,0},{7,1},{8,14},{9,15},{10,... | collective-permute-start | bytes 491528 | tf_op jit(solution)/shard_map/ppermute | solution.py:105
  80.0 8.2 %collective-permute-start.32 = (bf16[640,128]{1,0:T(8,128)(2,1)S(1)}, bf16[640,128]{1,0:T(8,128)(2,1)S(1)}, u32[]{:S(2)}, u32[]{:S(2)}) collective-permute-start(bf16[640,128]{1,0:T(8,128)(2,1)S(1)} %get-tuple-element.35.p0.refs_0_), channel_id=1, source_target_pairs={{0,1},{1,0},{2,3},{3,2},{4,5},{5,4},{6,7},{7,6},{8,9},{9,8},{10,11... | collective-permute-start | bytes 491528 | tf_op jit(solution)/shard_map/ppermute | solution.py:105
  83.3 4.8 %collective-permute-start.33 = (bf16[640,128]{1,0:T(8,128)(2,1)S(1)}, bf16[640,128]{1,0:T(8,128)(2,1)S(1)}, u32[]{:S(2)}, u32[]{:S(2)}) collective-permute-start(bf16[640,128]{1,0:T(8,128)(2,1)S(1)} %collective-permute-done.29.p1.refs_1_), channel_id=1, source_target_pairs={{0,1},{1,0},{2,3},{3,2},{4,5},{5,4},{6,7},{7,6},{8,9},{9,8},{10,11... | collective-permute-start | bytes 491528 | tf_op jit(solution)/shard_map/ppermute | solution.py:105
  86.7 1.5 %collective-permute-start.34 = (bf16[640,128]{1,0:T(8,128)(2,1)S(1)}, bf16[640,128]{1,0:T(8,128)(2,1)S(1)}, u32[]{:S(2)}, u32[]{:S(2)}) collective-permute-start(bf16[640,128]{1,0:T(8,128)(2,1)S(1)} %collective-permute-done.30.p2.refs_2_), channel_id=1, source_target_pairs={{0,1},{1,0},{2,3},{3,2},{4,5},{5,4},{6,7},{7,6},{8,9},{9,8},{10,11... | collective-permute-start | bytes 491528 | tf_op jit(solution)/shard_map/ppermute | solution.py:105
  86.7 1.6 %collective-permute-start.35 = (bf16[640,128]{1,0:T(8,128)(2,1)S(1)}, bf16[640,128]{1,0:T(8,128)(2,1)S(1)}, u32[]{:S(2)}, u32[]{:S(2)}) collective-permute-start(bf16[640,128]{1,0:T(8,128)(2,1)S(1)} %collective-permute-done.31.p3.refs_3_), channel_id=1, source_target_pairs={{0,1},{1,0},{2,3},{3,2},{4,5},{5,4},{6,7},{7,6},{8,9},{9,8},{10,11... | collective-permute-start | bytes 491528 | tf_op jit(solution)/shard_map/ppermute | solution.py:105

commit v7 on v5

--- a/solution.py
+++ b/solution.py
@@ -124,14 +124,13 @@
 
 def pack_body(pos, *refs):
     tables, (features, cotangent, tiles, back_tiles) = refs[:4], refs[4:8]
-    outs, both_tiles, scalars, sems = refs[8:12], refs[12], refs[13:17], refs[17]
+    outs, tile_outs, scalars, sems = refs[8:12], refs[12:14], refs[14:18], refs[18]
     copies = [(table, scalar) for table, scalar in zip(tables, scalars)]
     for q, out in enumerate(outs):
         share = lanes_of(chip(pos) ^ q)
         copies.append((features.at[:, share], out.at[pl.ds(0, ROWS), pl.ds(0, LANES)]))
         copies.append((cotangent.at[:, share], out.at[pl.ds(0, ROWS), pl.ds(LANES, LANES)]))
-    copies.append((tiles, both_tiles.at[pl.ds(0, 2)]))
-    copies.append((back_tiles, both_tiles.at[pl.ds(2, 2)]))
+    copies += [(tiles, tile_outs[0]), (back_tiles, tile_outs[1])]
     copies = [pltpu.make_async_copy(a, b, sems.at[i]) for i, (a, b) in enumerate(copies)]
     for copy in copies:
         copy.start()
@@ -154,12 +153,13 @@
         copy.wait()
 
 
-def pack(pos, columns, counts, back_columns, back_counts, features, cotangent, tiles, back_tiles):
+def pack(pos, *operands):
+    operands = [pltpu.with_memory_space_constraint(operand, pltpu.HBM) for operand in operands]
+    tile_shape = jax.ShapeDtypeStruct((2, BLOCK, SLOTS * BLOCK), BF16)
     return call(
         pack_body,
-        (shaped(ROWS + 16, 2 * LANES),) * QUAD
-        + (jax.ShapeDtypeStruct((4, BLOCK, SLOTS * BLOCK), BF16),),
-        (pos, columns, counts, back_columns, back_counts, features, cotangent, tiles, back_tiles),
+        (shaped(ROWS + 16, 2 * LANES),) * QUAD + (tile_shape,) * 2,
+        (pos, *operands),
         [SMEM] + [HBM] * 8,
         [pltpu.SMEM((2, SLOTS), jnp.int32), pltpu.SMEM((2,), jnp.int32)] * 2
         + [pltpu.SemaphoreType.DMA((14,))],
@@ -186,7 +186,20 @@
     )
 
 
-def mix_rows(base, half, places, shares, tiles, table, picked, store):
+def join_body(t0, t1, t2, t3, first, second):
+    for i, tile in enumerate((t0, t1, t2, t3)):
+        (first, second)[i // 2][pl.ds(2 * (i % 2), 2)] = tile[...]
+
+
+def join(tiles):
+    shape = jax.ShapeDtypeStruct((4, BLOCK, SLOTS * BLOCK), BF16)
+    return call(join_body, (shape, shape), tiles, [VMEM] * 4)
+
+
+X_THEN_Y, Y_THEN_X = (0, 1, 2, 3), (0, 2, 1, 3)
+
+
+def mix_rows(base, half, order, places, shares, tiles, table, picked, store):
     for i, share in enumerate(shares):
         table[pl.ds(i * SPAN, SPAN), :] = share[:, pl.ds(half * LANES, LANES)]
     table[DEVICES * ROWS :, :] = jnp.zeros((BLOCK, LANES), BF16)
@@ -196,7 +209,8 @@
             for s in range(SLOTS):
                 first = pl.multiple_of(places[q * 8 + base + w, s] * BLOCK, BLOCK)
                 picked[row, pl.ds(s * BLOCK, BLOCK), :] = table[pl.ds(first, BLOCK), :]
-            total = jnp.dot(tiles[q][base + w], picked[row], preferred_element_type=F32)
+            tile = tiles[order[q] // 2][2 * (order[q] % 2) + w]
+            total = jnp.dot(tile, picked[row], preferred_element_type=F32)
             total = total + table[pl.ds(row * BLOCK, BLOCK), :].astype(F32)
             store(q, w, total.astype(BF16))
 
@@ -207,28 +221,28 @@
 )
 
 
-def mix_body(base, half, places, *refs):
-    shares, tiles, (out, table, picked) = refs[:8], refs[8:12], refs[12:]
+def mix_body(base, half, order, places, *refs):
+    shares, tiles, (out, table, picked) = refs[:8], refs[8:10], refs[10:]
 
     def store(q, w, rows):
         out[pl.ds(q * ROWS + w * BLOCK, BLOCK), :] = rows
 
-    mix_rows(base, half, places, shares, tiles, table, picked, store)
-
-
-def mix(places, base, half, shares, tiles):
-    return call(
-        functools.partial(mix_body, base, half),
+    mix_rows(base, half, order, places, shares, tiles, table, picked, store)
+
+
+def mix(places, base, half, order, shares, tiles):
+    return call(
+        functools.partial(mix_body, base, half, order),
         shaped(SPAN, LANES),
         (places, *shares, *tiles),
-        [SMEM] + [VMEM] * 12,
+        [SMEM] + [VMEM] * 10,
         MIX_SCRATCH,
     )
 
 
 def mix_beside_body(places, *refs):
-    shares, tiles, total = refs[:8], refs[8:12], refs[12]
-    outs, (table, picked) = refs[13:17], refs[17:]
+    shares, tiles, total = refs[:8], refs[8:10], refs[10]
+    outs, (table, picked) = refs[11:15], refs[15:]
     extent = total.shape[0]
     for out in outs:
         out[:extent, :] = total[...]
@@ -236,7 +250,7 @@
     def store(q, w, rows):
         outs[q][pl.ds(extent + w * BLOCK, BLOCK), :] = rows
 
-    mix_rows(0, 0, places, shares, tiles, table, picked, store)
+    mix_rows(0, 0, X_THEN_Y, places, shares, tiles, table, picked, store)
 
 
 def mix_beside(places, shares, tiles, total):
@@ -244,7 +258,7 @@
         mix_beside_body,
         (shaped(total.shape[0] + ROWS, LANES),) * QUAD,
         (places, *shares, *tiles, total),
-        [SMEM] + [VMEM] * 13,
+        [SMEM] + [VMEM] * 11,
         MIX_SCRATCH,
     )
 
@@ -382,7 +396,7 @@
     cotangent,
 ):
     pos = lax.axis_index(AXES).astype(jnp.int32).reshape(1)
-    *packed, both_tiles = pack(
+    *packed, tiles, back_tiles = pack(
         pos,
         tile_columns,
         tiles_per_row,
@@ -395,21 +409,28 @@
     )
     parts = [packed[0]] + [swap(packed[q], 2 * q) for q in range(1, QUAD)]
     share, places = unpack(pos, parts)
-    tiles = over_quad(both_tiles)
+    tiles, back_tiles = join((tiles, swap(tiles, 2), back_tiles, swap(back_tiles, 4)))
+    tiles = (tiles, swap(tiles, 4))
+    back_tiles = (back_tiles, swap(back_tiles, 2))
 
     def everywhere(own):
         planes = over_planes(own)
         return planes + [swap(plane, CORE) for plane in planes]
 
     shares = everywhere(share)
-    mixed_share = mix(places, 0, 0, shares, tiles)
-    spread_share = mix(places, 2, 1, shares, tiles)
+    mixed_share = mix(places, 0, 0, X_THEN_Y, shares, tiles)
+    spread_share = mix(places, 2, 1, Y_THEN_X, shares, back_tiles)
     mixed, hidden, hidden_share, slope = first_layer(pos, over_quad(mixed_share), w_first)
+    by_one, by_two = swap(hidden_share, 8), swap(hidden_share, 16)
     keep, send = gradients(pos, mixed, hidden, slope, over_quad(spread_share), w_second)
     total = (keep + swap(send, CORE)).astype(BF16)
-    for mask in (8, 16):
-        total = (total.astype(F32) + swap(total, mask).astype(F32)).astype(BF16)
-    beside = mix_beside(places, everywhere(hidden_share), tiles, total)
+    across = swap(total, 8)
+    total = (total.astype(F32) + across.astype(F32)).astype(BF16)
+    by_two, _ = lax.optimization_barrier((by_two, across))
+    planes = [hidden_share, by_one, by_two, swap(by_two, 8)]
+    total = (total.astype(F32) + swap(total, 16).astype(F32)).astype(BF16)
+    planes += [swap(plane, CORE) for plane in planes]
+    beside = mix_beside(places, planes, tiles, total)
     mine = [beside[0]] + [swap(beside[q], 2 * q) for q in range(1, QUAD)]
     z_out = second_layer(pos, mine, w_second)
     grad_first, grad_second = place(pos, mine, [swap(piece, CORE) for piece in mine])

time: 94 us -> 87 us (0.926)
  waiting for transfers between devices: 46.3 us -> 41.6 us
  local copies, waits for them, and re-layouts: 4.4 us -> 0.01 us
  starting transfers between devices: 32.6 us -> 34.3 us
    ppermute x36 -> x37, waiting for transfers between devices: 46.3 us -> 41.6 us  [swap(): return lax.ppermute(value, AXES, [(i, i ^ mask) for i in range(DEVICES)])]
    unnamed x20 -> x4, local copies, waits for them, and re-layouts: 4.4 us -> 0.01 us
    ppermute x36 -> x37, starting transfers between devices: 32.6 us -> 34.3 us  [swap(): return lax.ppermute(value, AXES, [(i, i ^ mask) for i in range(DEVICES)])]
    pallas_call x9 -> x10, Pallas kernels: 9.56 us -> 10.1 us  [call(): pl.pallas_call(body, out_shape=out_shape, in_specs=list(spaces), out_spec...]
  transfers between devices with their start and end apart: 36 -> 37, of which waited for: 18 -> 16; matrix products, arithmetic and copies ran while one was open for 0% -> 0% of each run, Pallas kernels for 4% -> 6%
where the time goes in v7:
time: 87 us; the launch traced here: 86.9 us
  waiting for transfers between devices  41.6 us (48%)
  starting transfers between devices  34.3 us (39%)
  Pallas kernels  10.1 us (12%)
    ppermute x37, waiting for transfers between devices, swap(): return lax.ppermute(value, AXES, [(i, i ^ mask) for i in range(DEVICES)])  41.6 us
    ppermute x37, starting transfers between devices, swap(): return lax.ppermute(value, AXES, [(i, i ^ mask) for i in range(DEVICES)])  34.3 us
    pallas_call x10, Pallas kernels, call(): pl.pallas_call(body, out_shape=out_shape, in_specs=list(spaces), out_spec...  10.1 us
  transfers between devices with their start and end apart: 37, of which 16 were waited for; matrix products, arithmetic and copies ran while one was open for 0% of the time, Pallas kernels for 6%

profile of v7, /device:TPU:0, one launch (start us, length us, event | category | flops | bytes accessed | tf_op | source)
XLA Modules:
  0.0 86.9 jit_solution(4008382139773744887)
XLA Ops:
  0.6 1.3 %shard_map.121 = (bf16[144,256]{1,0:T(8,128)(2,1)S(1)}, bf16[144,256]{1,0:T(8,128)(2,1)S(1)}, bf16[144,256]{1,0:T(8,128)(2,1)S(1)}, bf16[144,256]{1,0:T(8,128)(2...) custom-call(s32[1]{0:T(128)} %bitcast.pos, s32[2,16]{1,0:T(2,128)} %refs_0_.1, s32[2]{0:T(128)} %refs_1_.1, ...), custom_call_target="tpu_custom_call" | custom-call | tf_op jit(solution)/shard_map/pallas_call | solution.py:90
  2.0 3.0 %collective-permute-start = (bf16[144,256]{1,0:T(8,128)(2,1)S(1)}, bf16[144,256]{1,0:T(8,128)(2,1)S(1)}, u32[]{:S(2)}, u32[]{:S(2)}) collective-permute-start(bf16[144,256]{1,0:T(8,128)(2,1)S(1)} %get-tuple-element.27), channel_id=1, source_target_pairs={{0,2},{1,3},{2,0},{3,1},{4,6},{5,7},{6,4},{7,5},{8,10},{9,11},{10,... | collective-permute-start | bytes 221192 | tf_op jit(solution)/shard_map/ppermute | solution.py:105
  5.0 1.5 %collective-permute-start.1 = (bf16[144,256]{1,0:T(8,128)(2,1)S(1)}, bf16[144,256]{1,0:T(8,128)(2,1)S(1)}, u32[]{:S(2)}, u32[]{:S(2)}) collective-permute-start(bf16[144,256]{1,0:T(8,128)(2,1)S(1)} %get-tuple-element.28), channel_id=1, source_target_pairs={{0,4},{1,5},{2,6},{3,7},{4,0},{5,1},{6,2},{7,3},{8,12},{9,13},{10,... | collective-permute-start | bytes 221192 | tf_op jit(solution)/shard_map/ppermute | solution.py:105
  6.5 1.9 %collective-permute-start.10 = (bf16[2,64,1024]{2,1,0:T(8,128)(2,1)S(1)}, bf16[2,64,1024]{2,1,0:T(8,128)(2,1)S(1)}, u32[]{:S(2)}, u32[]{:S(2)}) collective-permute-start(bf16[2,64,1024]{2,1,0:T(8,128)(2,1)S(1)} %get-tuple-element.32.t0), channel_id=1, source_target_pairs={{0,2},{1,3},{2,0},{3,1},{4,6},{5,7},{6,4},{7,5},{8,10},{9,11},{10,... | collective-permute-start | bytes 786440 | tf_op jit(solution)/shard_map/ppermute | solution.py:105
  8.5 1.5 %collective-permute-start.11 = (bf16[2,64,1024]{2,1,0:T(8,128)(2,1)S(1)}, bf16[2,64,1024]{2,1,0:T(8,128)(2,1)S(1)}, u32[]{:S(2)}, u32[]{:S(2)}) collective-permute-start(bf16[2,64,1024]{2,1,0:T(8,128)(2,1)S(1)} %get-tuple-element.33.t2), channel_id=1, source_target_pairs={{0,4},{1,5},{2,6},{3,7},{4,0},{5,1},{6,2},{7,3},{8,12},{9,13},{10,... | collective-permute-start | bytes 786440 | tf_op jit(solution)/shard_map/ppermute | solution.py:105
  10.0 2.6 %collective-permute-done.2.refs_3_ = bf16[144,256]{1,0:T(8,128)(2,1)S(1)} collective-permute-done((bf16[144,256]{1,0:T(8,128)(2,1)S(1)}, bf16[144,256]{1,0:T(8,128)(2,1)S(1)}, u32[]{:S(2)}, u32[]{:S(2)}) %collective-permute-start.2) | collective-permute-done | bytes 73760 | tf_op jit(solution)/shard_map/ppermute | solution.py:105
  12.6 2.7 %collective-permute-start.4 = (bf16[512,256]{1,0:T(8,128)(2,1)S(1)}, bf16[512,256]{1,0:T(8,128)(2,1)S(1)}, u32[]{:S(2)}, u32[]{:S(2)}) collective-permute-start(bf16[512,256]{1,0:T(8,128)(2,1)S(1)} %get-tuple-element.31.refs_0_), channel_id=1, source_target_pairs={{0,16},{1,17},{2,18},{3,19},{4,20},{5,21},{6,22},{7,23},{8,24},{9,... | collective-permute-start | bytes 786440 | tf_op jit(solution)/shard_map/ppermute | solution.py:105
  15.3 1.6 %collective-permute-start.3 = (bf16[512,256]{1,0:T(8,128)(2,1)S(1)}, bf16[512,256]{1,0:T(8,128)(2,1)S(1)}, u32[]{:S(2)}, u32[]{:S(2)}) collective-permute-start(bf16[512,256]{1,0:T(8,128)(2,1)S(1)} %get-tuple-element.31.refs_0_), channel_id=1, source_target_pairs={{0,8},{1,9},{2,10},{3,11},{4,12},{5,13},{6,14},{7,15},{8,0},{9,1},... | collective-permute-start | bytes 786440 | tf_op jit(solution)/shard_map/ppermute | solution.py:105
  16.9 0.9 %collective-permute-start.12 = (bf16[4,64,1024]{2,1,0:T(8,128)(2,1)S(1)}, bf16[4,64,1024]{2,1,0:T(8,128)(2,1)S(1)}, u32[]{:S(2)}, u32[]{:S(2)}) collective-permute-start(bf16[4,64,1024]{2,1,0:T(8,128)(2,1)S(1)} %get-tuple-element.34.refs_8_), channel_id=1, source_target_pairs={{0,4},{1,5},{2,6},{3,7},{4,0},{5,1},{6,2},{7,3},{8,12},{9,13},{10,... | collective-permute-start | bytes 1572872 | tf_op jit(solution)/shard_map/ppermute | solution.py:105
  17.9 7.0 %collective-permute-done.4.refs_2_ = bf16[512,256]{1,0:T(8,128)(2,1)S(1)} collective-permute-done((bf16[512,256]{1,0:T(8,128)(2,1)S(1)}, bf16[512,256]{1,0:T(8,128)(2,1)S(1)}, u32[]{:S(2)}, u32[]{:S(2)}) %collective-permute-start.4) | collective-permute-done | bytes 262176 | tf_op jit(solution)/shard_map/ppermute | solution.py:105
  24.9 0.6 collective-permute-start.5
  25.5 1.0 %collective-permute-start.18 = (bf16[4,64,1024]{2,1,0:T(8,128)(2,1)S(1)}, bf16[4,64,1024]{2,1,0:T(8,128)(2,1)S(1)}, u32[]{:S(2)}, u32[]{:S(2)}) collective-permute-start(bf16[4,64,1024]{2,1,0:T(8,128)(2,1)S(1)} %get-tuple-element.39.refs_8_), channel_id=1, source_target_pairs={{0,2},{1,3},{2,0},{3,1},{4,6},{5,7},{6,4},{7,5},{8,10},{9,11},{10,... | collective-permute-start | bytes 1572872 | tf_op jit(solution)/shard_map/ppermute | solution.py:105
  26.6 1.4 %collective-permute-done.3.refs_1_ = bf16[512,256]{1,0:T(8,128)(2,1)S(1)} collective-permute-done((bf16[512,256]{1,0:T(8,128)(2,1)S(1)}, bf16[512,256]{1,0:T(8,128)(2,1)S(1)}, u32[]{:S(2)}, u32[]{:S(2)}) %collective-permute-start.3) | collective-permute-done | bytes 262176 | tf_op jit(solution)/shard_map/ppermute | solution.py:105
  27.9 5.4 %collective-permute-done.5.refs_3_ = bf16[512,256]{1,0:T(8,128)(2,1)S(1)} collective-permute-done((bf16[512,256]{1,0:T(8,128)(2,1)S(1)}, bf16[512,256]{1,0:T(8,128)(2,1)S(1)}, u32[]{:S(2)}, u32[]{:S(2)}) %collective-permute-start.5) | collective-permute-done | bytes 262176 | tf_op jit(solution)/shard_map/ppermute | solution.py:105
  33.4 1.5 %collective-permute-done.9.refs_7_ = bf16[512,256]{1,0:T(8,128)(2,1)S(1)} collective-permute-done((bf16[512,256]{1,0:T(8,128)(2,1)S(1)}, bf16[512,256]{1,0:T(8,128)(2,1)S(1)}, u32[]{:S(2)}, u32[]{:S(2)}) %collective-permute-start.9) | collective-permute-done | bytes 262176 | tf_op jit(solution)/shard_map/ppermute | solution.py:105
  34.9 1.6 %shard_map.124.p0 = bf16[512,128]{1,0:T(8,128)(2,1)S(1)} custom-call(s32[32,128]{1,0:T(8,128)S(1)} %get-tuple-element.30.places, bf16[512,256]{1,0:T(8,128)(2,1)S(1)} %get-tuple-element.31.refs_0_, bf16[512,256]{1,0:T(8,128)(2,1)S(1)} %collective-permute-done.3.refs_1_, bf16[512,256]{1,0:T(8,128)(2,1)S(1)} %collective-permute-done.4.refs_2_, ...), custom_call_target="tpu_custom_call" | custom-call | tf_op jit(solution)/shard_map/pallas_call | solution.py:90
  36.5 1.0 %collective-permute-start.15 = (bf16[512,128]{1,0:T(8,128)(2,1)S(1)}, bf16[512,128]{1,0:T(8,128)(2,1)S(1)}, u32[]{:S(2)}, u32[]{:S(2)}) collective-permute-start(bf16[512,128]{1,0:T(8,128)(2,1)S(1)} %shard_map.124.p0), channel_id=1, source_target_pairs={{0,6},{1,7},{2,4},{3,5},{4,2},{5,3},{6,0},{7,1},{8,14},{9,15},{10,... | collective-permute-start | bytes 393224 | tf_op jit(solution)/shard_map/ppermute | solution.py:105
  37.5 1.5 %collective-permute-start.14 = (bf16[512,128]{1,0:T(8,128)(2,1)S(1)}, bf16[512,128]{1,0:T(8,128)(2,1)S(1)}, u32[]{:S(2)}, u32[]{:S(2)}) collective-permute-start(bf16[512,128]{1,0:T(8,128)(2,1)S(1)} %shard_map.124.p0), channel_id=1, source_target_pairs={{0,4},{1,5},{2,6},{3,7},{4,0},{5,1},{6,2},{7,3},{8,12},{9,13},{10,... | collective-permute-start | bytes 393224 | tf_op jit(solution)/shard_map/ppermute | solution.py:105
  39.0 1.0 %collective-permute-start.13 = (bf16[512,128]{1,0:T(8,128)(2,1)S(1)}, bf16[512,128]{1,0:T(8,128)(2,1)S(1)}, u32[]{:S(2)}, u32[]{:S(2)}) collective-permute-start(bf16[512,128]{1,0:T(8,128)(2,1)S(1)} %shard_map.124.p0), channel_id=1, source_target_pairs={{0,2},{1,3},{2,0},{3,1},{4,6},{5,7},{6,4},{7,5},{8,10},{9,11},{10,... | collective-permute-start | bytes 393224 | tf_op jit(solution)/shard_map/ppermute | solution.py:105
  40.0 1.6 %shard_map.126.p0 = bf16[512,128]{1,0:T(8,128)(2,1)S(1)} custom-call(s32[32,128]{1,0:T(8,128)S(1)} %get-tuple-element.30.places, bf16[512,256]{1,0:T(8,128)(2,1)S(1)} %get-tuple-element.31.refs_0_, bf16[512,256]{1,0:T(8,128)(2,1)S(1)} %collective-permute-done.3.refs_1_, bf16[512,256]{1,0:T(8,128)(2,1)S(1)} %collective-permute-done.4.refs_2_, ...), custom_call_target="tpu_custom_call" | custom-call | tf_op jit(solution)/shard_map/pallas_call | solution.py:90
  41.6 1.0 %collective-permute-start.21 = (bf16[512,128]{1,0:T(8,128)(2,1)S(1)}, bf16[512,128]{1,0:T(8,128)(2,1)S(1)}, u32[]{:S(2)}, u32[]{:S(2)}) collective-permute-start(bf16[512,128]{1,0:T(8,128)(2,1)S(1)} %shard_map.126.p0), channel_id=1, source_target_pairs={{0,6},{1,7},{2,4},{3,5},{4,2},{5,3},{6,0},{7,1},{8,14},{9,15},{10,... | collective-permute-start | bytes 393224 | tf_op jit(solution)/shard_map/ppermute | solution.py:105
  42.7 1.5 %collective-permute-start.20 = (bf16[512,128]{1,0:T(8,128)(2,1)S(1)}, bf16[512,128]{1,0:T(8,128)(2,1)S(1)}, u32[]{:S(2)}, u32[]{:S(2)}) collective-permute-start(bf16[512,128]{1,0:T(8,128)(2,1)S(1)} %shard_map.126.p0), channel_id=1, source_target_pairs={{0,4},{1,5},{2,6},{3,7},{4,0},{5,1},{6,2},{7,3},{8,12},{9,13},{10,... | collective-permute-start | bytes 393224 | tf_op jit(solution)/shard_map/ppermute | solution.py:105
  44.2 1.0 %collective-permute-start.19 = (bf16[512,128]{1,0:T(8,128)(2,1)S(1)}, bf16[512,128]{1,0:T(8,128)(2,1)S(1)}, u32[]{:S(2)}, u32[]{:S(2)}) collective-permute-start(bf16[512,128]{1,0:T(8,128)(2,1)S(1)} %shard_map.126.p0), channel_id=1, source_target_pairs={{0,2},{1,3},{2,0},{3,1},{4,6},{5,7},{6,4},{7,5},{8,10},{9,11},{10,... | collective-permute-start | bytes 393224 | tf_op jit(solution)/shard_map/ppermute | solution.py:105
  45.2 1.5 %collective-permute-done.14.p2 = bf16[512,128]{1,0:T(8,128)(2,1)S(1)} collective-permute-done((bf16[512,128]{1,0:T(8,128)(2,1)S(1)}, bf16[512,128]{1,0:T(8,128)(2,1)S(1)}, u32[]{:S(2)}, u32[]{:S(2)}) %collective-permute-start.14) | collective-permute-done | bytes 131104 | tf_op jit(solution)/shard_map/ppermute | solution.py:105
  46.7 0.8 shard_map.125
  47.4 2.0 %collective-permute-done.21.p3 = bf16[512,128]{1,0:T(8,128)(2,1)S(1)} collective-permute-done((bf16[512,128]{1,0:T(8,128)(2,1)S(1)}, bf16[512,128]{1,0:T(8,128)(2,1)S(1)}, u32[]{:S(2)}, u32[]{:S(2)}) %collective-permute-start.21) | collective-permute-done | bytes 131104 | tf_op jit(solution)/shard_map/ppermute | solution.py:105
  49.5 1.7 %collective-permute-done.20.p2 = bf16[512,128]{1,0:T(8,128)(2,1)S(1)} collective-permute-done((bf16[512,128]{1,0:T(8,128)(2,1)S(1)}, bf16[512,128]{1,0:T(8,128)(2,1)S(1)}, u32[]{:S(2)}, u32[]{:S(2)}) %collective-permute-start.20) | collective-permute-done | bytes 131104 | tf_op jit(solution)/shard_map/ppermute | solution.py:105
  51.2 0.7 shard_map.127
  52.0 1.7 %collective-permute-start.17 = (bf16[512,128]{1,0:T(8,128)(2,1)S(1)}, bf16[512,128]{1,0:T(8,128)(2,1)S(1)}, u32[]{:S(2)}, u32[]{:S(2)}) collective-permute-start(bf16[512,128]{1,0:T(8,128)(2,1)S(1)} %get-tuple-element.35.refs_0_), channel_id=1, source_target_pairs={{0,16},{1,17},{2,18},{3,19},{4,20},{5,21},{6,22},{7,23},{8,24},{9,... | collective-permute-start | bytes 393224 | tf_op jit(solution)/shard_map/ppermute | solution.py:105
  53.7 2.0 %collective-permute-start.23 = (bf16[512,128]{1,0:T(8,128)(2,1)S(1)}, bf16[512,128]{1,0:T(8,128)(2,1)S(1)}, u32[]{:S(2)}, u32[]{:S(2)}) collective-permute-start(bf16[512,128]{1,0:T(8,128)(2,1)S(1)} %add_convert_fusion.2), channel_id=1, source_target_pairs={{0,8},{1,9},{2,10},{3,11},{4,12},{5,13},{6,14},{7,15},{8,0},{9,1},... | collective-permute-start | bytes 393224 | tf_op jit(solution)/shard_map/ppermute | solution.py:105
  55.8 5.9 %collective-permute-done.17.refs_2_ = bf16[512,128]{1,0:T(8,128)(2,1)S(1)} collective-permute-done((bf16[512,128]{1,0:T(8,128)(2,1)S(1)}, bf16[512,128]{1,0:T(8,128)(2,1)S(1)}, u32[]{:S(2)}, u32[]{:S(2)}) %collective-permute-start.17) | collective-permute-done | bytes 131104 | tf_op jit(solution)/shard_map/ppermute | solution.py:105
  61.7 0.7 collective-permute-done.23
  62.5 0.4 collective-permute-start.24
  62.9 3.5 %collective-permute-start.29 = (bf16[512,128]{1,0:T(8,128)(2,1)S(1)}, bf16[512,128]{1,0:T(8,128)(2,1)S(1)}, u32[]{:S(2)}, u32[]{:S(2)}) collective-permute-start(bf16[512,128]{1,0:T(8,128)(2,1)S(1)} %add_convert_fusion.1), channel_id=1, source_target_pairs={{0,16},{1,17},{2,18},{3,19},{4,20},{5,21},{6,22},{7,23},{8,24},{9,... | collective-permute-start | bytes 393224 | tf_op jit(solution)/shard_map/ppermute | solution.py:105
  66.4 0.5 collective-permute-start.26
  66.9 3.1 %collective-permute-done.24.refs_3_ = bf16[512,128]{1,0:T(8,128)(2,1)S(1)} collective-permute-done((bf16[512,128]{1,0:T(8,128)(2,1)S(1)}, bf16[512,128]{1,0:T(8,128)(2,1)S(1)}, u32[]{:S(2)}, u32[]{:S(2)}) %collective-permute-start.24) | collective-permute-done | bytes 131104 | tf_op jit(solution)/shard_map/ppermute | solution.py:105
  70.0 1.2 %collective-permute-done.29 = bf16[512,128]{1,0:T(8,128)(2,1)S(1)} collective-permute-done((bf16[512,128]{1,0:T(8,128)(2,1)S(1)}, bf16[512,128]{1,0:T(8,128)(2,1)S(1)}, u32[]{:S(2)}, u32[]{:S(2)}) %collective-permute-start.29) | collective-permute-done | bytes 131104 | tf_op jit(solution)/shard_map/ppermute | solution.py:105
  71.3 0.1 collective-permute-done.28.refs_7_
  71.4 1.6 %shard_map.128 = (bf16[640,128]{1,0:T(8,128)(2,1)S(1)}, bf16[640,128]{1,0:T(8,128)(2,1)S(1)}, bf16[640,128]{1,0:T(8,128)(2,1)S(1)}, bf16[640,128]{1,0:T(8,128)(2,1)S(1)}) custom-call(s32[32,128]{1,0:T(8,128)S(1)} %get-tuple-element.30.places, bf16[512,128]{1,0:T(8,128)(2,1)S(1)} %get-tuple-element.35.refs_0_, ...), custom_call_target="tpu_custom_call" | custom-call | tf_op jit(solution)/shard_map/pallas_call | solution.py:90
  72.9 1.5 %collective-permute-start.30 = (bf16[640,128]{1,0:T(8,128)(2,1)S(1)}, bf16[640,128]{1,0:T(8,128)(2,1)S(1)}, u32[]{:S(2)}, u32[]{:S(2)}) collective-permute-start(bf16[640,128]{1,0:T(8,128)(2,1)S(1)} %get-tuple-element.44), channel_id=1, source_target_pairs={{0,2},{1,3},{2,0},{3,1},{4,6},{5,7},{6,4},{7,5},{8,10},{9,11},{10,... | collective-permute-start | bytes 491528 | tf_op jit(solution)/shard_map/ppermute | solution.py:105
  74.4 0.7 collective-permute-start.31
  75.1 1.3 %collective-permute-start.32 = (bf16[640,128]{1,0:T(8,128)(2,1)S(1)}, bf16[640,128]{1,0:T(8,128)(2,1)S(1)}, u32[]{:S(2)}, u32[]{:S(2)}) collective-permute-start(bf16[640,128]{1,0:T(8,128)(2,1)S(1)} %get-tuple-element.46), channel_id=1, source_target_pairs={{0,6},{1,7},{2,4},{3,5},{4,2},{5,3},{6,0},{7,1},{8,14},{9,15},{10,... | collective-permute-start | bytes 491528 | tf_op jit(solution)/shard_map/ppermute | solution.py:105
  76.5 3.6 %collective-permute-done.30.p1.refs_1_ = bf16[640,128]{1,0:T(8,128)(2,1)S(1)} collective-permute-done((bf16[640,128]{1,0:T(8,128)(2,1)S(1)}, bf16[640,128]{1,0:T(8,128)(2,1)S(1)}, u32[]{:S(2)}, u32[]{:S(2)}) %collective-permute-start.30) | collective-permute-done | bytes 163872 | tf_op jit(solution)/shard_map/ppermute | solution.py:105
  80.0 3.6 %collective-permute-done.31.p2.refs_2_ = bf16[640,128]{1,0:T(8,128)(2,1)S(1)} collective-permute-done((bf16[640,128]{1,0:T(8,128)(2,1)S(1)}, bf16[640,128]{1,0:T(8,128)(2,1)S(1)}, u32[]{:S(2)}, u32[]{:S(2)}) %collective-permute-start.31) | collective-permute-done | bytes 163872 | tf_op jit(solution)/shard_map/ppermute | solution.py:105
  83.7 0.5 collective-permute-start.36
  84.2 0.9 %shard_map.129 = bf16[128,512]{1,0:T(8,128)(2,1)} custom-call(s32[1]{0:T(128)} %bitcast.pos, bf16[640,128]{1,0:T(8,128)(2,1)S(1)} %get-tuple-element.43.p0.refs_0_, bf16[640,128]{1,0:T(8,128)(2,1)S(1)} %collective-permute-done.30.p1.refs_1_, bf16[640,128]{1,0:T(8,128)(2,1)S(1)} %collective-permute-done.31.p2.refs_2_, ...), custom_call_target="tpu_custom_call" | custom-call | tf_op jit(solution)/shard_map/pallas_call | solution.py:90
  85.1 0.2 collective-permute-done.36.refs_7_
  85.3 1.6 %shard_map.130 = (f32[512,512]{1,0:T(8,128)}, f32[512,512]{1,0:T(8,128)}) custom-call(s32[1]{0:T(128)} %bitcast.pos, bf16[640,128]{1,0:T(8,128)(2,1)S(1)} %get-tuple-element.43.p0.refs_0_, bf16[640,128]{1,0:T(8,128)(2,1)S(1)} %collective-permute-done.30.p1.refs_1_, bf16[640,128]{1,0:T(8,128)(2,1)S(1)} %collective-permute-done.31.p2.refs_2_, ...), custom_call_target="tpu_custom_call" | custom-call | tf_op jit(solution)/shard_map/pallas_call | solution.py:90
  (43 shorter events, 0.5 us)
Async XLA Ops:
  2.0 8.0 %collective-permute-start = (bf16[144,256]{1,0:T(8,128)(2,1)S(1)}, bf16[144,256]{1,0:T(8,128)(2,1)S(1)}, u32[]{:S(2)}, u32[]{:S(2)}) collective-permute-start(bf16[144,256]{1,0:T(8,128)(2,1)S(1)} %get-tuple-element.27), channel_id=1, source_target_pairs={{0,2},{1,3},{2,0},{3,1},{4,6},{5,7},{6,4},{7,5},{8,10},{9,11},{10,... | collective-permute-start | bytes 221192 | tf_op jit(solution)/shard_map/ppermute | solution.py:105
  5.0 5.0 %collective-permute-start.1 = (bf16[144,256]{1,0:T(8,128)(2,1)S(1)}, bf16[144,256]{1,0:T(8,128)(2,1)S(1)}, u32[]{:S(2)}, u32[]{:S(2)}) collective-permute-start(bf16[144,256]{1,0:T(8,128)(2,1)S(1)} %get-tuple-element.28), channel_id=1, source_target_pairs={{0,4},{1,5},{2,6},{3,7},{4,0},{5,1},{6,2},{7,3},{8,12},{9,13},{10,... | collective-permute-start | bytes 221192 | tf_op jit(solution)/shard_map/ppermute | solution.py:105
  6.5 6.1 %collective-permute-start.2 = (bf16[144,256]{1,0:T(8,128)(2,1)S(1)}, bf16[144,256]{1,0:T(8,128)(2,1)S(1)}, u32[]{:S(2)}, u32[]{:S(2)}) collective-permute-start(bf16[144,256]{1,0:T(8,128)(2,1)S(1)} %get-tuple-element.29), channel_id=1, source_target_pairs={{0,6},{1,7},{2,4},{3,5},{4,2},{5,3},{6,0},{7,1},{8,14},{9,15},{10,... | collective-permute-start | bytes 221192 | tf_op jit(solution)/shard_map/ppermute | solution.py:105
  6.5 10.4 %collective-permute-start.10 = (bf16[2,64,1024]{2,1,0:T(8,128)(2,1)S(1)}, bf16[2,64,1024]{2,1,0:T(8,128)(2,1)S(1)}, u32[]{:S(2)}, u32[]{:S(2)}) collective-permute-start(bf16[2,64,1024]{2,1,0:T(8,128)(2,1)S(1)} %get-tuple-element.32.t0), channel_id=1, source_target_pairs={{0,2},{1,3},{2,0},{3,1},{4,6},{5,7},{6,4},{7,5},{8,10},{9,11},{10,... | collective-permute-start | bytes 786440 | tf_op jit(solution)/shard_map/ppermute | solution.py:105
  8.5 8.4 %collective-permute-start.11 = (bf16[2,64,1024]{2,1,0:T(8,128)(2,1)S(1)}, bf16[2,64,1024]{2,1,0:T(8,128)(2,1)S(1)}, u32[]{:S(2)}, u32[]{:S(2)}) collective-permute-start(bf16[2,64,1024]{2,1,0:T(8,128)(2,1)S(1)} %get-tuple-element.33.t2), channel_id=1, source_target_pairs={{0,4},{1,5},{2,6},{3,7},{4,0},{5,1},{6,2},{7,3},{8,12},{9,13},{10,... | collective-permute-start | bytes 786440 | tf_op jit(solution)/shard_map/ppermute | solution.py:105
  12.6 12.3 %collective-permute-start.4 = (bf16[512,256]{1,0:T(8,128)(2,1)S(1)}, bf16[512,256]{1,0:T(8,128)(2,1)S(1)}, u32[]{:S(2)}, u32[]{:S(2)}) collective-permute-start(bf16[512,256]{1,0:T(8,128)(2,1)S(1)} %get-tuple-element.31.refs_0_), channel_id=1, source_target_pairs={{0,16},{1,17},{2,18},{3,19},{4,20},{5,21},{6,22},{7,23},{8,24},{9,... | collective-permute-start | bytes 786440 | tf_op jit(solution)/shard_map/ppermute | solution.py:105
  15.3 11.3 %collective-permute-start.6 = (bf16[512,256]{1,0:T(8,128)(2,1)S(1)}, bf16[512,256]{1,0:T(8,128)(2,1)S(1)}, u32[]{:S(2)}, u32[]{:S(2)}) collective-permute-start(bf16[512,256]{1,0:T(8,128)(2,1)S(1)} %get-tuple-element.31.refs_0_), channel_id=1, source_target_pairs={{0,1},{1,0},{2,3},{3,2},{4,5},{5,4},{6,7},{7,6},{8,9},{9,8},{10,11... | collective-permute-start | bytes 786440 | tf_op jit(solution)/shard_map/ppermute | solution.py:105
  15.3 12.7 %collective-permute-start.3 = (bf16[512,256]{1,0:T(8,128)(2,1)S(1)}, bf16[512,256]{1,0:T(8,128)(2,1)S(1)}, u32[]{:S(2)}, u32[]{:S(2)}) collective-permute-start(bf16[512,256]{1,0:T(8,128)(2,1)S(1)} %get-tuple-element.31.refs_0_), channel_id=1, source_target_pairs={{0,8},{1,9},{2,10},{3,11},{4,12},{5,13},{6,14},{7,15},{8,0},{9,1},... | collective-permute-start | bytes 786440 | tf_op jit(solution)/shard_map/ppermute | solution.py:105
  16.9 16.4 %collective-permute-start.12 = (bf16[4,64,1024]{2,1,0:T(8,128)(2,1)S(1)}, bf16[4,64,1024]{2,1,0:T(8,128)(2,1)S(1)}, u32[]{:S(2)}, u32[]{:S(2)}) collective-permute-start(bf16[4,64,1024]{2,1,0:T(8,128)(2,1)S(1)} %get-tuple-element.34.refs_8_), channel_id=1, source_target_pairs={{0,4},{1,5},{2,6},{3,7},{4,0},{5,1},{6,2},{7,3},{8,12},{9,13},{10,... | collective-permute-start | bytes 1572872 | tf_op jit(solution)/shard_map/ppermute | solution.py:105
  24.9 8.4 %collective-permute-start.5 = (bf16[512,256]{1,0:T(8,128)(2,1)S(1)}, bf16[512,256]{1,0:T(8,128)(2,1)S(1)}, u32[]{:S(2)}, u32[]{:S(2)}) collective-permute-start(bf16[512,256]{1,0:T(8,128)(2,1)S(1)} %collective-permute-done.4.refs_2_), channel_id=1, source_target_pairs={{0,8},{1,9},{2,10},{3,11},{4,12},{5,13},{6,14},{7,15},{8,0},{9,1},... | collective-permute-start | bytes 786440 | tf_op jit(solution)/shard_map/ppermute | solution.py:105
  25.5 14.5 %collective-permute-start.18 = (bf16[4,64,1024]{2,1,0:T(8,128)(2,1)S(1)}, bf16[4,64,1024]{2,1,0:T(8,128)(2,1)S(1)}, u32[]{:S(2)}, u32[]{:S(2)}) collective-permute-start(bf16[4,64,1024]{2,1,0:T(8,128)(2,1)S(1)} %get-tuple-element.39.refs_8_), channel_id=1, source_target_pairs={{0,2},{1,3},{2,0},{3,1},{4,6},{5,7},{6,4},{7,5},{8,10},{9,11},{10,... | collective-permute-start | bytes 1572872 | tf_op jit(solution)/shard_map/ppermute | solution.py:105
  26.5 6.8 %collective-permute-start.8 = (bf16[512,256]{1,0:T(8,128)(2,1)S(1)}, bf16[512,256]{1,0:T(8,128)(2,1)S(1)}, u32[]{:S(2)}, u32[]{:S(2)}) collective-permute-start(bf16[512,256]{1,0:T(8,128)(2,1)S(1)} %collective-permute-done.4.refs_2_), channel_id=1, source_target_pairs={{0,1},{1,0},{2,3},{3,2},{4,5},{5,4},{6,7},{7,6},{8,9},{9,8},{10,11... | collective-permute-start | bytes 786440 | tf_op jit(solution)/shard_map/ppermute | solution.py:105
  27.9 5.4 %collective-permute-start.7 = (bf16[512,256]{1,0:T(8,128)(2,1)S(1)}, bf16[512,256]{1,0:T(8,128)(2,1)S(1)}, u32[]{:S(2)}, u32[]{:S(2)}) collective-permute-start(bf16[512,256]{1,0:T(8,128)(2,1)S(1)} %collective-permute-done.3.refs_1_), channel_id=1, source_target_pairs={{0,1},{1,0},{2,3},{3,2},{4,5},{5,4},{6,7},{7,6},{8,9},{9,8},{10,11... | collective-permute-start | bytes 786440 | tf_op jit(solution)/shard_map/ppermute | solution.py:105
  33.3 1.5 %collective-permute-start.9 = (bf16[512,256]{1,0:T(8,128)(2,1)S(1)}, bf16[512,256]{1,0:T(8,128)(2,1)S(1)}, u32[]{:S(2)}, u32[]{:S(2)}) collective-permute-start(bf16[512,256]{1,0:T(8,128)(2,1)S(1)} %collective-permute-done.5.refs_3_), channel_id=1, source_target_pairs={{0,1},{1,0},{2,3},{3,2},{4,5},{5,4},{6,7},{7,6},{8,9},{9,8},{10,11... | collective-permute-start | bytes 786440 | tf_op jit(solution)/shard_map/ppermute | solution.py:105
  36.5 10.2 %copy-start.1 = (bf16[512,512]{1,0:T(8,128)(2,1)S(1)}, bf16[512,512]{1,0:T(8,128)(2,1)}, u32[]{:S(2)}) copy-start(bf16[512,512]{1,0:T(8,128)(2,1)} %w_first.1) | copy-start | bytes 1572868
  36.5 7.7 %collective-permute-start.15 = (bf16[512,128]{1,0:T(8,128)(2,1)S(1)}, bf16[512,128]{1,0:T(8,128)(2,1)S(1)}, u32[]{:S(2)}, u32[]{:S(2)}) collective-permute-start(bf16[512,128]{1,0:T(8,128)(2,1)S(1)} %shard_map.124.p0), channel_id=1, source_target_pairs={{0,6},{1,7},{2,4},{3,5},{4,2},{5,3},{6,0},{7,1},{8,14},{9,15},{10,... | collective-permute-start | bytes 393224 | tf_op jit(solution)/shard_map/ppermute | solution.py:105
  37.5 9.2 %collective-permute-start.14 = (bf16[512,128]{1,0:T(8,128)(2,1)S(1)}, bf16[512,128]{1,0:T(8,128)(2,1)S(1)}, u32[]{:S(2)}, u32[]{:S(2)}) collective-permute-start(bf16[512,128]{1,0:T(8,128)(2,1)S(1)} %shard_map.124.p0), channel_id=1, source_target_pairs={{0,4},{1,5},{2,6},{3,7},{4,0},{5,1},{6,2},{7,3},{8,12},{9,13},{10,... | collective-permute-start | bytes 393224 | tf_op jit(solution)/shard_map/ppermute | solution.py:105
  39.0 7.7 %collective-permute-start.13 = (bf16[512,128]{1,0:T(8,128)(2,1)S(1)}, bf16[512,128]{1,0:T(8,128)(2,1)S(1)}, u32[]{:S(2)}, u32[]{:S(2)}) collective-permute-start(bf16[512,128]{1,0:T(8,128)(2,1)S(1)} %shard_map.124.p0), channel_id=1, source_target_pairs={{0,2},{1,3},{2,0},{3,1},{4,6},{5,7},{6,4},{7,5},{8,10},{9,11},{10,... | collective-permute-start | bytes 393224 | tf_op jit(solution)/shard_map/ppermute | solution.py:105
  41.6 9.6 %copy-start = (bf16[512,512]{1,0:T(8,128)(2,1)S(1)}, bf16[512,512]{1,0:T(8,128)(2,1)}, u32[]{:S(2)}) copy-start(bf16[512,512]{1,0:T(8,128)(2,1)} %w_second.3) | copy-start | bytes 1572868
  41.6 7.9 %collective-permute-start.21 = (bf16[512,128]{1,0:T(8,128)(2,1)S(1)}, bf16[512,128]{1,0:T(8,128)(2,1)S(1)}, u32[]{:S(2)}, u32[]{:S(2)}) collective-permute-start(bf16[512,128]{1,0:T(8,128)(2,1)S(1)} %shard_map.126.p0), channel_id=1, source_target_pairs={{0,6},{1,7},{2,4},{3,5},{4,2},{5,3},{6,0},{7,1},{8,14},{9,15},{10,... | collective-permute-start | bytes 393224 | tf_op jit(solution)/shard_map/ppermute | solution.py:105
  42.7 8.5 %collective-permute-start.20 = (bf16[512,128]{1,0:T(8,128)(2,1)S(1)}, bf16[512,128]{1,0:T(8,128)(2,1)S(1)}, u32[]{:S(2)}, u32[]{:S(2)}) collective-permute-start(bf16[512,128]{1,0:T(8,128)(2,1)S(1)} %shard_map.126.p0), channel_id=1, source_target_pairs={{0,4},{1,5},{2,6},{3,7},{4,0},{5,1},{6,2},{7,3},{8,12},{9,13},{10,... | collective-permute-start | bytes 393224 | tf_op jit(solution)/shard_map/ppermute | solution.py:105
  44.2 7.0 %collective-permute-start.19 = (bf16[512,128]{1,0:T(8,128)(2,1)S(1)}, bf16[512,128]{1,0:T(8,128)(2,1)S(1)}, u32[]{:S(2)}, u32[]{:S(2)}) collective-permute-start(bf16[512,128]{1,0:T(8,128)(2,1)S(1)} %shard_map.126.p0), channel_id=1, source_target_pairs={{0,2},{1,3},{2,0},{3,1},{4,6},{5,7},{6,4},{7,5},{8,10},{9,11},{10,... | collective-permute-start | bytes 393224 | tf_op jit(solution)/shard_map/ppermute | solution.py:105
  51.9 1.8 %collective-permute-start.22 = (f32[512,128]{1,0:T(8,128)S(1)}, f32[512,128]{1,0:T(8,128)S(1)}, u32[]{:S(2)}, u32[]{:S(2)}) collective-permute-start(f32[512,128]{1,0:T(8,128)S(1)} %get-tuple-element.41), channel_id=1, source_target_pairs={{0,1},{1,0},{2,3},{3,2},{4,5},{5,4},{6,7},{7,6},{8,9},{9,8},{10,11... | collective-permute-start | bytes 786440 | tf_op jit(solution)/shard_map/ppermute | solution.py:105
  52.0 9.7 %collective-permute-start.17 = (bf16[512,128]{1,0:T(8,128)(2,1)S(1)}, bf16[512,128]{1,0:T(8,128)(2,1)S(1)}, u32[]{:S(2)}, u32[]{:S(2)}) collective-permute-start(bf16[512,128]{1,0:T(8,128)(2,1)S(1)} %get-tuple-element.35.refs_0_), channel_id=1, source_target_pairs={{0,16},{1,17},{2,18},{3,19},{4,20},{5,21},{6,22},{7,23},{8,24},{9,... | collective-permute-start | bytes 393224 | tf_op jit(solution)/shard_map/ppermute | solution.py:105
  53.7 8.7 %collective-permute-start.23 = (bf16[512,128]{1,0:T(8,128)(2,1)S(1)}, bf16[512,128]{1,0:T(8,128)(2,1)S(1)}, u32[]{:S(2)}, u32[]{:S(2)}) collective-permute-start(bf16[512,128]{1,0:T(8,128)(2,1)S(1)} %add_convert_fusion.2), channel_id=1, source_target_pairs={{0,8},{1,9},{2,10},{3,11},{4,12},{5,13},{6,14},{7,15},{8,0},{9,1},... | collective-permute-start | bytes 393224 | tf_op jit(solution)/shard_map/ppermute | solution.py:105
  55.8 10.6 %collective-permute-start.16 = (bf16[512,128]{1,0:T(8,128)(2,1)S(1)}, bf16[512,128]{1,0:T(8,128)(2,1)S(1)}, u32[]{:S(2)}, u32[]{:S(2)}) collective-permute-start(bf16[512,128]{1,0:T(8,128)(2,1)S(1)} %get-tuple-element.35.refs_0_), channel_id=1, source_target_pairs={{0,8},{1,9},{2,10},{3,11},{4,12},{5,13},{6,14},{7,15},{8,0},{9,1},... | collective-permute-start | bytes 393224 | tf_op jit(solution)/shard_map/ppermute | solution.py:105
  62.5 7.6 %collective-permute-start.24 = (bf16[512,128]{1,0:T(8,128)(2,1)S(1)}, bf16[512,128]{1,0:T(8,128)(2,1)S(1)}, u32[]{:S(2)}, u32[]{:S(2)}) collective-permute-start(bf16[512,128]{1,0:T(8,128)(2,1)S(1)} %collective-permute-done.17.refs_2_), channel_id=1, source_target_pairs={{0,8},{1,9},{2,10},{3,11},{4,12},{5,13},{6,14},{7,15},{8,0},{9,1},... | collective-permute-start | bytes 393224 | tf_op jit(solution)/shard_map/ppermute | solution.py:105
  62.9 8.3 %collective-permute-start.29 = (bf16[512,128]{1,0:T(8,128)(2,1)S(1)}, bf16[512,128]{1,0:T(8,128)(2,1)S(1)}, u32[]{:S(2)}, u32[]{:S(2)}) collective-permute-start(bf16[512,128]{1,0:T(8,128)(2,1)S(1)} %add_convert_fusion.1), channel_id=1, source_target_pairs={{0,16},{1,17},{2,18},{3,19},{4,20},{5,21},{6,22},{7,23},{8,24},{9,... | collective-permute-start | bytes 393224 | tf_op jit(solution)/shard_map/ppermute | solution.py:105
  66.4 4.9 %collective-permute-start.25 = (bf16[512,128]{1,0:T(8,128)(2,1)S(1)}, bf16[512,128]{1,0:T(8,128)(2,1)S(1)}, u32[]{:S(2)}, u32[]{:S(2)}) collective-permute-start(bf16[512,128]{1,0:T(8,128)(2,1)S(1)} %get-tuple-element.35.refs_0_), channel_id=1, source_target_pairs={{0,1},{1,0},{2,3},{3,2},{4,5},{5,4},{6,7},{7,6},{8,9},{9,8},{10,11... | collective-permute-start | bytes 393224 | tf_op jit(solution)/shard_map/ppermute | solution.py:105
  66.4 4.9 %collective-permute-start.26 = (bf16[512,128]{1,0:T(8,128)(2,1)S(1)}, bf16[512,128]{1,0:T(8,128)(2,1)S(1)}, u32[]{:S(2)}, u32[]{:S(2)}) collective-permute-start(bf16[512,128]{1,0:T(8,128)(2,1)S(1)} %collective-permute-done.16.refs_1_), channel_id=1, source_target_pairs={{0,1},{1,0},{2,3},{3,2},{4,5},{5,4},{6,7},{7,6},{8,9},{9,8},{10,11... | collective-permute-start | bytes 393224 | tf_op jit(solution)/shard_map/ppermute | solution.py:105
  66.9 4.4 %collective-permute-start.27 = (bf16[512,128]{1,0:T(8,128)(2,1)S(1)}, bf16[512,128]{1,0:T(8,128)(2,1)S(1)}, u32[]{:S(2)}, u32[]{:S(2)}) collective-permute-start(bf16[512,128]{1,0:T(8,128)(2,1)S(1)} %collective-permute-done.17.refs_2_), channel_id=1, source_target_pairs={{0,1},{1,0},{2,3},{3,2},{4,5},{5,4},{6,7},{7,6},{8,9},{9,8},{10,11... | collective-permute-start | bytes 393224 | tf_op jit(solution)/shard_map/ppermute | solution.py:105
  70.0 1.3 %collective-permute-start.28 = (bf16[512,128]{1,0:T(8,128)(2,1)S(1)}, bf16[512,128]{1,0:T(8,128)(2,1)S(1)}, u32[]{:S(2)}, u32[]{:S(2)}) collective-permute-start(bf16[512,128]{1,0:T(8,128)(2,1)S(1)} %collective-permute-done.24.refs_3_), channel_id=1, source_target_pairs={{0,1},{1,0},{2,3},{3,2},{4,5},{5,4},{6,7},{7,6},{8,9},{9,8},{10,11... | collective-permute-start | bytes 393224 | tf_op jit(solution)/shard_map/ppermute | solution.py:105
  72.9 7.1 %collective-permute-start.30 = (bf16[640,128]{1,0:T(8,128)(2,1)S(1)}, bf16[640,128]{1,0:T(8,128)(2,1)S(1)}, u32[]{:S(2)}, u32[]{:S(2)}) collective-permute-start(bf16[640,128]{1,0:T(8,128)(2,1)S(1)} %get-tuple-element.44), channel_id=1, source_target_pairs={{0,2},{1,3},{2,0},{3,1},{4,6},{5,7},{6,4},{7,5},{8,10},{9,11},{10,... | collective-permute-start | bytes 491528 | tf_op jit(solution)/shard_map/ppermute | solution.py:105
  74.4 9.3 %collective-permute-start.31 = (bf16[640,128]{1,0:T(8,128)(2,1)S(1)}, bf16[640,128]{1,0:T(8,128)(2,1)S(1)}, u32[]{:S(2)}, u32[]{:S(2)}) collective-permute-start(bf16[640,128]{1,0:T(8,128)(2,1)S(1)} %get-tuple-element.45), channel_id=1, source_target_pairs={{0,4},{1,5},{2,6},{3,7},{4,0},{5,1},{6,2},{7,3},{8,12},{9,13},{10,... | collective-permute-start | bytes 491528 | tf_op jit(solution)/shard_map/ppermute | solution.py:105
  75.1 8.5 %collective-permute-start.32 = (bf16[640,128]{1,0:T(8,128)(2,1)S(1)}, bf16[640,128]{1,0:T(8,128)(2,1)S(1)}, u32[]{:S(2)}, u32[]{:S(2)}) collective-permute-start(bf16[640,128]{1,0:T(8,128)(2,1)S(1)} %get-tuple-element.46), channel_id=1, source_target_pairs={{0,6},{1,7},{2,4},{3,5},{4,2},{5,3},{6,0},{7,1},{8,14},{9,15},{10,... | collective-permute-start | bytes 491528 | tf_op jit(solution)/shard_map/ppermute | solution.py:105
  76.5 8.6 %collective-permute-start.33 = (bf16[640,128]{1,0:T(8,128)(2,1)S(1)}, bf16[640,128]{1,0:T(8,128)(2,1)S(1)}, u32[]{:S(2)}, u32[]{:S(2)}) collective-permute-start(bf16[640,128]{1,0:T(8,128)(2,1)S(1)} %get-tuple-element.43.p0.refs_0_), channel_id=1, source_target_pairs={{0,1},{1,0},{2,3},{3,2},{4,5},{5,4},{6,7},{7,6},{8,9},{9,8},{10,11... | collective-permute-start | bytes 491528 | tf_op jit(solution)/shard_map/ppermute | solution.py:105
  80.0 5.1 %collective-permute-start.34 = (bf16[640,128]{1,0:T(8,128)(2,1)S(1)}, bf16[640,128]{1,0:T(8,128)(2,1)S(1)}, u32[]{:S(2)}, u32[]{:S(2)}) collective-permute-start(bf16[640,128]{1,0:T(8,128)(2,1)S(1)} %collective-permute-done.30.p1.refs_1_), channel_id=1, source_target_pairs={{0,1},{1,0},{2,3},{3,2},{4,5},{5,4},{6,7},{7,6},{8,9},{9,8},{10,11... | collective-permute-start | bytes 491528 | tf_op jit(solution)/shard_map/ppermute | solution.py:105
  83.7 1.5 %collective-permute-start.35 = (bf16[640,128]{1,0:T(8,128)(2,1)S(1)}, bf16[640,128]{1,0:T(8,128)(2,1)S(1)}, u32[]{:S(2)}, u32[]{:S(2)}) collective-permute-start(bf16[640,128]{1,0:T(8,128)(2,1)S(1)} %collective-permute-done.31.p2.refs_2_), channel_id=1, source_target_pairs={{0,1},{1,0},{2,3},{3,2},{4,5},{5,4},{6,7},{7,6},{8,9},{9,8},{10,11... | collective-permute-start | bytes 491528 | tf_op jit(solution)/shard_map/ppermute | solution.py:105
  83.7 1.6 %collective-permute-start.36 = (bf16[640,128]{1,0:T(8,128)(2,1)S(1)}, bf16[640,128]{1,0:T(8,128)(2,1)S(1)}, u32[]{:S(2)}, u32[]{:S(2)}) collective-permute-start(bf16[640,128]{1,0:T(8,128)(2,1)S(1)} %collective-permute-done.32.p3.refs_3_), channel_id=1, source_target_pairs={{0,1},{1,0},{2,3},{3,2},{4,5},{5,4},{6,7},{7,6},{8,9},{9,8},{10,11... | collective-permute-start | bytes 491528 | tf_op jit(solution)/shard_map/ppermute | solution.py:105

commit v8 on v7

--- a/solution.py
+++ b/solution.py
@@ -77,6 +77,7 @@
 
 CORE = 1
 DEVICES, QUAD, PLANES, SLOTS, BLOCK = 32, 4, 4, 16, 64
+GROUP = 8
 LANES = 128
 ROWS = 128
 SPAN = QUAD * ROWS
@@ -199,35 +200,38 @@
 X_THEN_Y, Y_THEN_X = (0, 1, 2, 3), (0, 2, 1, 3)
 
 
-def mix_rows(base, half, order, places, shares, tiles, table, picked, store):
+def mix_rows(base, half, order, places, shares, tiles, table, store):
     for i, share in enumerate(shares):
         table[pl.ds(i * SPAN, SPAN), :] = share[:, pl.ds(half * LANES, LANES)]
     table[DEVICES * ROWS :, :] = jnp.zeros((BLOCK, LANES), BF16)
     for q in range(QUAD):
         for w in range(2):
             row = q * 2 + w
-            for s in range(SLOTS):
-                first = pl.multiple_of(places[q * 8 + base + w, s] * BLOCK, BLOCK)
-                picked[row, pl.ds(s * BLOCK, BLOCK), :] = table[pl.ds(first, BLOCK), :]
-            tile = tiles[order[q] // 2][2 * (order[q] % 2) + w]
-            total = jnp.dot(tile, picked[row], preferred_element_type=F32)
-            total = total + table[pl.ds(row * BLOCK, BLOCK), :].astype(F32)
+            tile = tiles[order[q] // 2].at[2 * (order[q] % 2) + w]
+            total = table[pl.ds(row * BLOCK, BLOCK), :].astype(F32)
+            for start in range(0, SLOTS, GROUP):
+                blocks = []
+                for s in range(start, start + GROUP):
+                    first = pl.multiple_of(places[q * 8 + base + w, s] * BLOCK, BLOCK)
+                    blocks.append(table[pl.ds(first, BLOCK), :])
+                total = total + jnp.dot(
+                    tile[:, pl.ds(start * BLOCK, GROUP * BLOCK)],
+                    jnp.concatenate(blocks, axis=0),
+                    preferred_element_type=F32,
+                )
             store(q, w, total.astype(BF16))
 
 
-MIX_SCRATCH = (
-    pltpu.VMEM((DEVICES * ROWS + BLOCK, LANES), BF16),
-    pltpu.VMEM((2 * QUAD, SLOTS * BLOCK, LANES), BF16),
-)
+MIX_SCRATCH = (pltpu.VMEM((DEVICES * ROWS + BLOCK, LANES), BF16),)
 
 
 def mix_body(base, half, order, places, *refs):
-    shares, tiles, (out, table, picked) = refs[:8], refs[8:10], refs[10:]
+    shares, tiles, (out, table) = refs[:8], refs[8:10], refs[10:]
 
     def store(q, w, rows):
         out[pl.ds(q * ROWS + w * BLOCK, BLOCK), :] = rows
 
-    mix_rows(base, half, order, places, shares, tiles, table, picked, store)
+    mix_rows(base, half, order, places, shares, tiles, table, store)
 
 
 def mix(places, base, half, order, shares, tiles):
@@ -242,7 +246,7 @@
 
 def mix_beside_body(places, *refs):
     shares, tiles, total = refs[:8], refs[8:10], refs[10]
-    outs, (table, picked) = refs[11:15], refs[15:]
+    outs, table = refs[11:15], refs[15]
     extent = total.shape[0]
     for out in outs:
         out[:extent, :] = total[...]
@@ -250,7 +254,7 @@
     def store(q, w, rows):
         outs[q][pl.ds(extent + w * BLOCK, BLOCK), :] = rows
 
-    mix_rows(0, 0, X_THEN_Y, places, shares, tiles, table, picked, store)
+    mix_rows(0, 0, X_THEN_Y, places, shares, tiles, table, store)
 
 
 def mix_beside(places, shares, tiles, total):
@@ -431,7 +435,7 @@
     total = (total.astype(F32) + swap(total, 16).astype(F32)).astype(BF16)
     planes += [swap(plane, CORE) for plane in planes]
     beside = mix_beside(places, planes, tiles, total)
-    mine = [beside[0]] + [swap(beside[q], 2 * q) for q in range(1, QUAD)]
+    mine = [beside[0]] + [swap(beside[q], 2 * q) for q in (3, 2, 1)][::-1]
     z_out = second_layer(pos, mine, w_second)
     grad_first, grad_second = place(pos, mine, [swap(piece, CORE) for piece in mine])
     return (z_out, grad_first, grad_second)

time: 87 us -> 86.6 us (level)
  transfers between devices with their start and end apart: 37 -> 37, of which waited for: 16 -> 15; matrix products, arithmetic and copies ran while one was open for 0% -> 0% of each run, Pallas kernels for 6% -> 5%
where the time goes in v8:
time: 86.6 us; the launch traced here: 86.5 us
  waiting for transfers between devices  41.6 us (48%)
  starting transfers between devices  34.3 us (40%)
  Pallas kernels  9.75 us (11%)
    ppermute x37, waiting for transfers between devices, swap(): return lax.ppermute(value, AXES, [(i, i ^ mask) for i in range(DEVICES)])  41.6 us
    ppermute x37, starting transfers between devices, swap(): return lax.ppermute(value, AXES, [(i, i ^ mask) for i in range(DEVICES)])  34.3 us
    pallas_call x10, Pallas kernels, call(): pl.pallas_call(body, out_shape=out_shape, in_specs=list(spaces), out_spec...  9.75 us
  transfers between devices with their start and end apart: 37, of which 15 were waited for; matrix products, arithmetic and copies ran while one was open for 0% of the time, Pallas kernels for 5%

profile of v8, /device:TPU:0, one launch (start us, length us, event | category | flops | bytes accessed | tf_op | source)
XLA Modules:
  0.0 86.5 jit_solution(1591036680590525651)
XLA Ops:
  0.6 1.3 %shard_map.121 = (bf16[144,256]{1,0:T(8,128)(2,1)S(1)}, bf16[144,256]{1,0:T(8,128)(2,1)S(1)}, bf16[144,256]{1,0:T(8,128)(2,1)S(1)}, bf16[144,256]{1,0:T(8,128)(2...) custom-call(s32[1]{0:T(128)} %bitcast.pos, s32[2,16]{1,0:T(2,128)} %refs_0_.1, s32[2]{0:T(128)} %refs_1_.1, ...), custom_call_target="tpu_custom_call" | custom-call | tf_op jit(solution)/shard_map/pallas_call | solution.py:91
  2.0 3.0 %collective-permute-start = (bf16[144,256]{1,0:T(8,128)(2,1)S(1)}, bf16[144,256]{1,0:T(8,128)(2,1)S(1)}, u32[]{:S(2)}, u32[]{:S(2)}) collective-permute-start(bf16[144,256]{1,0:T(8,128)(2,1)S(1)} %get-tuple-element.27), channel_id=1, source_target_pairs={{0,2},{1,3},{2,0},{3,1},{4,6},{5,7},{6,4},{7,5},{8,10},{9,11},{10,... | collective-permute-start | bytes 221192 | tf_op jit(solution)/shard_map/ppermute | solution.py:106
  5.0 1.5 %collective-permute-start.1 = (bf16[144,256]{1,0:T(8,128)(2,1)S(1)}, bf16[144,256]{1,0:T(8,128)(2,1)S(1)}, u32[]{:S(2)}, u32[]{:S(2)}) collective-permute-start(bf16[144,256]{1,0:T(8,128)(2,1)S(1)} %get-tuple-element.28), channel_id=1, source_target_pairs={{0,4},{1,5},{2,6},{3,7},{4,0},{5,1},{6,2},{7,3},{8,12},{9,13},{10,... | collective-permute-start | bytes 221192 | tf_op jit(solution)/shard_map/ppermute | solution.py:106
  6.5 1.9 %collective-permute-start.10 = (bf16[2,64,1024]{2,1,0:T(8,128)(2,1)S(1)}, bf16[2,64,1024]{2,1,0:T(8,128)(2,1)S(1)}, u32[]{:S(2)}, u32[]{:S(2)}) collective-permute-start(bf16[2,64,1024]{2,1,0:T(8,128)(2,1)S(1)} %get-tuple-element.32.t0), channel_id=1, source_target_pairs={{0,2},{1,3},{2,0},{3,1},{4,6},{5,7},{6,4},{7,5},{8,10},{9,11},{10,... | collective-permute-start | bytes 786440 | tf_op jit(solution)/shard_map/ppermute | solution.py:106
  8.5 1.5 %collective-permute-start.11 = (bf16[2,64,1024]{2,1,0:T(8,128)(2,1)S(1)}, bf16[2,64,1024]{2,1,0:T(8,128)(2,1)S(1)}, u32[]{:S(2)}, u32[]{:S(2)}) collective-permute-start(bf16[2,64,1024]{2,1,0:T(8,128)(2,1)S(1)} %get-tuple-element.33.t2), channel_id=1, source_target_pairs={{0,4},{1,5},{2,6},{3,7},{4,0},{5,1},{6,2},{7,3},{8,12},{9,13},{10,... | collective-permute-start | bytes 786440 | tf_op jit(solution)/shard_map/ppermute | solution.py:106
  10.0 2.6 %collective-permute-done.2.refs_3_ = bf16[144,256]{1,0:T(8,128)(2,1)S(1)} collective-permute-done((bf16[144,256]{1,0:T(8,128)(2,1)S(1)}, bf16[144,256]{1,0:T(8,128)(2,1)S(1)}, u32[]{:S(2)}, u32[]{:S(2)}) %collective-permute-start.2) | collective-permute-done | bytes 73760 | tf_op jit(solution)/shard_map/ppermute | solution.py:106
  12.6 2.7 %collective-permute-start.4 = (bf16[512,256]{1,0:T(8,128)(2,1)S(1)}, bf16[512,256]{1,0:T(8,128)(2,1)S(1)}, u32[]{:S(2)}, u32[]{:S(2)}) collective-permute-start(bf16[512,256]{1,0:T(8,128)(2,1)S(1)} %get-tuple-element.31.refs_0_), channel_id=1, source_target_pairs={{0,16},{1,17},{2,18},{3,19},{4,20},{5,21},{6,22},{7,23},{8,24},{9,... | collective-permute-start | bytes 786440 | tf_op jit(solution)/shard_map/ppermute | solution.py:106
  15.3 1.6 %collective-permute-start.3 = (bf16[512,256]{1,0:T(8,128)(2,1)S(1)}, bf16[512,256]{1,0:T(8,128)(2,1)S(1)}, u32[]{:S(2)}, u32[]{:S(2)}) collective-permute-start(bf16[512,256]{1,0:T(8,128)(2,1)S(1)} %get-tuple-element.31.refs_0_), channel_id=1, source_target_pairs={{0,8},{1,9},{2,10},{3,11},{4,12},{5,13},{6,14},{7,15},{8,0},{9,1},... | collective-permute-start | bytes 786440 | tf_op jit(solution)/shard_map/ppermute | solution.py:106
  16.9 0.9 %collective-permute-start.12 = (bf16[4,64,1024]{2,1,0:T(8,128)(2,1)S(1)}, bf16[4,64,1024]{2,1,0:T(8,128)(2,1)S(1)}, u32[]{:S(2)}, u32[]{:S(2)}) collective-permute-start(bf16[4,64,1024]{2,1,0:T(8,128)(2,1)S(1)} %get-tuple-element.34.refs_8_), channel_id=1, source_target_pairs={{0,4},{1,5},{2,6},{3,7},{4,0},{5,1},{6,2},{7,3},{8,12},{9,13},{10,... | collective-permute-start | bytes 1572872 | tf_op jit(solution)/shard_map/ppermute | solution.py:106
  17.9 7.0 %collective-permute-done.4.refs_2_ = bf16[512,256]{1,0:T(8,128)(2,1)S(1)} collective-permute-done((bf16[512,256]{1,0:T(8,128)(2,1)S(1)}, bf16[512,256]{1,0:T(8,128)(2,1)S(1)}, u32[]{:S(2)}, u32[]{:S(2)}) %collective-permute-start.4) | collective-permute-done | bytes 262176 | tf_op jit(solution)/shard_map/ppermute | solution.py:106
  24.9 0.6 collective-permute-start.5
  25.5 1.0 %collective-permute-start.18 = (bf16[4,64,1024]{2,1,0:T(8,128)(2,1)S(1)}, bf16[4,64,1024]{2,1,0:T(8,128)(2,1)S(1)}, u32[]{:S(2)}, u32[]{:S(2)}) collective-permute-start(bf16[4,64,1024]{2,1,0:T(8,128)(2,1)S(1)} %get-tuple-element.39.refs_8_), channel_id=1, source_target_pairs={{0,2},{1,3},{2,0},{3,1},{4,6},{5,7},{6,4},{7,5},{8,10},{9,11},{10,... | collective-permute-start | bytes 1572872 | tf_op jit(solution)/shard_map/ppermute | solution.py:106
  26.6 1.4 %collective-permute-done.3.refs_1_ = bf16[512,256]{1,0:T(8,128)(2,1)S(1)} collective-permute-done((bf16[512,256]{1,0:T(8,128)(2,1)S(1)}, bf16[512,256]{1,0:T(8,128)(2,1)S(1)}, u32[]{:S(2)}, u32[]{:S(2)}) %collective-permute-start.3) | collective-permute-done | bytes 262176 | tf_op jit(solution)/shard_map/ppermute | solution.py:106
  27.9 5.4 %collective-permute-done.5.refs_3_ = bf16[512,256]{1,0:T(8,128)(2,1)S(1)} collective-permute-done((bf16[512,256]{1,0:T(8,128)(2,1)S(1)}, bf16[512,256]{1,0:T(8,128)(2,1)S(1)}, u32[]{:S(2)}, u32[]{:S(2)}) %collective-permute-start.5) | collective-permute-done | bytes 262176 | tf_op jit(solution)/shard_map/ppermute | solution.py:106
  33.4 1.5 %collective-permute-done.9.refs_7_ = bf16[512,256]{1,0:T(8,128)(2,1)S(1)} collective-permute-done((bf16[512,256]{1,0:T(8,128)(2,1)S(1)}, bf16[512,256]{1,0:T(8,128)(2,1)S(1)}, u32[]{:S(2)}, u32[]{:S(2)}) %collective-permute-start.9) | collective-permute-done | bytes 262176 | tf_op jit(solution)/shard_map/ppermute | solution.py:106
  34.9 1.4 %shard_map.124.p0 = bf16[512,128]{1,0:T(8,128)(2,1)S(1)} custom-call(s32[32,128]{1,0:T(8,128)S(1)} %get-tuple-element.30.places, bf16[512,256]{1,0:T(8,128)(2,1)S(1)} %get-tuple-element.31.refs_0_, bf16[512,256]{1,0:T(8,128)(2,1)S(1)} %collective-permute-done.3.refs_1_, bf16[512,256]{1,0:T(8,128)(2,1)S(1)} %collective-permute-done.4.refs_2_, ...), custom_call_target="tpu_custom_call" | custom-call | tf_op jit(solution)/shard_map/pallas_call | solution.py:91
  36.3 1.0 %collective-permute-start.15 = (bf16[512,128]{1,0:T(8,128)(2,1)S(1)}, bf16[512,128]{1,0:T(8,128)(2,1)S(1)}, u32[]{:S(2)}, u32[]{:S(2)}) collective-permute-start(bf16[512,128]{1,0:T(8,128)(2,1)S(1)} %shard_map.124.p0), channel_id=1, source_target_pairs={{0,6},{1,7},{2,4},{3,5},{4,2},{5,3},{6,0},{7,1},{8,14},{9,15},{10,... | collective-permute-start | bytes 393224 | tf_op jit(solution)/shard_map/ppermute | solution.py:106
  37.4 1.5 %collective-permute-start.14 = (bf16[512,128]{1,0:T(8,128)(2,1)S(1)}, bf16[512,128]{1,0:T(8,128)(2,1)S(1)}, u32[]{:S(2)}, u32[]{:S(2)}) collective-permute-start(bf16[512,128]{1,0:T(8,128)(2,1)S(1)} %shard_map.124.p0), channel_id=1, source_target_pairs={{0,4},{1,5},{2,6},{3,7},{4,0},{5,1},{6,2},{7,3},{8,12},{9,13},{10,... | collective-permute-start | bytes 393224 | tf_op jit(solution)/shard_map/ppermute | solution.py:106
  38.9 1.0 %collective-permute-start.13 = (bf16[512,128]{1,0:T(8,128)(2,1)S(1)}, bf16[512,128]{1,0:T(8,128)(2,1)S(1)}, u32[]{:S(2)}, u32[]{:S(2)}) collective-permute-start(bf16[512,128]{1,0:T(8,128)(2,1)S(1)} %shard_map.124.p0), channel_id=1, source_target_pairs={{0,2},{1,3},{2,0},{3,1},{4,6},{5,7},{6,4},{7,5},{8,10},{9,11},{10,... | collective-permute-start | bytes 393224 | tf_op jit(solution)/shard_map/ppermute | solution.py:106
  39.9 1.4 %shard_map.126.p0 = bf16[512,128]{1,0:T(8,128)(2,1)S(1)} custom-call(s32[32,128]{1,0:T(8,128)S(1)} %get-tuple-element.30.places, bf16[512,256]{1,0:T(8,128)(2,1)S(1)} %get-tuple-element.31.refs_0_, bf16[512,256]{1,0:T(8,128)(2,1)S(1)} %collective-permute-done.3.refs_1_, bf16[512,256]{1,0:T(8,128)(2,1)S(1)} %collective-permute-done.4.refs_2_, ...), custom_call_target="tpu_custom_call" | custom-call | tf_op jit(solution)/shard_map/pallas_call | solution.py:91
  41.4 1.0 %collective-permute-start.21 = (bf16[512,128]{1,0:T(8,128)(2,1)S(1)}, bf16[512,128]{1,0:T(8,128)(2,1)S(1)}, u32[]{:S(2)}, u32[]{:S(2)}) collective-permute-start(bf16[512,128]{1,0:T(8,128)(2,1)S(1)} %shard_map.126.p0), channel_id=1, source_target_pairs={{0,6},{1,7},{2,4},{3,5},{4,2},{5,3},{6,0},{7,1},{8,14},{9,15},{10,... | collective-permute-start | bytes 393224 | tf_op jit(solution)/shard_map/ppermute | solution.py:106
  42.4 1.5 %collective-permute-start.20 = (bf16[512,128]{1,0:T(8,128)(2,1)S(1)}, bf16[512,128]{1,0:T(8,128)(2,1)S(1)}, u32[]{:S(2)}, u32[]{:S(2)}) collective-permute-start(bf16[512,128]{1,0:T(8,128)(2,1)S(1)} %shard_map.126.p0), channel_id=1, source_target_pairs={{0,4},{1,5},{2,6},{3,7},{4,0},{5,1},{6,2},{7,3},{8,12},{9,13},{10,... | collective-permute-start | bytes 393224 | tf_op jit(solution)/shard_map/ppermute | solution.py:106
  43.9 1.0 %collective-permute-start.19 = (bf16[512,128]{1,0:T(8,128)(2,1)S(1)}, bf16[512,128]{1,0:T(8,128)(2,1)S(1)}, u32[]{:S(2)}, u32[]{:S(2)}) collective-permute-start(bf16[512,128]{1,0:T(8,128)(2,1)S(1)} %shard_map.126.p0), channel_id=1, source_target_pairs={{0,2},{1,3},{2,0},{3,1},{4,6},{5,7},{6,4},{7,5},{8,10},{9,11},{10,... | collective-permute-start | bytes 393224 | tf_op jit(solution)/shard_map/ppermute | solution.py:106
  44.9 1.6 %collective-permute-done.14.p2 = bf16[512,128]{1,0:T(8,128)(2,1)S(1)} collective-permute-done((bf16[512,128]{1,0:T(8,128)(2,1)S(1)}, bf16[512,128]{1,0:T(8,128)(2,1)S(1)}, u32[]{:S(2)}, u32[]{:S(2)}) %collective-permute-start.14) | collective-permute-done | bytes 131104 | tf_op jit(solution)/shard_map/ppermute | solution.py:106
  46.6 0.8 shard_map.125
  47.3 2.0 %collective-permute-done.21.p3 = bf16[512,128]{1,0:T(8,128)(2,1)S(1)} collective-permute-done((bf16[512,128]{1,0:T(8,128)(2,1)S(1)}, bf16[512,128]{1,0:T(8,128)(2,1)S(1)}, u32[]{:S(2)}, u32[]{:S(2)}) %collective-permute-start.21) | collective-permute-done | bytes 131104 | tf_op jit(solution)/shard_map/ppermute | solution.py:106
  49.4 1.7 %collective-permute-done.20.p2 = bf16[512,128]{1,0:T(8,128)(2,1)S(1)} collective-permute-done((bf16[512,128]{1,0:T(8,128)(2,1)S(1)}, bf16[512,128]{1,0:T(8,128)(2,1)S(1)}, u32[]{:S(2)}, u32[]{:S(2)}) %collective-permute-start.20) | collective-permute-done | bytes 131104 | tf_op jit(solution)/shard_map/ppermute | solution.py:106
  51.1 0.7 shard_map.127
  51.9 1.8 %collective-permute-start.17 = (bf16[512,128]{1,0:T(8,128)(2,1)S(1)}, bf16[512,128]{1,0:T(8,128)(2,1)S(1)}, u32[]{:S(2)}, u32[]{:S(2)}) collective-permute-start(bf16[512,128]{1,0:T(8,128)(2,1)S(1)} %get-tuple-element.35.refs_0_), channel_id=1, source_target_pairs={{0,16},{1,17},{2,18},{3,19},{4,20},{5,21},{6,22},{7,23},{8,24},{9,... | collective-permute-start | bytes 393224 | tf_op jit(solution)/shard_map/ppermute | solution.py:106
  53.7 1.9 %collective-permute-start.23 = (bf16[512,128]{1,0:T(8,128)(2,1)S(1)}, bf16[512,128]{1,0:T(8,128)(2,1)S(1)}, u32[]{:S(2)}, u32[]{:S(2)}) collective-permute-start(bf16[512,128]{1,0:T(8,128)(2,1)S(1)} %add_convert_fusion.2), channel_id=1, source_target_pairs={{0,8},{1,9},{2,10},{3,11},{4,12},{5,13},{6,14},{7,15},{8,0},{9,1},... | collective-permute-start | bytes 393224 | tf_op jit(solution)/shard_map/ppermute | solution.py:106
  55.6 0.2 collective-permute-start.16
  55.8 5.7 %collective-permute-done.17.refs_2_ = bf16[512,128]{1,0:T(8,128)(2,1)S(1)} collective-permute-done((bf16[512,128]{1,0:T(8,128)(2,1)S(1)}, bf16[512,128]{1,0:T(8,128)(2,1)S(1)}, u32[]{:S(2)}, u32[]{:S(2)}) %collective-permute-start.17) | collective-permute-done | bytes 131104 | tf_op jit(solution)/shard_map/ppermute | solution.py:106
  61.6 0.9 %collective-permute-done.23 = bf16[512,128]{1,0:T(8,128)(2,1)S(1)} collective-permute-done((bf16[512,128]{1,0:T(8,128)(2,1)S(1)}, bf16[512,128]{1,0:T(8,128)(2,1)S(1)}, u32[]{:S(2)}, u32[]{:S(2)}) %collective-permute-start.23) | collective-permute-done | bytes 131104 | tf_op jit(solution)/shard_map/ppermute | solution.py:106
  62.5 0.4 collective-permute-start.24
  62.9 3.3 %collective-permute-start.29 = (bf16[512,128]{1,0:T(8,128)(2,1)S(1)}, bf16[512,128]{1,0:T(8,128)(2,1)S(1)}, u32[]{:S(2)}, u32[]{:S(2)}) collective-permute-start(bf16[512,128]{1,0:T(8,128)(2,1)S(1)} %add_convert_fusion.1), channel_id=1, source_target_pairs={{0,16},{1,17},{2,18},{3,19},{4,20},{5,21},{6,22},{7,23},{8,24},{9,... | collective-permute-start | bytes 393224 | tf_op jit(solution)/shard_map/ppermute | solution.py:106
  66.2 0.5 collective-permute-start.26
  66.8 3.1 %collective-permute-done.24.refs_3_ = bf16[512,128]{1,0:T(8,128)(2,1)S(1)} collective-permute-done((bf16[512,128]{1,0:T(8,128)(2,1)S(1)}, bf16[512,128]{1,0:T(8,128)(2,1)S(1)}, u32[]{:S(2)}, u32[]{:S(2)}) %collective-permute-start.24) | collective-permute-done | bytes 131104 | tf_op jit(solution)/shard_map/ppermute | solution.py:106
  69.9 1.3 %collective-permute-done.29 = bf16[512,128]{1,0:T(8,128)(2,1)S(1)} collective-permute-done((bf16[512,128]{1,0:T(8,128)(2,1)S(1)}, bf16[512,128]{1,0:T(8,128)(2,1)S(1)}, u32[]{:S(2)}, u32[]{:S(2)}) %collective-permute-start.29) | collective-permute-done | bytes 131104 | tf_op jit(solution)/shard_map/ppermute | solution.py:106
  71.3 1.4 %shard_map.128 = (bf16[640,128]{1,0:T(8,128)(2,1)S(1)}, bf16[640,128]{1,0:T(8,128)(2,1)S(1)}, bf16[640,128]{1,0:T(8,128)(2,1)S(1)}, bf16[640,128]{1,0:T(8,128)(2,1)S(1)}) custom-call(s32[32,128]{1,0:T(8,128)S(1)} %get-tuple-element.30.places, bf16[512,128]{1,0:T(8,128)(2,1)S(1)} %get-tuple-element.35.refs_0_, ...), custom_call_target="tpu_custom_call" | custom-call | tf_op jit(solution)/shard_map/pallas_call | solution.py:91
  72.7 1.6 %collective-permute-start.30 = (bf16[640,128]{1,0:T(8,128)(2,1)S(1)}, bf16[640,128]{1,0:T(8,128)(2,1)S(1)}, u32[]{:S(2)}, u32[]{:S(2)}) collective-permute-start(bf16[640,128]{1,0:T(8,128)(2,1)S(1)} %get-tuple-element.44), channel_id=1, source_target_pairs={{0,2},{1,3},{2,0},{3,1},{4,6},{5,7},{6,4},{7,5},{8,10},{9,11},{10,... | collective-permute-start | bytes 491528 | tf_op jit(solution)/shard_map/ppermute | solution.py:106
  74.3 0.7 collective-permute-start.31
  74.9 1.3 %collective-permute-start.32 = (bf16[640,128]{1,0:T(8,128)(2,1)S(1)}, bf16[640,128]{1,0:T(8,128)(2,1)S(1)}, u32[]{:S(2)}, u32[]{:S(2)}) collective-permute-start(bf16[640,128]{1,0:T(8,128)(2,1)S(1)} %get-tuple-element.46), channel_id=1, source_target_pairs={{0,6},{1,7},{2,4},{3,5},{4,2},{5,3},{6,0},{7,1},{8,14},{9,15},{10,... | collective-permute-start | bytes 491528 | tf_op jit(solution)/shard_map/ppermute | solution.py:106
  76.2 3.6 %collective-permute-done.30.p1.refs_1_ = bf16[640,128]{1,0:T(8,128)(2,1)S(1)} collective-permute-done((bf16[640,128]{1,0:T(8,128)(2,1)S(1)}, bf16[640,128]{1,0:T(8,128)(2,1)S(1)}, u32[]{:S(2)}, u32[]{:S(2)}) %collective-permute-start.30) | collective-permute-done | bytes 163872 | tf_op jit(solution)/shard_map/ppermute | solution.py:106
  79.8 3.4 %collective-permute-done.31.p2.refs_2_ = bf16[640,128]{1,0:T(8,128)(2,1)S(1)} collective-permute-done((bf16[640,128]{1,0:T(8,128)(2,1)S(1)}, bf16[640,128]{1,0:T(8,128)(2,1)S(1)}, u32[]{:S(2)}, u32[]{:S(2)}) %collective-permute-start.31) | collective-permute-done | bytes 163872 | tf_op jit(solution)/shard_map/ppermute | solution.py:106
  83.2 0.5 collective-permute-start.36
  83.8 0.9 %shard_map.129 = bf16[128,512]{1,0:T(8,128)(2,1)} custom-call(s32[1]{0:T(128)} %bitcast.pos, bf16[640,128]{1,0:T(8,128)(2,1)S(1)} %get-tuple-element.43.p0.refs_0_, bf16[640,128]{1,0:T(8,128)(2,1)S(1)} %collective-permute-done.30.p1.refs_1_, bf16[640,128]{1,0:T(8,128)(2,1)S(1)} %collective-permute-done.31.p2.refs_2_, ...), custom_call_target="tpu_custom_call" | custom-call | tf_op jit(solution)/shard_map/pallas_call | solution.py:91
  84.7 0.2 collective-permute-done.36.refs_7_
  84.9 1.6 %shard_map.130 = (f32[512,512]{1,0:T(8,128)}, f32[512,512]{1,0:T(8,128)}) custom-call(s32[1]{0:T(128)} %bitcast.pos, bf16[640,128]{1,0:T(8,128)(2,1)S(1)} %get-tuple-element.43.p0.refs_0_, bf16[640,128]{1,0:T(8,128)(2,1)S(1)} %collective-permute-done.30.p1.refs_1_, bf16[640,128]{1,0:T(8,128)(2,1)S(1)} %collective-permute-done.31.p2.refs_2_, ...), custom_call_target="tpu_custom_call" | custom-call | tf_op jit(solution)/shard_map/pallas_call | solution.py:91
  (43 shorter events, 0.4 us)
Async XLA Ops:
  2.0 8.0 %collective-permute-start = (bf16[144,256]{1,0:T(8,128)(2,1)S(1)}, bf16[144,256]{1,0:T(8,128)(2,1)S(1)}, u32[]{:S(2)}, u32[]{:S(2)}) collective-permute-start(bf16[144,256]{1,0:T(8,128)(2,1)S(1)} %get-tuple-element.27), channel_id=1, source_target_pairs={{0,2},{1,3},{2,0},{3,1},{4,6},{5,7},{6,4},{7,5},{8,10},{9,11},{10,... | collective-permute-start | bytes 221192 | tf_op jit(solution)/shard_map/ppermute | solution.py:106
  5.0 5.0 %collective-permute-start.1 = (bf16[144,256]{1,0:T(8,128)(2,1)S(1)}, bf16[144,256]{1,0:T(8,128)(2,1)S(1)}, u32[]{:S(2)}, u32[]{:S(2)}) collective-permute-start(bf16[144,256]{1,0:T(8,128)(2,1)S(1)} %get-tuple-element.28), channel_id=1, source_target_pairs={{0,4},{1,5},{2,6},{3,7},{4,0},{5,1},{6,2},{7,3},{8,12},{9,13},{10,... | collective-permute-start | bytes 221192 | tf_op jit(solution)/shard_map/ppermute | solution.py:106
  6.5 6.1 %collective-permute-start.2 = (bf16[144,256]{1,0:T(8,128)(2,1)S(1)}, bf16[144,256]{1,0:T(8,128)(2,1)S(1)}, u32[]{:S(2)}, u32[]{:S(2)}) collective-permute-start(bf16[144,256]{1,0:T(8,128)(2,1)S(1)} %get-tuple-element.29), channel_id=1, source_target_pairs={{0,6},{1,7},{2,4},{3,5},{4,2},{5,3},{6,0},{7,1},{8,14},{9,15},{10,... | collective-permute-start | bytes 221192 | tf_op jit(solution)/shard_map/ppermute | solution.py:106
  6.5 10.4 %collective-permute-start.10 = (bf16[2,64,1024]{2,1,0:T(8,128)(2,1)S(1)}, bf16[2,64,1024]{2,1,0:T(8,128)(2,1)S(1)}, u32[]{:S(2)}, u32[]{:S(2)}) collective-permute-start(bf16[2,64,1024]{2,1,0:T(8,128)(2,1)S(1)} %get-tuple-element.32.t0), channel_id=1, source_target_pairs={{0,2},{1,3},{2,0},{3,1},{4,6},{5,7},{6,4},{7,5},{8,10},{9,11},{10,... | collective-permute-start | bytes 786440 | tf_op jit(solution)/shard_map/ppermute | solution.py:106
  8.5 8.4 %collective-permute-start.11 = (bf16[2,64,1024]{2,1,0:T(8,128)(2,1)S(1)}, bf16[2,64,1024]{2,1,0:T(8,128)(2,1)S(1)}, u32[]{:S(2)}, u32[]{:S(2)}) collective-permute-start(bf16[2,64,1024]{2,1,0:T(8,128)(2,1)S(1)} %get-tuple-element.33.t2), channel_id=1, source_target_pairs={{0,4},{1,5},{2,6},{3,7},{4,0},{5,1},{6,2},{7,3},{8,12},{9,13},{10,... | collective-permute-start | bytes 786440 | tf_op jit(solution)/shard_map/ppermute | solution.py:106
  12.6 12.3 %collective-permute-start.4 = (bf16[512,256]{1,0:T(8,128)(2,1)S(1)}, bf16[512,256]{1,0:T(8,128)(2,1)S(1)}, u32[]{:S(2)}, u32[]{:S(2)}) collective-permute-start(bf16[512,256]{1,0:T(8,128)(2,1)S(1)} %get-tuple-element.31.refs_0_), channel_id=1, source_target_pairs={{0,16},{1,17},{2,18},{3,19},{4,20},{5,21},{6,22},{7,23},{8,24},{9,... | collective-permute-start | bytes 786440 | tf_op jit(solution)/shard_map/ppermute | solution.py:106
  15.3 11.3 %collective-permute-start.6 = (bf16[512,256]{1,0:T(8,128)(2,1)S(1)}, bf16[512,256]{1,0:T(8,128)(2,1)S(1)}, u32[]{:S(2)}, u32[]{:S(2)}) collective-permute-start(bf16[512,256]{1,0:T(8,128)(2,1)S(1)} %get-tuple-element.31.refs_0_), channel_id=1, source_target_pairs={{0,1},{1,0},{2,3},{3,2},{4,5},{5,4},{6,7},{7,6},{8,9},{9,8},{10,11... | collective-permute-start | bytes 786440 | tf_op jit(solution)/shard_map/ppermute | solution.py:106
  15.3 12.7 %collective-permute-start.3 = (bf16[512,256]{1,0:T(8,128)(2,1)S(1)}, bf16[512,256]{1,0:T(8,128)(2,1)S(1)}, u32[]{:S(2)}, u32[]{:S(2)}) collective-permute-start(bf16[512,256]{1,0:T(8,128)(2,1)S(1)} %get-tuple-element.31.refs_0_), channel_id=1, source_target_pairs={{0,8},{1,9},{2,10},{3,11},{4,12},{5,13},{6,14},{7,15},{8,0},{9,1},... | collective-permute-start | bytes 786440 | tf_op jit(solution)/shard_map/ppermute | solution.py:106
  16.9 16.4 %collective-permute-start.12 = (bf16[4,64,1024]{2,1,0:T(8,128)(2,1)S(1)}, bf16[4,64,1024]{2,1,0:T(8,128)(2,1)S(1)}, u32[]{:S(2)}, u32[]{:S(2)}) collective-permute-start(bf16[4,64,1024]{2,1,0:T(8,128)(2,1)S(1)} %get-tuple-element.34.refs_8_), channel_id=1, source_target_pairs={{0,4},{1,5},{2,6},{3,7},{4,0},{5,1},{6,2},{7,3},{8,12},{9,13},{10,... | collective-permute-start | bytes 1572872 | tf_op jit(solution)/shard_map/ppermute | solution.py:106
  24.9 8.4 %collective-permute-start.5 = (bf16[512,256]{1,0:T(8,128)(2,1)S(1)}, bf16[512,256]{1,0:T(8,128)(2,1)S(1)}, u32[]{:S(2)}, u32[]{:S(2)}) collective-permute-start(bf16[512,256]{1,0:T(8,128)(2,1)S(1)} %collective-permute-done.4.refs_2_), channel_id=1, source_target_pairs={{0,8},{1,9},{2,10},{3,11},{4,12},{5,13},{6,14},{7,15},{8,0},{9,1},... | collective-permute-start | bytes 786440 | tf_op jit(solution)/shard_map/ppermute | solution.py:106
  25.5 14.4 %collective-permute-start.18 = (bf16[4,64,1024]{2,1,0:T(8,128)(2,1)S(1)}, bf16[4,64,1024]{2,1,0:T(8,128)(2,1)S(1)}, u32[]{:S(2)}, u32[]{:S(2)}) collective-permute-start(bf16[4,64,1024]{2,1,0:T(8,128)(2,1)S(1)} %get-tuple-element.39.refs_8_), channel_id=1, source_target_pairs={{0,2},{1,3},{2,0},{3,1},{4,6},{5,7},{6,4},{7,5},{8,10},{9,11},{10,... | collective-permute-start | bytes 1572872 | tf_op jit(solution)/shard_map/ppermute | solution.py:106
  26.5 6.8 %collective-permute-start.8 = (bf16[512,256]{1,0:T(8,128)(2,1)S(1)}, bf16[512,256]{1,0:T(8,128)(2,1)S(1)}, u32[]{:S(2)}, u32[]{:S(2)}) collective-permute-start(bf16[512,256]{1,0:T(8,128)(2,1)S(1)} %collective-permute-done.4.refs_2_), channel_id=1, source_target_pairs={{0,1},{1,0},{2,3},{3,2},{4,5},{5,4},{6,7},{7,6},{8,9},{9,8},{10,11... | collective-permute-start | bytes 786440 | tf_op jit(solution)/shard_map/ppermute | solution.py:106
  27.9 5.4 %collective-permute-start.7 = (bf16[512,256]{1,0:T(8,128)(2,1)S(1)}, bf16[512,256]{1,0:T(8,128)(2,1)S(1)}, u32[]{:S(2)}, u32[]{:S(2)}) collective-permute-start(bf16[512,256]{1,0:T(8,128)(2,1)S(1)} %collective-permute-done.3.refs_1_), channel_id=1, source_target_pairs={{0,1},{1,0},{2,3},{3,2},{4,5},{5,4},{6,7},{7,6},{8,9},{9,8},{10,11... | collective-permute-start | bytes 786440 | tf_op jit(solution)/shard_map/ppermute | solution.py:106
  33.3 1.5 %collective-permute-start.9 = (bf16[512,256]{1,0:T(8,128)(2,1)S(1)}, bf16[512,256]{1,0:T(8,128)(2,1)S(1)}, u32[]{:S(2)}, u32[]{:S(2)}) collective-permute-start(bf16[512,256]{1,0:T(8,128)(2,1)S(1)} %collective-permute-done.5.refs_3_), channel_id=1, source_target_pairs={{0,1},{1,0},{2,3},{3,2},{4,5},{5,4},{6,7},{7,6},{8,9},{9,8},{10,11... | collective-permute-start | bytes 786440 | tf_op jit(solution)/shard_map/ppermute | solution.py:106
  36.3 10.2 %copy-start.1 = (bf16[512,512]{1,0:T(8,128)(2,1)S(1)}, bf16[512,512]{1,0:T(8,128)(2,1)}, u32[]{:S(2)}) copy-start(bf16[512,512]{1,0:T(8,128)(2,1)} %w_first.1) | copy-start | bytes 1572868
  36.3 7.6 %collective-permute-start.15 = (bf16[512,128]{1,0:T(8,128)(2,1)S(1)}, bf16[512,128]{1,0:T(8,128)(2,1)S(1)}, u32[]{:S(2)}, u32[]{:S(2)}) collective-permute-start(bf16[512,128]{1,0:T(8,128)(2,1)S(1)} %shard_map.124.p0), channel_id=1, source_target_pairs={{0,6},{1,7},{2,4},{3,5},{4,2},{5,3},{6,0},{7,1},{8,14},{9,15},{10,... | collective-permute-start | bytes 393224 | tf_op jit(solution)/shard_map/ppermute | solution.py:106
  37.4 9.2 %collective-permute-start.14 = (bf16[512,128]{1,0:T(8,128)(2,1)S(1)}, bf16[512,128]{1,0:T(8,128)(2,1)S(1)}, u32[]{:S(2)}, u32[]{:S(2)}) collective-permute-start(bf16[512,128]{1,0:T(8,128)(2,1)S(1)} %shard_map.124.p0), channel_id=1, source_target_pairs={{0,4},{1,5},{2,6},{3,7},{4,0},{5,1},{6,2},{7,3},{8,12},{9,13},{10,... | collective-permute-start | bytes 393224 | tf_op jit(solution)/shard_map/ppermute | solution.py:106
  38.9 7.7 %collective-permute-start.13 = (bf16[512,128]{1,0:T(8,128)(2,1)S(1)}, bf16[512,128]{1,0:T(8,128)(2,1)S(1)}, u32[]{:S(2)}, u32[]{:S(2)}) collective-permute-start(bf16[512,128]{1,0:T(8,128)(2,1)S(1)} %shard_map.124.p0), channel_id=1, source_target_pairs={{0,2},{1,3},{2,0},{3,1},{4,6},{5,7},{6,4},{7,5},{8,10},{9,11},{10,... | collective-permute-start | bytes 393224 | tf_op jit(solution)/shard_map/ppermute | solution.py:106
  41.3 9.7 %copy-start = (bf16[512,512]{1,0:T(8,128)(2,1)S(1)}, bf16[512,512]{1,0:T(8,128)(2,1)}, u32[]{:S(2)}) copy-start(bf16[512,512]{1,0:T(8,128)(2,1)} %w_second.3) | copy-start | bytes 1572868
  41.4 8.0 %collective-permute-start.21 = (bf16[512,128]{1,0:T(8,128)(2,1)S(1)}, bf16[512,128]{1,0:T(8,128)(2,1)S(1)}, u32[]{:S(2)}, u32[]{:S(2)}) collective-permute-start(bf16[512,128]{1,0:T(8,128)(2,1)S(1)} %shard_map.126.p0), channel_id=1, source_target_pairs={{0,6},{1,7},{2,4},{3,5},{4,2},{5,3},{6,0},{7,1},{8,14},{9,15},{10,... | collective-permute-start | bytes 393224 | tf_op jit(solution)/shard_map/ppermute | solution.py:106
  42.4 8.7 %collective-permute-start.20 = (bf16[512,128]{1,0:T(8,128)(2,1)S(1)}, bf16[512,128]{1,0:T(8,128)(2,1)S(1)}, u32[]{:S(2)}, u32[]{:S(2)}) collective-permute-start(bf16[512,128]{1,0:T(8,128)(2,1)S(1)} %shard_map.126.p0), channel_id=1, source_target_pairs={{0,4},{1,5},{2,6},{3,7},{4,0},{5,1},{6,2},{7,3},{8,12},{9,13},{10,... | collective-permute-start | bytes 393224 | tf_op jit(solution)/shard_map/ppermute | solution.py:106
  43.9 7.1 %collective-permute-start.19 = (bf16[512,128]{1,0:T(8,128)(2,1)S(1)}, bf16[512,128]{1,0:T(8,128)(2,1)S(1)}, u32[]{:S(2)}, u32[]{:S(2)}) collective-permute-start(bf16[512,128]{1,0:T(8,128)(2,1)S(1)} %shard_map.126.p0), channel_id=1, source_target_pairs={{0,2},{1,3},{2,0},{3,1},{4,6},{5,7},{6,4},{7,5},{8,10},{9,11},{10,... | collective-permute-start | bytes 393224 | tf_op jit(solution)/shard_map/ppermute | solution.py:106
  51.8 1.9 %collective-permute-start.22 = (f32[512,128]{1,0:T(8,128)S(1)}, f32[512,128]{1,0:T(8,128)S(1)}, u32[]{:S(2)}, u32[]{:S(2)}) collective-permute-start(f32[512,128]{1,0:T(8,128)S(1)} %get-tuple-element.41), channel_id=1, source_target_pairs={{0,1},{1,0},{2,3},{3,2},{4,5},{5,4},{6,7},{7,6},{8,9},{9,8},{10,11... | collective-permute-start | bytes 786440 | tf_op jit(solution)/shard_map/ppermute | solution.py:106
  51.9 9.7 %collective-permute-start.17 = (bf16[512,128]{1,0:T(8,128)(2,1)S(1)}, bf16[512,128]{1,0:T(8,128)(2,1)S(1)}, u32[]{:S(2)}, u32[]{:S(2)}) collective-permute-start(bf16[512,128]{1,0:T(8,128)(2,1)S(1)} %get-tuple-element.35.refs_0_), channel_id=1, source_target_pairs={{0,16},{1,17},{2,18},{3,19},{4,20},{5,21},{6,22},{7,23},{8,24},{9,... | collective-permute-start | bytes 393224 | tf_op jit(solution)/shard_map/ppermute | solution.py:106
  53.7 8.7 %collective-permute-start.23 = (bf16[512,128]{1,0:T(8,128)(2,1)S(1)}, bf16[512,128]{1,0:T(8,128)(2,1)S(1)}, u32[]{:S(2)}, u32[]{:S(2)}) collective-permute-start(bf16[512,128]{1,0:T(8,128)(2,1)S(1)} %add_convert_fusion.2), channel_id=1, source_target_pairs={{0,8},{1,9},{2,10},{3,11},{4,12},{5,13},{6,14},{7,15},{8,0},{9,1},... | collective-permute-start | bytes 393224 | tf_op jit(solution)/shard_map/ppermute | solution.py:106
  55.6 10.6 %collective-permute-start.16 = (bf16[512,128]{1,0:T(8,128)(2,1)S(1)}, bf16[512,128]{1,0:T(8,128)(2,1)S(1)}, u32[]{:S(2)}, u32[]{:S(2)}) collective-permute-start(bf16[512,128]{1,0:T(8,128)(2,1)S(1)} %get-tuple-element.35.refs_0_), channel_id=1, source_target_pairs={{0,8},{1,9},{2,10},{3,11},{4,12},{5,13},{6,14},{7,15},{8,0},{9,1},... | collective-permute-start | bytes 393224 | tf_op jit(solution)/shard_map/ppermute | solution.py:106
  62.5 7.4 %collective-permute-start.24 = (bf16[512,128]{1,0:T(8,128)(2,1)S(1)}, bf16[512,128]{1,0:T(8,128)(2,1)S(1)}, u32[]{:S(2)}, u32[]{:S(2)}) collective-permute-start(bf16[512,128]{1,0:T(8,128)(2,1)S(1)} %collective-permute-done.17.refs_2_), channel_id=1, source_target_pairs={{0,8},{1,9},{2,10},{3,11},{4,12},{5,13},{6,14},{7,15},{8,0},{9,1},... | collective-permute-start | bytes 393224 | tf_op jit(solution)/shard_map/ppermute | solution.py:106
  62.9 8.3 %collective-permute-start.29 = (bf16[512,128]{1,0:T(8,128)(2,1)S(1)}, bf16[512,128]{1,0:T(8,128)(2,1)S(1)}, u32[]{:S(2)}, u32[]{:S(2)}) collective-permute-start(bf16[512,128]{1,0:T(8,128)(2,1)S(1)} %add_convert_fusion.1), channel_id=1, source_target_pairs={{0,16},{1,17},{2,18},{3,19},{4,20},{5,21},{6,22},{7,23},{8,24},{9,... | collective-permute-start | bytes 393224 | tf_op jit(solution)/shard_map/ppermute | solution.py:106
  66.2 5.0 %collective-permute-start.25 = (bf16[512,128]{1,0:T(8,128)(2,1)S(1)}, bf16[512,128]{1,0:T(8,128)(2,1)S(1)}, u32[]{:S(2)}, u32[]{:S(2)}) collective-permute-start(bf16[512,128]{1,0:T(8,128)(2,1)S(1)} %get-tuple-element.35.refs_0_), channel_id=1, source_target_pairs={{0,1},{1,0},{2,3},{3,2},{4,5},{5,4},{6,7},{7,6},{8,9},{9,8},{10,11... | collective-permute-start | bytes 393224 | tf_op jit(solution)/shard_map/ppermute | solution.py:106
  66.2 5.0 %collective-permute-start.26 = (bf16[512,128]{1,0:T(8,128)(2,1)S(1)}, bf16[512,128]{1,0:T(8,128)(2,1)S(1)}, u32[]{:S(2)}, u32[]{:S(2)}) collective-permute-start(bf16[512,128]{1,0:T(8,128)(2,1)S(1)} %collective-permute-done.16.refs_1_), channel_id=1, source_target_pairs={{0,1},{1,0},{2,3},{3,2},{4,5},{5,4},{6,7},{7,6},{8,9},{9,8},{10,11... | collective-permute-start | bytes 393224 | tf_op jit(solution)/shard_map/ppermute | solution.py:106
  66.8 4.5 %collective-permute-start.27 = (bf16[512,128]{1,0:T(8,128)(2,1)S(1)}, bf16[512,128]{1,0:T(8,128)(2,1)S(1)}, u32[]{:S(2)}, u32[]{:S(2)}) collective-permute-start(bf16[512,128]{1,0:T(8,128)(2,1)S(1)} %collective-permute-done.17.refs_2_), channel_id=1, source_target_pairs={{0,1},{1,0},{2,3},{3,2},{4,5},{5,4},{6,7},{7,6},{8,9},{9,8},{10,11... | collective-permute-start | bytes 393224 | tf_op jit(solution)/shard_map/ppermute | solution.py:106
  69.9 1.4 %collective-permute-start.28 = (bf16[512,128]{1,0:T(8,128)(2,1)S(1)}, bf16[512,128]{1,0:T(8,128)(2,1)S(1)}, u32[]{:S(2)}, u32[]{:S(2)}) collective-permute-start(bf16[512,128]{1,0:T(8,128)(2,1)S(1)} %collective-permute-done.24.refs_3_), channel_id=1, source_target_pairs={{0,1},{1,0},{2,3},{3,2},{4,5},{5,4},{6,7},{7,6},{8,9},{9,8},{10,11... | collective-permute-start | bytes 393224 | tf_op jit(solution)/shard_map/ppermute | solution.py:106
  72.7 7.1 %collective-permute-start.30 = (bf16[640,128]{1,0:T(8,128)(2,1)S(1)}, bf16[640,128]{1,0:T(8,128)(2,1)S(1)}, u32[]{:S(2)}, u32[]{:S(2)}) collective-permute-start(bf16[640,128]{1,0:T(8,128)(2,1)S(1)} %get-tuple-element.44), channel_id=1, source_target_pairs={{0,2},{1,3},{2,0},{3,1},{4,6},{5,7},{6,4},{7,5},{8,10},{9,11},{10,... | collective-permute-start | bytes 491528 | tf_op jit(solution)/shard_map/ppermute | solution.py:106
  74.3 9.0 %collective-permute-start.31 = (bf16[640,128]{1,0:T(8,128)(2,1)S(1)}, bf16[640,128]{1,0:T(8,128)(2,1)S(1)}, u32[]{:S(2)}, u32[]{:S(2)}) collective-permute-start(bf16[640,128]{1,0:T(8,128)(2,1)S(1)} %get-tuple-element.45), channel_id=1, source_target_pairs={{0,4},{1,5},{2,6},{3,7},{4,0},{5,1},{6,2},{7,3},{8,12},{9,13},{10,... | collective-permute-start | bytes 491528 | tf_op jit(solution)/shard_map/ppermute | solution.py:106
  74.9 8.3 %collective-permute-start.32 = (bf16[640,128]{1,0:T(8,128)(2,1)S(1)}, bf16[640,128]{1,0:T(8,128)(2,1)S(1)}, u32[]{:S(2)}, u32[]{:S(2)}) collective-permute-start(bf16[640,128]{1,0:T(8,128)(2,1)S(1)} %get-tuple-element.46), channel_id=1, source_target_pairs={{0,6},{1,7},{2,4},{3,5},{4,2},{5,3},{6,0},{7,1},{8,14},{9,15},{10,... | collective-permute-start | bytes 491528 | tf_op jit(solution)/shard_map/ppermute | solution.py:106
  76.2 8.5 %collective-permute-start.33 = (bf16[640,128]{1,0:T(8,128)(2,1)S(1)}, bf16[640,128]{1,0:T(8,128)(2,1)S(1)}, u32[]{:S(2)}, u32[]{:S(2)}) collective-permute-start(bf16[640,128]{1,0:T(8,128)(2,1)S(1)} %get-tuple-element.43.p0.refs_0_), channel_id=1, source_target_pairs={{0,1},{1,0},{2,3},{3,2},{4,5},{5,4},{6,7},{7,6},{8,9},{9,8},{10,11... | collective-permute-start | bytes 491528 | tf_op jit(solution)/shard_map/ppermute | solution.py:106
  79.8 4.9 %collective-permute-start.34 = (bf16[640,128]{1,0:T(8,128)(2,1)S(1)}, bf16[640,128]{1,0:T(8,128)(2,1)S(1)}, u32[]{:S(2)}, u32[]{:S(2)}) collective-permute-start(bf16[640,128]{1,0:T(8,128)(2,1)S(1)} %collective-permute-done.30.p1.refs_1_), channel_id=1, source_target_pairs={{0,1},{1,0},{2,3},{3,2},{4,5},{5,4},{6,7},{7,6},{8,9},{9,8},{10,11... | collective-permute-start | bytes 491528 | tf_op jit(solution)/shard_map/ppermute | solution.py:106
  83.2 1.5 %collective-permute-start.35 = (bf16[640,128]{1,0:T(8,128)(2,1)S(1)}, bf16[640,128]{1,0:T(8,128)(2,1)S(1)}, u32[]{:S(2)}, u32[]{:S(2)}) collective-permute-start(bf16[640,128]{1,0:T(8,128)(2,1)S(1)} %collective-permute-done.31.p2.refs_2_), channel_id=1, source_target_pairs={{0,1},{1,0},{2,3},{3,2},{4,5},{5,4},{6,7},{7,6},{8,9},{9,8},{10,11... | collective-permute-start | bytes 491528 | tf_op jit(solution)/shard_map/ppermute | solution.py:106
  83.2 1.6 %collective-permute-start.36 = (bf16[640,128]{1,0:T(8,128)(2,1)S(1)}, bf16[640,128]{1,0:T(8,128)(2,1)S(1)}, u32[]{:S(2)}, u32[]{:S(2)}) collective-permute-start(bf16[640,128]{1,0:T(8,128)(2,1)S(1)} %collective-permute-done.32.p3.refs_3_), channel_id=1, source_target_pairs={{0,1},{1,0},{2,3},{3,2},{4,5},{5,4},{6,7},{7,6},{8,9},{9,8},{10,11... | collective-permute-start | bytes 491528 | tf_op jit(solution)/shard_map/ppermute | solution.py:106

commit v9 on v8

--- a/solution.py
+++ b/solution.py
@@ -301,23 +301,20 @@
     )
 
 
-def second_body(pos, p0, p1, p2, p3, w_second, z_out):
-    total = jnp.zeros(z_out.shape, F32)
+def second_body(pos, p0, p1, p2, p3, w_second, z_out, mixed):
     for p, piece in enumerate((p0, p1, p2, p3)):
-        total = total + jnp.dot(
-            piece[piece.shape[0] - ROWS :, :],
-            w_second[lanes_of(chip(pos) ^ p), :],
-            preferred_element_type=F32,
-        )
-    z_out[...] = total.astype(BF16)
+        mixed[:, lanes_of(chip(pos) ^ p)] = piece[piece.shape[0] - ROWS :, :]
+    z_out[...] = jnp.dot(mixed[...], w_second[...], preferred_element_type=F32).astype(BF16)
 
 
 def second_layer(pos, pieces, w_second):
+    channels = w_second.shape[0]
     return call(
         second_body,
-        shaped(ROWS, w_second.shape[0]),
+        shaped(ROWS, channels),
         (pos, *pieces, w_second),
         [SMEM] + [VMEM] * 5,
+        [pltpu.VMEM((ROWS, channels), BF16)],
     )
 
 
@@ -358,33 +355,44 @@
 
 
 def place_body(pos, *refs):
-    mine, other, (first, second) = refs[:QUAD], refs[QUAD : 2 * QUAD], refs[2 * QUAD :]
-    extent = first.shape[0]
+    mine, other = refs[:QUAD], refs[QUAD : 2 * QUAD]
+    outs, staged, sems = refs[2 * QUAD : 2 * QUAD + 2], refs[2 * QUAD + 2 : -1], refs[-1]
     keeps_first = (pos[0] & 1) == 0
-
-    def fill(mine_out, other_out):
-        for p in range(QUAD):
-            share = lanes_of(chip(pos) ^ p)
-            mine_out[:, share] = mine[p][:extent, :].astype(F32)
-            other_out[:, share] = other[p][:extent, :].astype(F32)
-
-    @pl.when(keeps_first)
-    def _():
-        fill(first, second)
-
-    @pl.when(jnp.logical_not(keeps_first))
-    def _():
-        fill(second, first)
+    chunk = outs[0].shape[0] // 4
+    copies = []
+    for i in range(4):
+        rows = pl.ds(i * chunk, chunk)
+
+        def fill(mine_out, other_out):
+            for p in range(QUAD):
+                share = lanes_of(chip(pos) ^ p)
+                mine_out[rows, share] = mine[p][rows, :].astype(F32)
+                other_out[rows, share] = other[p][rows, :].astype(F32)
+
+        pl.when(keeps_first)(functools.partial(fill, staged[0], staged[1]))
+        pl.when(jnp.logical_not(keeps_first))(functools.partial(fill, staged[1], staged[0]))
+        for g in range(2):
+            copies.append(
+                pltpu.make_async_copy(
+                    staged[g].at[rows, :], outs[g].at[rows, :], sems.at[2 * i + g]
+                )
+            )
+            copies[-1].start()
+    for copy in copies:
+        copy.wait()
 
 
 def place(pos, mine, other):
     channels = QUAD * LANES
-    return call(
+    return pl.pallas_call(
         place_body,
-        (shaped(channels, channels, F32),) * 2,
-        (pos, *mine, *other),
-        [SMEM] + [VMEM] * (2 * QUAD),
-    )
+        out_shape=(shaped(channels, channels, F32),) * 2,
+        in_specs=[SMEM] + [VMEM] * (2 * QUAD),
+        out_specs=(HBM, HBM),
+        scratch_shapes=[pltpu.VMEM((channels, channels), F32)] * 2
+        + [pltpu.SemaphoreType.DMA((8,))],
+        compiler_params=PARAMS,
+    )(pos, *mine, *other)
 
 
 def planned_shards(

time: 86.6 us -> 86.5 us (level)
    pallas_call x10 -> x9, Pallas kernels: 9.75 us -> 8.11 us  [call(): pl.pallas_call(body, out_shape=out_shape, in_specs=list(spaces), out_spec...]
    pallas_call x0 -> x1, Pallas kernels: none -> 1.44 us  [place(): pl.pallas_call(place_body, out_shape=(shaped(channels, channels, F32),) *...]
where the time goes in v9:
time: 86.5 us; the launch traced here: 86.3 us
  waiting for transfers between devices  41.6 us (48%)
  starting transfers between devices  34.3 us (40%)
  Pallas kernels  9.55 us (11%)
    ppermute x37, waiting for transfers between devices, swap(): return lax.ppermute(value, AXES, [(i, i ^ mask) for i in range(DEVICES)])  41.6 us
    ppermute x37, starting transfers between devices, swap(): return lax.ppermute(value, AXES, [(i, i ^ mask) for i in range(DEVICES)])  34.3 us
    pallas_call x9, Pallas kernels, call(): pl.pallas_call(body, out_shape=out_shape, in_specs=list(spaces), out_spec...  8.11 us
  transfers between devices with their start and end apart: 37, of which 15 were waited for; matrix products, arithmetic and copies ran while one was open for 0% of the time, Pallas kernels for 5%

profile of v9, /device:TPU:0, one launch (start us, length us, event | category | flops | bytes accessed | tf_op | source)
XLA Modules:
  0.0 86.3 jit_solution(5171882445901522104)
XLA Ops:
  0.6 1.3 %shard_map.121 = (bf16[144,256]{1,0:T(8,128)(2,1)S(1)}, bf16[144,256]{1,0:T(8,128)(2,1)S(1)}, bf16[144,256]{1,0:T(8,128)(2,1)S(1)}, bf16[144,256]{1,0:T(8,128)(2...) custom-call(s32[1]{0:T(128)} %bitcast.pos, s32[2,16]{1,0:T(2,128)} %refs_0_.1, s32[2]{0:T(128)} %refs_1_.1, ...), custom_call_target="tpu_custom_call" | custom-call | tf_op jit(solution)/shard_map/pallas_call | solution.py:91
  2.0 3.0 %collective-permute-start = (bf16[144,256]{1,0:T(8,128)(2,1)S(1)}, bf16[144,256]{1,0:T(8,128)(2,1)S(1)}, u32[]{:S(2)}, u32[]{:S(2)}) collective-permute-start(bf16[144,256]{1,0:T(8,128)(2,1)S(1)} %get-tuple-element.27), channel_id=1, source_target_pairs={{0,2},{1,3},{2,0},{3,1},{4,6},{5,7},{6,4},{7,5},{8,10},{9,11},{10,... | collective-permute-start | bytes 221192 | tf_op jit(solution)/shard_map/ppermute | solution.py:106
  5.0 1.5 %collective-permute-start.1 = (bf16[144,256]{1,0:T(8,128)(2,1)S(1)}, bf16[144,256]{1,0:T(8,128)(2,1)S(1)}, u32[]{:S(2)}, u32[]{:S(2)}) collective-permute-start(bf16[144,256]{1,0:T(8,128)(2,1)S(1)} %get-tuple-element.28), channel_id=1, source_target_pairs={{0,4},{1,5},{2,6},{3,7},{4,0},{5,1},{6,2},{7,3},{8,12},{9,13},{10,... | collective-permute-start | bytes 221192 | tf_op jit(solution)/shard_map/ppermute | solution.py:106
  6.5 1.9 %collective-permute-start.10 = (bf16[2,64,1024]{2,1,0:T(8,128)(2,1)S(1)}, bf16[2,64,1024]{2,1,0:T(8,128)(2,1)S(1)}, u32[]{:S(2)}, u32[]{:S(2)}) collective-permute-start(bf16[2,64,1024]{2,1,0:T(8,128)(2,1)S(1)} %get-tuple-element.32.t0), channel_id=1, source_target_pairs={{0,2},{1,3},{2,0},{3,1},{4,6},{5,7},{6,4},{7,5},{8,10},{9,11},{10,... | collective-permute-start | bytes 786440 | tf_op jit(solution)/shard_map/ppermute | solution.py:106
  8.5 1.5 %collective-permute-start.11 = (bf16[2,64,1024]{2,1,0:T(8,128)(2,1)S(1)}, bf16[2,64,1024]{2,1,0:T(8,128)(2,1)S(1)}, u32[]{:S(2)}, u32[]{:S(2)}) collective-permute-start(bf16[2,64,1024]{2,1,0:T(8,128)(2,1)S(1)} %get-tuple-element.33.t2), channel_id=1, source_target_pairs={{0,4},{1,5},{2,6},{3,7},{4,0},{5,1},{6,2},{7,3},{8,12},{9,13},{10,... | collective-permute-start | bytes 786440 | tf_op jit(solution)/shard_map/ppermute | solution.py:106
  10.0 2.6 %collective-permute-done.2.refs_3_ = bf16[144,256]{1,0:T(8,128)(2,1)S(1)} collective-permute-done((bf16[144,256]{1,0:T(8,128)(2,1)S(1)}, bf16[144,256]{1,0:T(8,128)(2,1)S(1)}, u32[]{:S(2)}, u32[]{:S(2)}) %collective-permute-start.2) | collective-permute-done | bytes 73760 | tf_op jit(solution)/shard_map/ppermute | solution.py:106
  12.6 2.7 %collective-permute-start.4 = (bf16[512,256]{1,0:T(8,128)(2,1)S(1)}, bf16[512,256]{1,0:T(8,128)(2,1)S(1)}, u32[]{:S(2)}, u32[]{:S(2)}) collective-permute-start(bf16[512,256]{1,0:T(8,128)(2,1)S(1)} %get-tuple-element.31.refs_0_), channel_id=1, source_target_pairs={{0,16},{1,17},{2,18},{3,19},{4,20},{5,21},{6,22},{7,23},{8,24},{9,... | collective-permute-start | bytes 786440 | tf_op jit(solution)/shard_map/ppermute | solution.py:106
  15.3 1.6 %collective-permute-start.3 = (bf16[512,256]{1,0:T(8,128)(2,1)S(1)}, bf16[512,256]{1,0:T(8,128)(2,1)S(1)}, u32[]{:S(2)}, u32[]{:S(2)}) collective-permute-start(bf16[512,256]{1,0:T(8,128)(2,1)S(1)} %get-tuple-element.31.refs_0_), channel_id=1, source_target_pairs={{0,8},{1,9},{2,10},{3,11},{4,12},{5,13},{6,14},{7,15},{8,0},{9,1},... | collective-permute-start | bytes 786440 | tf_op jit(solution)/shard_map/ppermute | solution.py:106
  16.9 0.9 %collective-permute-start.12 = (bf16[4,64,1024]{2,1,0:T(8,128)(2,1)S(1)}, bf16[4,64,1024]{2,1,0:T(8,128)(2,1)S(1)}, u32[]{:S(2)}, u32[]{:S(2)}) collective-permute-start(bf16[4,64,1024]{2,1,0:T(8,128)(2,1)S(1)} %get-tuple-element.34.refs_8_), channel_id=1, source_target_pairs={{0,4},{1,5},{2,6},{3,7},{4,0},{5,1},{6,2},{7,3},{8,12},{9,13},{10,... | collective-permute-start | bytes 1572872 | tf_op jit(solution)/shard_map/ppermute | solution.py:106
  17.9 7.0 %collective-permute-done.4.refs_2_ = bf16[512,256]{1,0:T(8,128)(2,1)S(1)} collective-permute-done((bf16[512,256]{1,0:T(8,128)(2,1)S(1)}, bf16[512,256]{1,0:T(8,128)(2,1)S(1)}, u32[]{:S(2)}, u32[]{:S(2)}) %collective-permute-start.4) | collective-permute-done | bytes 262176 | tf_op jit(solution)/shard_map/ppermute | solution.py:106
  24.9 0.6 collective-permute-start.5
  25.5 1.0 %collective-permute-start.18 = (bf16[4,64,1024]{2,1,0:T(8,128)(2,1)S(1)}, bf16[4,64,1024]{2,1,0:T(8,128)(2,1)S(1)}, u32[]{:S(2)}, u32[]{:S(2)}) collective-permute-start(bf16[4,64,1024]{2,1,0:T(8,128)(2,1)S(1)} %get-tuple-element.39.refs_8_), channel_id=1, source_target_pairs={{0,2},{1,3},{2,0},{3,1},{4,6},{5,7},{6,4},{7,5},{8,10},{9,11},{10,... | collective-permute-start | bytes 1572872 | tf_op jit(solution)/shard_map/ppermute | solution.py:106
  26.6 1.4 %collective-permute-done.3.refs_1_ = bf16[512,256]{1,0:T(8,128)(2,1)S(1)} collective-permute-done((bf16[512,256]{1,0:T(8,128)(2,1)S(1)}, bf16[512,256]{1,0:T(8,128)(2,1)S(1)}, u32[]{:S(2)}, u32[]{:S(2)}) %collective-permute-start.3) | collective-permute-done | bytes 262176 | tf_op jit(solution)/shard_map/ppermute | solution.py:106
  27.9 5.4 %collective-permute-done.5.refs_3_ = bf16[512,256]{1,0:T(8,128)(2,1)S(1)} collective-permute-done((bf16[512,256]{1,0:T(8,128)(2,1)S(1)}, bf16[512,256]{1,0:T(8,128)(2,1)S(1)}, u32[]{:S(2)}, u32[]{:S(2)}) %collective-permute-start.5) | collective-permute-done | bytes 262176 | tf_op jit(solution)/shard_map/ppermute | solution.py:106
  33.4 1.5 %collective-permute-done.9.refs_7_ = bf16[512,256]{1,0:T(8,128)(2,1)S(1)} collective-permute-done((bf16[512,256]{1,0:T(8,128)(2,1)S(1)}, bf16[512,256]{1,0:T(8,128)(2,1)S(1)}, u32[]{:S(2)}, u32[]{:S(2)}) %collective-permute-start.9) | collective-permute-done | bytes 262176 | tf_op jit(solution)/shard_map/ppermute | solution.py:106
  34.9 1.5 %shard_map.124.p0 = bf16[512,128]{1,0:T(8,128)(2,1)S(1)} custom-call(s32[32,128]{1,0:T(8,128)S(1)} %get-tuple-element.30.places, bf16[512,256]{1,0:T(8,128)(2,1)S(1)} %get-tuple-element.31.refs_0_, bf16[512,256]{1,0:T(8,128)(2,1)S(1)} %collective-permute-done.3.refs_1_, bf16[512,256]{1,0:T(8,128)(2,1)S(1)} %collective-permute-done.4.refs_2_, ...), custom_call_target="tpu_custom_call" | custom-call | tf_op jit(solution)/shard_map/pallas_call | solution.py:91
  36.3 1.0 %collective-permute-start.15 = (bf16[512,128]{1,0:T(8,128)(2,1)S(1)}, bf16[512,128]{1,0:T(8,128)(2,1)S(1)}, u32[]{:S(2)}, u32[]{:S(2)}) collective-permute-start(bf16[512,128]{1,0:T(8,128)(2,1)S(1)} %shard_map.124.p0), channel_id=1, source_target_pairs={{0,6},{1,7},{2,4},{3,5},{4,2},{5,3},{6,0},{7,1},{8,14},{9,15},{10,... | collective-permute-start | bytes 393224 | tf_op jit(solution)/shard_map/ppermute | solution.py:106
  37.4 1.5 %collective-permute-start.14 = (bf16[512,128]{1,0:T(8,128)(2,1)S(1)}, bf16[512,128]{1,0:T(8,128)(2,1)S(1)}, u32[]{:S(2)}, u32[]{:S(2)}) collective-permute-start(bf16[512,128]{1,0:T(8,128)(2,1)S(1)} %shard_map.124.p0), channel_id=1, source_target_pairs={{0,4},{1,5},{2,6},{3,7},{4,0},{5,1},{6,2},{7,3},{8,12},{9,13},{10,... | collective-permute-start | bytes 393224 | tf_op jit(solution)/shard_map/ppermute | solution.py:106
  38.9 1.0 %collective-permute-start.13 = (bf16[512,128]{1,0:T(8,128)(2,1)S(1)}, bf16[512,128]{1,0:T(8,128)(2,1)S(1)}, u32[]{:S(2)}, u32[]{:S(2)}) collective-permute-start(bf16[512,128]{1,0:T(8,128)(2,1)S(1)} %shard_map.124.p0), channel_id=1, source_target_pairs={{0,2},{1,3},{2,0},{3,1},{4,6},{5,7},{6,4},{7,5},{8,10},{9,11},{10,... | collective-permute-start | bytes 393224 | tf_op jit(solution)/shard_map/ppermute | solution.py:106
  39.9 1.5 %shard_map.126.p0 = bf16[512,128]{1,0:T(8,128)(2,1)S(1)} custom-call(s32[32,128]{1,0:T(8,128)S(1)} %get-tuple-element.30.places, bf16[512,256]{1,0:T(8,128)(2,1)S(1)} %get-tuple-element.31.refs_0_, bf16[512,256]{1,0:T(8,128)(2,1)S(1)} %collective-permute-done.3.refs_1_, bf16[512,256]{1,0:T(8,128)(2,1)S(1)} %collective-permute-done.4.refs_2_, ...), custom_call_target="tpu_custom_call" | custom-call | tf_op jit(solution)/shard_map/pallas_call | solution.py:91
  41.4 1.0 %collective-permute-start.21 = (bf16[512,128]{1,0:T(8,128)(2,1)S(1)}, bf16[512,128]{1,0:T(8,128)(2,1)S(1)}, u32[]{:S(2)}, u32[]{:S(2)}) collective-permute-start(bf16[512,128]{1,0:T(8,128)(2,1)S(1)} %shard_map.126.p0), channel_id=1, source_target_pairs={{0,6},{1,7},{2,4},{3,5},{4,2},{5,3},{6,0},{7,1},{8,14},{9,15},{10,... | collective-permute-start | bytes 393224 | tf_op jit(solution)/shard_map/ppermute | solution.py:106
  42.4 1.5 %collective-permute-start.20 = (bf16[512,128]{1,0:T(8,128)(2,1)S(1)}, bf16[512,128]{1,0:T(8,128)(2,1)S(1)}, u32[]{:S(2)}, u32[]{:S(2)}) collective-permute-start(bf16[512,128]{1,0:T(8,128)(2,1)S(1)} %shard_map.126.p0), channel_id=1, source_target_pairs={{0,4},{1,5},{2,6},{3,7},{4,0},{5,1},{6,2},{7,3},{8,12},{9,13},{10,... | collective-permute-start | bytes 393224 | tf_op jit(solution)/shard_map/ppermute | solution.py:106
  43.9 1.0 %collective-permute-start.19 = (bf16[512,128]{1,0:T(8,128)(2,1)S(1)}, bf16[512,128]{1,0:T(8,128)(2,1)S(1)}, u32[]{:S(2)}, u32[]{:S(2)}) collective-permute-start(bf16[512,128]{1,0:T(8,128)(2,1)S(1)} %shard_map.126.p0), channel_id=1, source_target_pairs={{0,2},{1,3},{2,0},{3,1},{4,6},{5,7},{6,4},{7,5},{8,10},{9,11},{10,... | collective-permute-start | bytes 393224 | tf_op jit(solution)/shard_map/ppermute | solution.py:106
  44.9 1.6 %collective-permute-done.14.p2 = bf16[512,128]{1,0:T(8,128)(2,1)S(1)} collective-permute-done((bf16[512,128]{1,0:T(8,128)(2,1)S(1)}, bf16[512,128]{1,0:T(8,128)(2,1)S(1)}, u32[]{:S(2)}, u32[]{:S(2)}) %collective-permute-start.14) | collective-permute-done | bytes 131104 | tf_op jit(solution)/shard_map/ppermute | solution.py:106
  46.6 0.8 shard_map.125
  47.3 2.0 %collective-permute-done.21.p3 = bf16[512,128]{1,0:T(8,128)(2,1)S(1)} collective-permute-done((bf16[512,128]{1,0:T(8,128)(2,1)S(1)}, bf16[512,128]{1,0:T(8,128)(2,1)S(1)}, u32[]{:S(2)}, u32[]{:S(2)}) %collective-permute-start.21) | collective-permute-done | bytes 131104 | tf_op jit(solution)/shard_map/ppermute | solution.py:106
  49.4 1.7 %collective-permute-done.20.p2 = bf16[512,128]{1,0:T(8,128)(2,1)S(1)} collective-permute-done((bf16[512,128]{1,0:T(8,128)(2,1)S(1)}, bf16[512,128]{1,0:T(8,128)(2,1)S(1)}, u32[]{:S(2)}, u32[]{:S(2)}) %collective-permute-start.20) | collective-permute-done | bytes 131104 | tf_op jit(solution)/shard_map/ppermute | solution.py:106
  51.1 0.7 shard_map.127
  51.9 1.8 %collective-permute-start.17 = (bf16[512,128]{1,0:T(8,128)(2,1)S(1)}, bf16[512,128]{1,0:T(8,128)(2,1)S(1)}, u32[]{:S(2)}, u32[]{:S(2)}) collective-permute-start(bf16[512,128]{1,0:T(8,128)(2,1)S(1)} %get-tuple-element.35.refs_0_), channel_id=1, source_target_pairs={{0,16},{1,17},{2,18},{3,19},{4,20},{5,21},{6,22},{7,23},{8,24},{9,... | collective-permute-start | bytes 393224 | tf_op jit(solution)/shard_map/ppermute | solution.py:106
  53.7 1.9 %collective-permute-start.23 = (bf16[512,128]{1,0:T(8,128)(2,1)S(1)}, bf16[512,128]{1,0:T(8,128)(2,1)S(1)}, u32[]{:S(2)}, u32[]{:S(2)}) collective-permute-start(bf16[512,128]{1,0:T(8,128)(2,1)S(1)} %add_convert_fusion.2), channel_id=1, source_target_pairs={{0,8},{1,9},{2,10},{3,11},{4,12},{5,13},{6,14},{7,15},{8,0},{9,1},... | collective-permute-start | bytes 393224 | tf_op jit(solution)/shard_map/ppermute | solution.py:106
  55.6 0.2 collective-permute-start.16
  55.8 5.8 %collective-permute-done.17.refs_2_ = bf16[512,128]{1,0:T(8,128)(2,1)S(1)} collective-permute-done((bf16[512,128]{1,0:T(8,128)(2,1)S(1)}, bf16[512,128]{1,0:T(8,128)(2,1)S(1)}, u32[]{:S(2)}, u32[]{:S(2)}) %collective-permute-start.17) | collective-permute-done | bytes 131104 | tf_op jit(solution)/shard_map/ppermute | solution.py:106
  61.6 0.9 %collective-permute-done.23 = bf16[512,128]{1,0:T(8,128)(2,1)S(1)} collective-permute-done((bf16[512,128]{1,0:T(8,128)(2,1)S(1)}, bf16[512,128]{1,0:T(8,128)(2,1)S(1)}, u32[]{:S(2)}, u32[]{:S(2)}) %collective-permute-start.23) | collective-permute-done | bytes 131104 | tf_op jit(solution)/shard_map/ppermute | solution.py:106
  62.5 0.4 collective-permute-start.24
  62.9 3.3 %collective-permute-start.29 = (bf16[512,128]{1,0:T(8,128)(2,1)S(1)}, bf16[512,128]{1,0:T(8,128)(2,1)S(1)}, u32[]{:S(2)}, u32[]{:S(2)}) collective-permute-start(bf16[512,128]{1,0:T(8,128)(2,1)S(1)} %add_convert_fusion.1), channel_id=1, source_target_pairs={{0,16},{1,17},{2,18},{3,19},{4,20},{5,21},{6,22},{7,23},{8,24},{9,... | collective-permute-start | bytes 393224 | tf_op jit(solution)/shard_map/ppermute | solution.py:106
  66.2 0.5 collective-permute-start.26
  66.8 3.1 %collective-permute-done.24.refs_3_ = bf16[512,128]{1,0:T(8,128)(2,1)S(1)} collective-permute-done((bf16[512,128]{1,0:T(8,128)(2,1)S(1)}, bf16[512,128]{1,0:T(8,128)(2,1)S(1)}, u32[]{:S(2)}, u32[]{:S(2)}) %collective-permute-start.24) | collective-permute-done | bytes 131104 | tf_op jit(solution)/shard_map/ppermute | solution.py:106
  69.9 1.3 %collective-permute-done.29 = bf16[512,128]{1,0:T(8,128)(2,1)S(1)} collective-permute-done((bf16[512,128]{1,0:T(8,128)(2,1)S(1)}, bf16[512,128]{1,0:T(8,128)(2,1)S(1)}, u32[]{:S(2)}, u32[]{:S(2)}) %collective-permute-start.29) | collective-permute-done | bytes 131104 | tf_op jit(solution)/shard_map/ppermute | solution.py:106
  71.3 1.4 %shard_map.128 = (bf16[640,128]{1,0:T(8,128)(2,1)S(1)}, bf16[640,128]{1,0:T(8,128)(2,1)S(1)}, bf16[640,128]{1,0:T(8,128)(2,1)S(1)}, bf16[640,128]{1,0:T(8,128)(2,1)S(1)}) custom-call(s32[32,128]{1,0:T(8,128)S(1)} %get-tuple-element.30.places, bf16[512,128]{1,0:T(8,128)(2,1)S(1)} %get-tuple-element.35.refs_0_, ...), custom_call_target="tpu_custom_call" | custom-call | tf_op jit(solution)/shard_map/pallas_call | solution.py:91
  72.7 1.6 %collective-permute-start.30 = (bf16[640,128]{1,0:T(8,128)(2,1)S(1)}, bf16[640,128]{1,0:T(8,128)(2,1)S(1)}, u32[]{:S(2)}, u32[]{:S(2)}) collective-permute-start(bf16[640,128]{1,0:T(8,128)(2,1)S(1)} %get-tuple-element.44), channel_id=1, source_target_pairs={{0,2},{1,3},{2,0},{3,1},{4,6},{5,7},{6,4},{7,5},{8,10},{9,11},{10,... | collective-permute-start | bytes 491528 | tf_op jit(solution)/shard_map/ppermute | solution.py:106
  74.3 0.7 collective-permute-start.31
  74.9 1.3 %collective-permute-start.32 = (bf16[640,128]{1,0:T(8,128)(2,1)S(1)}, bf16[640,128]{1,0:T(8,128)(2,1)S(1)}, u32[]{:S(2)}, u32[]{:S(2)}) collective-permute-start(bf16[640,128]{1,0:T(8,128)(2,1)S(1)} %get-tuple-element.46), channel_id=1, source_target_pairs={{0,6},{1,7},{2,4},{3,5},{4,2},{5,3},{6,0},{7,1},{8,14},{9,15},{10,... | collective-permute-start | bytes 491528 | tf_op jit(solution)/shard_map/ppermute | solution.py:106
  76.2 3.6 %collective-permute-done.30.p1.refs_1_ = bf16[640,128]{1,0:T(8,128)(2,1)S(1)} collective-permute-done((bf16[640,128]{1,0:T(8,128)(2,1)S(1)}, bf16[640,128]{1,0:T(8,128)(2,1)S(1)}, u32[]{:S(2)}, u32[]{:S(2)}) %collective-permute-start.30) | collective-permute-done | bytes 163872 | tf_op jit(solution)/shard_map/ppermute | solution.py:106
  79.8 3.4 %collective-permute-done.31.p2.refs_2_ = bf16[640,128]{1,0:T(8,128)(2,1)S(1)} collective-permute-done((bf16[640,128]{1,0:T(8,128)(2,1)S(1)}, bf16[640,128]{1,0:T(8,128)(2,1)S(1)}, u32[]{:S(2)}, u32[]{:S(2)}) %collective-permute-start.31) | collective-permute-done | bytes 163872 | tf_op jit(solution)/shard_map/ppermute | solution.py:106
  83.2 0.5 collective-permute-start.36
  83.8 0.9 %shard_map.129 = bf16[128,512]{1,0:T(8,128)(2,1)} custom-call(s32[1]{0:T(128)} %bitcast.pos, bf16[640,128]{1,0:T(8,128)(2,1)S(1)} %get-tuple-element.43.p0.refs_0_, bf16[640,128]{1,0:T(8,128)(2,1)S(1)} %collective-permute-done.30.p1.refs_1_, bf16[640,128]{1,0:T(8,128)(2,1)S(1)} %collective-permute-done.31.p2.refs_2_, ...), custom_call_target="tpu_custom_call" | custom-call | tf_op jit(solution)/shard_map/pallas_call | solution.py:91
  84.7 0.2 collective-permute-done.36.refs_7_
  84.9 1.4 %shard_map.130 = (f32[512,512]{1,0:T(8,128)}, f32[512,512]{1,0:T(8,128)}) custom-call(s32[1]{0:T(128)} %bitcast.pos, bf16[640,128]{1,0:T(8,128)(2,1)S(1)} %get-tuple-element.43.p0.refs_0_, bf16[640,128]{1,0:T(8,128)(2,1)S(1)} %collective-permute-done.30.p1.refs_1_, bf16[640,128]{1,0:T(8,128)(2,1)S(1)} %collective-permute-done.31.p2.refs_2_, ...), custom_call_target="tpu_custom_call" | custom-call | tf_op jit(solution)/shard_map/pallas_call | solution.py:387
  (43 shorter events, 0.4 us)
Async XLA Ops:
  2.0 8.0 %collective-permute-start = (bf16[144,256]{1,0:T(8,128)(2,1)S(1)}, bf16[144,256]{1,0:T(8,128)(2,1)S(1)}, u32[]{:S(2)}, u32[]{:S(2)}) collective-permute-start(bf16[144,256]{1,0:T(8,128)(2,1)S(1)} %get-tuple-element.27), channel_id=1, source_target_pairs={{0,2},{1,3},{2,0},{3,1},{4,6},{5,7},{6,4},{7,5},{8,10},{9,11},{10,... | collective-permute-start | bytes 221192 | tf_op jit(solution)/shard_map/ppermute | solution.py:106
  5.0 5.0 %collective-permute-start.1 = (bf16[144,256]{1,0:T(8,128)(2,1)S(1)}, bf16[144,256]{1,0:T(8,128)(2,1)S(1)}, u32[]{:S(2)}, u32[]{:S(2)}) collective-permute-start(bf16[144,256]{1,0:T(8,128)(2,1)S(1)} %get-tuple-element.28), channel_id=1, source_target_pairs={{0,4},{1,5},{2,6},{3,7},{4,0},{5,1},{6,2},{7,3},{8,12},{9,13},{10,... | collective-permute-start | bytes 221192 | tf_op jit(solution)/shard_map/ppermute | solution.py:106
  6.5 6.1 %collective-permute-start.2 = (bf16[144,256]{1,0:T(8,128)(2,1)S(1)}, bf16[144,256]{1,0:T(8,128)(2,1)S(1)}, u32[]{:S(2)}, u32[]{:S(2)}) collective-permute-start(bf16[144,256]{1,0:T(8,128)(2,1)S(1)} %get-tuple-element.29), channel_id=1, source_target_pairs={{0,6},{1,7},{2,4},{3,5},{4,2},{5,3},{6,0},{7,1},{8,14},{9,15},{10,... | collective-permute-start | bytes 221192 | tf_op jit(solution)/shard_map/ppermute | solution.py:106
  6.5 10.4 %collective-permute-start.10 = (bf16[2,64,1024]{2,1,0:T(8,128)(2,1)S(1)}, bf16[2,64,1024]{2,1,0:T(8,128)(2,1)S(1)}, u32[]{:S(2)}, u32[]{:S(2)}) collective-permute-start(bf16[2,64,1024]{2,1,0:T(8,128)(2,1)S(1)} %get-tuple-element.32.t0), channel_id=1, source_target_pairs={{0,2},{1,3},{2,0},{3,1},{4,6},{5,7},{6,4},{7,5},{8,10},{9,11},{10,... | collective-permute-start | bytes 786440 | tf_op jit(solution)/shard_map/ppermute | solution.py:106
  8.5 8.4 %collective-permute-start.11 = (bf16[2,64,1024]{2,1,0:T(8,128)(2,1)S(1)}, bf16[2,64,1024]{2,1,0:T(8,128)(2,1)S(1)}, u32[]{:S(2)}, u32[]{:S(2)}) collective-permute-start(bf16[2,64,1024]{2,1,0:T(8,128)(2,1)S(1)} %get-tuple-element.33.t2), channel_id=1, source_target_pairs={{0,4},{1,5},{2,6},{3,7},{4,0},{5,1},{6,2},{7,3},{8,12},{9,13},{10,... | collective-permute-start | bytes 786440 | tf_op jit(solution)/shard_map/ppermute | solution.py:106
  12.6 12.3 %collective-permute-start.4 = (bf16[512,256]{1,0:T(8,128)(2,1)S(1)}, bf16[512,256]{1,0:T(8,128)(2,1)S(1)}, u32[]{:S(2)}, u32[]{:S(2)}) collective-permute-start(bf16[512,256]{1,0:T(8,128)(2,1)S(1)} %get-tuple-element.31.refs_0_), channel_id=1, source_target_pairs={{0,16},{1,17},{2,18},{3,19},{4,20},{5,21},{6,22},{7,23},{8,24},{9,... | collective-permute-start | bytes 786440 | tf_op jit(solution)/shard_map/ppermute | solution.py:106
  15.3 11.3 %collective-permute-start.6 = (bf16[512,256]{1,0:T(8,128)(2,1)S(1)}, bf16[512,256]{1,0:T(8,128)(2,1)S(1)}, u32[]{:S(2)}, u32[]{:S(2)}) collective-permute-start(bf16[512,256]{1,0:T(8,128)(2,1)S(1)} %get-tuple-element.31.refs_0_), channel_id=1, source_target_pairs={{0,1},{1,0},{2,3},{3,2},{4,5},{5,4},{6,7},{7,6},{8,9},{9,8},{10,11... | collective-permute-start | bytes 786440 | tf_op jit(solution)/shard_map/ppermute | solution.py:106
  15.3 12.7 %collective-permute-start.3 = (bf16[512,256]{1,0:T(8,128)(2,1)S(1)}, bf16[512,256]{1,0:T(8,128)(2,1)S(1)}, u32[]{:S(2)}, u32[]{:S(2)}) collective-permute-start(bf16[512,256]{1,0:T(8,128)(2,1)S(1)} %get-tuple-element.31.refs_0_), channel_id=1, source_target_pairs={{0,8},{1,9},{2,10},{3,11},{4,12},{5,13},{6,14},{7,15},{8,0},{9,1},... | collective-permute-start | bytes 786440 | tf_op jit(solution)/shard_map/ppermute | solution.py:106
  16.9 16.4 %collective-permute-start.12 = (bf16[4,64,1024]{2,1,0:T(8,128)(2,1)S(1)}, bf16[4,64,1024]{2,1,0:T(8,128)(2,1)S(1)}, u32[]{:S(2)}, u32[]{:S(2)}) collective-permute-start(bf16[4,64,1024]{2,1,0:T(8,128)(2,1)S(1)} %get-tuple-element.34.refs_8_), channel_id=1, source_target_pairs={{0,4},{1,5},{2,6},{3,7},{4,0},{5,1},{6,2},{7,3},{8,12},{9,13},{10,... | collective-permute-start | bytes 1572872 | tf_op jit(solution)/shard_map/ppermute | solution.py:106
  24.9 8.4 %collective-permute-start.5 = (bf16[512,256]{1,0:T(8,128)(2,1)S(1)}, bf16[512,256]{1,0:T(8,128)(2,1)S(1)}, u32[]{:S(2)}, u32[]{:S(2)}) collective-permute-start(bf16[512,256]{1,0:T(8,128)(2,1)S(1)} %collective-permute-done.4.refs_2_), channel_id=1, source_target_pairs={{0,8},{1,9},{2,10},{3,11},{4,12},{5,13},{6,14},{7,15},{8,0},{9,1},... | collective-permute-start | bytes 786440 | tf_op jit(solution)/shard_map/ppermute | solution.py:106
  25.5 14.4 %collective-permute-start.18 = (bf16[4,64,1024]{2,1,0:T(8,128)(2,1)S(1)}, bf16[4,64,1024]{2,1,0:T(8,128)(2,1)S(1)}, u32[]{:S(2)}, u32[]{:S(2)}) collective-permute-start(bf16[4,64,1024]{2,1,0:T(8,128)(2,1)S(1)} %get-tuple-element.39.refs_8_), channel_id=1, source_target_pairs={{0,2},{1,3},{2,0},{3,1},{4,6},{5,7},{6,4},{7,5},{8,10},{9,11},{10,... | collective-permute-start | bytes 1572872 | tf_op jit(solution)/shard_map/ppermute | solution.py:106
  26.5 6.8 %collective-permute-start.8 = (bf16[512,256]{1,0:T(8,128)(2,1)S(1)}, bf16[512,256]{1,0:T(8,128)(2,1)S(1)}, u32[]{:S(2)}, u32[]{:S(2)}) collective-permute-start(bf16[512,256]{1,0:T(8,128)(2,1)S(1)} %collective-permute-done.4.refs_2_), channel_id=1, source_target_pairs={{0,1},{1,0},{2,3},{3,2},{4,5},{5,4},{6,7},{7,6},{8,9},{9,8},{10,11... | collective-permute-start | bytes 786440 | tf_op jit(solution)/shard_map/ppermute | solution.py:106
  27.9 5.4 %collective-permute-start.7 = (bf16[512,256]{1,0:T(8,128)(2,1)S(1)}, bf16[512,256]{1,0:T(8,128)(2,1)S(1)}, u32[]{:S(2)}, u32[]{:S(2)}) collective-permute-start(bf16[512,256]{1,0:T(8,128)(2,1)S(1)} %collective-permute-done.3.refs_1_), channel_id=1, source_target_pairs={{0,1},{1,0},{2,3},{3,2},{4,5},{5,4},{6,7},{7,6},{8,9},{9,8},{10,11... | collective-permute-start | bytes 786440 | tf_op jit(solution)/shard_map/ppermute | solution.py:106
  33.3 1.5 %collective-permute-start.9 = (bf16[512,256]{1,0:T(8,128)(2,1)S(1)}, bf16[512,256]{1,0:T(8,128)(2,1)S(1)}, u32[]{:S(2)}, u32[]{:S(2)}) collective-permute-start(bf16[512,256]{1,0:T(8,128)(2,1)S(1)} %collective-permute-done.5.refs_3_), channel_id=1, source_target_pairs={{0,1},{1,0},{2,3},{3,2},{4,5},{5,4},{6,7},{7,6},{8,9},{9,8},{10,11... | collective-permute-start | bytes 786440 | tf_op jit(solution)/shard_map/ppermute | solution.py:106
  36.3 10.2 %copy-start.1 = (bf16[512,512]{1,0:T(8,128)(2,1)S(1)}, bf16[512,512]{1,0:T(8,128)(2,1)}, u32[]{:S(2)}) copy-start(bf16[512,512]{1,0:T(8,128)(2,1)} %w_first.1) | copy-start | bytes 1572868
  36.3 7.6 %collective-permute-start.15 = (bf16[512,128]{1,0:T(8,128)(2,1)S(1)}, bf16[512,128]{1,0:T(8,128)(2,1)S(1)}, u32[]{:S(2)}, u32[]{:S(2)}) collective-permute-start(bf16[512,128]{1,0:T(8,128)(2,1)S(1)} %shard_map.124.p0), channel_id=1, source_target_pairs={{0,6},{1,7},{2,4},{3,5},{4,2},{5,3},{6,0},{7,1},{8,14},{9,15},{10,... | collective-permute-start | bytes 393224 | tf_op jit(solution)/shard_map/ppermute | solution.py:106
  37.4 9.2 %collective-permute-start.14 = (bf16[512,128]{1,0:T(8,128)(2,1)S(1)}, bf16[512,128]{1,0:T(8,128)(2,1)S(1)}, u32[]{:S(2)}, u32[]{:S(2)}) collective-permute-start(bf16[512,128]{1,0:T(8,128)(2,1)S(1)} %shard_map.124.p0), channel_id=1, source_target_pairs={{0,4},{1,5},{2,6},{3,7},{4,0},{5,1},{6,2},{7,3},{8,12},{9,13},{10,... | collective-permute-start | bytes 393224 | tf_op jit(solution)/shard_map/ppermute | solution.py:106
  38.9 7.7 %collective-permute-start.13 = (bf16[512,128]{1,0:T(8,128)(2,1)S(1)}, bf16[512,128]{1,0:T(8,128)(2,1)S(1)}, u32[]{:S(2)}, u32[]{:S(2)}) collective-permute-start(bf16[512,128]{1,0:T(8,128)(2,1)S(1)} %shard_map.124.p0), channel_id=1, source_target_pairs={{0,2},{1,3},{2,0},{3,1},{4,6},{5,7},{6,4},{7,5},{8,10},{9,11},{10,... | collective-permute-start | bytes 393224 | tf_op jit(solution)/shard_map/ppermute | solution.py:106
  41.4 9.7 %copy-start = (bf16[512,512]{1,0:T(8,128)(2,1)S(1)}, bf16[512,512]{1,0:T(8,128)(2,1)}, u32[]{:S(2)}) copy-start(bf16[512,512]{1,0:T(8,128)(2,1)} %w_second.3) | copy-start | bytes 1572868
  41.4 8.0 %collective-permute-start.21 = (bf16[512,128]{1,0:T(8,128)(2,1)S(1)}, bf16[512,128]{1,0:T(8,128)(2,1)S(1)}, u32[]{:S(2)}, u32[]{:S(2)}) collective-permute-start(bf16[512,128]{1,0:T(8,128)(2,1)S(1)} %shard_map.126.p0), channel_id=1, source_target_pairs={{0,6},{1,7},{2,4},{3,5},{4,2},{5,3},{6,0},{7,1},{8,14},{9,15},{10,... | collective-permute-start | bytes 393224 | tf_op jit(solution)/shard_map/ppermute | solution.py:106
  42.4 8.7 %collective-permute-start.20 = (bf16[512,128]{1,0:T(8,128)(2,1)S(1)}, bf16[512,128]{1,0:T(8,128)(2,1)S(1)}, u32[]{:S(2)}, u32[]{:S(2)}) collective-permute-start(bf16[512,128]{1,0:T(8,128)(2,1)S(1)} %shard_map.126.p0), channel_id=1, source_target_pairs={{0,4},{1,5},{2,6},{3,7},{4,0},{5,1},{6,2},{7,3},{8,12},{9,13},{10,... | collective-permute-start | bytes 393224 | tf_op jit(solution)/shard_map/ppermute | solution.py:106
  43.9 7.1 %collective-permute-start.19 = (bf16[512,128]{1,0:T(8,128)(2,1)S(1)}, bf16[512,128]{1,0:T(8,128)(2,1)S(1)}, u32[]{:S(2)}, u32[]{:S(2)}) collective-permute-start(bf16[512,128]{1,0:T(8,128)(2,1)S(1)} %shard_map.126.p0), channel_id=1, source_target_pairs={{0,2},{1,3},{2,0},{3,1},{4,6},{5,7},{6,4},{7,5},{8,10},{9,11},{10,... | collective-permute-start | bytes 393224 | tf_op jit(solution)/shard_map/ppermute | solution.py:106
  51.8 1.9 %collective-permute-start.22 = (f32[512,128]{1,0:T(8,128)S(1)}, f32[512,128]{1,0:T(8,128)S(1)}, u32[]{:S(2)}, u32[]{:S(2)}) collective-permute-start(f32[512,128]{1,0:T(8,128)S(1)} %get-tuple-element.41), channel_id=1, source_target_pairs={{0,1},{1,0},{2,3},{3,2},{4,5},{5,4},{6,7},{7,6},{8,9},{9,8},{10,11... | collective-permute-start | bytes 786440 | tf_op jit(solution)/shard_map/ppermute | solution.py:106
  51.9 9.7 %collective-permute-start.17 = (bf16[512,128]{1,0:T(8,128)(2,1)S(1)}, bf16[512,128]{1,0:T(8,128)(2,1)S(1)}, u32[]{:S(2)}, u32[]{:S(2)}) collective-permute-start(bf16[512,128]{1,0:T(8,128)(2,1)S(1)} %get-tuple-element.35.refs_0_), channel_id=1, source_target_pairs={{0,16},{1,17},{2,18},{3,19},{4,20},{5,21},{6,22},{7,23},{8,24},{9,... | collective-permute-start | bytes 393224 | tf_op jit(solution)/shard_map/ppermute | solution.py:106
  53.7 8.7 %collective-permute-start.23 = (bf16[512,128]{1,0:T(8,128)(2,1)S(1)}, bf16[512,128]{1,0:T(8,128)(2,1)S(1)}, u32[]{:S(2)}, u32[]{:S(2)}) collective-permute-start(bf16[512,128]{1,0:T(8,128)(2,1)S(1)} %add_convert_fusion.2), channel_id=1, source_target_pairs={{0,8},{1,9},{2,10},{3,11},{4,12},{5,13},{6,14},{7,15},{8,0},{9,1},... | collective-permute-start | bytes 393224 | tf_op jit(solution)/shard_map/ppermute | solution.py:106
  55.6 10.6 %collective-permute-start.16 = (bf16[512,128]{1,0:T(8,128)(2,1)S(1)}, bf16[512,128]{1,0:T(8,128)(2,1)S(1)}, u32[]{:S(2)}, u32[]{:S(2)}) collective-permute-start(bf16[512,128]{1,0:T(8,128)(2,1)S(1)} %get-tuple-element.35.refs_0_), channel_id=1, source_target_pairs={{0,8},{1,9},{2,10},{3,11},{4,12},{5,13},{6,14},{7,15},{8,0},{9,1},... | collective-permute-start | bytes 393224 | tf_op jit(solution)/shard_map/ppermute | solution.py:106
  62.5 7.4 %collective-permute-start.24 = (bf16[512,128]{1,0:T(8,128)(2,1)S(1)}, bf16[512,128]{1,0:T(8,128)(2,1)S(1)}, u32[]{:S(2)}, u32[]{:S(2)}) collective-permute-start(bf16[512,128]{1,0:T(8,128)(2,1)S(1)} %collective-permute-done.17.refs_2_), channel_id=1, source_target_pairs={{0,8},{1,9},{2,10},{3,11},{4,12},{5,13},{6,14},{7,15},{8,0},{9,1},... | collective-permute-start | bytes 393224 | tf_op jit(solution)/shard_map/ppermute | solution.py:106
  62.9 8.3 %collective-permute-start.29 = (bf16[512,128]{1,0:T(8,128)(2,1)S(1)}, bf16[512,128]{1,0:T(8,128)(2,1)S(1)}, u32[]{:S(2)}, u32[]{:S(2)}) collective-permute-start(bf16[512,128]{1,0:T(8,128)(2,1)S(1)} %add_convert_fusion.1), channel_id=1, source_target_pairs={{0,16},{1,17},{2,18},{3,19},{4,20},{5,21},{6,22},{7,23},{8,24},{9,... | collective-permute-start | bytes 393224 | tf_op jit(solution)/shard_map/ppermute | solution.py:106
  66.2 5.0 %collective-permute-start.25 = (bf16[512,128]{1,0:T(8,128)(2,1)S(1)}, bf16[512,128]{1,0:T(8,128)(2,1)S(1)}, u32[]{:S(2)}, u32[]{:S(2)}) collective-permute-start(bf16[512,128]{1,0:T(8,128)(2,1)S(1)} %get-tuple-element.35.refs_0_), channel_id=1, source_target_pairs={{0,1},{1,0},{2,3},{3,2},{4,5},{5,4},{6,7},{7,6},{8,9},{9,8},{10,11... | collective-permute-start | bytes 393224 | tf_op jit(solution)/shard_map/ppermute | solution.py:106
  66.2 5.0 %collective-permute-start.26 = (bf16[512,128]{1,0:T(8,128)(2,1)S(1)}, bf16[512,128]{1,0:T(8,128)(2,1)S(1)}, u32[]{:S(2)}, u32[]{:S(2)}) collective-permute-start(bf16[512,128]{1,0:T(8,128)(2,1)S(1)} %collective-permute-done.16.refs_1_), channel_id=1, source_target_pairs={{0,1},{1,0},{2,3},{3,2},{4,5},{5,4},{6,7},{7,6},{8,9},{9,8},{10,11... | collective-permute-start | bytes 393224 | tf_op jit(solution)/shard_map/ppermute | solution.py:106
  66.8 4.5 %collective-permute-start.27 = (bf16[512,128]{1,0:T(8,128)(2,1)S(1)}, bf16[512,128]{1,0:T(8,128)(2,1)S(1)}, u32[]{:S(2)}, u32[]{:S(2)}) collective-permute-start(bf16[512,128]{1,0:T(8,128)(2,1)S(1)} %collective-permute-done.17.refs_2_), channel_id=1, source_target_pairs={{0,1},{1,0},{2,3},{3,2},{4,5},{5,4},{6,7},{7,6},{8,9},{9,8},{10,11... | collective-permute-start | bytes 393224 | tf_op jit(solution)/shard_map/ppermute | solution.py:106
  69.9 1.4 %collective-permute-start.28 = (bf16[512,128]{1,0:T(8,128)(2,1)S(1)}, bf16[512,128]{1,0:T(8,128)(2,1)S(1)}, u32[]{:S(2)}, u32[]{:S(2)}) collective-permute-start(bf16[512,128]{1,0:T(8,128)(2,1)S(1)} %collective-permute-done.24.refs_3_), channel_id=1, source_target_pairs={{0,1},{1,0},{2,3},{3,2},{4,5},{5,4},{6,7},{7,6},{8,9},{9,8},{10,11... | collective-permute-start | bytes 393224 | tf_op jit(solution)/shard_map/ppermute | solution.py:106
  72.7 7.1 %collective-permute-start.30 = (bf16[640,128]{1,0:T(8,128)(2,1)S(1)}, bf16[640,128]{1,0:T(8,128)(2,1)S(1)}, u32[]{:S(2)}, u32[]{:S(2)}) collective-permute-start(bf16[640,128]{1,0:T(8,128)(2,1)S(1)} %get-tuple-element.44), channel_id=1, source_target_pairs={{0,2},{1,3},{2,0},{3,1},{4,6},{5,7},{6,4},{7,5},{8,10},{9,11},{10,... | collective-permute-start | bytes 491528 | tf_op jit(solution)/shard_map/ppermute | solution.py:106
  74.3 9.0 %collective-permute-start.31 = (bf16[640,128]{1,0:T(8,128)(2,1)S(1)}, bf16[640,128]{1,0:T(8,128)(2,1)S(1)}, u32[]{:S(2)}, u32[]{:S(2)}) collective-permute-start(bf16[640,128]{1,0:T(8,128)(2,1)S(1)} %get-tuple-element.45), channel_id=1, source_target_pairs={{0,4},{1,5},{2,6},{3,7},{4,0},{5,1},{6,2},{7,3},{8,12},{9,13},{10,... | collective-permute-start | bytes 491528 | tf_op jit(solution)/shard_map/ppermute | solution.py:106
  74.9 8.3 %collective-permute-start.32 = (bf16[640,128]{1,0:T(8,128)(2,1)S(1)}, bf16[640,128]{1,0:T(8,128)(2,1)S(1)}, u32[]{:S(2)}, u32[]{:S(2)}) collective-permute-start(bf16[640,128]{1,0:T(8,128)(2,1)S(1)} %get-tuple-element.46), channel_id=1, source_target_pairs={{0,6},{1,7},{2,4},{3,5},{4,2},{5,3},{6,0},{7,1},{8,14},{9,15},{10,... | collective-permute-start | bytes 491528 | tf_op jit(solution)/shard_map/ppermute | solution.py:106
  76.2 8.4 %collective-permute-start.33 = (bf16[640,128]{1,0:T(8,128)(2,1)S(1)}, bf16[640,128]{1,0:T(8,128)(2,1)S(1)}, u32[]{:S(2)}, u32[]{:S(2)}) collective-permute-start(bf16[640,128]{1,0:T(8,128)(2,1)S(1)} %get-tuple-element.43.p0.refs_0_), channel_id=1, source_target_pairs={{0,1},{1,0},{2,3},{3,2},{4,5},{5,4},{6,7},{7,6},{8,9},{9,8},{10,11... | collective-permute-start | bytes 491528 | tf_op jit(solution)/shard_map/ppermute | solution.py:106
  79.8 4.9 %collective-permute-start.34 = (bf16[640,128]{1,0:T(8,128)(2,1)S(1)}, bf16[640,128]{1,0:T(8,128)(2,1)S(1)}, u32[]{:S(2)}, u32[]{:S(2)}) collective-permute-start(bf16[640,128]{1,0:T(8,128)(2,1)S(1)} %collective-permute-done.30.p1.refs_1_), channel_id=1, source_target_pairs={{0,1},{1,0},{2,3},{3,2},{4,5},{5,4},{6,7},{7,6},{8,9},{9,8},{10,11... | collective-permute-start | bytes 491528 | tf_op jit(solution)/shard_map/ppermute | solution.py:106
  83.2 1.4 %collective-permute-start.35 = (bf16[640,128]{1,0:T(8,128)(2,1)S(1)}, bf16[640,128]{1,0:T(8,128)(2,1)S(1)}, u32[]{:S(2)}, u32[]{:S(2)}) collective-permute-start(bf16[640,128]{1,0:T(8,128)(2,1)S(1)} %collective-permute-done.31.p2.refs_2_), channel_id=1, source_target_pairs={{0,1},{1,0},{2,3},{3,2},{4,5},{5,4},{6,7},{7,6},{8,9},{9,8},{10,11... | collective-permute-start | bytes 491528 | tf_op jit(solution)/shard_map/ppermute | solution.py:106
  83.2 1.6 %collective-permute-start.36 = (bf16[640,128]{1,0:T(8,128)(2,1)S(1)}, bf16[640,128]{1,0:T(8,128)(2,1)S(1)}, u32[]{:S(2)}, u32[]{:S(2)}) collective-permute-start(bf16[640,128]{1,0:T(8,128)(2,1)S(1)} %collective-permute-done.32.p3.refs_3_), channel_id=1, source_target_pairs={{0,1},{1,0},{2,3},{3,2},{4,5},{5,4},{6,7},{7,6},{8,9},{9,8},{10,11... | collective-permute-start | bytes 491528 | tf_op jit(solution)/shard_map/ppermute | solution.py:106
